TPU v7x, 32 devices: a whole 2x2x4 slice. The times are simulated.
32 devices in a mesh: dp: 4 (over y, x), seq: 2 (over core), head: 4 (over z).
Axes of the slice: x: 2, y: 2, z: 4, core: 2. Of those that a mesh axis runs over, the one named last changes fastest.
Arguments:
- inputs: bfloat16 [8, 1024, 1024], P('dp', ('seq', 'head')), may hold values from -6 to 6
- cotangent: bfloat16 [8, 1024, 1024], P('dp', ('seq', 'head')), may hold values from -6 to 6
- routes: int32 [2, 8, 1024, 2, 4, 2], P(None, 'dp', ('seq', 'head')), may hold values from 0 to 4, all different within a row
- lengths: int32 [8], P('dp'), may hold values from 1 to 1024, as said below
- matrix: float32 [2, 1024, 13568], P(None, ('dp', 'seq', 'head'))
- matrix_first: float32 [2, 1024, 13568], P(None, ('dp', 'seq', 'head'))
- matrix_second: float32 [2, 1024, 13568], P(None, ('dp', 'seq', 'head'))
- small: float32 [2, 1024, 44], P(None, ('dp', 'seq', 'head'))
- small_first: float32 [2, 1024, 44], P(None, ('dp', 'seq', 'head'))
- small_second: float32 [2, 1024, 44], P(None, ('dp', 'seq', 'head'))
Outputs:
- output: bfloat16 [8, 1024, 1024], P('dp', ('seq', 'head'))
- input_grad: bfloat16 [8, 1024, 1024], P('dp', ('seq', 'head'))
- matrix_grad: float32 [2, 1024, 13568], P(None, ('dp', 'seq', 'head'))
- matrix_new: float32 [2, 1024, 13568], P(None, ('dp', 'seq', 'head'))
- matrix_copy: bfloat16 [2, 1024, 13568], P(None, ('dp', 'seq', 'head'))
- matrix_first_new: float32 [2, 1024, 13568], P(None, ('dp', 'seq', 'head'))
- matrix_second_new: float32 [2, 1024, 13568], P(None, ('dp', 'seq', 'head'))
- small_grad: float32 [2, 1024, 44], P(None, ('dp', 'seq', 'head'))
- small_new: float32 [2, 1024, 44], P(None, ('dp', 'seq', 'head'))
- small_copy: bfloat16 [2, 1024, 44], P(None, ('dp', 'seq', 'head'))
- small_first_new: float32 [2, 1024, 44], P(None, ('dp', 'seq', 'head'))
- small_second_new: float32 [2, 1024, 44], P(None, ('dp', 'seq', 'head'))
- loads: float32 [2, 2, 4, 5], replicated
Inputs may be any that keep to these rules, and one draw needn't show every extreme that they name: `lengths`: in each aligned group of 2 entries (the sequences of one index of dp), one equals 1024. `routes`: each row names 2 different experts.
All inputs are finite; a program needn't handle non-finite values.
Results may differ from a plain program's by a relative error of at most 0.02.
Values may be sent and summed in bfloat16 or wider, within the bound.
A program may use at most 320 MiB of HBM per device.

v0:
```python
import math

import jax
import jax.numpy as jnp
from jax import lax
from jax.sharding import PartitionSpec as P

D = 1024
HEADS = 4
HEAD_DIM = 112
EXPERTS = 5
FF = 4096
LAYERS = 2
STEP = 10


NORM_EPS = 1e-05
BETA_ONE = 0.9
BETA_TWO = 0.95
ADAM_EPS = 1e-08
WEIGHT_DECAY = 0.1
NORM_RATE = 0.5
MASKED = -1e30


def passed_along(value, axis, by):
    devices = lax.axis_size(axis)
    pairs = [(i, i + by) for i in range(devices) if 0 <= i + by < devices]
    return lax.ppermute(value, axis, pairs)


def column_bounds():
    query_end = 2 * HEADS * HEAD_DIM
    value_end = query_end + HEADS * EXPERTS * HEAD_DIM
    output_end = value_end + HEADS * EXPERTS * HEAD_DIM
    return (query_end, value_end, output_end, output_end + FF)


def column_rates(segment):
    query_end, value_end, output_end, up_end = column_bounds()
    column = jnp.arange(up_end + FF)
    inner = D ** (-0.5)
    outer = 0.7 * math.sqrt(segment) / HEAD_DIM
    rates = jnp.where(
        column < value_end,
        inner,
        jnp.where(column < output_end, outer, jnp.where(column < up_end, inner, FF ** (-0.5))),
    )
    return rates.astype(jnp.float32)


def small_rates():
    column = jnp.arange(2 * HEADS * EXPERTS + 4)
    return jnp.where(column < 2 * HEADS * EXPERTS, 0.7 * D ** (-0.5), NORM_RATE).astype(jnp.float32)


def adam_update(weight, grad, first, second, rates, decay):
    first_new = BETA_ONE * first + (1.0 - BETA_ONE) * grad
    second_new = BETA_TWO * second + (1.0 - BETA_TWO) * grad * grad
    first_hat = first_new / (1.0 - BETA_ONE**STEP)
    second_hat = second_new / (1.0 - BETA_TWO**STEP)
    new = weight - rates * (first_hat / (jnp.sqrt(second_hat) + ADAM_EPS) + decay * weight)
    return (new, first_new, second_new)


def rotary_tables(positions):
    half = HEAD_DIM // 2
    inverse = jnp.exp(-math.log(10000.0) * jnp.arange(half, dtype=jnp.float32) / half)
    angle = positions.astype(jnp.float32)[:, None] * inverse[None, :]
    return (jnp.cos(angle), jnp.sin(angle))


def rotate_pairs(tensor, cosines, sines):
    half = tensor.shape[-1] // 2
    first, second = (tensor[..., :half], tensor[..., half:])
    return jnp.concatenate(
        [first * cosines - second * sines, second * cosines + first * sines], axis=-1
    )


def rotate_back(tensor, cosines, sines):
    half = tensor.shape[-1] // 2
    first, second = (tensor[..., :half], tensor[..., half:])
    return jnp.concatenate(
        [first * cosines + second * sines, second * cosines - first * sines], axis=-1
    )


def layer_stats(values):
    mean = jnp.mean(values, axis=-1, keepdims=True)
    centered = values - mean
    variance = jnp.mean(centered * centered, axis=-1, keepdims=True)
    inverse = lax.rsqrt(variance + NORM_EPS)
    return (centered * inverse, inverse)


def norm_back(grad_normed, normed, inverse, gain):
    scaled = grad_normed * gain
    return inverse * (
        scaled
        - jnp.mean(scaled, axis=-1, keepdims=True)
        - normed * jnp.mean(scaled * normed, axis=-1, keepdims=True)
    )


def contract_last(left, right):
    return lax.dot_general(
        left, right, (((1,), (1,)), ((), ())), preferred_element_type=jnp.float32
    )


def contract_first(left, right):
    return lax.dot_general(
        left, right, (((0,), (0,)), ((), ())), preferred_element_type=jnp.float32
    )


def head_major(tensor):
    seq_count, sub_rows, head_total, head_dim = tensor.shape
    return tensor.transpose(0, 2, 1, 3).reshape(seq_count, head_total, sub_rows * head_dim)


def token_major(tensor, sub_rows):
    seq_count, head_total, flat = tensor.shape
    return tensor.reshape(seq_count, head_total, sub_rows, flat // sub_rows).transpose(0, 2, 1, 3)


def expert_columns(attn_w, head_first, local_heads):
    query_end, value_end, output_end, up_end = column_bounds()
    width = attn_w.shape[0]
    per_head = EXPERTS * HEAD_DIM
    value_cols = lax.dynamic_slice_in_dim(
        attn_w[:, query_end:value_end].reshape(width, HEADS, per_head), head_first, local_heads, 1
    ).reshape(width, local_heads * per_head)
    output_cols = lax.dynamic_slice_in_dim(
        attn_w[:, value_end:output_end].reshape(width, HEADS, per_head), head_first, local_heads, 1
    ).reshape(width, local_heads * per_head)
    return (value_cols, output_cols)


def block_scores(query_block, keys, query_pos, key_pos, lengths):
    raw = jnp.einsum("shqc,shkc->shqk", query_block, keys, preferred_element_type=jnp.float32)
    later = key_pos[None, None, :] <= query_pos[None, :, None]
    inside = key_pos[None, None, :] >= 0
    used = (key_pos[None, None, :] < lengths[:, None, None]) | (
        key_pos[None, None, :] == query_pos[None, :, None]
    )
    allowed = later & inside & used
    return jnp.where(allowed[:, None], raw * HEAD_DIM ** (-0.5), MASKED)


def attend_forward(query_heads, keys, values, seq_start, lengths, segment):
    rows = min(512, segment)
    key_pos = seq_start - segment + jnp.arange(2 * segment, dtype=jnp.int32)
    outputs, tops, totals = ([], [], [])
    query_pos = seq_start + 0 + jnp.arange(rows, dtype=jnp.int32)
    scores = block_scores(query_heads, keys, query_pos, key_pos, lengths)
    top = jnp.max(scores, axis=-1, keepdims=True)
    weights = jnp.exp(scores - top)
    total = jnp.sum(weights, axis=-1, keepdims=True)
    probs = (weights / total).astype(jnp.bfloat16)
    outputs.append(jnp.einsum("shqk,shkc->shqc", probs, values, preferred_element_type=jnp.float32))
    tops.append(top)
    totals.append(total)
    return (outputs[0], tops, totals)


def attend_backward(
    query_heads, keys, values, grad_heads, tops, totals, seq_start, lengths, segment
):
    rows = min(512, segment)
    key_pos = seq_start - segment + jnp.arange(2 * segment, dtype=jnp.int32)
    grad_keys = jnp.zeros(keys.shape, jnp.float32)
    grad_values = jnp.zeros(values.shape, jnp.float32)
    grad_queries = []
    for index, start in enumerate(range(0, segment, rows)):
        query_pos = seq_start + start + jnp.arange(rows, dtype=jnp.int32)
        scores = block_scores(query_heads, keys, query_pos, key_pos, lengths)
        probs = jnp.exp(scores - tops[index]) / totals[index]
        grad_probs = jnp.einsum(
            "shqc,shkc->shqk", grad_heads, values, preferred_element_type=jnp.float32
        )
        delta = jnp.sum(probs * grad_probs, axis=-1, keepdims=True)
        grad_raw = (probs * (grad_probs - delta) * HEAD_DIM ** (-0.5)).astype(jnp.bfloat16)
        grad_queries.append(
            jnp.einsum("shqk,shkc->shqc", grad_raw, keys, preferred_element_type=jnp.float32)
        )
        grad_keys = jnp.einsum(
            "shqk,shqc->shkc", grad_raw, query_heads, preferred_element_type=jnp.float32
        )
        grad_values = jnp.einsum(
            "shqk,shqc->shkc",
            probs.astype(jnp.bfloat16),
            grad_heads,
            preferred_element_type=jnp.float32,
        )
    return (grad_queries[0], grad_keys, grad_values)


def gelu_tanh(values):
    return jax.nn.gelu(values, approximate=True)


def local(
    inputs,
    cotangent,
    routes,
    lengths,
    matrix,
    matrix_first,
    matrix_second,
    small,
    small_first,
    small_second,
):
    head_count = lax.axis_size("head")
    seq_count, sub_rows, width = inputs.shape
    segment = sub_rows * head_count
    tokens = seq_count * sub_rows
    block_rows = seq_count * segment
    local_heads = HEADS // head_count
    head_first = lax.axis_index("head") * local_heads
    router_cols = 2 * HEADS * EXPERTS
    expert_cols = HEADS * EXPERTS * HEAD_DIM
    per_head = EXPERTS * HEAD_DIM
    query_end, value_end, output_end, up_end = column_bounds()
    seq_start = lax.axis_index("seq") * segment
    positions = (
        seq_start + lax.axis_index("head") * sub_rows + jnp.arange(sub_rows, dtype=jnp.int32)
    )
    valid = (positions[None, :] < lengths[:, None]).astype(jnp.float32)
    cosines, sines = rotary_tables(positions)
    cosines = cosines[:, None, :]
    sines = sines[:, None, :]
    chosen = jnp.sum(
        (routes[..., None] == jnp.arange(EXPERTS, dtype=jnp.int32)).astype(jnp.float32), axis=-2
    )
    loads = lax.psum(
        jnp.sum(chosen * valid[None, :, :, None, None, None], axis=(1, 2)), ("dp", "seq", "head")
    )
    matrix_low = matrix.astype(jnp.bfloat16)
    small_low = small.astype(jnp.bfloat16)
    split_shape = (seq_count, local_heads, segment, HEAD_DIM)
    flat_shape = (seq_count, local_heads, segment * HEAD_DIM)
    hidden = inputs.astype(jnp.float32).reshape(tokens, width)
    kept = []
    for layer in range(LAYERS):
        attn_w, small_w = (
            lax.all_gather(
                matrix_low[layer, :, :output_end], ("dp", "seq", "head"), axis=0, tiled=True
            ),
            lax.all_gather(small_low[layer], ("dp", "seq", "head"), axis=0, tiled=True),
        )
        gains = small_w[:, router_cols:].astype(jnp.float32)
        normed_one, inverse_one = layer_stats(hidden)
        first_in = (normed_one * gains[:, 0] + gains[:, 1]).astype(jnp.bfloat16)
        query_key = jnp.dot(
            first_in, attn_w[:, :query_end], preferred_element_type=jnp.float32
        ).reshape(seq_count, sub_rows, 2, HEADS, HEAD_DIM)
        query_send = head_major(
            rotate_pairs(query_key[:, :, 0], cosines, sines).astype(jnp.bfloat16)
        )
        key_send = head_major(rotate_pairs(query_key[:, :, 1], cosines, sines).astype(jnp.bfloat16))
        first_blk, chosen_blk = (
            lax.all_gather(
                first_in.reshape(seq_count, sub_rows, width), "head", axis=1, tiled=True
            ),
            lax.all_gather(
                chosen[layer].reshape(seq_count, sub_rows, router_cols).astype(jnp.bfloat16),
                "head",
                axis=1,
                tiled=True,
            ),
        )
        expert_in = first_blk.reshape(block_rows, width)
        value_cols, output_cols = expert_columns(attn_w, head_first, local_heads)
        all_prob = jax.nn.sigmoid(
            jnp.dot(expert_in, small_w[:, :router_cols], preferred_element_type=jnp.float32)
        ).reshape(block_rows, 2, HEADS, EXPERTS)
        gate_prob = lax.dynamic_slice_in_dim(all_prob, head_first, local_heads, 2)
        chosen_here = lax.dynamic_slice_in_dim(
            chosen_blk.astype(jnp.float32).reshape(block_rows, 2, HEADS, EXPERTS),
            head_first,
            local_heads,
            2,
        )
        gates = gate_prob * chosen_here
        projected = jnp.dot(expert_in, value_cols, preferred_element_type=jnp.float32).reshape(
            block_rows, local_heads, EXPERTS, HEAD_DIM
        )
        value_rows = jnp.sum(gates[:, 0, :, :, None] * projected, axis=2).astype(jnp.bfloat16)
        value_heads = (
            value_rows.reshape(seq_count, segment, local_heads, HEAD_DIM)
            .transpose(0, 2, 1, 3)
            .reshape(flat_shape)
        )
        query_heads, key_heads = (
            lax.all_to_all(query_send, "head", split_axis=1, concat_axis=2, tiled=True),
            lax.all_to_all(key_send, "head", split_axis=1, concat_axis=2, tiled=True),
        )
        key_mem, value_mem = passed_along((key_heads, value_heads), "seq", 1)
        query_heads = query_heads.reshape(split_shape)
        keys = jnp.concatenate(
            [key_mem.reshape(split_shape), key_heads.reshape(split_shape)], axis=2
        )
        values = jnp.concatenate(
            [value_mem.reshape(split_shape), value_heads.reshape(split_shape)], axis=2
        )
        attended, tops, totals = attend_forward(
            query_heads, keys, values, seq_start, lengths, segment
        )
        attended_low = attended.astype(jnp.bfloat16)
        attended_rows = attended_low.transpose(0, 2, 1, 3).reshape(
            block_rows, local_heads, HEAD_DIM
        )
        mixed = (
            (gates[:, 1, :, :, None] * attended_rows[:, :, None, :].astype(jnp.float32))
            .astype(jnp.bfloat16)
            .reshape(block_rows, local_heads * per_head)
        )
        out_part = contract_last(mixed, output_cols).reshape(seq_count, segment, width)
        residual = hidden + lax.psum_scatter(
            out_part.astype(jnp.bfloat16), "head", scatter_dimension=1, tiled=True
        ).astype(jnp.float32).reshape(tokens, width)
        ffn_w = lax.all_gather(
            matrix_low[layer, :, output_end:], ("dp", "seq", "head"), axis=0, tiled=True
        )
        normed_two, inverse_two = layer_stats(residual)
        second_in = (normed_two * gains[:, 2] + gains[:, 3]).astype(jnp.bfloat16)
        up = jnp.dot(second_in, ffn_w[:, :FF], preferred_element_type=jnp.float32)
        act = gelu_tanh(up).astype(jnp.bfloat16)
        hidden = residual + contract_last(act, ffn_w[:, FF:])
        kept.append(
            (
                attn_w,
                small_w,
                ffn_w,
                normed_one,
                inverse_one,
                first_in,
                expert_in,
                gate_prob,
                chosen_here,
                gates,
                projected,
                query_heads,
                keys,
                values,
                tops,
                totals,
                attended_rows,
                mixed,
                normed_two,
                inverse_two,
                second_in,
                up,
                act,
            )
        )
    output = hidden.reshape(seq_count, sub_rows, width).astype(jnp.bfloat16)
    grad_hidden = (cotangent.astype(jnp.float32) * valid[:, :, None]).reshape(tokens, width)
    matrix_rows = [None] * LAYERS
    small_rows = [None] * LAYERS
    for layer in reversed(range(LAYERS)):
        (
            attn_w,
            small_w,
            ffn_w,
            normed_one,
            inverse_one,
            first_in,
            expert_in,
            gate_prob,
            chosen_here,
            gates,
            projected,
            query_heads,
            keys,
            values,
            tops,
            totals,
            attended_rows,
            mixed,
            normed_two,
            inverse_two,
            second_in,
            up,
            act,
        ) = kept[layer]
        gains = small_w[:, router_cols:].astype(jnp.float32)
        grad_low = grad_hidden.astype(jnp.bfloat16)
        grad_act = jnp.dot(grad_low, ffn_w[:, FF:], preferred_element_type=jnp.float32)
        gelu_value, gelu_pull = jax.vjp(gelu_tanh, up)
        grad_up = gelu_pull(grad_act)[0].astype(jnp.bfloat16)
        grad_upw = contract_first(second_in, grad_up)
        grad_downw = contract_first(grad_low, act)
        grad_second = contract_last(grad_up, ffn_w[:, :FF])
        gain_two_grad = jnp.sum(grad_second * normed_two, axis=0)
        bias_two_grad = jnp.sum(grad_second, axis=0)
        grad_residual = grad_hidden + norm_back(grad_second, normed_two, inverse_two, gains[:, 2])
        residual_low = grad_residual.astype(jnp.bfloat16)
        value_cols, output_cols = expert_columns(attn_w, head_first, local_heads)
        grad_res_blk = lax.all_gather(
            residual_low.reshape(seq_count, sub_rows, width), "head", axis=1, tiled=True
        ).reshape(block_rows, width)
        grad_mixed = jnp.dot(grad_res_blk, output_cols, preferred_element_type=jnp.float32).reshape(
            block_rows, local_heads, EXPERTS, HEAD_DIM
        )
        grad_outw = contract_first(grad_res_blk, mixed)
        grad_gate_out = jnp.sum(
            grad_mixed * attended_rows[:, :, None, :].astype(jnp.float32), axis=-1
        )
        grad_att_rows = jnp.sum(grad_mixed * gates[:, 1, :, :, None], axis=2).astype(jnp.bfloat16)
        grad_heads_in = grad_att_rows.reshape(seq_count, segment, local_heads, HEAD_DIM).transpose(
            0, 2, 1, 3
        )
        grad_query, grad_keys, grad_values = attend_backward(
            query_heads, keys, values, grad_heads_in, tops, totals, seq_start, lengths, segment
        )
        key_back, value_back = passed_along(
            (
                grad_keys[:, :, :segment].astype(jnp.bfloat16),
                grad_values[:, :, :segment].astype(jnp.bfloat16),
            ),
            "seq",
            -1,
        )
        grad_key_own = (grad_keys[:, :, segment:] + key_back.astype(jnp.float32)).astype(
            jnp.bfloat16
        )
        grad_value_own = (grad_values[:, :, segment:] + value_back.astype(jnp.float32)).astype(
            jnp.bfloat16
        )
        query_ret, key_ret = (
            lax.all_to_all(
                grad_query.astype(jnp.bfloat16).reshape(flat_shape),
                "head",
                split_axis=2,
                concat_axis=1,
                tiled=True,
            ),
            lax.all_to_all(
                grad_key_own.reshape(flat_shape), "head", split_axis=2, concat_axis=1, tiled=True
            ),
        )
        grad_value_rows = (
            grad_value_own.transpose(0, 2, 1, 3)
            .reshape(block_rows, local_heads, HEAD_DIM)
            .astype(jnp.float32)
        )
        grad_query_tok = rotate_back(
            token_major(query_ret, sub_rows).astype(jnp.float32), cosines, sines
        )
        grad_key_tok = rotate_back(
            token_major(key_ret, sub_rows).astype(jnp.float32), cosines, sines
        )
        grad_qk = (
            jnp.stack([grad_query_tok, grad_key_tok], axis=2)
            .astype(jnp.bfloat16)
            .reshape(tokens, query_end)
        )
        rows_here = grad_value_rows.shape[0]
        grad_proj = (
            (gates[:, 0, :, :, None] * grad_value_rows[:, :, None, :])
            .astype(jnp.bfloat16)
            .reshape(rows_here, -1)
        )
        grad_gate_value = jnp.sum(projected * grad_value_rows[:, :, None, :], axis=-1)
        grad_gates = jnp.stack([grad_gate_value, grad_gate_out], axis=1) * chosen_here
        grad_logit = (
            (grad_gates * gate_prob * (1.0 - gate_prob)).astype(jnp.bfloat16).reshape(rows_here, -1)
        )
        grad_valuew = contract_first(expert_in, grad_proj)
        grad_router_part = contract_first(expert_in, grad_logit)
        grad_qkw = contract_first(first_in, grad_qk)
        router_head = lax.dynamic_slice_in_dim(
            small_w[:, :router_cols].reshape(width, 2, HEADS, EXPERTS), head_first, local_heads, 2
        ).reshape(width, 2 * local_heads * EXPERTS)
        expert_back = contract_last(grad_proj, value_cols) + contract_last(grad_logit, router_head)
        grad_first = contract_last(grad_qk, attn_w[:, :query_end]) + lax.psum_scatter(
            expert_back.reshape(seq_count, segment, width).astype(jnp.bfloat16),
            "head",
            scatter_dimension=1,
            tiled=True,
        ).astype(jnp.float32).reshape(tokens, width)
        grad_router = lax.dynamic_update_slice_in_dim(
            jnp.zeros((width, 2, HEADS, EXPERTS), jnp.float32),
            grad_router_part.reshape(width, 2, local_heads, EXPERTS),
            head_first,
            2,
        ).reshape(width, router_cols)
        gain_one_grad = jnp.sum(grad_first * normed_one, axis=0)
        bias_one_grad = jnp.sum(grad_first, axis=0)
        grad_hidden = grad_residual + norm_back(grad_first, normed_one, inverse_one, gains[:, 0])
        small_full = jnp.concatenate(
            [
                grad_router,
                jnp.stack([gain_one_grad, bias_one_grad, gain_two_grad, bias_two_grad], axis=1),
            ],
            axis=1,
        )
        qk_share, small_share, up_share, down_share = (
            lax.psum_scatter(grad_qkw, ("dp", "seq", "head"), scatter_dimension=0, tiled=True),
            lax.psum_scatter(small_full, ("dp", "seq", "head"), scatter_dimension=0, tiled=True),
            lax.psum_scatter(grad_upw, ("dp", "seq", "head"), scatter_dimension=0, tiled=True),
            lax.psum_scatter(grad_downw, ("dp", "seq", "head"), scatter_dimension=0, tiled=True),
        )
        expert_both = jnp.concatenate(
            [
                grad_valuew.reshape(width, local_heads, per_head),
                grad_outw.reshape(width, local_heads, per_head),
            ],
            axis=2,
        )
        expert_sum = lax.psum_scatter(
            expert_both.astype(jnp.bfloat16), ("dp", "seq"), scatter_dimension=0, tiled=True
        ).astype(jnp.float32)
        expert_owned = lax.all_to_all(
            expert_sum.astype(jnp.bfloat16), "head", split_axis=0, concat_axis=1, tiled=True
        ).astype(expert_sum.dtype)
        value_share = expert_owned[:, :, :per_head].reshape(expert_owned.shape[0], expert_cols)
        out_share = expert_owned[:, :, per_head:].reshape(expert_owned.shape[0], expert_cols)
        matrix_rows[layer] = jnp.concatenate(
            [qk_share, value_share, out_share, up_share, down_share], axis=1
        )
        small_rows[layer] = small_share
    input_grad = grad_hidden.reshape(seq_count, sub_rows, width).astype(jnp.bfloat16)
    matrix_grad = jnp.stack(matrix_rows, axis=0)
    small_grad = jnp.stack(small_rows, axis=0)
    matrix_new, matrix_first_new, matrix_second_new = adam_update(
        matrix, matrix_grad, matrix_first, matrix_second, column_rates(segment), WEIGHT_DECAY
    )
    small_new, small_first_new, small_second_new = adam_update(
        small, small_grad, small_first, small_second, small_rates(), 0.0
    )
    return (
        output,
        input_grad,
        matrix_grad,
        matrix_new,
        matrix_new.astype(jnp.bfloat16),
        matrix_first_new,
        matrix_second_new,
        small_grad,
        small_new,
        small_new.astype(jnp.bfloat16),
        small_first_new,
        small_second_new,
        loads,
    )


def solution(mesh):
    in_specs = (
        P("dp", ("seq", "head"), None),
        P("dp", ("seq", "head"), None),
        P(None, "dp", ("seq", "head"), None, None, None),
        P("dp"),
        P(None, ("dp", "seq", "head"), None),
        P(None, ("dp", "seq", "head"), None),
        P(None, ("dp", "seq", "head"), None),
        P(None, ("dp", "seq", "head"), None),
        P(None, ("dp", "seq", "head"), None),
        P(None, ("dp", "seq", "head"), None),
    )
    out_specs = (
        P("dp", ("seq", "head"), None),
        P("dp", ("seq", "head"), None),
        P(None, ("dp", "seq", "head"), None),
        P(None, ("dp", "seq", "head"), None),
        P(None, ("dp", "seq", "head"), None),
        P(None, ("dp", "seq", "head"), None),
        P(None, ("dp", "seq", "head"), None),
        P(None, ("dp", "seq", "head"), None),
        P(None, ("dp", "seq", "head"), None),
        P(None, ("dp", "seq", "head"), None),
        P(None, ("dp", "seq", "head"), None),
        P(None, ("dp", "seq", "head"), None),
        P(),
    )
    return jax.shard_map(local, mesh=mesh, in_specs=in_specs, out_specs=out_specs, check_vma=False)
```

profile of v0, /device:TPU:0, one launch (start us, length us, event | category | flops | bytes accessed | tf_op | source)
XLA Modules:
  0.0 4924.9 jit_solution(884512873479707001)
XLA Ops:
  12.3 71.8 %all-gather = bf16[1,1024,44]{2,1,0:T(8,128)(2,1)S(1)} all-gather(bf16[1,32,44]{2,1,0:T(8,128)(2,1)S(1)} %get-tuple-element.173), channel_id=2, replica_groups=mesh['dp'=4,'seq'=2,'head'=4] {'dp','seq','head'}, dimensions={1}, use_global_device_ids=true | all-gather | bytes 92928 | tf_op jit(solution)/shard_map/all_gather | solution.py:252
  92.9 9.5 all_gather.38
  103.3 26.5 all-gather.15.cloned.1.call-done
  132.9 88.1 %all-gather.23.cloned.1.call-done = bf16[1,1024,5376]{2,1,0:T(8,128)(2,1)} async-done(((bf16[1,32,5376]{2,1,0:T(8,128)(2,1)}), bf16[1,1024,5376]{2,1,0:T(8,128)(2,1)}) %all-gather.23.cloned.1.call-update) | async-done | bytes 11010064 | tf_op jit(solution)/shard_map/all_gather | solution.py:249
  221.0 14.7 copy.361
  237.4 8.3 fusion.265
  278.8 5.1 fusion.273
  296.1 71.9 %all-gather.3 = bf16[1,1024,44]{2,1,0:T(8,128)(2,1)S(1)} all-gather(bf16[1,32,44]{2,1,0:T(8,128)(2,1)S(1)} %copy-done.109), channel_id=5, replica_groups=mesh['dp'=4,'seq'=2,'head'=4] {'dp','seq','head'}, dimensions={1}, use_global_device_ids=true | all-gather | bytes 92928 | tf_op jit(solution)/shard_map/all_gather | solution.py:252
  373.3 87.1 %all-gather.25.cloned.1.call-done = bf16[1,1024,8192]{2,1,0:T(8,128)(2,1)} async-done(((bf16[1,32,8192]{2,1,0:T(8,128)(2,1)}), bf16[1,1024,8192]{2,1,0:T(8,128)(2,1)}) %all-gather.25.cloned.1.call-update) | async-done | bytes 16777232 | tf_op jit(solution)/shard_map/all_gather | solution.py:325
  460.4 5.7 fusion.18
  466.1 8.0 fusion.274
  475.5 75.5 %all-gather.27.cloned.1.call-done = bf16[1,1024,5376]{2,1,0:T(8,128)(2,1)} async-done(((bf16[1,32,5376]{2,1,0:T(8,128)(2,1)}), bf16[1,1024,5376]{2,1,0:T(8,128)(2,1)}) %all-gather.27.cloned.1.call-update) | async-done | bytes 11010064 | tf_op jit(solution)/shard_map/all_gather | solution.py:249
  551.0 14.8 copy.378
  573.8 16.6 all_gather.43
  591.9 6.3 all-to-all-start.2
  600.4 8.3 fusion.264
  622.7 5.0 fusion.275
  642.8 42.9 reduce-scatter.25.cloned.1.call-done
  687.2 116.3 %all-gather.29.cloned.1.call-done = bf16[1,1024,8192]{2,1,0:T(8,128)(2,1)} async-done(((bf16[1,32,8192]{2,1,0:T(8,128)(2,1)}), bf16[1,1024,8192]{2,1,0:T(8,128)(2,1)}) %all-gather.29.cloned.1.call-update) | async-done | bytes 16777232 | tf_op jit(solution)/shard_map/all_gather | solution.py:325
  803.5 6.0 fusion.10
  823.2 44.2 all-gather.19.cloned.1.call-done
  890.5 11.2 fusion.95
  903.1 11.3 fusion.104
  915.2 44.1 copy.398
  959.8 311.6 %reduce.40 = bf16[57344,2]{1,0:T(8,128)(2,1)} reduce(bf16[57344,1,2]{2,1,0:T(2,128)(2,1)} %bitcast.475, bf16[]{:T(256)} %broadcast.753), dimensions={1}, to_apply=%bitcast.411.reduce_sub_computation | reduce | bytes 458754
  1271.4 32.5 reshape.1429
  1308.2 44.0 copy.403
  1352.2 311.7 %reduce.41 = bf16[57344,2]{1,0:T(8,128)(2,1)} reduce(bf16[57344,1,2]{2,1,0:T(2,128)(2,1)} %bitcast.476, bf16[]{:T(256)} %broadcast.753), dimensions={1}, to_apply=%bitcast.413.reduce_sub_computation | reduce | bytes 458754
  1663.8 32.3 reshape.1431
  1696.1 5.1 all-to-all-start.5
  1701.2 45.5 reshape.1430
  1746.7 52.9 %copy.399 = bf16[2,1,57344]{2,0,1:T(2,128)(2,1)S(1)} copy(bf16[2,1,57344]{0,1,2:T(2,128)(2,1)} %bitcast.477) | data formatting | bytes 458752 | tf_op jit(solution)/shard_map/all_to_all | solution.py:435
  1800.1 45.1 reshape.1432
  1845.2 53.1 %copy.404 = bf16[2,1,57344]{2,0,1:T(2,128)(2,1)S(1)} copy(bf16[2,1,57344]{0,1,2:T(2,128)(2,1)} %bitcast.478) | data formatting | bytes 458752 | tf_op jit(solution)/shard_map/all_to_all | solution.py:442
  1903.7 7.2 fusion.26
  1915.9 47.5 all-gather.21.cloned.1.call-done
  2004.0 11.6 fusion.92
  2017.4 11.3 fusion.101
  2029.4 44.0 copy.412
  2073.4 311.6 %reduce.42 = bf16[57344,2]{1,0:T(8,128)(2,1)} reduce(bf16[57344,1,2]{2,1,0:T(2,128)(2,1)} %bitcast.479, bf16[]{:T(256)} %broadcast.753), dimensions={1}, to_apply=%bitcast.415.reduce_sub_computation | reduce | bytes 458754
  2385.0 32.3 reshape.1433
  2421.7 44.0 copy.417
  2465.7 311.6 %reduce.43 = bf16[57344,2]{1,0:T(8,128)(2,1)} reduce(bf16[57344,1,2]{2,1,0:T(2,128)(2,1)} %bitcast.480, bf16[]{:T(256)} %broadcast.753), dimensions={1}, to_apply=%bitcast.417.reduce_sub_computation | reduce | bytes 458754
  2777.3 32.3 reshape.1435
  2809.6 5.2 all-to-all-start.7
  2819.3 45.5 reshape.1434
  2864.8 52.9 %copy.413 = bf16[2,1,57344]{2,0,1:T(2,128)(2,1)S(1)} copy(bf16[2,1,57344]{0,1,2:T(2,128)(2,1)} %bitcast.481) | data formatting | bytes 458752 | tf_op jit(solution)/shard_map/all_to_all | solution.py:435
  2918.3 45.0 reshape.1436
  2963.3 53.1 %copy.418 = bf16[2,1,57344]{2,0,1:T(2,128)(2,1)S(1)} copy(bf16[2,1,57344]{0,1,2:T(2,128)(2,1)} %bitcast.482) | data formatting | bytes 458752 | tf_op jit(solution)/shard_map/all_to_all | solution.py:442
  3025.2 10.5 fusion.256
  3037.0 9.9 fusion.255
  3051.6 10.5 fusion.186
  3063.1 9.7 fusion.276
  3073.5 40.8 psum.7
  3122.1 8.2 fusion.98
  3142.3 6.7 all-to-all-done.8
  3153.3 5.4 reduce-scatter.47.cloned.1.call-done
  3160.1 141.7 %reduce-scatter.37.cloned.1.call-done = f32[32,896]{1,0:T(8,128)} async-done(((f32[1024,896]{1,0:T(8,128)}), f32[32,896]{1,0:T(8,128)}) %reduce-scatter.37.cloned.1.call-update) | async-done | bytes 114704 | tf_op jit(solution)/shard_map/reduce_scatter | solution.py:503
  3301.9 365.0 %reduce-scatter.41.cloned.1.call-done = f32[32,4096]{1,0:T(8,128)} async-done(((f32[1024,4096]{1,0:T(8,128)}), f32[32,4096]{1,0:T(8,128)}) %reduce-scatter.41.cloned.1.call-update) | async-done | bytes 524304 | tf_op jit(solution)/shard_map/reduce_scatter | solution.py:506
  3666.9 364.6 %reduce-scatter.39.cloned.1.call-done = f32[32,4096]{1,0:T(8,128)} async-done(((f32[1024,4096]{1,0:T(8,128)}), f32[32,4096]{1,0:T(8,128)}) %reduce-scatter.39.cloned.1.call-update) | async-done | bytes 524304 | tf_op jit(solution)/shard_map/reduce_scatter | solution.py:505
  4034.1 142.0 %reduce-scatter.31.cloned.1.call-done = f32[32,896]{1,0:T(8,128)} async-done(((f32[1024,896]{1,0:T(8,128)}), f32[32,896]{1,0:T(8,128)}) %reduce-scatter.31.cloned.1.call-update) | async-done | bytes 114704 | tf_op jit(solution)/shard_map/reduce_scatter | solution.py:503
  4176.1 365.1 %reduce-scatter.35.cloned.1.call-done = f32[32,4096]{1,0:T(8,128)} async-done(((f32[1024,4096]{1,0:T(8,128)}), f32[32,4096]{1,0:T(8,128)}) %reduce-scatter.35.cloned.1.call-update) | async-done | bytes 524304 | tf_op jit(solution)/shard_map/reduce_scatter | solution.py:506
  4541.2 364.5 %reduce-scatter.33.cloned.1.call-done = f32[32,4096]{1,0:T(8,128)} async-done(((f32[1024,4096]{1,0:T(8,128)}), f32[32,4096]{1,0:T(8,128)}) %reduce-scatter.33.cloned.1.call-update) | async-done | bytes 524304 | tf_op jit(solution)/shard_map/reduce_scatter | solution.py:505
  4908.2 9.5 fusion.259
  (606 shorter events, 265.2 us)
Async XLA Ops:
  7.2 78.7 %copy-start = (bf16[2,128,1024]{2,1,0:T(8,128)(2,1)S(1)}, bf16[2,128,1024]{2,1,0:T(8,128)(2,1)}, u32[]{:S(2)}) copy-start(bf16[2,128,1024]{2,1,0:T(8,128)(2,1)} %param.10) | copy-start | bytes 1572868
  7.2 122.6 %all-gather.15.cloned.1.call-start = ((), (), s32[]{:S(2)}) async-start(), calls=%async_computation.24 | async-start | bytes 2621440 | tf_op jit(solution)/shard_map/all_gather | solution.py:265
  85.3 286.6 %copy-start.102 = (f32[1024]{0:T(1024)}, f32[1024]{0:T(1024)S(1)}, u32[]{:S(2)}) copy-start(f32[1024]{0:T(1024)S(1)} %get-tuple-element.102) | copy-start | bytes 12292
  87.0 134.0 %all-gather.23.cloned.1.call-start = ((), (), s32[]{:S(2)}) async-start(), calls=%async_computation.38 | async-start | bytes 11354112 | tf_op jit(solution)/shard_map/all_gather | solution.py:249
  102.4 133.3 %copy-start.64 = (f32[1024,2,4,5]{0,3,2,1:T(8,128)}, f32[1024,2,4,5]{0,3,2,1:T(8,128)S(1)}, u32[]{:S(2)}) copy-start(f32[1024,2,4,5]{0,3,2,1:T(8,128)S(1)} %reshape.1374) | copy-start | bytes 491524
  103.3 143.2 %copy-start.56 = (f32[128,56]{0,1:T(8,128)}, f32[128,56]{0,1:T(8,128)S(1)}, u32[]{:S(2)}) copy-start(f32[128,56]{0,1:T(8,128)S(1)} %get-tuple-element.182) | copy-start | bytes 86020
  103.3 143.2 %copy-start.60 = (f32[128,56]{0,1:T(8,128)}, f32[128,56]{0,1:T(8,128)S(1)}, u32[]{:S(2)}) copy-start(f32[128,56]{0,1:T(8,128)S(1)} %get-tuple-element.183) | copy-start | bytes 86020
  132.2 103.5 %copy-start.66 = (f32[1024,2,4,5]{0,3,2,1:T(8,128)}, f32[1024,2,4,5]{0,3,2,1:T(8,128)S(1)}, u32[]{:S(2)}) copy-start(f32[1024,2,4,5]{0,3,2,1:T(8,128)S(1)} %reshape.1304) | copy-start | bytes 491524
  248.0 13.4 all-to-all-start.1
  258.6 15.3 collective-permute-start.1
  261.4 15.2 all-to-all-start
  266.2 103.1 %reduce-scatter.23.cloned.1.call-start = ((), (), s32[]{:S(2)}) async-start(), calls=%async_computation.25 | async-start | bytes 2621440 | tf_op jit(solution)/shard_map/reduce_scatter | solution.py:322
  266.2 11.0 collective-permute-start
  294.4 166.0 %all-gather.25.cloned.1.call-start = ((), (), s32[]{:S(2)}) async-start(), calls=%async_computation.39 | async-start | bytes 17301504 | tf_op jit(solution)/shard_map/all_gather | solution.py:325
  295.5 255.6 %all-gather.27.cloned.1.call-start = ((), (), s32[]{:S(2)}) async-start(), calls=%async_computation.40 | async-start | bytes 11354112 | tf_op jit(solution)/shard_map/all_gather | solution.py:249
  296.1 315.7 %all-gather.17.cloned.1.call-start = ((), (), s32[]{:S(2)}) async-start(), calls=%async_computation.26 | async-start | bytes 2621440 | tf_op jit(solution)/shard_map/all_gather | solution.py:265
  369.2 105.2 %copy-start.104 = (f32[1024]{0:T(1024)}, f32[1024]{0:T(1024)S(1)}, u32[]{:S(2)}) copy-start(f32[1024]{0:T(1024)S(1)} %get-tuple-element.101) | copy-start | bytes 12292
  369.2 434.3 %copy-start.96 = (f32[1024]{0:T(1024)}, f32[1024]{0:T(1024)S(1)}, u32[]{:S(2)}) copy-start(f32[1024]{0:T(1024)S(1)} %get-tuple-element.99) | copy-start | bytes 12292
  369.2 452.3 %copy-start.84 = (f32[1024]{0:T(1024)}, f32[1024]{0:T(1024)S(1)}, u32[]{:S(2)}) copy-start(f32[1024]{0:T(1024)S(1)} %get-tuple-element.98) | copy-start | bytes 12292
  370.5 95.5 %copy-start.114 = (f32[256]{0:T(256)}, f32[256]{0:T(256)S(1)}, u32[]{:S(2)}) copy-start(f32[256]{0:T(256)S(1)} %get-tuple-element.180) | copy-start | bytes 3076
  371.9 94.2 %copy-start.116 = (f32[256]{0:T(256)}, f32[256]{0:T(256)S(1)}, u32[]{:S(2)}) copy-start(f32[256]{0:T(256)S(1)} %rsqrt_bitcast_fusion) | copy-start | bytes 3076
  373.3 92.8 %copy-start.34 = (bf16[256,1024]{1,0:T(8,128)(2,1)}, bf16[256,1024]{1,0:T(8,128)(2,1)S(1)}, u32[]{:S(2)}) copy-start(bf16[256,1024]{1,0:T(8,128)(2,1)S(1)} %get-tuple-element.130) | copy-start | bytes 1572868
  474.1 91.7 %copy-start.112 = (f32[256]{0:T(256)}, f32[256]{0:T(256)S(1)}, u32[]{:S(2)}) copy-start(f32[256]{0:T(256)S(1)} %broadcast_multiply_fusion.9) | copy-start | bytes 3076
  474.4 91.4 %copy-start.120 = (f32[256]{0:T(256)}, f32[256]{0:T(256)S(1)}, u32[]{:S(2)}) copy-start(f32[256]{0:T(256)S(1)} %add_rsqrt_fusion.1) | copy-start | bytes 3076
  475.5 90.4 %copy-start.18 = (bf16[256,1024]{1,0:T(8,128)(2,1)S(1)}, bf16[256,1024]{1,0:T(8,128)(2,1)}, u32[]{:S(2)}) copy-start(bf16[256,1024]{1,0:T(8,128)(2,1)} %add_convert_fusion.1) | copy-start | bytes 1572868
  570.3 21.6 all-to-all-start.3
  591.9 18.1 all-to-all-start.2
  598.2 87.5 %reduce-scatter.25.cloned.1.call-start = ((), (), s32[]{:S(2)}) async-start(), calls=%async_computation.27 | async-start | bytes 2621440 | tf_op jit(solution)/shard_map/reduce_scatter | solution.py:322
  598.2 12.3 collective-permute-start.2
  620.7 7.2 collective-permute-start.3
  640.8 162.7 %all-gather.29.cloned.1.call-start = ((), (), s32[]{:S(2)}) async-start(), calls=%async_computation.41 | async-start | bytes 17301504 | tf_op jit(solution)/shard_map/all_gather | solution.py:325
  641.6 225.8 %all-gather.19.cloned.1.call-start = ((), (), s32[]{:S(2)}) async-start(), calls=%async_computation.28 | async-start | bytes 2621440 | tf_op jit(solution)/shard_map/all_gather | solution.py:403
  686.9 134.6 %copy-start.2 = (f32[256,1024]{1,0:T(8,128)}, f32[256,1024]{1,0:T(8,128)S(1)}, u32[]{:S(2)}) copy-start(f32[256,1024]{1,0:T(8,128)S(1)} %get-tuple-element.121) | copy-start | bytes 3145732
  686.9 134.6 %copy-start.106 = (f32[256]{0:T(256)}, f32[256]{0:T(256)S(1)}, u32[]{:S(2)}) copy-start(f32[256]{0:T(256)S(1)} %broadcast_multiply_fusion.8) | copy-start | bytes 3076
  687.2 134.4 %copy-start.110 = (f32[256]{0:T(256)}, f32[256]{0:T(256)S(1)}, u32[]{:S(2)}) copy-start(f32[256]{0:T(256)S(1)} %add_rsqrt_fusion) | copy-start | bytes 3076
  823.1 1076.5 %reduce-scatter.27.cloned.1.call-start = ((), (), s32[]{:S(2)}) async-start(), calls=%async_computation.29 | async-start | bytes 2621440 | tf_op jit(solution)/shard_map/reduce_scatter | solution.py:480
  875.0 3.4 collective-permute-start.5
  901.8 405.6 %collective-permute-start.4 = (bf16[2,1,512,112]{2,3,0,1:T(8,128)(2,1)S(1)}, bf16[2,1,512,112]{2,3,0,1:T(8,128)(2,1)S(1)}, u32[]{:S(2)}, u32[]{:S(2)}) collective-permute-start(bf16[2,1,512,112]{2,3,0,1:T(8,128)(2,1)S(1)} %slice.467), channel_id=1, source_target_pairs={{4,0},{5,1},{6,2},{7,3},{12,8},{13,9},{14,10},{15,11},{20,16},{21,... | collective-permute-start | bytes 688136 | tf_op jit(solution)/shard_map/ppermute | solution.py:29
  1303.8 392.3 %all-to-all-start.4 = ((bf16[4,2,14336]{2,1,0:T(2,128)(2,1)}), bf16[4,2,14336]{2,1,0:T(2,128)(2,1)S(1)}, u32[]{:S(2)}, u32[]{:S(2)}) async-start(bf16[4,2,14336]{2,1,0:T(2,128)(2,1)} %reshape.1429), calls=%async_computation.6 | async-start | bytes 458752 | tf_op jit(solution)/shard_map/all_to_all | solution.py:435
  1696.1 104.0 %all-to-all-start.5 = ((bf16[4,2,14336]{2,1,0:T(2,128)(2,1)}), bf16[4,2,14336]{2,1,0:T(2,128)(2,1)S(1)}, u32[]{:S(2)}, u32[]{:S(2)}) async-start(bf16[4,2,14336]{2,1,0:T(2,128)(2,1)} %reshape.1431), calls=%async_computation.7 | async-start | bytes 458752 | tf_op jit(solution)/shard_map/all_to_all | solution.py:442
  1701.2 262.1 %all-gather.21.cloned.1.call-start = ((), (), s32[]{:S(2)}) async-start(), calls=%async_computation.30 | async-start | bytes 2621440 | tf_op jit(solution)/shard_map/all_gather | solution.py:403
  1845.2 53.7 %copy-start.58 = (f32[128,56]{0,1:T(8,128)S(1)}, f32[128,56]{0,1:T(8,128)}, u32[]{:S(2)}) copy-start(f32[128,56]{0,1:T(8,128)} %copy-done.56) | copy-start | bytes 86020
  1845.2 53.7 %copy-start.62 = (f32[128,56]{0,1:T(8,128)S(1)}, f32[128,56]{0,1:T(8,128)}, u32[]{:S(2)}) copy-start(f32[128,56]{0,1:T(8,128)} %copy-done.60) | copy-start | bytes 86020
  1915.8 50.9 %copy-start.77 = (f32[1024,5]{0,1:T(8,128)S(1)}, f32[1024,5]{0,1:T(8,128)}, u32[]{:S(2)}) copy-start(f32[1024,5]{0,1:T(8,128)} %get-tuple-element.160) | copy-start | bytes 61444
  1915.8 1101.9 %reduce-scatter.29.cloned.1.call-start = ((), (), s32[]{:S(2)}) async-start(), calls=%async_computation.31 | async-start | bytes 2621440 | tf_op jit(solution)/shard_map/reduce_scatter | solution.py:480
  1973.8 3.7 collective-permute-start.7
  1986.4 1128.7 %reduce-scatter.45.cloned.1.call-start = ((), (), s32[]{:S(2)}) async-start(), calls=%async_computation.43 | async-start | bytes 2654208
  1993.6 1139.1 %reduce-scatter.43.cloned.1.call-start = ((), (), s32[]{:S(2)}) async-start(), calls=%async_computation.42 | async-start | bytes 2654208
  2015.6 405.3 %collective-permute-start.6 = (bf16[2,1,512,112]{2,3,0,1:T(8,128)(2,1)S(1)}, bf16[2,1,512,112]{2,3,0,1:T(8,128)(2,1)S(1)}, u32[]{:S(2)}, u32[]{:S(2)}) collective-permute-start(bf16[2,1,512,112]{2,3,0,1:T(8,128)(2,1)S(1)} %slice.465), channel_id=1, source_target_pairs={{4,0},{5,1},{6,2},{7,3},{12,8},{13,9},{14,10},{15,11},{20,16},{21,... | collective-permute-start | bytes 688136 | tf_op jit(solution)/shard_map/ppermute | solution.py:29
  2417.2 392.4 %all-to-all-start.6 = ((bf16[4,2,14336]{2,1,0:T(2,128)(2,1)}), bf16[4,2,14336]{2,1,0:T(2,128)(2,1)S(1)}, u32[]{:S(2)}, u32[]{:S(2)}) async-start(bf16[4,2,14336]{2,1,0:T(2,128)(2,1)} %reshape.1433), calls=%async_computation.9 | async-start | bytes 458752 | tf_op jit(solution)/shard_map/all_to_all | solution.py:435
  2809.6 108.6 %all-to-all-start.7 = ((bf16[4,2,14336]{2,1,0:T(2,128)(2,1)}), bf16[4,2,14336]{2,1,0:T(2,128)(2,1)S(1)}, u32[]{:S(2)}, u32[]{:S(2)}) async-start(bf16[4,2,14336]{2,1,0:T(2,128)(2,1)} %reshape.1435), calls=%async_computation.10 | async-start | bytes 458752 | tf_op jit(solution)/shard_map/all_to_all | solution.py:442
  2814.9 338.5 %reduce-scatter.49.cloned.1.call-start = ((), (), s32[]{:S(2)}) async-start(), calls=%async_computation.45 | async-start | bytes 540672 | tf_op jit(solution)/shard_map/reduce_scatter | solution.py:504
  2818.7 339.9 %reduce-scatter.47.cloned.1.call-start = ((), (), s32[]{:S(2)}) async-start(), calls=%async_computation.44 | async-start | bytes 540672 | tf_op jit(solution)/shard_map/reduce_scatter | solution.py:504
  2963.3 53.7 %copy-start.59 = (f32[128,56]{0,1:T(8,128)S(1)}, f32[128,56]{0,1:T(8,128)}, u32[]{:S(2)}) copy-start(f32[128,56]{0,1:T(8,128)} %copy-done.56) | copy-start | bytes 86020
  2963.3 53.7 %copy-start.63 = (f32[128,56]{0,1:T(8,128)S(1)}, f32[128,56]{0,1:T(8,128)}, u32[]{:S(2)}) copy-start(f32[128,56]{0,1:T(8,128)} %copy-done.60) | copy-start | bytes 86020
  3022.5 279.3 %reduce-scatter.37.cloned.1.call-start = ((), (), s32[]{:S(2)}) async-start(), calls=%async_computation.35 | async-start | bytes 3784704 | tf_op jit(solution)/shard_map/reduce_scatter | solution.py:503
  3025.2 641.7 %reduce-scatter.41.cloned.1.call-start = ((), (), s32[]{:S(2)}) async-start(), calls=%async_computation.37 | async-start | bytes 17301504 | tf_op jit(solution)/shard_map/reduce_scatter | solution.py:506
  3035.8 995.7 %reduce-scatter.39.cloned.1.call-start = ((), (), s32[]{:S(2)}) async-start(), calls=%async_computation.36 | async-start | bytes 17301504 | tf_op jit(solution)/shard_map/reduce_scatter | solution.py:505
  3046.9 1129.2 %reduce-scatter.31.cloned.1.call-start = ((), (), s32[]{:S(2)}) async-start(), calls=%async_computation.32 | async-start | bytes 3784704 | tf_op jit(solution)/shard_map/reduce_scatter | solution.py:503
  3051.5 1489.7 %reduce-scatter.35.cloned.1.call-start = ((), (), s32[]{:S(2)}) async-start(), calls=%async_computation.34 | async-start | bytes 17301504 | tf_op jit(solution)/shard_map/reduce_scatter | solution.py:506
  3062.1 1843.6 %reduce-scatter.33.cloned.1.call-start = ((), (), s32[]{:S(2)}) async-start(), calls=%async_computation.33 | async-start | bytes 17301504 | tf_op jit(solution)/shard_map/reduce_scatter | solution.py:505
  3118.4 13.7 all-to-all-start.9
  3136.1 12.9 all-to-all-start.8
  3153.3 1754.9 %copy-start.4 = (f32[2,32,13568]{2,1,0:T(8,128)S(1)}, f32[2,32,13568]{2,1,0:T(8,128)}, u32[]{:S(2)}) copy-start(f32[2,32,13568]{2,1,0:T(8,128)} %param.14) | copy-start | bytes 10420228
  (113 other events, 871.4 us)
Sparse Core Ops, SparseCore 0:
  87.1 42.6 all-gather.14
  133.2 87.7 all-gather.22
  294.5 47.3 reduce-scatter.22
  345.7 114.6 all-gather.24
  464.0 87.0 all-gather.26
  552.6 53.1 all-gather.16
  640.9 44.7 reduce-scatter.24
  689.3 114.1 all-gather.28
  823.3 44.0 all-gather.18
  887.8 42.5 reduce-scatter.26
  1915.9 47.3 all-gather.20
  1986.5 42.5 reduce-scatter.28
  2033.0 41.8 reduce-scatter.44
  2079.0 42.4 reduce-scatter.42
  2818.9 135.5 reduce-scatter.48
  3022.7 135.9 reduce-scatter.46
  3160.8 141.0 reduce-scatter.36
  3304.1 362.7 reduce-scatter.40
  3669.3 362.1 reduce-scatter.38
  4033.8 142.2 reduce-scatter.30
  4178.4 362.7 reduce-scatter.34
  4543.5 362.1 reduce-scatter.32
where the time goes:
time: 4940 us; the launch traced here: 4920 us
  waiting for transfers between devices  2290 us (46%)
  other arithmetic  1290 us (26%)
  local copies, waits for them, and re-layouts  824 us (17%)
  matrix products  230 us (5%)
  blocking collectives  211 us (4%)
  starting transfers between devices  58.9 us (1%)
    unnamed x7, other arithmetic  1250 us
    reduce_scatter x2, waiting for transfers between devices, local(): lax.psum_scatter(grad_downw, ('dp', 'seq', 'head'), scatter_dimension=0,...  730 us
    reduce_scatter x2, waiting for transfers between devices, local(): lax.psum_scatter(grad_upw, ('dp', 'seq', 'head'), scatter_dimension=0, ti...  729 us
    unnamed x301, local copies, waits for them, and re-layouts  338 us
    reduce_scatter x2, waiting for transfers between devices, local(): lax.psum_scatter(grad_qkw, ('dp', 'seq', 'head'), scatter_dimension=0, ti...  284 us
    all_gather x2, waiting for transfers between devices, local(): lax.all_gather(matrix_low[layer, :, output_end:], ('dp', 'seq', 'head'),...  203 us
    all_gather x2, waiting for transfers between devices, local(): lax.all_gather(matrix_low[layer, :, :output_end], ('dp', 'seq', 'head'),...  164 us
    all_gather x2, blocking collectives, local(): lax.all_gather(small_low[layer], ('dp', 'seq', 'head'), axis=0, tiled=True)  144 us
  transfers between devices with their start and end apart: 40, of which 19 were waited for; matrix products, arithmetic and copies ran while one was open for 44% of the time, Pallas kernels for 0%

commit v1 on v0

v1 whole, which is shorter than its diff:
```python
import math

import jax
import jax.numpy as jnp
from jax import lax
from jax.sharding import PartitionSpec as P

D = 1024
HEADS = 4
HEAD_DIM = 112
EXPERTS = 5
FF = 4096
LAYERS = 2
STEP = 10


NORM_EPS = 1e-05
BETA_ONE = 0.9
BETA_TWO = 0.95
ADAM_EPS = 1e-08
WEIGHT_DECAY = 0.1
NORM_RATE = 0.5
MASKED = -1e30


def passed_along(value, axis, by):
    devices = lax.axis_size(axis)
    pairs = [(i, i + by) for i in range(devices) if 0 <= i + by < devices]
    return lax.ppermute(value, axis, pairs)


def column_bounds():
    query_end = 2 * HEADS * HEAD_DIM
    value_end = query_end + HEADS * EXPERTS * HEAD_DIM
    output_end = value_end + HEADS * EXPERTS * HEAD_DIM
    return (query_end, value_end, output_end, output_end + FF)


def column_rates(segment):
    query_end, value_end, output_end, up_end = column_bounds()
    column = jnp.arange(up_end + FF)
    inner = D ** (-0.5)
    outer = 0.7 * math.sqrt(segment) / HEAD_DIM
    rates = jnp.where(
        column < value_end,
        inner,
        jnp.where(column < output_end, outer, jnp.where(column < up_end, inner, FF ** (-0.5))),
    )
    return rates.astype(jnp.float32)


def small_rates():
    column = jnp.arange(2 * HEADS * EXPERTS + 4)
    return jnp.where(column < 2 * HEADS * EXPERTS, 0.7 * D ** (-0.5), NORM_RATE).astype(jnp.float32)


def adam_update(weight, grad, first, second, rates, decay):
    first_new = BETA_ONE * first + (1.0 - BETA_ONE) * grad
    second_new = BETA_TWO * second + (1.0 - BETA_TWO) * grad * grad
    first_hat = first_new / (1.0 - BETA_ONE**STEP)
    second_hat = second_new / (1.0 - BETA_TWO**STEP)
    new = weight - rates * (first_hat / (jnp.sqrt(second_hat) + ADAM_EPS) + decay * weight)
    return (new, first_new, second_new)


def rotary_tables(positions):
    half = HEAD_DIM // 2
    inverse = jnp.exp(-math.log(10000.0) * jnp.arange(half, dtype=jnp.float32) / half)
    angle = positions.astype(jnp.float32)[:, None] * inverse[None, :]
    return (jnp.cos(angle), jnp.sin(angle))


def rotate_pairs(tensor, cosines, sines):
    half = tensor.shape[-1] // 2
    first, second = (tensor[..., :half], tensor[..., half:])
    return jnp.concatenate(
        [first * cosines - second * sines, second * cosines + first * sines], axis=-1
    )


def rotate_back(tensor, cosines, sines):
    half = tensor.shape[-1] // 2
    first, second = (tensor[..., :half], tensor[..., half:])
    return jnp.concatenate(
        [first * cosines + second * sines, second * cosines - first * sines], axis=-1
    )


def layer_stats(values):
    mean = jnp.mean(values, axis=-1, keepdims=True)
    centered = values - mean
    variance = jnp.mean(centered * centered, axis=-1, keepdims=True)
    inverse = lax.rsqrt(variance + NORM_EPS)
    return (centered * inverse, inverse)


def norm_back(grad_normed, normed, inverse, gain):
    scaled = grad_normed * gain
    return inverse * (
        scaled
        - jnp.mean(scaled, axis=-1, keepdims=True)
        - normed * jnp.mean(scaled * normed, axis=-1, keepdims=True)
    )


def contract_last(left, right):
    return lax.dot_general(
        left, right, (((1,), (1,)), ((), ())), preferred_element_type=jnp.float32
    )


def contract_first(left, right):
    return lax.dot_general(
        left, right, (((0,), (0,)), ((), ())), preferred_element_type=jnp.float32
    )


def reduction_order(tensor):
    dp, seq, head = (lax.axis_size("dp"), lax.axis_size("seq"), lax.axis_size("head"))
    count, width = tensor.shape
    split = tensor.reshape(count, dp, seq, width // (dp * seq))
    return split.transpose(0, 2, 1, 3).reshape(count, width)


def reduce_rows(grad):
    parts = lax.psum_scatter(grad, "seq", scatter_dimension=0, tiled=True)
    parts = lax.psum_scatter(parts, "dp", scatter_dimension=0, tiled=True)
    return lax.psum_scatter(parts, "head", scatter_dimension=0, tiled=True)


def weight_grad(left, right):
    return contract_first(reduction_order(left), right).astype(jnp.bfloat16)


def to_heads(tensor, pieces):
    seq_count, sub_rows = tensor.shape[:2]
    heads = HEADS
    sent = tensor.transpose(3, 2, 0, 1, 4)
    got = lax.all_to_all(sent, "head", split_axis=0, concat_axis=0, tiled=True)
    return got.transpose(1, 2, 0, 3, 4).reshape(pieces, seq_count, heads * sub_rows, HEAD_DIM)


def to_tokens(tensor, sub_rows):
    pieces, seq_count, segment, head_dim = tensor.shape
    sent = tensor.reshape(pieces, seq_count, segment // sub_rows, sub_rows, head_dim)
    sent = sent.transpose(2, 0, 1, 3, 4)
    got = lax.all_to_all(sent, "head", split_axis=0, concat_axis=0, tiled=True)
    return got.transpose(2, 3, 1, 0, 4)


def block_scores(query_block, keys, query_pos, key_pos, lengths):
    raw = jnp.einsum("sqc,skc->sqk", query_block, keys, preferred_element_type=jnp.float32)
    later = key_pos[None, None, :] <= query_pos[None, :, None]
    inside = key_pos[None, None, :] >= 0
    used = (key_pos[None, None, :] < lengths[:, None, None]) | (
        key_pos[None, None, :] == query_pos[None, :, None]
    )
    allowed = later & inside & used
    return jnp.where(allowed, raw * HEAD_DIM ** (-0.5), MASKED)


def attend_forward(query_heads, keys, values, seq_start, lengths, segment):
    rows = min(512, segment)
    key_pos = seq_start - segment + jnp.arange(2 * segment, dtype=jnp.int32)
    outputs, tops, totals = ([], [], [])
    query_pos = seq_start + 0 + jnp.arange(rows, dtype=jnp.int32)
    scores = block_scores(query_heads, keys, query_pos, key_pos, lengths)
    top = jnp.max(scores, axis=-1, keepdims=True)
    weights = jnp.exp(scores - top)
    total = jnp.sum(weights, axis=-1, keepdims=True)
    probs = (weights / total).astype(jnp.bfloat16)
    outputs.append(jnp.einsum("sqk,skc->sqc", probs, values, preferred_element_type=jnp.float32))
    tops.append(top)
    totals.append(total)
    return (outputs[0], tops, totals)


def attend_backward(
    query_heads, keys, values, grad_heads, tops, totals, seq_start, lengths, segment
):
    rows = min(512, segment)
    key_pos = seq_start - segment + jnp.arange(2 * segment, dtype=jnp.int32)
    grad_keys = jnp.zeros(keys.shape, jnp.float32)
    grad_values = jnp.zeros(values.shape, jnp.float32)
    grad_queries = []
    for index, start in enumerate(range(0, segment, rows)):
        query_pos = seq_start + start + jnp.arange(rows, dtype=jnp.int32)
        scores = block_scores(query_heads, keys, query_pos, key_pos, lengths)
        probs = jnp.exp(scores - tops[index]) / totals[index]
        grad_probs = jnp.einsum(
            "sqc,skc->sqk", grad_heads, values, preferred_element_type=jnp.float32
        )
        delta = jnp.sum(probs * grad_probs, axis=-1, keepdims=True)
        grad_raw = (probs * (grad_probs - delta) * HEAD_DIM ** (-0.5)).astype(jnp.bfloat16)
        grad_queries.append(
            jnp.einsum("sqk,skc->sqc", grad_raw, keys, preferred_element_type=jnp.float32)
        )
        grad_keys = jnp.einsum(
            "sqk,sqc->skc", grad_raw, query_heads, preferred_element_type=jnp.float32
        )
        grad_values = jnp.einsum(
            "sqk,sqc->skc",
            probs.astype(jnp.bfloat16),
            grad_heads,
            preferred_element_type=jnp.float32,
        )
    return (grad_queries[0], grad_keys, grad_values)


def gelu_tanh(values):
    return jax.nn.gelu(values, approximate=True)


def local(
    inputs,
    cotangent,
    routes,
    lengths,
    matrix,
    matrix_first,
    matrix_second,
    small,
    small_first,
    small_second,
):
    head_count = lax.axis_size("head")
    seq_count, sub_rows, width = inputs.shape
    segment = sub_rows * head_count
    tokens = seq_count * sub_rows
    router_cols = 2 * HEADS * EXPERTS
    group = HEADS * EXPERTS
    query_end, value_end, output_end, up_end = column_bounds()
    seq_start = lax.axis_index("seq") * segment
    positions = (
        seq_start + lax.axis_index("head") * sub_rows + jnp.arange(sub_rows, dtype=jnp.int32)
    )
    valid = (positions[None, :] < lengths[:, None]).astype(jnp.float32)
    cosines, sines = rotary_tables(positions)
    cosines = cosines[:, None, None, :]
    sines = sines[:, None, None, :]
    chosen = jnp.sum(
        (routes[..., None] == jnp.arange(EXPERTS, dtype=jnp.int32)).astype(jnp.float32), axis=-2
    )
    load_part = jnp.sum(chosen * valid[None, :, :, None, None, None], axis=(1, 2))
    matrix_low = matrix.astype(jnp.bfloat16)
    small_size = small.size
    carried = jnp.concatenate([small.reshape(-1), load_part.reshape(-1)])
    carried = jnp.pad(carried, (0, (-carried.size) % 1024))[None]
    carried = lax.all_gather(carried, ("dp", "seq", "head"), axis=0, tiled=True)
    loads = jnp.sum(carried[:, small_size : small_size + load_part.size], axis=0).reshape(load_part.shape)
    small_all = (
        carried[:, :small_size]
        .reshape(carried.shape[0], LAYERS, small.shape[1], small.shape[2])
        .transpose(1, 0, 2, 3)
        .reshape(LAYERS, width, small.shape[2])
        .astype(jnp.bfloat16)
    )
    hidden = inputs.astype(jnp.float32).reshape(tokens, width)
    kept = []
    gathered = [
        lax.all_gather(part, ("dp", "seq", "head"), axis=0, tiled=True)
        for layer in range(LAYERS)
        for part in (matrix_low[layer, :, :output_end], matrix_low[layer, :, output_end:])
    ]
    for layer in range(LAYERS):
        attn_w, ffn_w = (gathered[2 * layer], gathered[2 * layer + 1])
        small_w = small_all[layer]
        gains = small_w[:, router_cols:].astype(jnp.float32)
        normed_one, inverse_one = layer_stats(hidden)
        first_in = (normed_one * gains[:, 0] + gains[:, 1]).astype(jnp.bfloat16)
        gate_prob = jax.nn.sigmoid(
            jnp.dot(first_in, small_w[:, :router_cols], preferred_element_type=jnp.float32)
        ).reshape(tokens, 2, HEADS, EXPERTS)
        chosen_here = chosen[layer].reshape(tokens, 2, HEADS, EXPERTS)
        gates = gate_prob * chosen_here
        query_key = jnp.dot(
            first_in, attn_w[:, :query_end], preferred_element_type=jnp.float32
        ).reshape(seq_count, sub_rows, 2, HEADS, HEAD_DIM)
        rotated = rotate_pairs(query_key, cosines, sines).astype(jnp.bfloat16)
        projected = jnp.dot(
            first_in, attn_w[:, query_end:value_end], preferred_element_type=jnp.float32
        ).reshape(tokens, HEADS, EXPERTS, HEAD_DIM)
        value_rows = jnp.sum(gates[:, 0, :, :, None] * projected, axis=2).astype(jnp.bfloat16)
        heads_in = to_heads(
            jnp.concatenate(
                [rotated, value_rows.reshape(seq_count, sub_rows, 1, HEADS, HEAD_DIM)], axis=2
            ),
            3,
        )
        memory = passed_along(heads_in[1:], "seq", 1)
        query_heads = heads_in[0]
        keys = jnp.concatenate([memory[0], heads_in[1]], axis=1)
        values = jnp.concatenate([memory[1], heads_in[2]], axis=1)
        attended, tops, totals = attend_forward(
            query_heads, keys, values, seq_start, lengths, segment
        )
        attended_rows = to_tokens(attended.astype(jnp.bfloat16)[None], sub_rows).reshape(
            tokens, HEADS, HEAD_DIM
        )
        mixed = (
            (gates[:, 1, :, :, None] * attended_rows[:, :, None, :].astype(jnp.float32))
            .astype(jnp.bfloat16)
            .reshape(tokens, group * HEAD_DIM)
        )
        residual = hidden + contract_last(mixed, attn_w[:, value_end:])
        normed_two, inverse_two = layer_stats(residual)
        second_in = (normed_two * gains[:, 2] + gains[:, 3]).astype(jnp.bfloat16)
        up = jnp.dot(second_in, ffn_w[:, :FF], preferred_element_type=jnp.float32)
        act = gelu_tanh(up).astype(jnp.bfloat16)
        hidden = residual + contract_last(act, ffn_w[:, FF:])
        kept.append(
            (
                normed_one,
                inverse_one,
                first_in,
                gate_prob,
                chosen_here,
                gates,
                projected,
                query_heads,
                keys,
                values,
                tops,
                totals,
                attended_rows,
                mixed,
                normed_two,
                inverse_two,
                second_in,
                up,
                act,
            )
        )
    output = hidden.reshape(seq_count, sub_rows, width).astype(jnp.bfloat16)
    grad_hidden = (cotangent.astype(jnp.float32) * valid[:, :, None]).reshape(tokens, width)
    matrix_rows = [None] * LAYERS
    small_rows = [None] * LAYERS
    for layer in reversed(range(LAYERS)):
        (
            normed_one,
            inverse_one,
            first_in,
            gate_prob,
            chosen_here,
            gates,
            projected,
            query_heads,
            keys,
            values,
            tops,
            totals,
            attended_rows,
            mixed,
            normed_two,
            inverse_two,
            second_in,
            up,
            act,
        ) = kept[layer]
        attn_w, ffn_w = (gathered[2 * layer], gathered[2 * layer + 1])
        small_w = small_all[layer]
        gains = small_w[:, router_cols:].astype(jnp.float32)
        grad_low = grad_hidden.astype(jnp.bfloat16)
        grad_act = jnp.dot(grad_low, ffn_w[:, FF:], preferred_element_type=jnp.float32)
        gelu_value, gelu_pull = jax.vjp(gelu_tanh, up)
        grad_up = gelu_pull(grad_act)[0].astype(jnp.bfloat16)
        up_share = reduce_rows(weight_grad(second_in, grad_up))
        down_share = reduce_rows(weight_grad(grad_low, act))
        grad_second = contract_last(grad_up, ffn_w[:, :FF])
        gain_two_grad = jnp.sum(grad_second * normed_two, axis=0)
        bias_two_grad = jnp.sum(grad_second, axis=0)
        grad_residual = grad_hidden + norm_back(grad_second, normed_two, inverse_two, gains[:, 2])
        residual_low = grad_residual.astype(jnp.bfloat16)
        grad_mixed = jnp.dot(
            residual_low, attn_w[:, value_end:], preferred_element_type=jnp.float32
        ).reshape(tokens, HEADS, EXPERTS, HEAD_DIM)
        out_share = reduce_rows(weight_grad(residual_low, mixed))
        grad_gate_out = jnp.sum(
            grad_mixed * attended_rows[:, :, None, :].astype(jnp.float32), axis=-1
        )
        grad_att_rows = jnp.sum(grad_mixed * gates[:, 1, :, :, None], axis=2).astype(jnp.bfloat16)
        grad_heads_in = to_heads(
            grad_att_rows.reshape(seq_count, sub_rows, 1, HEADS, HEAD_DIM), 1
        )[0]
        grad_query, grad_keys, grad_values = attend_backward(
            query_heads, keys, values, grad_heads_in, tops, totals, seq_start, lengths, segment
        )
        grad_kv = jnp.stack([grad_keys, grad_values], axis=0)
        kv_back = passed_along(grad_kv[:, :, :segment].astype(jnp.bfloat16), "seq", -1)
        grad_kv_own = (grad_kv[:, :, segment:] + kv_back.astype(jnp.float32)).astype(jnp.bfloat16)
        grads_tok = to_tokens(
            jnp.concatenate([grad_query.astype(jnp.bfloat16)[None], grad_kv_own], axis=0), sub_rows
        )
        grads_tok = grads_tok.astype(jnp.float32)
        grad_qk = (
            rotate_back(grads_tok[:, :, :2], cosines, sines)
            .astype(jnp.bfloat16)
            .reshape(tokens, query_end)
        )
        grad_value_rows = grads_tok[:, :, 2].reshape(tokens, HEADS, HEAD_DIM)
        grad_proj = (
            (gates[:, 0, :, :, None] * grad_value_rows[:, :, None, :])
            .astype(jnp.bfloat16)
            .reshape(tokens, group * HEAD_DIM)
        )
        grad_gate_value = jnp.sum(projected * grad_value_rows[:, :, None, :], axis=-1)
        grad_gates = jnp.stack([grad_gate_value, grad_gate_out], axis=1) * chosen_here
        grad_logit = (
            (grad_gates * gate_prob * (1.0 - gate_prob)).astype(jnp.bfloat16).reshape(tokens, -1)
        )
        grad_in = jnp.concatenate([grad_qk, grad_proj], axis=1)
        grad_first = contract_last(grad_in, attn_w[:, :value_end]) + contract_last(
            grad_logit, small_w[:, :router_cols]
        )
        gain_one_grad = jnp.sum(grad_first * normed_one, axis=0)
        bias_one_grad = jnp.sum(grad_first, axis=0)
        grad_hidden = grad_residual + norm_back(grad_first, normed_one, inverse_one, gains[:, 0])
        norm_grads = jnp.stack(
            [gain_one_grad, bias_one_grad, gain_two_grad, bias_two_grad], axis=1
        )
        side = (-(value_end + router_cols + 4)) % 128
        in_share = reduce_rows(
            jnp.concatenate(
                [
                    weight_grad(first_in, grad_in),
                    weight_grad(first_in, grad_logit),
                    reduction_order(norm_grads.T).T.astype(jnp.bfloat16),
                    jnp.zeros((width, side), jnp.bfloat16),
                ],
                axis=1,
            )
        )
        matrix_rows[layer] = jnp.concatenate(
            [in_share[:, :value_end], out_share, up_share, down_share], axis=1
        ).astype(jnp.float32)
        small_rows[layer] = in_share[:, value_end : value_end + router_cols + 4].astype(jnp.float32)
    input_grad = grad_hidden.reshape(seq_count, sub_rows, width).astype(jnp.bfloat16)
    matrix_grad = jnp.stack(matrix_rows, axis=0)
    small_grad = jnp.stack(small_rows, axis=0)
    matrix_new, matrix_first_new, matrix_second_new = adam_update(
        matrix, matrix_grad, matrix_first, matrix_second, column_rates(segment), WEIGHT_DECAY
    )
    small_new, small_first_new, small_second_new = adam_update(
        small, small_grad, small_first, small_second, small_rates(), 0.0
    )
    return (
        output,
        input_grad,
        matrix_grad,
        matrix_new,
        matrix_new.astype(jnp.bfloat16),
        matrix_first_new,
        matrix_second_new,
        small_grad,
        small_new,
        small_new.astype(jnp.bfloat16),
        small_first_new,
        small_second_new,
        loads,
    )


def solution(mesh):
    in_specs = (
        P("dp", ("seq", "head"), None),
        P("dp", ("seq", "head"), None),
        P(None, "dp", ("seq", "head"), None, None, None),
        P("dp"),
        P(None, ("dp", "seq", "head"), None),
        P(None, ("dp", "seq", "head"), None),
        P(None, ("dp", "seq", "head"), None),
        P(None, ("dp", "seq", "head"), None),
        P(None, ("dp", "seq", "head"), None),
        P(None, ("dp", "seq", "head"), None),
    )
    out_specs = (
        P("dp", ("seq", "head"), None),
        P("dp", ("seq", "head"), None),
        P(None, ("dp", "seq", "head"), None),
        P(None, ("dp", "seq", "head"), None),
        P(None, ("dp", "seq", "head"), None),
        P(None, ("dp", "seq", "head"), None),
        P(None, ("dp", "seq", "head"), None),
        P(None, ("dp", "seq", "head"), None),
        P(None, ("dp", "seq", "head"), None),
        P(None, ("dp", "seq", "head"), None),
        P(None, ("dp", "seq", "head"), None),
        P(None, ("dp", "seq", "head"), None),
        P(),
    )
    return jax.shard_map(local, mesh=mesh, in_specs=in_specs, out_specs=out_specs, check_vma=False)
```

time: 4940 us -> 1520 us (0.31)
  waiting for transfers between devices: 2290 us -> 871 us
  other arithmetic: 1290 us -> 54.4 us
  local copies, waits for them, and re-layouts: 824 us -> 175 us
  blocking collectives: 211 us -> 128 us
    reduce_scatter x12 -> x20, waiting for transfers between devices: 1790 us -> 468 us  [the longest x4 221 us: reduce_rows(): parts = lax.psum_scatter(parts, 'dp', scatter_dimension=0, tiled=True)]
    unnamed x7 -> x1, other arithmetic: 1250 us -> 0.01 us
    all_gather x8 -> x4, waiting for transfers between devices: 485 us -> 141 us  [local(): lax.all_gather(part, ('dp', 'seq', 'head'), axis=0, tiled=True)]
    unnamed x301 -> x259, local copies, waits for them, and re-layouts: 338 us -> 39.9 us
    all_to_all x10 -> x0, local copies, waits for them, and re-layouts: 213 us -> none  [the longest x2 106 us: local(): lax.all_to_all(grad_key_own.reshape(flat_shape), 'head', split_axis=2, co...]
    reshape x42 -> x18, local copies, waits for them, and re-layouts: 196 us -> 7.8 us  [the longest x12 5.86 us: reduction_order(): split = tensor.reshape(count, dp, seq, width // (dp * seq))]
    unnamed x24 -> x32, waiting for transfers between devices: 1.6 us -> 183 us
    all_gather x4 -> x1, blocking collectives: 170 us -> 76.8 us  [local(): carried = lax.all_gather(carried, ('dp', 'seq', 'head'), axis=0, tiled=True)]
  transfers between devices with their start and end apart: 40 -> 37, of which waited for: 19 -> 29; matrix products, arithmetic and copies ran while one was open for 44% -> 21% of each run, Pallas kernels for 0% -> 0%
where the time goes in v1:
time: 1520 us; the launch traced here: 1510 us
  waiting for transfers between devices  871 us (57%)
  matrix products  227 us (15%)
  local copies, waits for them, and re-layouts  175 us (12%)
  blocking collectives  128 us (8%)
  other arithmetic  54.4 us (4%)
  starting transfers between devices  40.4 us (3%)
  between operations  17 us (1%)
    reduce_scatter x4, waiting for transfers between devices, reduce_rows(): parts = lax.psum_scatter(parts, 'dp', scatter_dimension=0, tiled=True)  221 us
    reduce_scatter x8, waiting for transfers between devices, reduce_rows(): return lax.psum_scatter(parts, 'head', scatter_dimension=0, tiled=True)  192 us
    unnamed x32, waiting for transfers between devices  183 us
    all_gather x4, waiting for transfers between devices, local(): lax.all_gather(part, ('dp', 'seq', 'head'), axis=0, tiled=True)  141 us
    all_gather x1, blocking collectives, local(): carried = lax.all_gather(carried, ('dp', 'seq', 'head'), axis=0, tiled=True)  76.8 us
    concatenate x2, local copies, waits for them, and re-layouts, local(): jnp.concatenate([weight_grad(first_in, grad_in), weight_grad(first_in, gr...  59 us
    reduce_scatter x8, waiting for transfers between devices, reduce_rows(): parts = lax.psum_scatter(grad, 'seq', scatter_dimension=0, tiled=True)  55 us
    all_to_all x3, blocking collectives, to_heads(): got = lax.all_to_all(sent, 'head', split_axis=0, concat_axis=0, tiled=True)  51 us
  transfers between devices with their start and end apart: 37, of which 29 were waited for; matrix products, arithmetic and copies ran while one was open for 21% of the time, Pallas kernels for 0%

profile of v1, /device:TPU:0, one launch (start us, length us, event | category | flops | bytes accessed | tf_op | source)
XLA Modules:
  0.0 1513.0 jit_solution(15691872830645147173)
XLA Ops:
  14.0 76.8 %all-gather = f32[98304]{0:T(1024)S(1)} all-gather(f32[3072]{0:T(1024)S(1)} %select_maximum_fusion), channel_id=2, replica_groups=mesh['dp'=4,'seq'=2,'head'=4] {'dp','seq','head'}, dimensions={0}, use_global_device_ids=true | all-gather | bytes 405504 | tf_op jit(solution)/shard_map/all_gather | solution.py:249
  95.8 8.6 all-gather.10.cloned.1.call-done
  104.4 4.8 slice_bitcast_fusion
  109.3 6.6 copy.345
  115.9 5.3 multiply_reduce_fusion.9
  134.6 32.8 %all-to-all-done = bf16[4,3,2,128,112]{3,4,1,2,0:T(8,128)(2,1)S(1)} async-done(((bf16[4,3,2,128,112]{3,4,1,2,0:T(8,128)(2,1)}), bf16[4,3,2,128,112]{3,4,1,2,0:T(8,128)(2,1)S(1)}, u32[]{:S(2)}, u32[]{:S(2)}) %all-to-all-start) | async-done | bytes 688160 | tf_op jit(solution)/shard_map/all_to_all | solution.py:139
  168.8 13.4 collective-permute-start
  183.2 5.0 fusion.205
  197.6 11.2 all-to-all-done.1
  209.6 5.8 fusion.206
  216.0 18.5 %all-gather.12.cloned.1.call-done = bf16[1,1024,8192]{2,1,0:T(8,128)(2,1)} async-done(((bf16[1,32,8192]{2,1,0:T(8,128)(2,1)}), bf16[1,1024,8192]{2,1,0:T(8,128)(2,1)}) %all-gather.12.cloned.1.call-update) | async-done | bytes 16777232 | tf_op jit(solution)/shard_map/all_gather | solution.py:261
  234.5 8.0 fusion.18
  244.1 5.3 fusion.207
  251.6 74.2 %all-gather.14.cloned.1.call-done = bf16[1,1024,5376]{2,1,0:T(8,128)(2,1)} async-done(((bf16[1,32,5376]{2,1,0:T(8,128)(2,1)}), bf16[1,1024,5376]{2,1,0:T(8,128)(2,1)}) %all-gather.14.cloned.1.call-update) | async-done | bytes 11010064 | tf_op jit(solution)/shard_map/all_gather | solution.py:261
  338.8 27.9 %all_to_all.40 = bf16[4,3,2,128,112]{3,4,1,2,0:T(8,128)(2,1)S(1)} all-to-all(bf16[4,3,2,128,112]{3,4,1,2,0:T(8,128)(2,1)S(1)} %copy.360), channel_id=1, replica_groups=mesh['dp'=4,'seq'=2,'head'=4] {'head'}, dimensions={0} | all-to-all | bytes 1376256 | tf_op jit(solution)/shard_map/all_to_all | solution.py:139
  376.8 5.3 fusion.208
  395.5 5.3 all-to-all-done.3
  406.3 5.7 fusion.209
  414.0 40.1 %all-gather.16.cloned.1.call-done = bf16[1,1024,8192]{2,1,0:T(8,128)(2,1)} async-done(((bf16[1,32,8192]{2,1,0:T(8,128)(2,1)}), bf16[1,1024,8192]{2,1,0:T(8,128)(2,1)}) %all-gather.16.cloned.1.call-update) | async-done | bytes 16777232 | tf_op jit(solution)/shard_map/all_gather | solution.py:261
  454.1 6.0 fusion.10
  464.1 5.1 fusion.39
  473.9 6.7 fusion.42
  481.7 11.5 all_to_all.41
  501.8 12.8 fusion.104
  517.7 11.6 fusion.113
  543.1 14.6 all-to-all-done.5
  568.4 5.3 fusion.22
  579.9 29.5 %concatenate.126 = bf16[1024,3200]{0,1:T(8,128)(2,1)} concatenate(bf16[1024,3136]{0,1:T(8,128)(2,1)} %convolution_convert_fusion.2, bf16[1024,40]{0,1:T(8,128)(2,1)S(1)} %convolution_convert_fusion.10, bf16[1024,4]{0,1:T(4,128)(2,1)S(1)} %bitcast.414, bf16[1024,20]{0,1:T(8,128)(2,1)S(1)} %broadcast.475), dimensions={1} | concatenate | bytes 13107200 | tf_op jit(solution)/shard_map/concatenate | solution.py:423
  613.0 8.2 fusion.32
  627.5 6.7 fusion.46
  635.2 11.6 all_to_all.42
  649.8 10.7 fusion.101
  665.6 11.2 fusion.110
  687.3 15.1 all-to-all-done.7
  713.1 5.4 fusion.20
  720.5 4.6 convolution_convert_fusion.5
  725.0 29.4 %concatenate.120 = bf16[1024,3200]{0,1:T(8,128)(2,1)} concatenate(bf16[1024,3136]{0,1:T(8,128)(2,1)} %convolution_convert_fusion.5, bf16[1024,40]{0,1:T(8,128)(2,1)S(1)} %convolution_convert_fusion.11, bf16[1024,4]{0,1:T(4,128)(2,1)S(1)} %bitcast.413, bf16[1024,20]{0,1:T(8,128)(2,1)S(1)} %broadcast.475), dimensions={1} | concatenate | bytes 13107200 | tf_op jit(solution)/shard_map/concatenate | solution.py:423
  761.5 7.8 convolution_convert_fusion.1
  771.2 8.6 convolution_convert_fusion
  786.8 7.4 convolution_convert_fusion.4
  794.3 6.1 copy.411
  801.4 8.4 convolution_convert_fusion.3
  810.0 5.8 copy.403
  824.9 15.9 %reduce-scatter.43.cloned.1.call-done = bf16[512,2240]{0,1:T(8,128)(2,1)} async-done(((bf16[1024,2240]{0,1:T(8,128)(2,1)}), bf16[512,2240]{0,1:T(8,128)(2,1)}) %reduce-scatter.43.cloned.1.call-update) | async-done | bytes 2293776 | tf_op jit(solution)/shard_map/reduce_scatter | solution.py:126
  845.1 16.0 %reduce-scatter.45.cloned.1.call-done = bf16[512,4096]{1,0:T(8,128)(2,1)} async-done(((bf16[1024,4096]{1,0:T(8,128)(2,1)}), bf16[512,4096]{1,0:T(8,128)(2,1)}) %reduce-scatter.45.cloned.1.call-update) | async-done | bytes 4194320 | tf_op jit(solution)/shard_map/reduce_scatter | solution.py:126
  861.2 50.0 %reduce-scatter.81.cloned.1.call-done = bf16[128,3200]{1,0:T(8,128)(2,1)} async-done(((bf16[512,3200]{1,0:T(8,128)(2,1)}), bf16[128,3200]{1,0:T(8,128)(2,1)}) %reduce-scatter.81.cloned.1.call-update) | async-done | bytes 819216
  911.3 19.1 %reduce-scatter.51.cloned.1.call-done = bf16[512,4096]{1,0:T(8,128)(2,1)} async-done(((bf16[1024,4096]{1,0:T(8,128)(2,1)}), bf16[512,4096]{1,0:T(8,128)(2,1)}) %reduce-scatter.51.cloned.1.call-update) | async-done | bytes 4194320 | tf_op jit(solution)/shard_map/reduce_scatter | solution.py:126
  930.5 49.7 %reduce-scatter.73.cloned.1.call-done = bf16[128,3200]{1,0:T(8,128)(2,1)} async-done(((bf16[512,3200]{1,0:T(8,128)(2,1)}), bf16[128,3200]{1,0:T(8,128)(2,1)}) %reduce-scatter.73.cloned.1.call-update) | async-done | bytes 819216
  980.3 40.8 %reduce-scatter.85.cloned.1.call-done = bf16[128,2240]{1,0:T(8,128)(2,1)} async-done(((bf16[512,2240]{1,0:T(8,128)(2,1)}), bf16[128,2240]{1,0:T(8,128)(2,1)}) %reduce-scatter.85.cloned.1.call-update) | async-done | bytes 573456
  1021.2 55.5 %reduce-scatter.63.cloned.1.call-done = bf16[128,4096]{1,0:T(8,128)(2,1)} async-done(((bf16[512,4096]{1,0:T(8,128)(2,1)}), bf16[128,4096]{1,0:T(8,128)(2,1)}) %reduce-scatter.63.cloned.1.call-update) | async-done | bytes 1048592 | tf_op jit(solution)/shard_map/reduce_scatter | solution.py:127
  1076.8 55.7 %reduce-scatter.69.cloned.1.call-done = bf16[128,4096]{1,0:T(8,128)(2,1)} async-done(((bf16[512,4096]{1,0:T(8,128)(2,1)}), bf16[128,4096]{1,0:T(8,128)(2,1)}) %reduce-scatter.69.cloned.1.call-update) | async-done | bytes 1048592 | tf_op jit(solution)/shard_map/reduce_scatter | solution.py:127
  1132.6 40.8 %reduce-scatter.77.cloned.1.call-done = bf16[128,2240]{1,0:T(8,128)(2,1)} async-done(((bf16[512,2240]{1,0:T(8,128)(2,1)}), bf16[128,2240]{1,0:T(8,128)(2,1)}) %reduce-scatter.77.cloned.1.call-update) | async-done | bytes 573456
  1174.2 54.9 %reduce-scatter.47.cloned.1.call-done = bf16[128,4096]{1,0:T(8,128)(2,1)} async-done(((bf16[512,4096]{1,0:T(8,128)(2,1)}), bf16[128,4096]{1,0:T(8,128)(2,1)}) %reduce-scatter.47.cloned.1.call-update) | async-done | bytes 1048592 | tf_op jit(solution)/shard_map/reduce_scatter | solution.py:127
  1230.1 8.3 fusion.107
  1239.7 15.3 %reduce-scatter.83.cloned.1.call-done = bf16[32,3200]{1,0:T(8,128)(2,1)} async-done(((bf16[128,3200]{1,0:T(8,128)(2,1)}), bf16[32,3200]{1,0:T(8,128)(2,1)}) %reduce-scatter.83.cloned.1.call-update) | async-done | bytes 204816 | tf_op jit(solution)/shard_map/reduce_scatter | solution.py:128
  1255.8 54.5 %reduce-scatter.53.cloned.1.call-done = bf16[128,4096]{1,0:T(8,128)(2,1)} async-done(((bf16[512,4096]{1,0:T(8,128)(2,1)}), bf16[128,4096]{1,0:T(8,128)(2,1)}) %reduce-scatter.53.cloned.1.call-update) | async-done | bytes 1048592 | tf_op jit(solution)/shard_map/reduce_scatter | solution.py:127
  1311.9 24.3 %reduce-scatter.75.cloned.1.call-done = bf16[32,3200]{1,0:T(8,128)(2,1)} async-done(((bf16[128,3200]{1,0:T(8,128)(2,1)}), bf16[32,3200]{1,0:T(8,128)(2,1)}) %reduce-scatter.75.cloned.1.call-update) | async-done | bytes 204816 | tf_op jit(solution)/shard_map/reduce_scatter | solution.py:128
  1340.1 19.8 %reduce-scatter.87.cloned.1.call-done = bf16[32,2240]{1,0:T(8,128)(2,1)} async-done(((bf16[128,2240]{1,0:T(8,128)(2,1)}), bf16[32,2240]{1,0:T(8,128)(2,1)}) %reduce-scatter.87.cloned.1.call-update) | async-done | bytes 143376 | tf_op jit(solution)/shard_map/reduce_scatter | solution.py:128
  1359.9 27.7 %reduce-scatter.65.cloned.1.call-done = bf16[32,4096]{1,0:T(8,128)(2,1)} async-done(((bf16[128,4096]{1,0:T(8,128)(2,1)}), bf16[32,4096]{1,0:T(8,128)(2,1)}) %reduce-scatter.65.cloned.1.call-update) | async-done | bytes 262160 | tf_op jit(solution)/shard_map/reduce_scatter | solution.py:128
  1387.6 28.2 %reduce-scatter.71.cloned.1.call-done = bf16[32,4096]{1,0:T(8,128)(2,1)} async-done(((bf16[128,4096]{1,0:T(8,128)(2,1)}), bf16[32,4096]{1,0:T(8,128)(2,1)}) %reduce-scatter.71.cloned.1.call-update) | async-done | bytes 262160 | tf_op jit(solution)/shard_map/reduce_scatter | solution.py:128
  1417.9 20.7 %reduce-scatter.79.cloned.1.call-done = bf16[32,2240]{1,0:T(8,128)(2,1)} async-done(((bf16[128,2240]{1,0:T(8,128)(2,1)}), bf16[32,2240]{1,0:T(8,128)(2,1)}) %reduce-scatter.79.cloned.1.call-update) | async-done | bytes 143376 | tf_op jit(solution)/shard_map/reduce_scatter | solution.py:128
  1438.7 27.6 %reduce-scatter.49.cloned.1.call-done = bf16[32,4096]{1,0:T(8,128)(2,1)} async-done(((bf16[128,4096]{1,0:T(8,128)(2,1)}), bf16[32,4096]{1,0:T(8,128)(2,1)}) %reduce-scatter.49.cloned.1.call-update) | async-done | bytes 262160 | tf_op jit(solution)/shard_map/reduce_scatter | solution.py:128
  1466.3 28.2 %reduce-scatter.55.cloned.1.call-done = bf16[32,4096]{1,0:T(8,128)(2,1)} async-done(((bf16[128,4096]{1,0:T(8,128)(2,1)}), bf16[32,4096]{1,0:T(8,128)(2,1)}) %reduce-scatter.55.cloned.1.call-update) | async-done | bytes 262160 | tf_op jit(solution)/shard_map/reduce_scatter | solution.py:128
  1496.6 9.3 fusion.191
  (555 shorter events, 222.2 us)
Async XLA Ops:
  7.2 97.2 %all-gather.10.cloned.1.call-start = ((), (), s32[]{:S(2)}) async-start(), calls=%async_computation.48 | async-start | bytes 11354112 | tf_op jit(solution)/shard_map/all_gather | solution.py:261
  10.3 83.2 %copy-start = (bf16[2,128,1024]{2,1,0:T(8,128)(2,1)S(1)}, bf16[2,128,1024]{2,1,0:T(8,128)(2,1)}, u32[]{:S(2)}) copy-start(bf16[2,128,1024]{2,1,0:T(8,128)(2,1)} %param.10) | copy-start | bytes 1572868
  10.3 224.1 %all-gather.12.cloned.1.call-start = ((), (), s32[]{:S(2)}) async-start(), calls=%async_computation.49 | async-start | bytes 17301504 | tf_op jit(solution)/shard_map/all_gather | solution.py:261
  11.5 314.3 %all-gather.14.cloned.1.call-start = ((), (), s32[]{:S(2)}) async-start(), calls=%async_computation.50 | async-start | bytes 11354112 | tf_op jit(solution)/shard_map/all_gather | solution.py:261
  12.2 441.9 %all-gather.16.cloned.1.call-start = ((), (), s32[]{:S(2)}) async-start(), calls=%async_computation.51 | async-start | bytes 17301504 | tf_op jit(solution)/shard_map/all_gather | solution.py:261
  93.2 16.1 %copy-start.23 = (bf16[1,32,32,44]{3,2,0,1:T(8,128)(2,1)}, bf16[1,32,32,44]{3,2,0,1:T(8,128)(2,1)S(1)}, u32[]{:S(2)}) copy-start(bf16[1,32,32,44]{3,2,0,1:T(8,128)(2,1)S(1)} %get-tuple-element.137) | copy-start | bytes 270340
  94.6 14.7 copy-start.73
  94.6 14.7 copy-start.75
  95.2 14.1 copy-start.51
  95.2 14.0 copy-start.53
  95.5 20.4 %copy-start.55 = (f32[256,4,5]{0,2,1:T(8,128)}, f32[256,4,5]{0,2,1:T(8,128)S(1)}, u32[]{:S(2)}) copy-start(f32[256,4,5]{0,2,1:T(8,128)S(1)} %get-tuple-element.151) | copy-start | bytes 61444
  95.5 113.8 %copy-start.58 = (f32[256,4,5]{0,2,1:T(8,128)}, f32[256,4,5]{0,2,1:T(8,128)S(1)}, u32[]{:S(2)}) copy-start(f32[256,4,5]{0,2,1:T(8,128)S(1)} %get-tuple-element.150) | copy-start | bytes 61444
  129.6 37.9 %all-to-all-start = ((bf16[4,3,2,128,112]{3,4,1,2,0:T(8,128)(2,1)}), bf16[4,3,2,128,112]{3,4,1,2,0:T(8,128)(2,1)S(1)}, u32[]{:S(2)}, u32[]{:S(2)}) async-start(bf16[4,3,2,128,112]{3,4,1,2,0:T(8,128)(2,1)} %copy.347), calls=%async_computation | async-start | bytes 1376256 | tf_op jit(solution)/shard_map/all_to_all | solution.py:139
  134.6 53.6 %copy-start.50 = (pred[512,1024]{1,0:T(8,128)(4,1)}, pred[512,1024]{1,0:T(8,128)(4,1)S(1)}, u32[]{:S(2)}) copy-start(pred[512,1024]{1,0:T(8,128)(4,1)S(1)} %get-tuple-element.160) | copy-start | bytes 1572868
  168.8 14.3 collective-permute-start
  192.5 16.3 %all-to-all-start.1 = ((bf16[4,1,2,128,112]{3,2,4,1,0:T(2,128)(2,1)}), bf16[4,1,2,128,112]{3,2,4,1,0:T(2,128)(2,1)S(1)}, u32[]{:S(2)}, u32[]{:S(2)}) async-start(bf16[4,1,2,128,112]{3,2,4,1,0:T(2,128)(2,1)} %bitcast.327), calls=%async_computation.1 | async-start | bytes 458752 | tf_op jit(solution)/shard_map/all_to_all | solution.py:147
  215.4 27.0 %copy-start.97 = (f32[256]{0:T(256)}, f32[256]{0:T(256)S(1)}, u32[]{:S(2)}) copy-start(f32[256]{0:T(256)S(1)} %broadcast_multiply_fusion.10) | copy-start | bytes 3076
  215.7 26.8 %copy-start.101 = (f32[256]{0:T(256)}, f32[256]{0:T(256)S(1)}, u32[]{:S(2)}) copy-start(f32[256]{0:T(256)S(1)} %add_rsqrt_fusion.2) | copy-start | bytes 3076
  216.0 18.5 %copy-start.31 = (bf16[256,1024]{1,0:T(8,128)(2,1)}, bf16[256,1024]{1,0:T(8,128)(2,1)S(1)}, u32[]{:S(2)}) copy-start(bf16[256,1024]{1,0:T(8,128)(2,1)S(1)} %add_convert_fusion.4) | copy-start | bytes 1572868
  250.6 81.8 %copy-start.10 = (bf16[256,1024]{1,0:T(8,128)(2,1)}, bf16[256,1024]{1,0:T(8,128)(2,1)S(1)}, u32[]{:S(2)}) copy-start(bf16[256,1024]{1,0:T(8,128)(2,1)S(1)} %add_convert_fusion.3) | copy-start | bytes 1572868
  251.6 78.5 %copy-start.56 = (f32[256,4,5]{0,2,1:T(8,128)}, f32[256,4,5]{0,2,1:T(8,128)S(1)}, u32[]{:S(2)}) copy-start(f32[256,4,5]{0,2,1:T(8,128)S(1)} %get-tuple-element.149) | copy-start | bytes 61444
  369.8 5.8 collective-permute-start.1
  388.2 12.7 all-to-all-start.3
  394.6 11.6 copy-start.5
  412.0 60.6 %copy-start.3 = (f32[256,1024]{1,0:T(8,128)}, f32[256,1024]{1,0:T(8,128)S(1)}, u32[]{:S(2)}) copy-start(f32[256,1024]{1,0:T(8,128)S(1)} %get-tuple-element.179) | copy-start | bytes 3145732
  480.7 17.2 %copy-start.110 = (pred[2,1024]{1,0:T(4,128)(4,1)S(1)}, pred[2,1024]{1,0:T(4,128)(4,1)}, u32[]{:S(2)}) copy-start(pred[2,1024]{1,0:T(4,128)(4,1)} %copy-done.108) | copy-start | bytes 6148
  480.7 17.2 %copy-start.120 = (f32[2,512]{1,0:T(2,128)S(1)}, f32[2,512]{1,0:T(2,128)}, u32[]{:S(2)}) copy-start(f32[2,512]{1,0:T(2,128)} %copy-done.119) | copy-start | bytes 12292
  501.8 12.8 copy-start.22
  516.4 13.7 collective-permute-start.2
  534.9 22.7 %all-to-all-start.5 = ((bf16[4,3,2,128,112]{3,4,1,2,0:T(8,128)(2,1)}), bf16[4,3,2,128,112]{3,4,1,2,0:T(8,128)(2,1)}, u32[]{:S(2)}, u32[]{:S(2)}) async-start(bf16[4,3,2,128,112]{3,4,1,2,0:T(8,128)(2,1)} %copy.368), calls=%async_computation.5 | async-start | bytes 1376256 | tf_op jit(solution)/shard_map/all_to_all | solution.py:147
  539.1 255.2 %reduce-scatter.57.cloned.1.call-start = ((), (), s32[]{:S(2)}) async-start(), calls=%async_computation.40 | async-start | bytes 9830400 | tf_op jit(solution)/shard_map/reduce_scatter | solution.py:126
  540.5 21.9 %copy-start.57 = (f32[256,4,5]{0,2,1:T(8,128)S(1)}, f32[256,4,5]{0,2,1:T(8,128)}, u32[]{:S(2)}) copy-start(f32[256,4,5]{0,2,1:T(8,128)} %copy-done.56) | copy-start | bytes 61444
  634.2 12.9 copy-start.41
  634.2 12.9 copy-start.44
  634.2 15.6 %copy-start.68 = (bf16[2,512,112]{1,2,0:T(8,128)(2,1)S(1)}, bf16[2,512,112]{1,2,0:T(8,128)(2,1)}, u32[]{:S(2)}) copy-start(bf16[2,512,112]{1,2,0:T(8,128)(2,1)} %copy-done.67) | copy-start | bytes 688132
  634.2 15.6 %copy-start.118 = (f32[2,512]{1,0:T(2,128)S(1)}, f32[2,512]{1,0:T(2,128)}, u32[]{:S(2)}) copy-start(f32[2,512]{1,0:T(2,128)} %copy-done.117) | copy-start | bytes 12292
  664.1 12.9 collective-permute-start.3
  679.7 22.8 %all-to-all-start.7 = ((bf16[4,3,2,128,112]{3,4,1,2,0:T(8,128)(2,1)}), bf16[4,3,2,128,112]{3,4,1,2,0:T(8,128)(2,1)}, u32[]{:S(2)}, u32[]{:S(2)}) async-start(bf16[4,3,2,128,112]{3,4,1,2,0:T(8,128)(2,1)} %copy.375), calls=%async_computation.7 | async-start | bytes 1376256 | tf_op jit(solution)/shard_map/all_to_all | solution.py:147
  683.9 126.1 %reduce-scatter.41.cloned.1.call-start = ((), (), s32[]{:S(2)}) async-start(), calls=%async_computation.32 | async-start | bytes 9830400 | tf_op jit(solution)/shard_map/reduce_scatter | solution.py:126
  687.3 23.5 %copy-start.8 = (f32[256,4,5,112]{0,3,2,1:T(8,128)S(1)}, f32[256,4,5,112]{0,3,2,1:T(8,128)}, u32[]{:S(2)}) copy-start(f32[256,4,5,112]{0,3,2,1:T(8,128)} %get-tuple-element.169) | copy-start | bytes 6881284
  754.5 61.4 %reduce-scatter.59.cloned.1.call-start = ((), (), s32[]{:S(2)}) async-start(), calls=%async_computation.41 | async-start | bytes 6881280 | tf_op jit(solution)/shard_map/reduce_scatter | solution.py:126
  760.5 60.0 %reduce-scatter.61.cloned.1.call-start = ((), (), s32[]{:S(2)}) async-start(), calls=%async_computation.42 | async-start | bytes 12582912 | tf_op jit(solution)/shard_map/reduce_scatter | solution.py:126
  769.3 55.5 %reduce-scatter.67.cloned.1.call-start = ((), (), s32[]{:S(2)}) async-start(), calls=%async_computation.45 | async-start | bytes 12582912 | tf_op jit(solution)/shard_map/reduce_scatter | solution.py:126
  779.9 60.9 %reduce-scatter.43.cloned.1.call-start = ((), (), s32[]{:S(2)}) async-start(), calls=%async_computation.33 | async-start | bytes 6881280 | tf_op jit(solution)/shard_map/reduce_scatter | solution.py:126
  785.6 75.5 %reduce-scatter.45.cloned.1.call-start = ((), (), s32[]{:S(2)}) async-start(), calls=%async_computation.34 | async-start | bytes 12582912 | tf_op jit(solution)/shard_map/reduce_scatter | solution.py:126
  794.2 117.0 %reduce-scatter.81.cloned.1.call-start = ((), (), s32[]{:S(2)}) async-start(), calls=%async_computation.56 | async-start | bytes 4096000
  800.4 130.0 %reduce-scatter.51.cloned.1.call-start = ((), (), s32[]{:S(2)}) async-start(), calls=%async_computation.37 | async-start | bytes 12582912 | tf_op jit(solution)/shard_map/reduce_scatter | solution.py:126
  809.9 170.4 %reduce-scatter.73.cloned.1.call-start = ((), (), s32[]{:S(2)}) async-start(), calls=%async_computation.52 | async-start | bytes 4096000
  815.8 205.3 %reduce-scatter.85.cloned.1.call-start = ((), (), s32[]{:S(2)}) async-start(), calls=%async_computation.58 | async-start | bytes 2949120
  820.4 256.3 %reduce-scatter.63.cloned.1.call-start = ((), (), s32[]{:S(2)}) async-start(), calls=%async_computation.43 | async-start | bytes 5242880 | tf_op jit(solution)/shard_map/reduce_scatter | solution.py:127
  821.0 311.5 %reduce-scatter.69.cloned.1.call-start = ((), (), s32[]{:S(2)}) async-start(), calls=%async_computation.46 | async-start | bytes 5242880 | tf_op jit(solution)/shard_map/reduce_scatter | solution.py:127
  824.9 348.5 %reduce-scatter.77.cloned.1.call-start = ((), (), s32[]{:S(2)}) async-start(), calls=%async_computation.54 | async-start | bytes 2949120
  845.1 384.0 %reduce-scatter.47.cloned.1.call-start = ((), (), s32[]{:S(2)}) async-start(), calls=%async_computation.35 | async-start | bytes 5242880 | tf_op jit(solution)/shard_map/reduce_scatter | solution.py:127
  861.2 393.8 %reduce-scatter.83.cloned.1.call-start = ((), (), s32[]{:S(2)}) async-start(), calls=%async_computation.57 | async-start | bytes 1024000 | tf_op jit(solution)/shard_map/reduce_scatter | solution.py:128
  911.2 399.0 %reduce-scatter.53.cloned.1.call-start = ((), (), s32[]{:S(2)}) async-start(), calls=%async_computation.38 | async-start | bytes 5242880 | tf_op jit(solution)/shard_map/reduce_scatter | solution.py:127
  930.4 299.7 %copy-start.4 = (f32[256,1024]{1,0:T(8,128)S(1)}, f32[256,1024]{1,0:T(8,128)}, u32[]{:S(2)}) copy-start(f32[256,1024]{1,0:T(8,128)} %copy-done.3) | copy-start | bytes 3145732
  930.5 405.8 %reduce-scatter.75.cloned.1.call-start = ((), (), s32[]{:S(2)}) async-start(), calls=%async_computation.53 | async-start | bytes 1024000 | tf_op jit(solution)/shard_map/reduce_scatter | solution.py:128
  980.3 379.6 %reduce-scatter.87.cloned.1.call-start = ((), (), s32[]{:S(2)}) async-start(), calls=%async_computation.59 | async-start | bytes 737280 | tf_op jit(solution)/shard_map/reduce_scatter | solution.py:128
  1021.1 366.4 %reduce-scatter.65.cloned.1.call-start = ((), (), s32[]{:S(2)}) async-start(), calls=%async_computation.44 | async-start | bytes 1310720 | tf_op jit(solution)/shard_map/reduce_scatter | solution.py:128
  1076.7 339.1 %reduce-scatter.71.cloned.1.call-start = ((), (), s32[]{:S(2)}) async-start(), calls=%async_computation.47 | async-start | bytes 1310720 | tf_op jit(solution)/shard_map/reduce_scatter | solution.py:128
  1132.5 306.1 %reduce-scatter.79.cloned.1.call-start = ((), (), s32[]{:S(2)}) async-start(), calls=%async_computation.55 | async-start | bytes 737280 | tf_op jit(solution)/shard_map/reduce_scatter | solution.py:128
  1173.4 292.9 %reduce-scatter.49.cloned.1.call-start = ((), (), s32[]{:S(2)}) async-start(), calls=%async_computation.36 | async-start | bytes 1310720 | tf_op jit(solution)/shard_map/reduce_scatter | solution.py:128
  1229.1 265.4 %reduce-scatter.55.cloned.1.call-start = ((), (), s32[]{:S(2)}) async-start(), calls=%async_computation.39 | async-start | bytes 1310720 | tf_op jit(solution)/shard_map/reduce_scatter | solution.py:128
  1239.7 257.0 %copy-start.2 = (f32[2,32,13568]{2,1,0:T(8,128)S(1)}, f32[2,32,13568]{2,1,0:T(8,128)}, u32[]{:S(2)}) copy-start(f32[2,32,13568]{2,1,0:T(8,128)} %param.14) | copy-start | bytes 10420228
  (98 other events, 499.5 us)
Sparse Core Ops, SparseCore 0:
  11.4 92.9 all-gather.9
  108.0 126.4 all-gather.11
  237.8 87.8 all-gather.13
  329.1 124.9 all-gather.15
  609.6 13.3 reduce-scatter.56
  754.6 13.4 reduce-scatter.40
  770.4 13.5 reduce-scatter.58
  786.4 17.9 reduce-scatter.60
  806.7 18.0 reduce-scatter.66
  827.1 13.6 reduce-scatter.42
  843.1 17.9 reduce-scatter.44
  864.9 46.2 reduce-scatter.80
  913.6 16.7 reduce-scatter.50
  933.9 46.3 reduce-scatter.72
  983.7 37.3 reduce-scatter.84
  1023.9 52.6 reduce-scatter.62
  1079.8 52.6 reduce-scatter.68
  1136.0 37.3 reduce-scatter.76
  1176.4 52.6 reduce-scatter.46
  1231.4 23.6 reduce-scatter.82
  1258.3 51.9 reduce-scatter.52
  1312.6 23.6 reduce-scatter.74
  1338.6 21.3 reduce-scatter.86
  1362.1 25.4 reduce-scatter.64
  1390.0 25.7 reduce-scatter.70
  1418.0 20.6 reduce-scatter.78
  1440.8 25.4 reduce-scatter.48
  1468.7 25.7 reduce-scatter.54

commit v2 on v1

--- a/solution.py
+++ b/solution.py
@@ -3,6 +3,8 @@
 import jax
 import jax.numpy as jnp
 from jax import lax
+from jax.experimental import pallas as pl
+from jax.experimental.pallas import tpu as pltpu
 from jax.sharding import PartitionSpec as P
 
 D = 1024
@@ -21,6 +23,7 @@
 WEIGHT_DECAY = 0.1
 NORM_RATE = 0.5
 MASKED = -1e30
+CHUNK = 512
 
 
 def passed_along(value, axis, by):
@@ -115,21 +118,216 @@
     )
 
 
-def reduction_order(tensor):
-    dp, seq, head = (lax.axis_size("dp"), lax.axis_size("seq"), lax.axis_size("head"))
-    count, width = tensor.shape
-    split = tensor.reshape(count, dp, seq, width // (dp * seq))
-    return split.transpose(0, 2, 1, 3).reshape(count, width)
-
-
-def reduce_rows(grad):
-    parts = lax.psum_scatter(grad, "seq", scatter_dimension=0, tiled=True)
-    parts = lax.psum_scatter(parts, "dp", scatter_dimension=0, tiled=True)
-    return lax.psum_scatter(parts, "head", scatter_dimension=0, tiled=True)
-
-
-def weight_grad(left, right):
-    return contract_first(reduction_order(left), right).astype(jnp.bfloat16)
+AXES = ("dp", "seq", "head")
+
+
+def halving_plan(sizes, width):
+    dims = [
+        (axis, bit) for axis in AXES for bit in reversed(range(sizes[axis].bit_length() - 1))
+    ]
+    dp_dims, seq_dims, head_dims = (
+        [index for index, (axis, bit) in enumerate(dims) if axis == name] for name in AXES
+    )
+    orders = (
+        seq_dims[::-1] + dp_dims[::-1] + head_dims[::-1],
+        seq_dims[::-1] + dp_dims + head_dims[::-1],
+    )
+    stages = []
+    for stage in range(len(dims)):
+        together = set(orders[0][:stage]) == set(orders[1][:stage]) and (
+            orders[0][stage] == orders[1][stage]
+        )
+        columns = [(0, 0, width)] if together else [(0, 0, width // 2), (1, width // 2, width // 2)]
+        parts = []
+        for which, start, count in columns:
+            left = [d for d in range(len(dims)) if d not in orders[which][:stage]]
+            parts.append((start, count, orders[which][stage], left))
+        stages.append(parts)
+    lags = [2 if dims[parts[0][2]][0] == "dp" else 2 for parts in stages]
+    return dims, stages, lags
+
+
+def reduce_weight_grads(pairs, extras, width):
+    sizes = {axis: lax.axis_size(axis) for axis in AXES}
+    dims, stages, lags = halving_plan(sizes, width)
+    depth = len(dims)
+    tokens, model = pairs[0][0].shape
+    rows = model >> depth
+    firsts = [0]
+    for left, right in pairs:
+        firsts.append(firsts[-1] + right.shape[1] // width)
+    chunks = firsts[-1]
+    per_layer = len(pairs) // len(extras)
+    spots = [
+        (firsts[per_layer * index] + near // width, near % width)
+        for index, (_, near) in enumerate(extras)
+    ]
+    starts = [sum(lags[:stage]) for stage in range(depth + 1)]
+    count_pairs, count_extras = (len(pairs), len(extras))
+
+    def kernel(*refs):
+        lefts = refs[:count_pairs]
+        rights = refs[count_pairs : 2 * count_pairs]
+        added = refs[2 * count_pairs : 2 * count_pairs + count_extras]
+        rest = refs[2 * count_pairs + count_extras :]
+        out_ref, left_buf, turned, right_buf, load_sem = rest[:5]
+        pool = iter(rest[5:])
+        buffers = [[tuple(next(pool) for _ in range(4)) for _ in parts] for parts in stages]
+        step = pl.program_id(0)
+        place = {axis: lax.axis_index(axis) for axis in AXES}
+        bits = [lax.rem(place[axis] // (1 << bit), 2) for axis, bit in dims]
+        partners = [
+            {axis: place[axis] + (1 << bit) * (1 - 2 * bits[index])}
+            for index, (axis, bit) in enumerate(dims)
+        ]
+
+        def exchange(stage, part, slot):
+            start, count, dim, left = stages[stage][part]
+            own, got, send_sem, recv_sem = buffers[stage][part]
+            lead = (slot,) + (slice(None),) * left.index(dim)
+            return pltpu.make_async_remote_copy(
+                src_ref=own.at[lead + (1 - bits[dim],)],
+                dst_ref=got.at[slot],
+                send_sem=send_sem.at[slot],
+                recv_sem=recv_sem.at[slot],
+                device_id=partners[dim],
+                device_id_type=pl.DeviceIdType.MESH,
+            )
+
+        def load_left(index):
+            return pltpu.make_async_copy(lefts[index], left_buf, load_sem.at[2])
+
+        def load_right(index, chunk):
+            slot = lax.rem(chunk, 2)
+            columns = pl.ds(pl.multiple_of((chunk - firsts[index]) * width, width), width)
+            return pltpu.make_async_copy(
+                rights[index].at[:, columns], right_buf.at[slot], load_sem.at[slot]
+            )
+
+        def prefetch(chunk):
+            for index in range(count_pairs):
+
+                @pl.when((chunk >= firsts[index]) & (chunk < firsts[index + 1]))
+                def _(index=index):
+                    load_right(index, chunk).start()
+
+                @pl.when(chunk == firsts[index])
+                def _(index=index):
+                    load_left(index).start()
+
+        @pl.when(step == 0)
+        def _():
+            prefetch(step)
+            barrier = pltpu.get_barrier_semaphore()
+            for partner in partners:
+                pl.semaphore_signal(
+                    barrier, inc=1, device_id=partner, device_id_type=pl.DeviceIdType.MESH
+                )
+            pl.semaphore_wait(barrier, depth)
+
+        @pl.when(step + 1 < chunks)
+        def _():
+            prefetch(step + 1)
+
+        for stage in range(depth, -1, -1):
+            chunk = step - starts[stage]
+
+            @pl.when((chunk >= 0) & (chunk < chunks))
+            def _(stage=stage, chunk=chunk):
+                if stage == 0:
+                    for first in firsts[:-1]:
+
+                        @pl.when(chunk == first)
+                        def _():
+                            load_left(0).wait()
+                            turned[...] = left_buf[...].T
+
+                    load_right(0, lax.rem(chunk, 2)).wait()
+                    product = jnp.dot(
+                        turned[...],
+                        right_buf[lax.rem(chunk, 2)],
+                        preferred_element_type=jnp.float32,
+                    )
+                    slot = lax.rem(chunk, 2 * lags[0])
+                    for part, (start, count, dim, left) in enumerate(stages[0]):
+                        piece = product[:, start : start + count].astype(jnp.bfloat16)
+                        buffers[0][part][0][slot] = piece.reshape((2,) * depth + (rows, count))
+                    for index in range(count_extras):
+
+                        @pl.when(chunk == spots[index][0])
+                        def _(index=index):
+                            at = (slot, Ellipsis, slice(spots[index][1], spots[index][1] + 128))
+                            own = buffers[0][0][0]
+                            total = own[at].astype(jnp.float32) + added[index][...].astype(
+                                jnp.float32
+                            )
+                            own[at] = total.astype(jnp.bfloat16)
+
+                else:
+                    back = lax.rem(chunk, 2 * lags[stage - 1])
+                    for part, (start, count, dim, left) in enumerate(stages[stage - 1]):
+                        exchange(stage - 1, part, back).wait()
+                        own, got = buffers[stage - 1][part][:2]
+                        lead = (back,) + (slice(None),) * left.index(dim)
+                        total = own[lead + (bits[dim],)].astype(jnp.float32) + got[back].astype(
+                            jnp.float32
+                        )
+                        if stage == depth:
+                            out_ref[:, start : start + count] = total
+                            continue
+                        slot = lax.rem(chunk, 2 * lags[stage])
+                        low = total.astype(jnp.bfloat16)
+                        for other, (begin, length, _, kept) in enumerate(stages[stage]):
+                            lo, hi = max(start, begin), min(start + count, begin + length)
+                            if lo < hi:
+                                at = (slot,) + (slice(None),) * (len(kept) + 1)
+                                buffers[stage][other][0][at + (slice(lo - begin, hi - begin),)] = (
+                                    low[..., lo - start : hi - start]
+                                )
+                if stage < depth:
+                    for part in range(len(stages[stage])):
+                        exchange(stage, part, lax.rem(chunk, 2 * lags[stage])).start()
+
+    scratch = [
+        pltpu.VMEM((tokens, model), jnp.bfloat16),
+        pltpu.VMEM((model, tokens), jnp.bfloat16),
+        pltpu.VMEM((2, tokens, width), jnp.bfloat16),
+        pltpu.SemaphoreType.DMA((3,)),
+    ]
+    for stage, parts in enumerate(stages):
+        slots = 2 * lags[stage]
+        for start, count, dim, left in parts:
+            scratch += [
+                pltpu.VMEM((slots,) + (2,) * len(left) + (rows, count), jnp.bfloat16),
+                pltpu.VMEM((slots,) + (2,) * (len(left) - 1) + (rows, count), jnp.bfloat16),
+                pltpu.SemaphoreType.DMA((slots,)),
+                pltpu.SemaphoreType.DMA((slots,)),
+            ]
+    in_place = pl.BlockSpec(memory_space=pl.ANY)
+    whole = [value.reshape((2,) * depth + (rows, 128)) for value, _ in extras]
+    return pl.pallas_call(
+        kernel,
+        grid=(chunks + starts[depth],),
+        in_specs=[in_place] * (2 * count_pairs)
+        + [pl.BlockSpec(value.shape, lambda step: (0,) * (depth + 2)) for value in whole],
+        out_specs=pl.BlockSpec(
+            (rows, width), lambda step: (0, jnp.clip(step - starts[depth], 0, chunks - 1))
+        ),
+        out_shape=jax.ShapeDtypeStruct((rows, chunks * width), jnp.float32),
+        scratch_shapes=scratch,
+        compiler_params=pltpu.CompilerParams(
+            collective_id=1,
+            has_side_effects=True,
+            vmem_limit_bytes=48 << 20,
+            dimension_semantics=("arbitrary",),
+        ),
+    )(*[left for left, _ in pairs], *[right for _, right in pairs], *whole)
+
+
+def padded(pieces):
+    have = sum(piece.shape[1] for piece in pieces)
+    fill = jnp.zeros((pieces[0].shape[0], (-have) % CHUNK), pieces[0].dtype)
+    return jnp.concatenate(list(pieces) + [fill], axis=1)
 
 
 def to_heads(tensor, pieces):
@@ -333,8 +531,7 @@
         )
     output = hidden.reshape(seq_count, sub_rows, width).astype(jnp.bfloat16)
     grad_hidden = (cotangent.astype(jnp.float32) * valid[:, :, None]).reshape(tokens, width)
-    matrix_rows = [None] * LAYERS
-    small_rows = [None] * LAYERS
+    pairs, extras = ([], [])
     for layer in reversed(range(LAYERS)):
         (
             normed_one,
@@ -364,8 +561,6 @@
         grad_act = jnp.dot(grad_low, ffn_w[:, FF:], preferred_element_type=jnp.float32)
         gelu_value, gelu_pull = jax.vjp(gelu_tanh, up)
         grad_up = gelu_pull(grad_act)[0].astype(jnp.bfloat16)
-        up_share = reduce_rows(weight_grad(second_in, grad_up))
-        down_share = reduce_rows(weight_grad(grad_low, act))
         grad_second = contract_last(grad_up, ffn_w[:, :FF])
         gain_two_grad = jnp.sum(grad_second * normed_two, axis=0)
         bias_two_grad = jnp.sum(grad_second, axis=0)
@@ -374,7 +569,6 @@
         grad_mixed = jnp.dot(
             residual_low, attn_w[:, value_end:], preferred_element_type=jnp.float32
         ).reshape(tokens, HEADS, EXPERTS, HEAD_DIM)
-        out_share = reduce_rows(weight_grad(residual_low, mixed))
         grad_gate_out = jnp.sum(
             grad_mixed * attended_rows[:, :, None, :].astype(jnp.float32), axis=-1
         )
@@ -417,23 +611,35 @@
         grad_hidden = grad_residual + norm_back(grad_first, normed_one, inverse_one, gains[:, 0])
         norm_grads = jnp.stack(
             [gain_one_grad, bias_one_grad, gain_two_grad, bias_two_grad], axis=1
-        )
-        side = (-(value_end + router_cols + 4)) % 128
-        in_share = reduce_rows(
-            jnp.concatenate(
-                [
-                    weight_grad(first_in, grad_in),
-                    weight_grad(first_in, grad_logit),
-                    reduction_order(norm_grads.T).T.astype(jnp.bfloat16),
-                    jnp.zeros((width, side), jnp.bfloat16),
-                ],
-                axis=1,
+        ).astype(jnp.bfloat16)
+        at = value_end + router_cols
+        near = at // 128 * 128
+        norm_grads = jnp.pad(norm_grads, ((0, 0), (at - near, 128 - 4 - (at - near))))
+        pairs += [
+            (first_in, padded([grad_in, grad_logit, jnp.zeros((tokens, 4), jnp.bfloat16)])),
+            (residual_low, padded([mixed])),
+            (second_in, grad_up),
+            (grad_low, act),
+        ]
+        extras.append((norm_grads, near))
+    reduced = reduce_weight_grads(pairs, extras, CHUNK)
+    matrix_rows = [None] * LAYERS
+    small_rows = [None] * LAYERS
+    start = 0
+    for slot, layer in enumerate(reversed(range(LAYERS))):
+        widths = [right.shape[1] for _, right in pairs[4 * slot : 4 * slot + 4]]
+        begins = [start + sum(widths[:group_index]) for group_index in range(4)]
+        start += sum(widths)
+        shares = [
+            reduced[:, begin : begin + used]
+            for begin, used in zip(
+                begins, (value_end, output_end - value_end, FF, FF)
             )
-        )
-        matrix_rows[layer] = jnp.concatenate(
-            [in_share[:, :value_end], out_share, up_share, down_share], axis=1
-        ).astype(jnp.float32)
-        small_rows[layer] = in_share[:, value_end : value_end + router_cols + 4].astype(jnp.float32)
+        ]
+        matrix_rows[layer] = jnp.concatenate(shares, axis=1)
+        small_rows[layer] = reduced[
+            :, begins[0] + value_end : begins[0] + value_end + router_cols + 4
+        ]
     input_grad = grad_hidden.reshape(seq_count, sub_rows, width).astype(jnp.bfloat16)
     matrix_grad = jnp.stack(matrix_rows, axis=0)
     small_grad = jnp.stack(small_rows, axis=0)

time: 1520 us -> 1020 us (0.67)
  waiting for transfers between devices: 871 us -> 239 us
  Pallas kernels: 0 us -> 254 us
  local copies, waits for them, and re-layouts: 175 us -> 115 us
  matrix products: 227 us -> 180 us
    reduce_scatter x20 -> x0, waiting for transfers between devices: 468 us -> none  [the longest x4 221 us: reduce_rows(): parts = lax.psum_scatter(parts, 'dp', scatter_dimension=0, tiled=True)]
    pallas_call x0 -> x1, Pallas kernels: none -> 254 us  [reduce_weight_grads(): pl.pallas_call(kernel, grid=(chunks + starts[depth],), in_specs=[in_place...]
    unnamed x32 -> x4, waiting for transfers between devices: 183 us -> 1.24 us
    concatenate x6, local copies, waits for them, and re-layouts: 66.5 us -> 14.2 us  [the longest x4 10.1 us: padded(): return jnp.concatenate(list(pieces) + [fill], axis=1)]
    dot_general x10 -> x0, matrix products: 49.4 us -> none  [contract_first(): lax.dot_general(left, right, (((0,), (0,)), ((), ())), preferred_element_...]
    unnamed x259 -> x233, local copies, waits for them, and re-layouts: 39.9 us -> 19.9 us
    all_gather x4, waiting for transfers between devices: 141 us -> 157 us  [local(): lax.all_gather(part, ('dp', 'seq', 'head'), axis=0, tiled=True)]
  transfers between devices with their start and end apart: 37 -> 13, of which waited for: 29 -> 9; matrix products, arithmetic and copies ran while one was open for 21% -> 16% of each run, Pallas kernels for 0% -> 0%
where the time goes in v2:
time: 1020 us; the launch traced here: 1010 us
  Pallas kernels  254 us (25%)
  waiting for transfers between devices  239 us (23%)
  matrix products  180 us (18%)
  blocking collectives  128 us (13%)
  local copies, waits for them, and re-layouts  115 us (11%)
  other arithmetic  53.7 us (5%)
  starting transfers between devices  27 us (3%)
  between operations  16.3 us (2%)
    pallas_call x1, Pallas kernels, reduce_weight_grads(): pl.pallas_call(kernel, grid=(chunks + starts[depth],), in_specs=[in_place...  254 us
    all_gather x4, waiting for transfers between devices, local(): lax.all_gather(part, ('dp', 'seq', 'head'), axis=0, tiled=True)  157 us
    all_gather x1, blocking collectives, local(): carried = lax.all_gather(carried, ('dp', 'seq', 'head'), axis=0, tiled=True)  76.7 us
    all_to_all x3, blocking collectives, to_heads(): got = lax.all_to_all(sent, 'head', split_axis=0, concat_axis=0, tiled=True)  51.1 us
    all_to_all x4, waiting for transfers between devices, to_tokens(): got = lax.all_to_all(sent, 'head', split_axis=0, concat_axis=0, tiled=True)  45.6 us
    dot_general x10, matrix products, contract_last(): lax.dot_general(left, right, (((1,), (1,)), ((), ())), preferred_element_...  43.9 us
    all_to_all x1, waiting for transfers between devices, to_heads(): got = lax.all_to_all(sent, 'head', split_axis=0, concat_axis=0, tiled=True)  34.9 us
    dot_general x2, matrix products, attend_backward(): jnp.einsum('sqk,skc->sqc', grad_raw, keys, preferred_element_type=jnp.flo...  24 us
  transfers between devices with their start and end apart: 13, of which 9 were waited for; matrix products, arithmetic and copies ran while one was open for 16% of the time, Pallas kernels for 0%

profile of v2, /device:TPU:0, one launch (start us, length us, event | category | flops | bytes accessed | tf_op | source)
XLA Modules:
  0.0 1013.1 jit_solution(5770436528968070933)
XLA Ops:
  14.6 76.7 %all-gather = f32[98304]{0:T(1024)S(1)} all-gather(f32[3072]{0:T(1024)S(1)} %select_maximum_fusion), channel_id=2, replica_groups=mesh['dp'=4,'seq'=2,'head'=4] {'dp','seq','head'}, dimensions={0}, use_global_device_ids=true | all-gather | bytes 405504 | tf_op jit(solution)/shard_map/all_gather | solution.py:447
  96.5 8.0 all-gather.10.cloned.1.call-done
  104.5 2.9 slice_bitcast_fusion.1
  107.4 2.9 copy.308
  110.3 4.8 slice_bitcast_fusion
  115.1 6.7 copy.309
  121.8 5.8 multiply_reduce_fusion.9
  132.1 3.5 all-to-all-start
  137.1 34.9 %all-to-all-done = bf16[4,3,2,128,112]{3,4,1,2,0:T(8,128)(2,1)S(1)} async-done(((bf16[4,3,2,128,112]{3,4,1,2,0:T(8,128)(2,1)}), bf16[4,3,2,128,112]{3,4,1,2,0:T(8,128)(2,1)S(1)}, u32[]{:S(2)}, u32[]{:S(2)}) %all-to-all-start) | async-done | bytes 688160 | tf_op jit(solution)/shard_map/all_to_all | solution.py:337
  173.4 2.9 collective-permute-start
  178.3 5.5 fusion.204
  183.9 3.3 convolution_convert_fusion.1
  188.2 3.4 all-to-all-start.1
  193.1 14.0 %all-to-all-done.1 = bf16[4,1,2,128,112]{3,2,4,1,0:T(2,128)(2,1)S(1)} async-done(((bf16[4,1,2,128,112]{3,2,4,1,0:T(2,128)(2,1)}), bf16[4,1,2,128,112]{3,2,4,1,0:T(2,128)(2,1)S(1)}, u32[]{:S(2)}, u32[]{:S(2)}) %all-to-all-start.1) | async-done | bytes 229408 | tf_op jit(solution)/shard_map/all_to_all | solution.py:345
  207.9 5.8 fusion.205
  214.3 22.6 %all-gather.12.cloned.1.call-done = bf16[1,1024,8192]{2,1,0:T(8,128)(2,1)} async-done(((bf16[1,32,8192]{2,1,0:T(8,128)(2,1)}), bf16[1,1024,8192]{2,1,0:T(8,128)(2,1)}) %all-gather.12.cloned.1.call-update) | async-done | bytes 16777232 | tf_op jit(solution)/shard_map/all_gather | solution.py:459
  236.9 8.7 multiply_convert_fusion.3
  246.3 2.4 fusion.206
  249.7 78.6 %all-gather.14.cloned.1.call-done = bf16[1,1024,5376]{2,1,0:T(8,128)(2,1)} async-done(((bf16[1,32,5376]{2,1,0:T(8,128)(2,1)}), bf16[1,1024,5376]{2,1,0:T(8,128)(2,1)}) %all-gather.14.cloned.1.call-update) | async-done | bytes 11010064 | tf_op jit(solution)/shard_map/all_gather | solution.py:459
  328.3 3.3 fusion.87
  333.8 4.7 fusion.24
  340.6 28.5 %all_to_all.40 = bf16[4,3,2,128,112]{3,4,1,2,0:T(8,128)(2,1)S(1)} all-to-all(bf16[4,3,2,128,112]{3,4,1,2,0:T(8,128)(2,1)S(1)} %copy.328), channel_id=1, replica_groups=mesh['dp'=4,'seq'=2,'head'=4] {'head'}, dimensions={0} | all-to-all | bytes 1376256 | tf_op jit(solution)/shard_map/all_to_all | solution.py:337
  373.9 5.2 fusion.207
  379.2 3.4 convolution_convert_fusion
  383.6 3.6 all-to-all-start.3
  388.5 13.9 %all-to-all-done.3 = bf16[4,1,2,128,112]{3,2,4,1,0:T(2,128)(2,1)S(1)} async-done(((bf16[4,1,2,128,112]{3,2,4,1,0:T(2,128)(2,1)}), bf16[4,1,2,128,112]{3,2,4,1,0:T(2,128)(2,1)S(1)}, u32[]{:S(2)}, u32[]{:S(2)}) %all-to-all-start.3) | async-done | bytes 229408 | tf_op jit(solution)/shard_map/all_to_all | solution.py:345
  405.6 6.5 fusion.208
  413.4 47.5 %all-gather.16.cloned.1.call-done = bf16[1,1024,8192]{2,1,0:T(8,128)(2,1)} async-done(((bf16[1,32,8192]{2,1,0:T(8,128)(2,1)}), bf16[1,1024,8192]{2,1,0:T(8,128)(2,1)}) %all-gather.16.cloned.1.call-update) | async-done | bytes 16777232 | tf_op jit(solution)/shard_map/all_gather | solution.py:459
  460.9 8.1 multiply_convert_fusion.2
  469.8 5.2 fusion.39.refs_10_
  475.0 3.2 multiply_reduce_fusion.12
  479.6 6.5 fusion.42
  487.1 11.2 %all_to_all.41 = bf16[4,1,2,128,112]{3,2,4,1,0:T(2,128)(2,1)S(1)} all-to-all(bf16[4,1,2,128,112]{3,2,4,1,0:T(2,128)(2,1)S(1)} %bitcast.300), channel_id=1, replica_groups=mesh['dp'=4,'seq'=2,'head'=4] {'head'}, dimensions={0} | all-to-all | bytes 458752 | tf_op jit(solution)/shard_map/all_to_all | solution.py:337
  498.6 4.7 convolution_bitcast_fusion.1
  503.4 2.8 fusion.147
  506.2 9.6 fusion.110
  518.7 12.0 %fusion.119 = bf16[2,512,112]{1,2,0:T(8,128)(2,1)} fusion(f32[2,512,1024]{2,1,0:T(8,128)} %fusion.147, bf16[2,512,112]{1,2,0:T(8,128)(2,1)} %copy-done.68, bf16[2,512,112]{1,2,0:T(8,128)(2,1)} %copy-done.65, f32[2,512,1024]{2,1,0:T(8,128)} %get-tuple-element.120, f32[2,512]{1,0:T(2,128)S(1)} %copy-done.107), kind=kOutput, calls=%fused_computation.133 | convolution fusion | flops 243255296 | bytes 9080832 | tf_op jit(solution)/shard_map/sqk,skc->sqc/dot_general | solution.py:394
  536.2 4.2 all-to-all-start.5
  541.9 17.8 %all-to-all-done.5 = bf16[4,3,2,128,112]{3,4,1,2,0:T(8,128)(2,1)} async-done(((bf16[4,3,2,128,112]{3,4,1,2,0:T(8,128)(2,1)}), bf16[4,3,2,128,112]{3,4,1,2,0:T(8,128)(2,1)}, u32[]{:S(2)}, u32[]{:S(2)}) %all-to-all-start.5) | async-done | bytes 688160 | tf_op jit(solution)/shard_map/all_to_all | solution.py:345
  564.2 3.0 multiply_reduce_fusion.6
  568.0 5.2 fusion.22
  575.9 7.2 fusion.32.refs_14_
  583.7 3.2 multiply_reduce_fusion.10
  588.2 6.5 fusion.46
  595.8 11.3 %all_to_all.42 = bf16[4,1,2,128,112]{3,2,4,1,0:T(2,128)(2,1)S(1)} all-to-all(bf16[4,1,2,128,112]{3,2,4,1,0:T(2,128)(2,1)S(1)} %bitcast.302), channel_id=1, replica_groups=mesh['dp'=4,'seq'=2,'head'=4] {'head'}, dimensions={0} | all-to-all | bytes 458752 | tf_op jit(solution)/shard_map/all_to_all | solution.py:337
  608.0 3.9 convolution_bitcast_fusion
  611.9 3.7 fusion.148
  615.6 12.5 %fusion.107 = f32[1,2,1024,112]{2,3,1,0:T(8,128)} fusion(bf16[2,512,112]{1,2,0:T(8,128)(2,1)} %copy-done.67, f32[2,512,1024]{2,1,0:T(8,128)} %fusion.148, f32[2,512,1024]{2,1,0:T(8,128)} %get-tuple-element.112, f32[2,512]{1,0:T(2,128)S(1)} %copy-done.105), kind=kOutput, calls=%fused_computation.127 | convolution fusion | flops 242223104 | bytes 9539584 | tf_op jit(solution)/shard_map/sqk,sqc->skc/dot_general | solution.py:396
  634.5 12.0 %fusion.116 = bf16[2,512,112]{1,2,0:T(8,128)(2,1)} fusion(f32[2,512,1024]{2,1,0:T(8,128)} %fusion.148, bf16[2,512,112]{1,2,0:T(8,128)(2,1)} %copy-done.66, bf16[2,512,112]{1,2,0:T(8,128)(2,1)} %copy-done.64, f32[2,512,1024]{2,1,0:T(8,128)} %get-tuple-element.112, f32[2,512]{1,0:T(2,128)} %copy-done.104), kind=kOutput, calls=%fused_computation.132 | convolution fusion | flops 243255296 | bytes 9080832 | tf_op jit(solution)/shard_map/sqk,skc->sqc/dot_general | solution.py:394
  651.9 4.4 all-to-all-start.7
  659.6 2.4 copy.356
  663.5 7.4 fusion.113
  672.8 2.4 copy.355
  678.8 3.8 concatenate.100.refs_8_
  692.5 2.7 multiply_reduce_fusion.3
  696.2 6.0 fusion.20
  702.3 2.4 copy.358
  709.4 3.0 multiply_reduce_fusion.11
  715.1 3.8 concatenate.102.refs_12_
  724.9 254.3 %shard_map.201 = f32[32,28672]{1,0:T(8,128)} custom-call(bf16[256,1024]{1,0:T(8,128)(2,1)S(1)} %copy-done.5, bf16[256,1024]{1,0:T(8,128)(2,1)S(1)} %get-tuple-element.47.refs_1_, bf16[256,1024]{1,0:T(8,128)(2,1)S(1)} %copy-done.7, bf16[256,1024]{1,0:T(8,128)(2,1)S(1)} %bitcast_convert_fusion.refs_3_, bf16[256,1024]{1,0:T(8,128)(2,1)S(1)} %copy-done.1, ...), custom_call_target="tpu_custom_call" | custom-call | tf_op jit(solution)/shard_map/pallas_call | solution.py:308
  984.4 2.7 fusion.192
  989.6 2.7 concatenate.105
  992.3 3.0 add_convert_fusion
  996.8 9.3 fusion.187
  (441 shorter events, 122.8 us)
Async XLA Ops:
  7.2 97.3 %all-gather.10.cloned.1.call-start = ((), (), s32[]{:S(2)}) async-start(), calls=%async_computation.8 | async-start | bytes 11354112 | tf_op jit(solution)/shard_map/all_gather | solution.py:459
  10.3 83.6 %copy-start.11 = (bf16[2,128,1024]{2,1,0:T(8,128)(2,1)S(1)}, bf16[2,128,1024]{2,1,0:T(8,128)(2,1)}, u32[]{:S(2)}) copy-start(bf16[2,128,1024]{2,1,0:T(8,128)(2,1)} %param.10) | copy-start | bytes 1572868
  10.4 226.5 %all-gather.12.cloned.1.call-start = ((), (), s32[]{:S(2)}) async-start(), calls=%async_computation.9 | async-start | bytes 17301504 | tf_op jit(solution)/shard_map/all_gather | solution.py:459
  11.5 316.8 %all-gather.14.cloned.1.call-start = ((), (), s32[]{:S(2)}) async-start(), calls=%async_computation.10 | async-start | bytes 11354112 | tf_op jit(solution)/shard_map/all_gather | solution.py:459
  12.2 448.7 %all-gather.16.cloned.1.call-start = ((), (), s32[]{:S(2)}) async-start(), calls=%async_computation.11 | async-start | bytes 17301504 | tf_op jit(solution)/shard_map/all_gather | solution.py:459
  93.7 10.8 %copy-start.30 = (bf16[1,32,32,44]{3,2,0,1:T(8,128)(2,1)}, bf16[1,32,32,44]{3,2,0,1:T(8,128)(2,1)S(1)}, u32[]{:S(2)}) copy-start(bf16[1,32,32,44]{3,2,0,1:T(8,128)(2,1)S(1)} %get-tuple-element.78) | copy-start | bytes 270340
  93.7 155.6 %copy-start.24 = (bf16[1,32,32,44]{3,2,0,1:T(8,128)(2,1)}, bf16[1,32,32,44]{3,2,0,1:T(8,128)(2,1)S(1)}, u32[]{:S(2)}) copy-start(bf16[1,32,32,44]{3,2,0,1:T(8,128)(2,1)S(1)} %get-tuple-element.77) | copy-start | bytes 270340
  94.1 13.3 %copy-start.84 = (f32[256]{0:T(256)}, f32[256]{0:T(256)S(1)}, u32[]{:S(2)}) copy-start(f32[256]{0:T(256)S(1)} %get-tuple-element.105) | copy-start | bytes 3076
  94.4 15.8 %copy-start.86 = (f32[256]{0:T(256)}, f32[256]{0:T(256)S(1)}, u32[]{:S(2)}) copy-start(f32[256]{0:T(256)S(1)} %get-tuple-element.107) | copy-start | bytes 3076
  94.5 15.8 %copy-start.74 = (f32[1024,1]{0,1:T(1,128)}, f32[1024,1]{0,1:T(1,128)S(1)}, u32[]{:S(2)}) copy-start(f32[1024,1]{0,1:T(1,128)S(1)} %get-tuple-element.99) | copy-start | bytes 12292
  95.9 8.7 copy-start.48
  96.2 244.1 %copy-start.40 = (f32[128,56]{0,1:T(8,128)}, f32[128,56]{0,1:T(8,128)S(1)}, u32[]{:S(2)}) copy-start(f32[128,56]{0,1:T(8,128)S(1)} %get-tuple-element.103) | copy-start | bytes 86020
  96.2 244.1 %copy-start.43 = (f32[128,56]{0,1:T(8,128)}, f32[128,56]{0,1:T(8,128)S(1)}, u32[]{:S(2)}) copy-start(f32[128,56]{0,1:T(8,128)S(1)} %get-tuple-element.104) | copy-start | bytes 86020
  96.2 25.6 %copy-start.56 = (f32[256,4,5]{0,2,1:T(8,128)}, f32[256,4,5]{0,2,1:T(8,128)S(1)}, u32[]{:S(2)}) copy-start(f32[256,4,5]{0,2,1:T(8,128)S(1)} %get-tuple-element.92) | copy-start | bytes 61444
  96.2 111.5 %copy-start.59 = (f32[256,4,5]{0,2,1:T(8,128)}, f32[256,4,5]{0,2,1:T(8,128)S(1)}, u32[]{:S(2)}) copy-start(f32[256,4,5]{0,2,1:T(8,128)S(1)} %get-tuple-element.91) | copy-start | bytes 61444
  132.1 39.9 %all-to-all-start = ((bf16[4,3,2,128,112]{3,4,1,2,0:T(8,128)(2,1)}), bf16[4,3,2,128,112]{3,4,1,2,0:T(8,128)(2,1)S(1)}, u32[]{:S(2)}, u32[]{:S(2)}) async-start(bf16[4,3,2,128,112]{3,4,1,2,0:T(8,128)(2,1)} %copy.311), calls=%async_computation | async-start | bytes 1376256 | tf_op jit(solution)/shard_map/all_to_all | solution.py:337
  137.1 46.8 %copy-start.47 = (pred[512,1024]{1,0:T(8,128)(4,1)}, pred[512,1024]{1,0:T(8,128)(4,1)S(1)}, u32[]{:S(2)}) copy-start(pred[512,1024]{1,0:T(8,128)(4,1)S(1)} %get-tuple-element.101) | copy-start | bytes 1572868
  173.4 3.8 collective-permute-start
  176.4 7.5 copy-start.92
  188.2 18.9 %all-to-all-start.1 = ((bf16[4,1,2,128,112]{3,2,4,1,0:T(2,128)(2,1)}), bf16[4,1,2,128,112]{3,2,4,1,0:T(2,128)(2,1)S(1)}, u32[]{:S(2)}, u32[]{:S(2)}) async-start(bf16[4,1,2,128,112]{3,2,4,1,0:T(2,128)(2,1)} %bitcast.255), calls=%async_computation.1 | async-start | bytes 458752 | tf_op jit(solution)/shard_map/all_to_all | solution.py:345
  213.7 32.0 %copy-start.12 = (f32[256,1024]{1,0:T(8,128)}, f32[256,1024]{1,0:T(8,128)S(1)}, u32[]{:S(2)}) copy-start(f32[256,1024]{1,0:T(8,128)S(1)} %get-tuple-element.114) | copy-start | bytes 3145732
  213.7 31.9 %copy-start.80 = (f32[256]{0:T(256)}, f32[256]{0:T(256)S(1)}, u32[]{:S(2)}) copy-start(f32[256]{0:T(256)S(1)} %broadcast_multiply_fusion.10) | copy-start | bytes 3076
  214.0 31.7 %copy-start.82 = (f32[256]{0:T(256)}, f32[256]{0:T(256)S(1)}, u32[]{:S(2)}) copy-start(f32[256]{0:T(256)S(1)} %add_rsqrt_fusion.2) | copy-start | bytes 3076
  214.3 31.4 %copy-start.2 = (bf16[256,1024]{1,0:T(8,128)(2,1)}, bf16[256,1024]{1,0:T(8,128)(2,1)S(1)}, u32[]{:S(2)}) copy-start(bf16[256,1024]{1,0:T(8,128)(2,1)S(1)} %add_convert_fusion.3.refs_6_) | copy-start | bytes 1572868
  236.9 9.4 copy-start.102
  249.0 84.2 %copy-start.77 = (f32[256]{0:T(256)}, f32[256]{0:T(256)S(1)}, u32[]{:S(2)}) copy-start(f32[256]{0:T(256)S(1)} %add_rsqrt_fusion.1) | copy-start | bytes 3076
  249.3 89.3 %copy-start.4 = (bf16[256,1024]{1,0:T(8,128)(2,1)}, bf16[256,1024]{1,0:T(8,128)(2,1)S(1)}, u32[]{:S(2)}) copy-start(bf16[256,1024]{1,0:T(8,128)(2,1)S(1)} %add_convert_fusion.2.refs_0_) | copy-start | bytes 1572868
  249.6 78.7 %copy-start.49 = (f32[256,40]{1,0:T(8,128)}, f32[256,40]{1,0:T(8,128)S(1)}, u32[]{:S(2)}) copy-start(f32[256,40]{1,0:T(8,128)S(1)} %fusion.124) | copy-start | bytes 122884
  370.4 3.4 collective-permute-start.1
  379.2 8.0 copy-start.89
  383.6 18.7 %all-to-all-start.3 = ((bf16[4,1,2,128,112]{3,2,4,1,0:T(2,128)(2,1)}), bf16[4,1,2,128,112]{3,2,4,1,0:T(2,128)(2,1)S(1)}, u32[]{:S(2)}, u32[]{:S(2)}) async-start(bf16[4,1,2,128,112]{3,2,4,1,0:T(2,128)(2,1)} %bitcast.254), calls=%async_computation.3 | async-start | bytes 458752 | tf_op jit(solution)/shard_map/all_to_all | solution.py:345
  388.4 23.7 %copy-start.16 = (f32[2,128,1024]{2,1,0:T(8,128)}, f32[2,128,1024]{2,1,0:T(8,128)S(1)}, u32[]{:S(2)}) copy-start(f32[2,128,1024]{2,1,0:T(8,128)S(1)} %convert_multiply_fusion) | copy-start | bytes 3145732
  405.6 7.5 copy-start.79
  413.4 55.6 %copy-start.6 = (bf16[256,1024]{1,0:T(8,128)(2,1)}, bf16[256,1024]{1,0:T(8,128)(2,1)S(1)}, u32[]{:S(2)}) copy-start(bf16[256,1024]{1,0:T(8,128)(2,1)S(1)} %add_convert_fusion.1.refs_2_) | copy-start | bytes 1572868
  460.9 8.9 copy-start.101
  486.1 12.5 %copy-start.94 = (pred[2,1024]{1,0:T(4,128)(4,1)S(1)}, pred[2,1024]{1,0:T(4,128)(4,1)}, u32[]{:S(2)}) copy-start(pred[2,1024]{1,0:T(4,128)(4,1)} %copy-done.92) | copy-start | bytes 6148
  486.1 12.5 %copy-start.107 = (f32[2,512]{1,0:T(2,128)S(1)}, f32[2,512]{1,0:T(2,128)}, u32[]{:S(2)}) copy-start(f32[2,512]{1,0:T(2,128)} %copy-done.106) | copy-start | bytes 12292
  517.0 15.4 %collective-permute-start.2 = (bf16[2,2,512,112]{2,3,1,0:T(8,128)(2,1)S(1)}, bf16[2,2,512,112]{2,3,1,0:T(8,128)(2,1)S(1)}, u32[]{:S(2)}, u32[]{:S(2)}) collective-permute-start(bf16[2,2,512,112]{2,3,1,0:T(8,128)(2,1)S(1)} %fusion.140), channel_id=1, source_target_pairs={{4,0},{5,1},{6,2},{7,3},{12,8},{13,9},{14,10},{15,11},{20,16},{21,... | collective-permute-start | bytes 1376264 | tf_op jit(solution)/shard_map/ppermute | solution.py:32
  533.7 27.2 %copy-start.41 = (f32[128,56]{0,1:T(8,128)S(1)}, f32[128,56]{0,1:T(8,128)}, u32[]{:S(2)}) copy-start(f32[128,56]{0,1:T(8,128)} %copy-done.40) | copy-start | bytes 86020
  533.7 27.2 %copy-start.44 = (f32[128,56]{0,1:T(8,128)S(1)}, f32[128,56]{0,1:T(8,128)}, u32[]{:S(2)}) copy-start(f32[128,56]{0,1:T(8,128)} %copy-done.43) | copy-start | bytes 86020
  536.2 23.5 %all-to-all-start.5 = ((bf16[4,3,2,128,112]{3,4,1,2,0:T(8,128)(2,1)}), bf16[4,3,2,128,112]{3,4,1,2,0:T(8,128)(2,1)}, u32[]{:S(2)}, u32[]{:S(2)}) async-start(bf16[4,3,2,128,112]{3,4,1,2,0:T(8,128)(2,1)} %copy.336), calls=%async_computation.5 | async-start | bytes 1376256 | tf_op jit(solution)/shard_map/all_to_all | solution.py:345
  561.7 11.6 %copy-start.29 = (bf16[112,8,2,128]{3,1,2,0:T(8,128)(2,1)}, bf16[112,8,2,128]{3,1,2,0:T(8,128)(2,1)S(1)}, u32[]{:S(2)}) copy-start(bf16[112,8,2,128]{3,1,2,0:T(8,128)(2,1)S(1)} %copy.398) | copy-start | bytes 1376260
  574.6 8.5 slice-start
  575.9 7.3 copy-start.81
  575.9 7.3 copy-start.83
  575.9 7.3 slice-start.1
  575.9 7.3 slice-start.2
  575.9 7.8 slice-start.3
  594.7 13.3 %copy-start.95 = (pred[2,1024]{1,0:T(4,128)(4,1)S(1)}, pred[2,1024]{1,0:T(4,128)(4,1)}, u32[]{:S(2)}) copy-start(pred[2,1024]{1,0:T(4,128)(4,1)} %copy-done.92) | copy-start | bytes 6148
  594.7 13.3 %copy-start.105 = (f32[2,512]{1,0:T(2,128)S(1)}, f32[2,512]{1,0:T(2,128)}, u32[]{:S(2)}) copy-start(f32[2,512]{1,0:T(2,128)} %copy-done.104) | copy-start | bytes 12292
  615.6 16.1 %copy-start.54 = (f32[1,2,128,2,4,5]{2,1,5,4,3,0:T(2,128)S(1)}, f32[1,2,128,2,4,5]{2,1,5,4,3,0:T(2,128)}, u32[]{:S(2)}) copy-start(f32[1,2,128,2,4,5]{2,1,5,4,3,0:T(2,128)} %copy-done.53) | copy-start | bytes 122884
  629.2 19.0 %collective-permute-start.3 = (bf16[2,2,512,112]{2,3,1,0:T(8,128)(2,1)S(1)}, bf16[2,2,512,112]{2,3,1,0:T(8,128)(2,1)}, u32[]{:S(2)}, u32[]{:S(2)}) collective-permute-start(bf16[2,2,512,112]{2,3,1,0:T(8,128)(2,1)S(1)} %fusion.139), channel_id=1, source_target_pairs={{4,0},{5,1},{6,2},{7,3},{12,8},{13,9},{14,10},{15,11},{20,16},{21,... | collective-permute-start | bytes 1376264 | tf_op jit(solution)/shard_map/ppermute | solution.py:32
  651.9 30.7 %all-to-all-start.7 = ((bf16[4,3,2,128,112]{3,4,1,2,0:T(8,128)(2,1)}), bf16[4,3,2,128,112]{3,4,1,2,0:T(8,128)(2,1)}, u32[]{:S(2)}, u32[]{:S(2)}) async-start(bf16[4,3,2,128,112]{3,4,1,2,0:T(8,128)(2,1)} %copy.346), calls=%async_computation.7 | async-start | bytes 1376256 | tf_op jit(solution)/shard_map/all_to_all | solution.py:345
  663.4 11.8 %copy-start.99 = (bf16[1024]{0:T(1024)(128)(2,1)S(1)}, bf16[1024]{0:T(1024)(128)(2,1)}, u32[]{:S(2)}) copy-start(bf16[1024]{0:T(1024)(128)(2,1)} %get-tuple-element.17) | copy-start | bytes 6148
  663.4 11.8 %copy-start.91 = (bf16[1024]{0:T(1024)(128)(2,1)S(1)}, bf16[1024]{0:T(1024)(128)(2,1)}, u32[]{:S(2)}) copy-start(bf16[1024]{0:T(1024)(128)(2,1)} %get-tuple-element.19) | copy-start | bytes 6148
  663.4 11.8 %copy-start.98 = (bf16[1024]{0:T(1024)(128)(2,1)S(1)}, bf16[1024]{0:T(1024)(128)(2,1)}, u32[]{:S(2)}) copy-start(bf16[1024]{0:T(1024)(128)(2,1)} %get-tuple-element.30) | copy-start | bytes 6148
  663.5 11.8 %copy-start.90 = (bf16[1024]{0:T(1024)(128)(2,1)S(1)}, bf16[1024]{0:T(1024)(128)(2,1)}, u32[]{:S(2)}) copy-start(bf16[1024]{0:T(1024)(128)(2,1)} %get-tuple-element.31) | copy-start | bytes 6148
  672.8 11.0 %copy-start.42 = (f32[128,56]{0,1:T(8,128)S(1)}, f32[128,56]{0,1:T(8,128)}, u32[]{:S(2)}) copy-start(f32[128,56]{0,1:T(8,128)} %copy-done.40) | copy-start | bytes 86020
  672.8 11.0 %copy-start.45 = (f32[128,56]{0,1:T(8,128)S(1)}, f32[128,56]{0,1:T(8,128)}, u32[]{:S(2)}) copy-start(f32[128,56]{0,1:T(8,128)} %copy-done.43) | copy-start | bytes 86020
  684.7 7.8 copy-start.57
  696.2 8.4 copy-start.71
  696.2 13.1 %copy-start.75 = (f32[1024,1]{0,1:T(1,128)S(1)}, f32[1024,1]{0,1:T(1,128)}, u32[]{:S(2)}) copy-start(f32[1024,1]{0,1:T(1,128)} %copy-done.74) | copy-start | bytes 12292
  696.2 13.1 %copy-start.85 = (f32[256]{0:T(256)S(1)}, f32[256]{0:T(256)}, u32[]{:S(2)}) copy-start(f32[256]{0:T(256)} %copy-done.84) | copy-start | bytes 3076
  696.2 13.1 %copy-start.87 = (f32[256]{0:T(256)S(1)}, f32[256]{0:T(256)}, u32[]{:S(2)}) copy-start(f32[256]{0:T(256)} %copy-done.86) | copy-start | bytes 3076
  (61 other events, 245.9 us)
Sparse Core Ops, SparseCore 0:
  11.4 93.0 all-gather.9
  108.1 128.7 all-gather.11
  240.3 87.9 all-gather.13
  331.7 129.1 all-gather.15

commit v3 on v2

--- a/solution.py
+++ b/solution.py
@@ -121,35 +121,132 @@
 AXES = ("dp", "seq", "head")
 
 
-def halving_plan(sizes, width):
+def mesh_bits():
     dims = [
-        (axis, bit) for axis in AXES for bit in reversed(range(sizes[axis].bit_length() - 1))
+        (axis, bit)
+        for axis in AXES
+        for bit in reversed(range(lax.axis_size(axis).bit_length() - 1))
     ]
-    dp_dims, seq_dims, head_dims = (
-        [index for index, (axis, bit) in enumerate(dims) if axis == name] for name in AXES
-    )
+    groups = [[index for index, (axis, _) in enumerate(dims) if axis == name] for name in AXES]
+    return (dims, *groups)
+
+
+def my_bits(dims):
+    place = {axis: lax.axis_index(axis) for axis in AXES}
+    bits = [lax.rem(place[axis] // (1 << bit), 2) for axis, bit in dims]
+    partners = [
+        {axis: place[axis] + (1 << bit) * (1 - 2 * bits[index])}
+        for index, (axis, bit) in enumerate(dims)
+    ]
+    return (bits, partners)
+
+
+def greet(partners):
+    barrier = pltpu.get_barrier_semaphore()
+    for partner in partners:
+        pl.semaphore_signal(
+            barrier, inc=1, device_id=partner, device_id_type=pl.DeviceIdType.MESH
+        )
+    pl.semaphore_wait(barrier, len(partners))
+
+
+def gather_rows(shares, pieces, name):
+    dims, dp_dims, seq_dims, head_dims = mesh_bits()
     orders = (
-        seq_dims[::-1] + dp_dims[::-1] + head_dims[::-1],
-        seq_dims[::-1] + dp_dims + head_dims[::-1],
+        head_dims + dp_dims[::-1] + seq_dims,
+        head_dims + dp_dims + seq_dims,
+        dp_dims + head_dims + seq_dims,
+    )
+    depth = len(dims)
+    total = len(shares)
+    lag, slots = (2, 4)
+    steps = max(piece[3] for piece in pieces) + lag * depth
+
+    def kernel(*refs):
+        ins, outs = (refs[:total], refs[total : 2 * total])
+        send_sem, recv_sem, local_sem = refs[2 * total :]
+        bits, partners = my_bits(dims)
+        own = [
+            pltpu.make_async_copy(ins[index], outs[index].at[tuple(bits)], local_sem.at[index])
+            for index in range(total)
+        ]
+        for copy in own:
+            copy.start()
+        greet(partners)
+        for copy in own:
+            copy.wait()
+
+        def exchange(number, stage, chunk):
+            array, start, width, _, which = pieces[number]
+            done = orders[which][:stage]
+            at = tuple(slice(None) if dim in done else bits[dim] for dim in range(depth))
+            columns = pl.ds(pl.multiple_of(start + chunk * width, 128), width)
+            view = outs[array].at[at + (slice(None), columns)]
+            slot = lax.rem(chunk, slots)
+            return pltpu.make_async_remote_copy(
+                src_ref=view,
+                dst_ref=view,
+                send_sem=send_sem.at[number, stage, slot],
+                recv_sem=recv_sem.at[number, stage, slot],
+                device_id=partners[orders[which][stage]],
+                device_id_type=pl.DeviceIdType.MESH,
+            )
+
+        def body(step, carry):
+            for stage in range(depth, -1, -1):
+                chunk = step - lag * stage
+                for number, piece in enumerate(pieces):
+
+                    @pl.when((chunk >= 0) & (chunk < piece[3]))
+                    def _(stage=stage, chunk=chunk, number=number):
+                        if stage > 0:
+                            exchange(number, stage - 1, chunk).wait()
+                        if stage < depth:
+                            exchange(number, stage, chunk).start()
+
+            return carry
+
+        lax.fori_loop(0, steps, body, 0)
+
+    in_place = pl.BlockSpec(memory_space=pl.ANY)
+    semaphores = pltpu.SemaphoreType.DMA((len(pieces), depth, slots))
+    gathered = pl.pallas_call(
+        kernel,
+        in_specs=[in_place] * total,
+        out_specs=[in_place] * total,
+        out_shape=[
+            jax.ShapeDtypeStruct((2,) * depth + share.shape, share.dtype) for share in shares
+        ],
+        scratch_shapes=[semaphores, semaphores, pltpu.SemaphoreType.DMA((total,))],
+        compiler_params=pltpu.CompilerParams(collective_id=name, has_side_effects=True),
+    )(*shares)
+    return [value.reshape(-1, value.shape[-1]) for value in gathered]
+
+
+def halving_plan(width):
+    dims, dp_dims, seq_dims, head_dims = mesh_bits()
+    first = seq_dims[::-1]
+    orders = (
+        (0, width // 2, first + dp_dims[::-1] + head_dims[::-1]),
+        (width // 2, width // 4, first + dp_dims + head_dims[::-1]),
+        (3 * width // 4, width // 4, first + head_dims[::-1] + dp_dims[::-1]),
     )
     stages = []
     for stage in range(len(dims)):
-        together = set(orders[0][:stage]) == set(orders[1][:stage]) and (
-            orders[0][stage] == orders[1][stage]
-        )
-        columns = [(0, 0, width)] if together else [(0, 0, width // 2), (1, width // 2, width // 2)]
         parts = []
-        for which, start, count in columns:
-            left = [d for d in range(len(dims)) if d not in orders[which][:stage]]
-            parts.append((start, count, orders[which][stage], left))
+        for start, count, order in orders:
+            left = [dim for dim in range(len(dims)) if dim not in order[:stage]]
+            if parts and parts[-1][2:] == (order[stage], left):
+                parts[-1] = (parts[-1][0], parts[-1][1] + count, order[stage], left)
+            else:
+                parts.append((start, count, order[stage], left))
         stages.append(parts)
-    lags = [2 if dims[parts[0][2]][0] == "dp" else 2 for parts in stages]
+    lags = [1 if stage < len(seq_dims) else 2 for stage in range(len(dims))]
     return dims, stages, lags
 
 
 def reduce_weight_grads(pairs, extras, width):
-    sizes = {axis: lax.axis_size(axis) for axis in AXES}
-    dims, stages, lags = halving_plan(sizes, width)
+    dims, stages, lags = halving_plan(width)
     depth = len(dims)
     tokens, model = pairs[0][0].shape
     rows = model >> depth
@@ -174,12 +271,7 @@
         pool = iter(rest[5:])
         buffers = [[tuple(next(pool) for _ in range(4)) for _ in parts] for parts in stages]
         step = pl.program_id(0)
-        place = {axis: lax.axis_index(axis) for axis in AXES}
-        bits = [lax.rem(place[axis] // (1 << bit), 2) for axis, bit in dims]
-        partners = [
-            {axis: place[axis] + (1 << bit) * (1 - 2 * bits[index])}
-            for index, (axis, bit) in enumerate(dims)
-        ]
+        bits, partners = my_bits(dims)
 
         def exchange(stage, part, slot):
             start, count, dim, left = stages[stage][part]
@@ -218,12 +310,7 @@
         @pl.when(step == 0)
         def _():
             prefetch(step)
-            barrier = pltpu.get_barrier_semaphore()
-            for partner in partners:
-                pl.semaphore_signal(
-                    barrier, inc=1, device_id=partner, device_id_type=pl.DeviceIdType.MESH
-                )
-            pl.semaphore_wait(barrier, depth)
+            greet(partners)
 
         @pl.when(step + 1 < chunks)
         def _():
@@ -324,10 +411,29 @@
     )(*[left for left, _ in pairs], *[right for _, right in pairs], *whole)
 
 
-def padded(pieces):
+def lane_whole(count):
+    return count + (-count) % 128
+
+
+def chunk_whole(count):
+    return count + (-count) % CHUNK
+
+
+def padded(pieces, width):
     have = sum(piece.shape[1] for piece in pieces)
-    fill = jnp.zeros((pieces[0].shape[0], (-have) % CHUNK), pieces[0].dtype)
+    fill = jnp.zeros((pieces[0].shape[0], width - have), pieces[0].dtype)
     return jnp.concatenate(list(pieces) + [fill], axis=1)
+
+
+def columns_plan(array, width):
+    unit = 256 if width % 256 == 0 else 128
+    units = width // unit
+    near = (3 * units + 4) // 8
+    plan, start = ([], 0)
+    for which, count in ((0, near), (1, near), (2, units - 2 * near)):
+        plan.append((array, start, unit, count, which))
+        start += count * unit
+    return plan
 
 
 def to_heads(tensor, pieces):
@@ -440,44 +546,59 @@
         (routes[..., None] == jnp.arange(EXPERTS, dtype=jnp.int32)).astype(jnp.float32), axis=-2
     )
     load_part = jnp.sum(chosen * valid[None, :, :, None, None, None], axis=(1, 2))
+    in_width = lane_whole(value_end + router_cols + 4)
+    out_width = lane_whole(output_end - value_end)
     matrix_low = matrix.astype(jnp.bfloat16)
-    small_size = small.size
-    carried = jnp.concatenate([small.reshape(-1), load_part.reshape(-1)])
-    carried = jnp.pad(carried, (0, (-carried.size) % 1024))[None]
-    carried = lax.all_gather(carried, ("dp", "seq", "head"), axis=0, tiled=True)
-    loads = jnp.sum(carried[:, small_size : small_size + load_part.size], axis=0).reshape(load_part.shape)
-    small_all = (
-        carried[:, :small_size]
-        .reshape(carried.shape[0], LAYERS, small.shape[1], small.shape[2])
-        .transpose(1, 0, 2, 3)
-        .reshape(LAYERS, width, small.shape[2])
-        .astype(jnp.bfloat16)
-    )
+    small_low = small.astype(jnp.bfloat16)
+    in_low = [
+        padded([matrix_low[layer, :, :value_end], small_low[layer]], in_width)
+        for layer in range(LAYERS)
+    ]
+    out_low = [
+        padded([matrix_low[layer, :, value_end:output_end]], out_width) for layer in range(LAYERS)
+    ]
+    counts = jnp.pad(load_part.reshape(-1), (0, (-load_part.size) % 1024)).reshape(8, -1)
+    in_first, out_first, counts = gather_rows(
+        [in_low[0], out_low[0], counts],
+        columns_plan(0, in_width) + columns_plan(1, out_width) + [(2, 0, counts.shape[1], 1, 0)],
+        2,
+    )
+    loads = (
+        jnp.sum(counts.reshape(-1, load_part.size + (-load_part.size) % 1024), axis=0)[
+            : load_part.size
+        ]
+        .reshape(load_part.shape)
+    )
+    everyone = ("dp", "seq", "head")
+    in_ws, out_ws = ([in_first], [out_first])
+    ffn_ws = [lax.all_gather(matrix_low[0, :, output_end:], everyone, axis=0, tiled=True)]
+    for layer in range(1, LAYERS):
+        both = lax.all_gather(
+            jnp.concatenate([in_low[layer], out_low[layer]], axis=1), everyone, axis=0, tiled=True
+        )
+        in_ws.append(both[:, :in_width])
+        out_ws.append(both[:, in_width:])
+        ffn_ws.append(
+            lax.all_gather(matrix_low[layer, :, output_end:], everyone, axis=0, tiled=True)
+        )
     hidden = inputs.astype(jnp.float32).reshape(tokens, width)
     kept = []
-    gathered = [
-        lax.all_gather(part, ("dp", "seq", "head"), axis=0, tiled=True)
-        for layer in range(LAYERS)
-        for part in (matrix_low[layer, :, :output_end], matrix_low[layer, :, output_end:])
-    ]
     for layer in range(LAYERS):
-        attn_w, ffn_w = (gathered[2 * layer], gathered[2 * layer + 1])
-        small_w = small_all[layer]
-        gains = small_w[:, router_cols:].astype(jnp.float32)
+        in_w, out_w, ffn_w = (in_ws[layer], out_ws[layer], ffn_ws[layer])
+        gains = in_w[:, value_end + router_cols : value_end + router_cols + 4].astype(jnp.float32)
         normed_one, inverse_one = layer_stats(hidden)
         first_in = (normed_one * gains[:, 0] + gains[:, 1]).astype(jnp.bfloat16)
-        gate_prob = jax.nn.sigmoid(
-            jnp.dot(first_in, small_w[:, :router_cols], preferred_element_type=jnp.float32)
-        ).reshape(tokens, 2, HEADS, EXPERTS)
+        entered = lax.optimization_barrier(
+            jnp.dot(first_in, in_w, preferred_element_type=jnp.float32)
+        )
+        gate_prob = jax.nn.sigmoid(entered[:, value_end : value_end + router_cols]).reshape(
+            tokens, 2, HEADS, EXPERTS
+        )
         chosen_here = chosen[layer].reshape(tokens, 2, HEADS, EXPERTS)
         gates = gate_prob * chosen_here
-        query_key = jnp.dot(
-            first_in, attn_w[:, :query_end], preferred_element_type=jnp.float32
-        ).reshape(seq_count, sub_rows, 2, HEADS, HEAD_DIM)
+        query_key = entered[:, :query_end].reshape(seq_count, sub_rows, 2, HEADS, HEAD_DIM)
         rotated = rotate_pairs(query_key, cosines, sines).astype(jnp.bfloat16)
-        projected = jnp.dot(
-            first_in, attn_w[:, query_end:value_end], preferred_element_type=jnp.float32
-        ).reshape(tokens, HEADS, EXPERTS, HEAD_DIM)
+        projected = entered[:, query_end:value_end].reshape(tokens, HEADS, EXPERTS, HEAD_DIM)
         value_rows = jnp.sum(gates[:, 0, :, :, None] * projected, axis=2).astype(jnp.bfloat16)
         heads_in = to_heads(
             jnp.concatenate(
@@ -495,12 +616,15 @@
         attended_rows = to_tokens(attended.astype(jnp.bfloat16)[None], sub_rows).reshape(
             tokens, HEADS, HEAD_DIM
         )
-        mixed = (
-            (gates[:, 1, :, :, None] * attended_rows[:, :, None, :].astype(jnp.float32))
-            .astype(jnp.bfloat16)
-            .reshape(tokens, group * HEAD_DIM)
-        )
-        residual = hidden + contract_last(mixed, attn_w[:, value_end:])
+        mixed = padded(
+            [
+                (gates[:, 1, :, :, None] * attended_rows[:, :, None, :].astype(jnp.float32))
+                .astype(jnp.bfloat16)
+                .reshape(tokens, group * HEAD_DIM)
+            ],
+            out_width,
+        )
+        residual = hidden + contract_last(mixed, out_w)
         normed_two, inverse_two = layer_stats(residual)
         second_in = (normed_two * gains[:, 2] + gains[:, 3]).astype(jnp.bfloat16)
         up = jnp.dot(second_in, ffn_w[:, :FF], preferred_element_type=jnp.float32)
@@ -554,9 +678,8 @@
             up,
             act,
         ) = kept[layer]
-        attn_w, ffn_w = (gathered[2 * layer], gathered[2 * layer + 1])
-        small_w = small_all[layer]
-        gains = small_w[:, router_cols:].astype(jnp.float32)
+        in_w, out_w, ffn_w = (in_ws[layer], out_ws[layer], ffn_ws[layer])
+        gains = in_w[:, value_end + router_cols : value_end + router_cols + 4].astype(jnp.float32)
         grad_low = grad_hidden.astype(jnp.bfloat16)
         grad_act = jnp.dot(grad_low, ffn_w[:, FF:], preferred_element_type=jnp.float32)
         gelu_value, gelu_pull = jax.vjp(gelu_tanh, up)
@@ -566,9 +689,9 @@
         bias_two_grad = jnp.sum(grad_second, axis=0)
         grad_residual = grad_hidden + norm_back(grad_second, normed_two, inverse_two, gains[:, 2])
         residual_low = grad_residual.astype(jnp.bfloat16)
-        grad_mixed = jnp.dot(
-            residual_low, attn_w[:, value_end:], preferred_element_type=jnp.float32
-        ).reshape(tokens, HEADS, EXPERTS, HEAD_DIM)
+        grad_mixed = lax.optimization_barrier(
+            jnp.dot(residual_low, out_w, preferred_element_type=jnp.float32)
+        )[:, : group * HEAD_DIM].reshape(tokens, HEADS, EXPERTS, HEAD_DIM)
         grad_gate_out = jnp.sum(
             grad_mixed * attended_rows[:, :, None, :].astype(jnp.float32), axis=-1
         )
@@ -602,10 +725,8 @@
         grad_logit = (
             (grad_gates * gate_prob * (1.0 - gate_prob)).astype(jnp.bfloat16).reshape(tokens, -1)
         )
-        grad_in = jnp.concatenate([grad_qk, grad_proj], axis=1)
-        grad_first = contract_last(grad_in, attn_w[:, :value_end]) + contract_last(
-            grad_logit, small_w[:, :router_cols]
-        )
+        grad_in = padded([grad_qk, grad_proj, grad_logit], in_width)
+        grad_first = contract_last(grad_in, in_w)
         gain_one_grad = jnp.sum(grad_first * normed_one, axis=0)
         bias_one_grad = jnp.sum(grad_first, axis=0)
         grad_hidden = grad_residual + norm_back(grad_first, normed_one, inverse_one, gains[:, 0])
@@ -616,8 +737,8 @@
         near = at // 128 * 128
         norm_grads = jnp.pad(norm_grads, ((0, 0), (at - near, 128 - 4 - (at - near))))
         pairs += [
-            (first_in, padded([grad_in, grad_logit, jnp.zeros((tokens, 4), jnp.bfloat16)])),
-            (residual_low, padded([mixed])),
+            (first_in, padded([grad_in], chunk_whole(in_width))),
+            (residual_low, padded([mixed], chunk_whole(out_width))),
             (second_in, grad_up),
             (grad_low, act),
         ]

time: 1020 us -> 967 us (0.948)
  waiting for transfers between devices: 239 us -> 135 us
  Pallas kernels: 254 us -> 340 us
  blocking collectives: 128 us -> 59.8 us
  local copies, waits for them, and re-layouts: 115 us -> 142 us
  other arithmetic: 53.7 us -> 67 us
    pallas_call x0 -> x1, Pallas kernels: none -> 103 us  [gather_rows(): pl.pallas_call(kernel, in_specs=[in_place] * total, out_specs=[in_place]...]
    all_gather x4 -> x3, waiting for transfers between devices: 157 us -> 66.3 us  [the longest x1 53.3 us: local(): lax.all_gather(matrix_low[0, :, output_end:], everyone, axis=0, tiled=True)]
    all_gather x1 -> x0, blocking collectives: 76.7 us -> none  [local(): carried = lax.all_gather(carried, ('dp', 'seq', 'head'), axis=0, tiled=True)]
    pallas_call x1, Pallas kernels: 254 us -> 236 us  [reduce_weight_grads(): pl.pallas_call(kernel, grid=(chunks + starts[depth],), in_specs=[in_place...]
    dot_general x4 -> x0, local copies, waits for them, and re-layouts: 17.3 us -> none  [the longest x2 11.5 us: local(): jnp.dot(first_in, attn_w[:, query_end:value_end], preferred_element_type=...]
    slice x5 -> x10, local copies, waits for them, and re-layouts: 1.21 us -> 17 us  [the longest x4 7.6 us: local(): entered[:, query_end:value_end].reshape(tokens, HEADS, EXPERTS, HEAD_DIM)]
    dot_general x8 -> x4, matrix products: 28 us -> 17 us  [the longest x2 10.3 us: local(): jnp.dot(residual_low, out_w, preferred_element_type=jnp.float32)]
    unnamed x233 -> x240, local copies, waits for them, and re-layouts: 19.9 us -> 24.8 us
  transfers between devices with their start and end apart: 13 -> 12, of which waited for: 9 -> 6; matrix products, arithmetic and copies ran while one was open for 16% -> 18% of each run, Pallas kernels for 0% -> 11%
where the time goes in v3:
time: 967 us; the launch traced here: 956 us
  Pallas kernels  340 us (35%)
  matrix products  170 us (18%)
  local copies, waits for them, and re-layouts  142 us (15%)
  waiting for transfers between devices  135 us (14%)
  other arithmetic  67 us (7%)
  blocking collectives  59.8 us (6%)
  starting transfers between devices  27 us (3%)
  between operations  16.1 us (2%)
    pallas_call x1, Pallas kernels, reduce_weight_grads(): pl.pallas_call(kernel, grid=(chunks + starts[depth],), in_specs=[in_place...  236 us
    pallas_call x1, Pallas kernels, gather_rows(): pl.pallas_call(kernel, in_specs=[in_place] * total, out_specs=[in_place]...  103 us
    all_to_all x3, blocking collectives, to_heads(): got = lax.all_to_all(sent, 'head', split_axis=0, concat_axis=0, tiled=True)  59.8 us
    all_gather x1, waiting for transfers between devices, local(): lax.all_gather(matrix_low[0, :, output_end:], everyone, axis=0, tiled=True)  53.3 us
    dot_general x8, matrix products, contract_last(): lax.dot_general(left, right, (((1,), (1,)), ((), ())), preferred_element_...  44 us
    all_to_all x4, waiting for transfers between devices, to_tokens(): got = lax.all_to_all(sent, 'head', split_axis=0, concat_axis=0, tiled=True)  41.8 us
    all_to_all x1, waiting for transfers between devices, to_heads(): got = lax.all_to_all(sent, 'head', split_axis=0, concat_axis=0, tiled=True)  25.8 us
    dot_general x2, matrix products, attend_backward(): jnp.einsum('sqk,sqc->skc', grad_raw, query_heads, preferred_element_type=...  25.2 us
  transfers between devices with their start and end apart: 12, of which 6 were waited for; matrix products, arithmetic and copies ran while one was open for 18% of the time, Pallas kernels for 11%

profile of v3, /device:TPU:0, one launch (start us, length us, event | category | flops | bytes accessed | tf_op | source)
XLA Modules:
  0.0 956.2 jit_solution(15111990295869765521)
XLA Ops:
  14.9 103.3 %shard_map.201 = (bf16[2,2,2,2,2,32,3200]{6,5,4,3,2,1,0:T(8,128)(2,1)}, bf16[2,2,2,2,2,32,2304]{6,5,4,3,2,1,0:T(8,128)(2,1)}, f32[2,2,2,2,2,8,128]{6,5,4,3,2,1,0:T(8,128)}) custom-call(bf16[32,3200]{1,0:T(8,128)(2,1)} %concatenate.95.refs_0_, bf16[32,2304]{1,0:T(8,128)(2,1)} %concatenate.96.refs_1_, f32[8,128]{1,0:T(8,128)} %pad_bitcast_fusion.refs_2_), custom_call_target="tpu_custom_call" | custom-call | tf_op jit(solution)/shard_map/pallas_call | solution.py:213
  121.4 4.8 fusion.203
  134.8 2.3 reshape.628
  144.0 3.5 all-to-all-start
  148.3 25.8 %all-to-all-done = bf16[4,3,2,128,112]{3,2,4,1,0:T(2,128)(2,1)S(1)} async-done(((bf16[4,3,2,128,112]{3,2,4,1,0:T(2,128)(2,1)}), bf16[4,3,2,128,112]{3,2,4,1,0:T(2,128)(2,1)S(1)}, u32[]{:S(2)}, u32[]{:S(2)}) %all-to-all-start) | async-done | bytes 688160 | tf_op jit(solution)/shard_map/all_to_all | solution.py:443
  175.0 2.4 collective-permute-start
  178.7 3.9 fusion.198
  185.9 3.4 all-to-all-start.1
  189.4 14.1 %all-to-all-done.1 = bf16[4,1,2,128,112]{3,2,4,1,0:T(2,128)(2,1)S(1)} async-done(((bf16[4,1,2,128,112]{3,2,4,1,0:T(2,128)(2,1)}), bf16[4,1,2,128,112]{3,2,4,1,0:T(2,128)(2,1)S(1)}, u32[]{:S(2)}, u32[]{:S(2)}) %all-to-all-start.1) | async-done | bytes 229408 | tf_op jit(solution)/shard_map/all_to_all | solution.py:451
  204.8 3.9 fusion.199
  211.7 53.3 %all-gather.8.cloned.1.call-done = bf16[1,1024,8192]{2,1,0:T(8,128)(2,1)} async-done(((bf16[1,32,8192]{2,1,0:T(8,128)(2,1)}), bf16[1,1024,8192]{2,1,0:T(8,128)(2,1)}) %all-gather.8.cloned.1.call-update) | async-done | bytes 16777232 | tf_op jit(solution)/shard_map/all_gather | solution.py:574
  264.9 8.7 multiply_convert_fusion.3
  273.7 6.9 fusion.200
  291.6 2.3 reshape.630
  300.8 35.5 %all_to_all.40 = bf16[4,3,2,128,112]{3,2,4,1,0:T(2,128)(2,1)S(1)} all-to-all(bf16[4,3,2,128,112]{3,2,4,1,0:T(2,128)(2,1)S(1)} %copy.381), channel_id=1, replica_groups=mesh['dp'=4,'seq'=2,'head'=4] {'head'}, dimensions={0} | all-to-all | bytes 1376256 | tf_op jit(solution)/shard_map/all_to_all | solution.py:443
  339.7 2.5 collective-permute-start.1
  347.0 5.3 fusion.201
  352.3 4.2 convolution_convert_fusion
  358.4 3.6 all-to-all-start.3
  364.3 11.3 %all-to-all-done.3 = bf16[4,1,2,128,112]{3,2,4,1,0:T(2,128)(2,1)S(1)} async-done(((bf16[4,1,2,128,112]{3,2,4,1,0:T(2,128)(2,1)}), bf16[4,1,2,128,112]{3,2,4,1,0:T(2,128)(2,1)S(1)}, u32[]{:S(2)}, u32[]{:S(2)}) %all-to-all-start.3) | async-done | bytes 229408 | tf_op jit(solution)/shard_map/all_to_all | solution.py:451
  378.1 4.6 fusion.202
  384.0 13.0 %all-gather.10.cloned.1.call-done = bf16[1,1024,8192]{2,1,0:T(8,128)(2,1)} async-done(((bf16[1,32,8192]{2,1,0:T(8,128)(2,1)}), bf16[1,1024,8192]{2,1,0:T(8,128)(2,1)}) %all-gather.10.cloned.1.call-update) | async-done | bytes 16777232 | tf_op jit(solution)/shard_map/all_gather | solution.py:582
  397.1 8.1 multiply_convert_fusion.2
  406.0 4.9 fusion.37.refs_10_
  410.9 3.2 multiply_reduce_fusion.12
  415.5 5.1 fusion.40
  420.6 3.0 copy.387
  423.6 2.9 multiply_reduce_fusion.7
  428.2 12.6 %all_to_all.41 = bf16[4,1,2,128,112]{3,2,4,1,0:T(2,128)(2,1)S(1)} all-to-all(bf16[4,1,2,128,112]{3,2,4,1,0:T(2,128)(2,1)} %bitcast.276), channel_id=1, replica_groups=mesh['dp'=4,'seq'=2,'head'=4] {'head'}, dimensions={0} | all-to-all | bytes 458752 | tf_op jit(solution)/shard_map/all_to_all | solution.py:443
  443.3 4.0 fusion.139
  447.3 4.8 convolution_bitcast_fusion.1
  452.1 12.6 %fusion.106 = f32[1,2,1024,112]{2,3,1,0:T(8,128)} fusion(bf16[2,512,112]{1,2,0:T(8,128)(2,1)} %squeeze.66, f32[2,512,1024]{2,1,0:T(8,128)} %fusion.139, f32[2,512,1024]{2,1,0:T(8,128)} %get-tuple-element.129, f32[2,512]{1,0:T(2,128)S(1)} %get-tuple-element.128), kind=kOutput, calls=%fused_computation.122 | convolution fusion | flops 242223104 | bytes 9539584 | tf_op jit(solution)/shard_map/sqk,sqc->skc/dot_general | solution.py:502
  467.9 12.0 %fusion.115 = bf16[2,512,112]{1,2,0:T(8,128)(2,1)} fusion(f32[2,512,1024]{2,1,0:T(8,128)} %fusion.139, bf16[2,512,112]{1,2,0:T(8,128)(2,1)} %copy-done.65, bf16[2,512,112]{1,2,0:T(8,128)(2,1)} %copy-done.61, f32[2,512,1024]{2,1,0:T(8,128)} %get-tuple-element.129, f32[2,512]{1,0:T(2,128)S(1)} %get-tuple-element.128), kind=kOutput, calls=%fused_computation.128 | convolution fusion | flops 243255296 | bytes 9080832 | tf_op jit(solution)/shard_map/sqk,skc->sqc/dot_general | solution.py:500
  489.0 2.7 maximum_bitcast_fusion.2
  491.7 4.3 all-to-all-start.5
  498.2 16.4 %all-to-all-done.5 = bf16[4,3,2,128,112]{3,2,4,1,0:T(2,128)(2,1)} async-done(((bf16[4,3,2,128,112]{3,2,4,1,0:T(2,128)(2,1)}), bf16[4,3,2,128,112]{3,2,4,1,0:T(2,128)(2,1)}, u32[]{:S(2)}, u32[]{:S(2)}) %all-to-all-start.5) | async-done | bytes 688160 | tf_op jit(solution)/shard_map/all_to_all | solution.py:451
  520.0 2.4 multiply_convert_fusion.5
  526.0 6.9 multiply_reduce_fusion.13
  535.1 7.1 fusion.30.refs_14_
  542.9 3.2 multiply_reduce_fusion.10
  547.5 5.1 fusion.204
  552.6 3.3 copy.401
  555.9 2.6 multiply_reduce_fusion.4
  558.6 11.7 %all_to_all.42 = bf16[4,1,2,128,112]{3,2,4,1,0:T(2,128)(2,1)S(1)} all-to-all(bf16[4,1,2,128,112]{3,2,4,1,0:T(2,128)(2,1)S(1)} %bitcast.278), channel_id=1, replica_groups=mesh['dp'=4,'seq'=2,'head'=4] {'head'}, dimensions={0} | all-to-all | bytes 458752 | tf_op jit(solution)/shard_map/all_to_all | solution.py:443
  570.5 2.7 fusion.140
  573.3 3.7 convolution_bitcast_fusion
  577.0 12.6 %fusion.103 = f32[1,2,1024,112]{2,3,1,0:T(8,128)} fusion(bf16[2,512,112]{1,2,0:T(8,128)(2,1)} %copy-done.64, f32[2,512,1024]{2,1,0:T(8,128)} %fusion.140, f32[2,512,1024]{2,1,0:T(8,128)} %get-tuple-element.121, f32[2,512]{1,0:T(2,128)S(1)} %copy-done.106), kind=kOutput, calls=%fused_computation.121 | convolution fusion | flops 242223104 | bytes 9539584 | tf_op jit(solution)/shard_map/sqk,sqc->skc/dot_general | solution.py:502
  595.8 12.0 %fusion.112 = bf16[2,512,112]{1,2,0:T(8,128)(2,1)} fusion(f32[2,512,1024]{2,1,0:T(8,128)} %fusion.140, bf16[2,512,112]{1,2,0:T(8,128)(2,1)S(1)} %copy-done.63, bf16[2,512,112]{1,2,0:T(8,128)(2,1)S(1)} %copy-done.60, f32[2,512,1024]{2,1,0:T(8,128)} %get-tuple-element.121, f32[2,512]{1,0:T(2,128)} %copy-done.105), kind=kOutput, calls=%fused_computation.127 | convolution fusion | flops 243255296 | bytes 9080832 | tf_op jit(solution)/shard_map/sqk,skc->sqc/dot_general | solution.py:500
  611.7 2.7 maximum_bitcast_fusion.3
  614.3 4.6 all-to-all-start.7
  623.1 2.4 copy.417
  625.4 2.3 concatenate.119.refs_9_
  627.8 7.4 fusion.109
  637.2 2.4 copy.416
  644.9 3.7 concatenate.118.refs_8_
  654.0 3.2 multiply_convert_fusion.4
  664.1 2.4 copy.419
  666.5 8.0 multiply_reduce_fusion.11
  677.3 3.7 concatenate.120.refs_12_
  687.0 236.2 %shard_map.202 = f32[32,28672]{1,0:T(8,128)} custom-call(bf16[256,1024]{1,0:T(8,128)(2,1)S(1)} %copy-done.3, bf16[256,1024]{1,0:T(8,128)(2,1)S(1)} %get-tuple-element.57.refs_1_, bf16[256,1024]{1,0:T(8,128)(2,1)S(1)} %copy-done.5, bf16[256,1024]{1,0:T(8,128)(2,1)S(1)} %bitcast_convert_fusion.refs_3_, bf16[256,1024]{1,0:T(8,128)(2,1)S(1)} %copy-done.8, ...), custom_call_target="tpu_custom_call" | custom-call | tf_op jit(solution)/shard_map/pallas_call | solution.py:395
  927.0 2.7 fusion.188
  933.7 2.7 concatenate.122
  936.4 3.0 add_convert_fusion.1
  939.5 9.3 fusion.183
  (460 shorter events, 155.1 us)
Async XLA Ops:
  7.2 202.0 %all-gather.6.cloned.1.call-start = ((), (), s32[]{:S(2)}) async-start(), calls=%async_computation.8 | async-start | bytes 11624448 | tf_op jit(solution)/shard_map/all_gather | solution.py:576
  9.4 110.1 %copy-start.19 = (bf16[2,128,1024]{2,1,0:T(8,128)(2,1)S(1)}, bf16[2,128,1024]{2,1,0:T(8,128)(2,1)}, u32[]{:S(2)}) copy-start(bf16[2,128,1024]{2,1,0:T(8,128)(2,1)} %param.10) | copy-start | bytes 1572868
  10.5 254.4 %all-gather.8.cloned.1.call-start = ((), (), s32[]{:S(2)}) async-start(), calls=%async_computation.9 | async-start | bytes 17301504 | tf_op jit(solution)/shard_map/all_gather | solution.py:574
  11.7 385.4 %all-gather.10.cloned.1.call-start = ((), (), s32[]{:S(2)}) async-start(), calls=%async_computation.10 | async-start | bytes 17301504 | tf_op jit(solution)/shard_map/all_gather | solution.py:582
  13.2 113.0 %copy-start.86 = (f32[2,128]{1,0:T(2,128)}, f32[2,128]{1,0:T(2,128)S(1)}, u32[]{:S(2)}) copy-start(f32[2,128]{1,0:T(2,128)S(1)} %compare_convert_fusion) | copy-start | bytes 3076
  131.8 7.3 copy-start.9
  133.2 70.8 %copy-start.56 = (f32[256,4,5]{0,2,1:T(8,128)}, f32[256,4,5]{0,2,1:T(8,128)S(1)}, u32[]{:S(2)}) copy-start(f32[256,4,5]{0,2,1:T(8,128)S(1)} %get-tuple-element.104) | copy-start | bytes 61444
  142.4 373.4 %copy-start.41 = (f32[128,56]{0,1:T(8,128)}, f32[128,56]{0,1:T(8,128)S(1)}, u32[]{:S(2)}) copy-start(f32[128,56]{0,1:T(8,128)S(1)} %get-tuple-element.118) | copy-start | bytes 86020
  142.5 373.4 %copy-start.43 = (f32[128,56]{0,1:T(8,128)}, f32[128,56]{0,1:T(8,128)S(1)}, u32[]{:S(2)}) copy-start(f32[128,56]{0,1:T(8,128)S(1)} %get-tuple-element.119) | copy-start | bytes 86020
  144.0 30.0 %all-to-all-start = ((bf16[4,3,2,128,112]{3,2,4,1,0:T(2,128)(2,1)}), bf16[4,3,2,128,112]{3,2,4,1,0:T(2,128)(2,1)S(1)}, u32[]{:S(2)}, u32[]{:S(2)}) async-start(bf16[4,3,2,128,112]{3,2,4,1,0:T(2,128)(2,1)} %copy.365), calls=%async_computation | async-start | bytes 1376256 | tf_op jit(solution)/shard_map/all_to_all | solution.py:443
  148.3 34.3 %copy-start.49 = (pred[512,1024]{1,0:T(8,128)(4,1)}, pred[512,1024]{1,0:T(8,128)(4,1)S(1)}, u32[]{:S(2)}) copy-start(pred[512,1024]{1,0:T(8,128)(4,1)S(1)} %get-tuple-element.112) | copy-start | bytes 1572868
  148.3 34.3 %copy-start.50 = (pred[512,1024]{1,0:T(8,128)(4,1)}, pred[512,1024]{1,0:T(8,128)(4,1)S(1)}, u32[]{:S(2)}) copy-start(pred[512,1024]{1,0:T(8,128)(4,1)S(1)} %get-tuple-element.113) | copy-start | bytes 1572868
  175.0 3.7 collective-permute-start
  184.9 19.9 %copy-start.20 = (bf16[2,128,1024]{2,1,0:T(8,128)(2,1)S(1)}, bf16[2,128,1024]{2,1,0:T(8,128)(2,1)}, u32[]{:S(2)}) copy-start(bf16[2,128,1024]{2,1,0:T(8,128)(2,1)} %param.10) | copy-start | bytes 1572868
  185.9 17.5 %all-to-all-start.1 = ((bf16[4,1,2,128,112]{3,2,4,1,0:T(2,128)(2,1)}), bf16[4,1,2,128,112]{3,2,4,1,0:T(2,128)(2,1)S(1)}, u32[]{:S(2)}, u32[]{:S(2)}) async-start(bf16[4,1,2,128,112]{3,2,4,1,0:T(2,128)(2,1)} %bitcast.240), calls=%async_computation.1 | async-start | bytes 458752 | tf_op jit(solution)/shard_map/all_to_all | solution.py:451
  208.6 65.1 %copy-start.11 = (f32[256,1024]{1,0:T(8,128)}, f32[256,1024]{1,0:T(8,128)S(1)}, u32[]{:S(2)}) copy-start(f32[256,1024]{1,0:T(8,128)S(1)} %get-tuple-element.123) | copy-start | bytes 3145732
  209.2 64.5 %copy-start = (bf16[256,1024]{1,0:T(8,128)(2,1)}, bf16[256,1024]{1,0:T(8,128)(2,1)S(1)}, u32[]{:S(2)}) copy-start(bf16[256,1024]{1,0:T(8,128)(2,1)S(1)} %add_convert_fusion.4.refs_6_) | copy-start | bytes 1572868
  264.9 16.2 %slice-start = ((s8[11272192]{0:T(1024)(128)(4,1)}), s8[4194304]{0:T(1024)(128)(4,1)S(1)}, s32[]{:S(2)}) async-start(s8[11272192]{0:T(1024)(128)(4,1)} %bitcast.302), calls=%async_computation.11 | async-start | bytes 8388608
  264.9 16.3 %slice-start.1 = ((s8[11272192]{0:T(1024)(128)(4,1)}), s8[4194304]{0:T(1024)(128)(4,1)S(1)}, s32[]{:S(2)}) async-start(s8[11272192]{0:T(1024)(128)(4,1)} %bitcast.302), calls=%async_computation.12 | async-start | bytes 8388608
  273.7 7.5 slice-start.2
  336.3 10.7 %copy-start.92 = (pred[2,1024]{1,0:T(4,128)(4,1)S(1)}, pred[2,1024]{1,0:T(4,128)(4,1)}, u32[]{:S(2)}) copy-start(pred[2,1024]{1,0:T(4,128)(4,1)} %copy-done.91) | copy-start | bytes 6148
  339.7 6.1 collective-permute-start.1
  343.6 8.7 copy-start.39
  352.3 9.8 %copy-start.87 = (f32[2,128]{1,0:T(2,128)S(1)}, f32[2,128]{1,0:T(2,128)}, u32[]{:S(2)}) copy-start(f32[2,128]{1,0:T(2,128)} %copy-done.86) | copy-start | bytes 3076
  358.4 17.2 %all-to-all-start.3 = ((bf16[4,1,2,128,112]{3,2,4,1,0:T(2,128)(2,1)}), bf16[4,1,2,128,112]{3,2,4,1,0:T(2,128)(2,1)S(1)}, u32[]{:S(2)}, u32[]{:S(2)}) async-start(bf16[4,1,2,128,112]{3,2,4,1,0:T(2,128)(2,1)} %bitcast.239), calls=%async_computation.3 | async-start | bytes 458752 | tf_op jit(solution)/shard_map/all_to_all | solution.py:451
  384.0 21.1 %copy-start.4 = (bf16[256,1024]{1,0:T(8,128)(2,1)}, bf16[256,1024]{1,0:T(8,128)(2,1)S(1)}, u32[]{:S(2)}) copy-start(bf16[256,1024]{1,0:T(8,128)(2,1)S(1)} %add_convert_fusion.2.refs_2_) | copy-start | bytes 1572868
  397.1 8.9 copy-start.103
  466.6 16.8 %collective-permute-start.2 = (bf16[2,2,512,112]{2,3,1,0:T(8,128)(2,1)}, bf16[2,2,512,112]{2,3,1,0:T(8,128)(2,1)}, u32[]{:S(2)}, u32[]{:S(2)}) collective-permute-start(bf16[2,2,512,112]{2,3,1,0:T(8,128)(2,1)} %fusion.132), channel_id=1, source_target_pairs={{4,0},{5,1},{6,2},{7,3},{12,8},{13,9},{14,10},{15,11},{20,16},{21,... | collective-permute-start | bytes 1376264 | tf_op jit(solution)/shard_map/ppermute | solution.py:32
  491.7 22.9 %all-to-all-start.5 = ((bf16[4,3,2,128,112]{3,2,4,1,0:T(2,128)(2,1)}), bf16[4,3,2,128,112]{3,2,4,1,0:T(2,128)(2,1)}, u32[]{:S(2)}, u32[]{:S(2)}) async-start(bf16[4,3,2,128,112]{3,2,4,1,0:T(2,128)(2,1)} %maximum_bitcast_fusion.2), calls=%async_computation.5 | async-start | bytes 1376256 | tf_op jit(solution)/shard_map/all_to_all | solution.py:451
  517.8 8.1 copy-start.81
  517.8 8.1 copy-start.85
  517.8 8.1 copy-start.88
  524.3 8.6 copy-start.45
  532.9 9.3 slice-start.3
  535.0 7.2 slice-start.5
  535.1 7.8 slice-start.6
  552.6 17.9 %copy-start.35 = (bf16[2,512,112]{1,2,0:T(8,128)(2,1)S(1)}, bf16[2,512,112]{1,2,0:T(8,128)(2,1)}, u32[]{:S(2)}) copy-start(bf16[2,512,112]{1,2,0:T(8,128)(2,1)} %copy-done.34) | copy-start | bytes 688132
  552.6 17.9 %copy-start.38 = (bf16[2,512,112]{1,2,0:T(8,128)(2,1)S(1)}, bf16[2,512,112]{1,2,0:T(8,128)(2,1)}, u32[]{:S(2)}) copy-start(bf16[2,512,112]{1,2,0:T(8,128)(2,1)} %copy-done.37) | copy-start | bytes 688132
  555.9 17.3 %copy-start.93 = (pred[2,1024]{1,0:T(4,128)(4,1)S(1)}, pred[2,1024]{1,0:T(4,128)(4,1)}, u32[]{:S(2)}) copy-start(pred[2,1024]{1,0:T(4,128)(4,1)} %copy-done.91) | copy-start | bytes 6148
  555.9 17.3 %copy-start.106 = (f32[2,512]{1,0:T(2,128)S(1)}, f32[2,512]{1,0:T(2,128)}, u32[]{:S(2)}) copy-start(f32[2,512]{1,0:T(2,128)} %copy-done.105) | copy-start | bytes 12292
  577.0 15.8 %copy-start.52 = (f32[1,2,128,2,4,5]{2,1,5,4,3,0:T(2,128)S(1)}, f32[1,2,128,2,4,5]{2,1,5,4,3,0:T(2,128)}, u32[]{:S(2)}) copy-start(f32[1,2,128,2,4,5]{2,1,5,4,3,0:T(2,128)} %copy-done.51) | copy-start | bytes 122884
  577.0 18.8 %copy-start.60 = (bf16[2,512,112]{1,2,0:T(8,128)(2,1)S(1)}, bf16[2,512,112]{1,2,0:T(8,128)(2,1)}, u32[]{:S(2)}) copy-start(bf16[2,512,112]{1,2,0:T(8,128)(2,1)} %copy-done.59) | copy-start | bytes 688132
  577.0 18.8 %copy-start.63 = (bf16[2,512,112]{1,2,0:T(8,128)(2,1)S(1)}, bf16[2,512,112]{1,2,0:T(8,128)(2,1)}, u32[]{:S(2)}) copy-start(bf16[2,512,112]{1,2,0:T(8,128)(2,1)} %copy-done.62) | copy-start | bytes 688132
  591.5 18.3 %collective-permute-start.3 = (bf16[2,2,512,112]{2,3,1,0:T(8,128)(2,1)}, bf16[2,2,512,112]{2,3,1,0:T(8,128)(2,1)}, u32[]{:S(2)}, u32[]{:S(2)}) collective-permute-start(bf16[2,2,512,112]{2,3,1,0:T(8,128)(2,1)} %fusion.131), channel_id=1, source_target_pairs={{4,0},{5,1},{6,2},{7,3},{12,8},{13,9},{14,10},{15,11},{20,16},{21,... | collective-permute-start | bytes 1376264 | tf_op jit(solution)/shard_map/ppermute | solution.py:32
  614.3 34.3 %all-to-all-start.7 = ((bf16[4,3,2,128,112]{3,2,4,1,0:T(2,128)(2,1)}), bf16[4,3,2,128,112]{3,2,4,1,0:T(2,128)(2,1)}, u32[]{:S(2)}, u32[]{:S(2)}) async-start(bf16[4,3,2,128,112]{3,2,4,1,0:T(2,128)(2,1)} %maximum_bitcast_fusion.3), calls=%async_computation.7 | async-start | bytes 1376256 | tf_op jit(solution)/shard_map/all_to_all | solution.py:451
  627.8 11.8 %copy-start.97 = (bf16[1024]{0:T(1024)(128)(2,1)S(1)}, bf16[1024]{0:T(1024)(128)(2,1)}, u32[]{:S(2)}) copy-start(bf16[1024]{0:T(1024)(128)(2,1)} %get-tuple-element.37) | copy-start | bytes 6148
  627.8 11.8 %copy-start.96 = (bf16[1024]{0:T(1024)(128)(2,1)S(1)}, bf16[1024]{0:T(1024)(128)(2,1)}, u32[]{:S(2)}) copy-start(bf16[1024]{0:T(1024)(128)(2,1)} %get-tuple-element.25) | copy-start | bytes 6148
  627.8 15.2 %copy-start.98 = (bf16[1024]{0:T(1024)(128)(2,1)S(1)}, bf16[1024]{0:T(1024)(128)(2,1)}, u32[]{:S(2)}) copy-start(bf16[1024]{0:T(1024)(128)(2,1)} %get-tuple-element.23) | copy-start | bytes 6148
  635.2 9.7 %copy-start.46 = (bf16[256,40]{1,0:T(8,128)(2,1)S(1)}, bf16[256,40]{1,0:T(8,128)(2,1)}, u32[]{:S(2)}) copy-start(bf16[256,40]{1,0:T(8,128)(2,1)} %copy-done.45) | copy-start | bytes 61444
  639.6 10.4 %copy-start.42 = (f32[128,56]{0,1:T(8,128)S(1)}, f32[128,56]{0,1:T(8,128)}, u32[]{:S(2)}) copy-start(f32[128,56]{0,1:T(8,128)} %copy-done.41) | copy-start | bytes 86020
  639.6 10.4 %copy-start.44 = (f32[128,56]{0,1:T(8,128)S(1)}, f32[128,56]{0,1:T(8,128)}, u32[]{:S(2)}) copy-start(f32[128,56]{0,1:T(8,128)} %copy-done.43) | copy-start | bytes 86020
  649.9 7.3 copy-start.66
  657.2 9.3 copy-start.71
  657.2 9.3 copy-start.76
  657.2 9.3 copy-start.89
  666.5 8.0 copy-start.77
  666.5 10.7 %copy-start.47 = (bf16[256,24]{1,0:T(8,128)(2,1)S(1)}, bf16[256,24]{1,0:T(8,128)(2,1)}, u32[]{:S(2)}) copy-start(bf16[256,24]{1,0:T(8,128)(2,1)} %broadcast.466) | copy-start | bytes 36868
  923.3 7.8 copy-start.101
  923.3 8.4 copy-start.100
  939.4 9.4 copy-start.68
  939.5 9.4 copy-start.69
  939.5 9.4 copy-start.72
  939.5 9.4 copy-start.73
  939.5 9.3 copy-start.102
  (62 other events, 230.9 us)
Sparse Core Ops, SparseCore 0:
  11.4 121.0 all-gather.5
  136.1 128.7 all-gather.7
  268.5 128.4 all-gather.9

commit v4 on v3

--- a/solution.py
+++ b/solution.py
@@ -24,12 +24,6 @@
 NORM_RATE = 0.5
 MASKED = -1e30
 CHUNK = 512
-
-
-def passed_along(value, axis, by):
-    devices = lax.axis_size(axis)
-    pairs = [(i, i + by) for i in range(devices) if 0 <= i + by < devices]
-    return lax.ppermute(value, axis, pairs)
 
 
 def column_bounds():
@@ -71,22 +65,6 @@
     inverse = jnp.exp(-math.log(10000.0) * jnp.arange(half, dtype=jnp.float32) / half)
     angle = positions.astype(jnp.float32)[:, None] * inverse[None, :]
     return (jnp.cos(angle), jnp.sin(angle))
-
-
-def rotate_pairs(tensor, cosines, sines):
-    half = tensor.shape[-1] // 2
-    first, second = (tensor[..., :half], tensor[..., half:])
-    return jnp.concatenate(
-        [first * cosines - second * sines, second * cosines + first * sines], axis=-1
-    )
-
-
-def rotate_back(tensor, cosines, sines):
-    half = tensor.shape[-1] // 2
-    first, second = (tensor[..., :half], tensor[..., half:])
-    return jnp.concatenate(
-        [first * cosines + second * sines, second * cosines - first * sines], axis=-1
-    )
 
 
 def layer_stats(values):
@@ -436,79 +414,421 @@
     return plan
 
 
-def to_heads(tensor, pieces):
-    seq_count, sub_rows = tensor.shape[:2]
-    heads = HEADS
-    sent = tensor.transpose(3, 2, 0, 1, 4)
-    got = lax.all_to_all(sent, "head", split_axis=0, concat_axis=0, tiled=True)
-    return got.transpose(1, 2, 0, 3, 4).reshape(pieces, seq_count, heads * sub_rows, HEAD_DIM)
-
-
-def to_tokens(tensor, sub_rows):
-    pieces, seq_count, segment, head_dim = tensor.shape
-    sent = tensor.reshape(pieces, seq_count, segment // sub_rows, sub_rows, head_dim)
-    sent = sent.transpose(2, 0, 1, 3, 4)
-    got = lax.all_to_all(sent, "head", split_axis=0, concat_axis=0, tiled=True)
-    return got.transpose(2, 3, 1, 0, 4)
-
-
-def block_scores(query_block, keys, query_pos, key_pos, lengths):
-    raw = jnp.einsum("sqc,skc->sqk", query_block, keys, preferred_element_type=jnp.float32)
-    later = key_pos[None, None, :] <= query_pos[None, :, None]
-    inside = key_pos[None, None, :] >= 0
-    used = (key_pos[None, None, :] < lengths[:, None, None]) | (
-        key_pos[None, None, :] == query_pos[None, :, None]
-    )
-    allowed = later & inside & used
-    return jnp.where(allowed, raw * HEAD_DIM ** (-0.5), MASKED)
-
-
-def attend_forward(query_heads, keys, values, seq_start, lengths, segment):
-    rows = min(512, segment)
-    key_pos = seq_start - segment + jnp.arange(2 * segment, dtype=jnp.int32)
-    outputs, tops, totals = ([], [], [])
-    query_pos = seq_start + 0 + jnp.arange(rows, dtype=jnp.int32)
-    scores = block_scores(query_heads, keys, query_pos, key_pos, lengths)
-    top = jnp.max(scores, axis=-1, keepdims=True)
-    weights = jnp.exp(scores - top)
-    total = jnp.sum(weights, axis=-1, keepdims=True)
-    probs = (weights / total).astype(jnp.bfloat16)
-    outputs.append(jnp.einsum("sqk,skc->sqc", probs, values, preferred_element_type=jnp.float32))
-    tops.append(top)
-    totals.append(total)
-    return (outputs[0], tops, totals)
-
-
-def attend_backward(
-    query_heads, keys, values, grad_heads, tops, totals, seq_start, lengths, segment
+LANES = 128
+QUERY_TILE = 256
+
+
+def swap_halves(tensor):
+    half = HEAD_DIM // 2
+    return jnp.concatenate([tensor[:, half:], tensor[:, :half]], axis=1)
+
+
+def lane_filled(tensor):
+    fill = jnp.zeros((tensor.shape[0], LANES - tensor.shape[1]), tensor.dtype)
+    return jnp.concatenate([tensor, fill], axis=1)
+
+
+def weights_block(keys_mem, keys_own, query, start, first, segment, length):
+    contract = (((1,), (1,)), ((), ()))
+    raw = jnp.concatenate(
+        [
+            lax.dot_general(keys, query, contract, preferred_element_type=jnp.float32)
+            for keys in (keys_mem, keys_own)
+        ],
+        axis=0,
+    )
+    key_pos = start - segment + lax.broadcasted_iota(jnp.int32, raw.shape, 0)
+    query_pos = start + first + lax.broadcasted_iota(jnp.int32, raw.shape, 1)
+    used = (key_pos < length) & (key_pos < query_pos) & (key_pos >= 0)
+    allowed = used | (key_pos == query_pos)
+    scores = jnp.where(allowed, raw * HEAD_DIM ** (-0.5), MASKED)
+    weights = jnp.exp(scores - jnp.max(scores, axis=0, keepdims=True))
+    return weights * (1.0 / jnp.sum(weights, axis=0, keepdims=True))
+
+
+def contract_rows(left, right):
+    return lax.dot_general(
+        left, right, (((0,), (0,)), ((), ())), preferred_element_type=jnp.float32
+    )
+
+
+def across(axis, offset):
+    size = lax.axis_size(axis)
+    return {axis: lax.rem(lax.axis_index(axis) + offset + size, size)}
+
+
+def sent_to(source, target, send_sem, recv_sem, device):
+    return pltpu.make_async_remote_copy(
+        src_ref=source,
+        dst_ref=target,
+        send_sem=send_sem,
+        recv_sem=recv_sem,
+        device_id=device,
+        device_id_type=pl.DeviceIdType.MESH,
+    )
+
+
+def meet(memory_step):
+    barrier = pltpu.get_barrier_semaphore()
+    heads = lax.axis_size("head")
+    writers = [across("head", step) for step in range(1, heads)]
+    writers.append(across("seq", -memory_step))
+    for device in writers:
+        pl.semaphore_signal(barrier, inc=1, device_id=device, device_id_type=pl.DeviceIdType.MESH)
+    pl.semaphore_wait(barrier, len(writers))
+
+
+def gate_values(entered_ref, chosen_ref, rows):
+    at = column_bounds()[1]
+    logits = entered_ref[rows, at : at + 2 * HEADS * EXPERTS]
+    prob = 1.0 / (1.0 + jnp.exp(-logits))
+    return (prob, prob * chosen_ref[rows, :])
+
+
+def column(tensor, index):
+    return tensor[:, index : index + 1]
+
+
+def attention_forward(entered, chosen, turn_cos, turn_sin, lengths, mixed_width, name):
+    seq_count = lengths.shape[0]
+    tokens = entered.shape[0]
+    sub = tokens // seq_count
+    heads = lax.axis_size("head")
+    segment = heads * sub
+    query_end = column_bounds()[0]
+    sides = range(1, heads)
+
+    def kernel(*refs):
+        length_ref, entered_ref, chosen_ref, cos_ref, sin_ref = refs[:5]
+        mixed_ref, attended_ref, query_ref, key_ref, value_ref = refs[5:10]
+        out_buf, heads_buf, mem_buf, done_buf, back_buf = refs[10:15]
+        out_sem, in_sem, mem_sem, done_sem, back_sem = refs[15:]
+        me = lax.axis_index("head")
+        start = lax.axis_index("seq") * segment
+        turn, wind = (cos_ref[...], sin_ref[...])
+
+        def outward(b, side):
+            there = across("head", side)
+            return sent_to(
+                out_buf.at[b, there["head"]],
+                heads_buf.at[b, :, me],
+                out_sem.at[b, side - 1],
+                in_sem.at[b, side - 1],
+                there,
+            )
+
+        def onward(b):
+            return sent_to(
+                heads_buf.at[b, 1:3],
+                mem_buf.at[b],
+                mem_sem.at[0, b],
+                mem_sem.at[1, b],
+                across("seq", 1),
+            )
+
+        def homeward(b, side):
+            there = across("head", side)
+            return sent_to(
+                done_buf.at[b, there["head"]],
+                back_buf.at[b, me],
+                done_sem.at[b, side - 1],
+                back_sem.at[b, side - 1],
+                there,
+            )
+
+        meet(1)
+        gates_of = []
+        for b in range(seq_count):
+            rows = slice(b * sub, (b + 1) * sub)
+            gates = gate_values(entered_ref, chosen_ref, rows)[1]
+            gates_of.append(gates)
+            for head in range(HEADS):
+                for kind in range(2):
+                    at = (kind * HEADS + head) * HEAD_DIM
+                    vector = entered_ref[rows, at : at + HEAD_DIM]
+                    turned = vector * turn + swap_halves(vector) * wind
+                    out_buf[b, head, kind] = lane_filled(turned).astype(jnp.bfloat16)
+                value = jnp.zeros((sub, HEAD_DIM), jnp.float32)
+                for expert in range(EXPERTS):
+                    index = head * EXPERTS + expert
+                    at = query_end + index * HEAD_DIM
+                    value += column(gates, index) * entered_ref[rows, at : at + HEAD_DIM]
+                out_buf[b, head, 2] = lane_filled(value).astype(jnp.bfloat16)
+            for side in sides:
+                outward(b, side).start()
+            for kind in range(3):
+                heads_buf[b, kind, me] = out_buf[b, me, kind]
+        for b in range(seq_count):
+            for side in sides:
+                outward(b, side).wait_recv()
+            onward(b).start()
+        for b in range(seq_count):
+            onward(b).wait_recv()
+            keys_own = heads_buf[b, 1].reshape(segment, LANES)
+            values = jnp.concatenate(
+                [mem_buf[b, 1].reshape(segment, LANES), heads_buf[b, 2].reshape(segment, LANES)],
+                axis=0,
+            )
+            for first in range(0, segment, QUERY_TILE):
+                tile = slice(first // sub, (first + QUERY_TILE) // sub)
+                query = heads_buf[b, 0, tile].reshape(QUERY_TILE, LANES)
+                probs = weights_block(
+                    mem_buf[b, 0].reshape(segment, LANES),
+                    keys_own,
+                    query,
+                    start,
+                    first,
+                    segment,
+                    length_ref[b],
+                ).astype(jnp.bfloat16)
+                attended = contract_rows(values, probs).T.astype(jnp.bfloat16)
+                done_buf[b, tile] = attended.reshape(QUERY_TILE // sub, sub, LANES)
+            for side in sides:
+                homeward(b, side).start()
+            back_buf[b, me] = done_buf[b, me]
+        for b in range(seq_count):
+            query_ref[b] = heads_buf[b, 0]
+            key_ref[b, 0] = mem_buf[b, 0]
+            key_ref[b, 1] = heads_buf[b, 1]
+            value_ref[b, 0] = mem_buf[b, 1]
+            value_ref[b, 1] = heads_buf[b, 2]
+        used = HEADS * EXPERTS * HEAD_DIM
+        mixed_ref[:, used:] = jnp.zeros((tokens, mixed_width - used), jnp.bfloat16)
+        for b in range(seq_count):
+            rows = slice(b * sub, (b + 1) * sub)
+            for side in sides:
+                homeward(b, side).wait_recv()
+            for head in range(HEADS):
+                attended = back_buf[b, head]
+                attended_ref[rows, head * LANES : (head + 1) * LANES] = attended
+                wide = attended.astype(jnp.float32)[:, :HEAD_DIM]
+                for expert in range(EXPERTS):
+                    index = head * EXPERTS + expert
+                    gate = column(gates_of[b], HEADS * EXPERTS + index)
+                    mixed_ref[rows, index * HEAD_DIM : (index + 1) * HEAD_DIM] = (
+                        gate * wide
+                    ).astype(jnp.bfloat16)
+        for b in range(seq_count):
+            onward(b).wait_send()
+            for side in sides:
+                outward(b, side).wait_send()
+                homeward(b, side).wait_send()
+
+    def shape(*dims):
+        return jax.ShapeDtypeStruct(dims, jnp.bfloat16)
+
+    vmem = pl.BlockSpec(memory_space=pltpu.VMEM)
+    paired = pltpu.SemaphoreType.DMA((seq_count, heads - 1))
+    return pl.pallas_call(
+        kernel,
+        in_specs=[pl.BlockSpec(memory_space=pltpu.SMEM)] + [vmem] * 4,
+        out_specs=[vmem] * 5,
+        out_shape=[
+            shape(tokens, mixed_width),
+            shape(tokens, HEADS * LANES),
+            shape(seq_count, heads, sub, LANES),
+            shape(seq_count, 2, heads, sub, LANES),
+            shape(seq_count, 2, heads, sub, LANES),
+        ],
+        scratch_shapes=[
+            pltpu.VMEM((seq_count, heads, 3, sub, LANES), jnp.bfloat16),
+            pltpu.VMEM((seq_count, 3, heads, sub, LANES), jnp.bfloat16),
+            pltpu.VMEM((seq_count, 2, heads, sub, LANES), jnp.bfloat16),
+            pltpu.VMEM((seq_count, heads, sub, LANES), jnp.bfloat16),
+            pltpu.VMEM((seq_count, heads, sub, LANES), jnp.bfloat16),
+            paired,
+            paired,
+            pltpu.SemaphoreType.DMA((2, seq_count)),
+            paired,
+            paired,
+        ],
+        compiler_params=pltpu.CompilerParams(
+            collective_id=name, has_side_effects=True, vmem_limit_bytes=40 << 20
+        ),
+    )(lengths, entered, chosen, turn_cos, turn_sin)
+
+
+def attention_backward(
+    grad_mixed, attended, entered, chosen, turn_cos, turn_sin, lengths, saved, grad_width, name
 ):
-    rows = min(512, segment)
-    key_pos = seq_start - segment + jnp.arange(2 * segment, dtype=jnp.int32)
-    grad_keys = jnp.zeros(keys.shape, jnp.float32)
-    grad_values = jnp.zeros(values.shape, jnp.float32)
-    grad_queries = []
-    for index, start in enumerate(range(0, segment, rows)):
-        query_pos = seq_start + start + jnp.arange(rows, dtype=jnp.int32)
-        scores = block_scores(query_heads, keys, query_pos, key_pos, lengths)
-        probs = jnp.exp(scores - tops[index]) / totals[index]
-        grad_probs = jnp.einsum(
-            "sqc,skc->sqk", grad_heads, values, preferred_element_type=jnp.float32
-        )
-        delta = jnp.sum(probs * grad_probs, axis=-1, keepdims=True)
-        grad_raw = (probs * (grad_probs - delta) * HEAD_DIM ** (-0.5)).astype(jnp.bfloat16)
-        grad_queries.append(
-            jnp.einsum("sqk,skc->sqc", grad_raw, keys, preferred_element_type=jnp.float32)
-        )
-        grad_keys = jnp.einsum(
-            "sqk,sqc->skc", grad_raw, query_heads, preferred_element_type=jnp.float32
-        )
-        grad_values = jnp.einsum(
-            "sqk,sqc->skc",
-            probs.astype(jnp.bfloat16),
-            grad_heads,
-            preferred_element_type=jnp.float32,
-        )
-    return (grad_queries[0], grad_keys, grad_values)
+    query, keys, values = saved
+    seq_count = lengths.shape[0]
+    tokens = entered.shape[0]
+    sub = tokens // seq_count
+    heads = lax.axis_size("head")
+    segment = heads * sub
+    query_end, value_end = column_bounds()[:2]
+    router_cols = 2 * HEADS * EXPERTS
+    sides = range(1, heads)
+
+    def kernel(*refs):
+        length_ref, grad_ref, attended_ref, entered_ref, chosen_ref, cos_ref, sin_ref = refs[:7]
+        query_ref, key_ref, value_ref, result_ref = refs[7:11]
+        out_buf, heads_buf, mem_out, mem_in, own_buf, done_buf, back_buf = refs[11:18]
+        out_sem, in_sem, mem_sem, done_sem, back_sem = refs[18:]
+        me = lax.axis_index("head")
+        start = lax.axis_index("seq") * segment
+        turn, wind = (cos_ref[...], sin_ref[...])
+
+        def outward(b, side):
+            there = across("head", side)
+            return sent_to(
+                out_buf.at[b, there["head"]],
+                heads_buf.at[b, me],
+                out_sem.at[b, side - 1],
+                in_sem.at[b, side - 1],
+                there,
+            )
+
+        def onward(b):
+            return sent_to(
+                mem_out.at[b], mem_in.at[b], mem_sem.at[0, b], mem_sem.at[1, b], across("seq", -1)
+            )
+
+        def homeward(b, side):
+            there = across("head", side)
+            return sent_to(
+                done_buf.at[b, there["head"]],
+                back_buf.at[b, me],
+                done_sem.at[b, side - 1],
+                back_sem.at[b, side - 1],
+                there,
+            )
+
+        meet(-1)
+        lane = lax.broadcasted_iota(jnp.int32, (sub, router_cols), 1)
+        gate_grads, probs_of, gates_of = ([], [], [])
+        for b in range(seq_count):
+            rows = slice(b * sub, (b + 1) * sub)
+            prob, gates = gate_values(entered_ref, chosen_ref, rows)
+            probs_of.append(prob)
+            gates_of.append(gates)
+            gate_grad = jnp.zeros((sub, router_cols), jnp.float32)
+            for head in range(HEADS):
+                seen = attended_ref[rows, head * LANES : head * LANES + HEAD_DIM].astype(
+                    jnp.float32
+                )
+                total = jnp.zeros((sub, HEAD_DIM), jnp.float32)
+                for expert in range(EXPERTS):
+                    index = head * EXPERTS + expert
+                    part = grad_ref[rows, index * HEAD_DIM : (index + 1) * HEAD_DIM]
+                    total += column(gates, HEADS * EXPERTS + index) * part
+                    gate_grad = jnp.where(
+                        lane == HEADS * EXPERTS + index,
+                        jnp.sum(part * seen, axis=1, keepdims=True),
+                        gate_grad,
+                    )
+                out_buf[b, head] = lane_filled(total).astype(jnp.bfloat16)
+            gate_grads.append(gate_grad)
+            for side in sides:
+                outward(b, side).start()
+            heads_buf[b, me] = out_buf[b, me]
+        for b in range(seq_count):
+            for side in sides:
+                outward(b, side).wait_recv()
+            keys_mem = key_ref[b, 0].reshape(segment, LANES)
+            keys_own = key_ref[b, 1].reshape(segment, LANES)
+            keys_all = jnp.concatenate([keys_mem, keys_own], axis=0)
+            values_all = jnp.concatenate(
+                [value_ref[b, 0].reshape(segment, LANES), value_ref[b, 1].reshape(segment, LANES)],
+                axis=0,
+            )
+            grad_keys = jnp.zeros((2 * segment, LANES), jnp.float32)
+            grad_values = jnp.zeros((2 * segment, LANES), jnp.float32)
+            for first in range(0, segment, QUERY_TILE):
+                tile = slice(first // sub, (first + QUERY_TILE) // sub)
+                here = query_ref[b, tile].reshape(QUERY_TILE, LANES)
+                arrived = heads_buf[b, tile].reshape(QUERY_TILE, LANES)
+                probs = weights_block(
+                    keys_mem, keys_own, here, start, first, segment, length_ref[b]
+                )
+                grad_probs = contract_last(values_all, arrived)
+                delta = jnp.sum(probs * grad_probs, axis=0, keepdims=True)
+                grad_raw = (probs * (grad_probs - delta) * HEAD_DIM ** (-0.5)).astype(
+                    jnp.bfloat16
+                )
+                grad_values += jnp.dot(
+                    probs.astype(jnp.bfloat16), arrived, preferred_element_type=jnp.float32
+                )
+                grad_keys += jnp.dot(grad_raw, here, preferred_element_type=jnp.float32)
+                grad_query = contract_rows(keys_all, grad_raw).T.astype(jnp.bfloat16)
+                done_buf[b, tile, 0] = grad_query.reshape(QUERY_TILE // sub, sub, LANES)
+            for kind, grads in enumerate((grad_keys, grad_values)):
+                mem_out[b, kind] = grads[:segment].astype(jnp.bfloat16)
+                own_buf[b, kind] = grads[segment:]
+            onward(b).start()
+        for b in range(seq_count):
+            onward(b).wait_recv()
+            for kind in range(2):
+                total = own_buf[b, kind] + mem_in[b, kind].astype(jnp.float32)
+                done_buf[b, :, kind + 1] = total.astype(jnp.bfloat16).reshape(heads, sub, LANES)
+            for side in sides:
+                homeward(b, side).start()
+            back_buf[b, me] = done_buf[b, me]
+        used = value_end + router_cols
+        result_ref[:, used:] = jnp.zeros((tokens, grad_width - used), jnp.bfloat16)
+        for b in range(seq_count):
+            rows = slice(b * sub, (b + 1) * sub)
+            for side in sides:
+                homeward(b, side).wait_recv()
+            gate_grad = gate_grads[b]
+            for head in range(HEADS):
+                for kind in range(2):
+                    vector = back_buf[b, head, kind].astype(jnp.float32)[:, :HEAD_DIM]
+                    turned = vector * turn - swap_halves(vector) * wind
+                    at = (kind * HEADS + head) * HEAD_DIM
+                    result_ref[rows, at : at + HEAD_DIM] = turned.astype(jnp.bfloat16)
+                grad_value = back_buf[b, head, 2].astype(jnp.float32)[:, :HEAD_DIM]
+                for expert in range(EXPERTS):
+                    index = head * EXPERTS + expert
+                    at = query_end + index * HEAD_DIM
+                    gate_grad = jnp.where(
+                        lane == index,
+                        jnp.sum(
+                            entered_ref[rows, at : at + HEAD_DIM] * grad_value,
+                            axis=1,
+                            keepdims=True,
+                        ),
+                        gate_grad,
+                    )
+                    result_ref[rows, at : at + HEAD_DIM] = (
+                        column(gates_of[b], index) * grad_value
+                    ).astype(jnp.bfloat16)
+            prob = probs_of[b]
+            result_ref[rows, value_end:used] = (
+                gate_grad * chosen_ref[rows, :] * prob * (1.0 - prob)
+            ).astype(jnp.bfloat16)
+        for b in range(seq_count):
+            onward(b).wait_send()
+            for side in sides:
+                outward(b, side).wait_send()
+                homeward(b, side).wait_send()
+
+    vmem = pl.BlockSpec(memory_space=pltpu.VMEM)
+    paired = pltpu.SemaphoreType.DMA((seq_count, heads - 1))
+    return pl.pallas_call(
+        kernel,
+        in_specs=[pl.BlockSpec(memory_space=pltpu.SMEM)] + [vmem] * 9,
+        out_specs=vmem,
+        out_shape=jax.ShapeDtypeStruct((tokens, grad_width), jnp.bfloat16),
+        scratch_shapes=[
+            pltpu.VMEM((seq_count, heads, sub, LANES), jnp.bfloat16),
+            pltpu.VMEM((seq_count, heads, sub, LANES), jnp.bfloat16),
+            pltpu.VMEM((seq_count, 2, segment, LANES), jnp.bfloat16),
+            pltpu.VMEM((seq_count, 2, segment, LANES), jnp.bfloat16),
+            pltpu.VMEM((seq_count, 2, segment, LANES), jnp.float32),
+            pltpu.VMEM((seq_count, heads, 3, sub, LANES), jnp.bfloat16),
+            pltpu.VMEM((seq_count, heads, 3, sub, LANES), jnp.bfloat16),
+            paired,
+            paired,
+            pltpu.SemaphoreType.DMA((2, seq_count)),
+            paired,
+            paired,
+        ],
+        compiler_params=pltpu.CompilerParams(
+            collective_id=name, has_side_effects=True, vmem_limit_bytes=48 << 20
+        ),
+    )(lengths, grad_mixed, attended, entered, chosen, turn_cos, turn_sin, query, keys, values)
 
 
 def gelu_tanh(values):
@@ -540,8 +860,8 @@
     )
     valid = (positions[None, :] < lengths[:, None]).astype(jnp.float32)
     cosines, sines = rotary_tables(positions)
-    cosines = cosines[:, None, None, :]
-    sines = sines[:, None, None, :]
+    turn_cos = jnp.concatenate([cosines, cosines], axis=1)
+    turn_sin = jnp.concatenate([-sines, sines], axis=1)
     chosen = jnp.sum(
         (routes[..., None] == jnp.arange(EXPERTS, dtype=jnp.int32)).astype(jnp.float32), axis=-2
     )
@@ -573,14 +893,13 @@
     in_ws, out_ws = ([in_first], [out_first])
     ffn_ws = [lax.all_gather(matrix_low[0, :, output_end:], everyone, axis=0, tiled=True)]
     for layer in range(1, LAYERS):
-        both = lax.all_gather(
-            jnp.concatenate([in_low[layer], out_low[layer]], axis=1), everyone, axis=0, tiled=True
-        )
+        attn_low = jnp.concatenate([in_low[layer], out_low[layer]], axis=1)
+        ffn_ws[-1], attn_low = lax.optimization_barrier((ffn_ws[-1], attn_low))
+        both = lax.all_gather(attn_low, everyone, axis=0, tiled=True)
+        both, ffn_low = lax.optimization_barrier((both, matrix_low[layer, :, output_end:]))
         in_ws.append(both[:, :in_width])
         out_ws.append(both[:, in_width:])
-        ffn_ws.append(
-            lax.all_gather(matrix_low[layer, :, output_end:], everyone, axis=0, tiled=True)
-        )
+        ffn_ws.append(lax.all_gather(ffn_low, everyone, axis=0, tiled=True))
     hidden = inputs.astype(jnp.float32).reshape(tokens, width)
     kept = []
     for layer in range(LAYERS):
@@ -588,43 +907,18 @@
         gains = in_w[:, value_end + router_cols : value_end + router_cols + 4].astype(jnp.float32)
         normed_one, inverse_one = layer_stats(hidden)
         first_in = (normed_one * gains[:, 0] + gains[:, 1]).astype(jnp.bfloat16)
-        entered = lax.optimization_barrier(
-            jnp.dot(first_in, in_w, preferred_element_type=jnp.float32)
+        entered = jnp.dot(first_in, in_w, preferred_element_type=jnp.float32)
+        chosen_here = chosen[layer].reshape(tokens, router_cols)
+        mixed, attended, *saved = attention_forward(
+            entered,
+            chosen_here,
+            turn_cos,
+            turn_sin,
+            lengths,
+            chunk_whole(out_width),
+            3 + layer,
         )
-        gate_prob = jax.nn.sigmoid(entered[:, value_end : value_end + router_cols]).reshape(
-            tokens, 2, HEADS, EXPERTS
-        )
-        chosen_here = chosen[layer].reshape(tokens, 2, HEADS, EXPERTS)
-        gates = gate_prob * chosen_here
-        query_key = entered[:, :query_end].reshape(seq_count, sub_rows, 2, HEADS, HEAD_DIM)
-        rotated = rotate_pairs(query_key, cosines, sines).astype(jnp.bfloat16)
-        projected = entered[:, query_end:value_end].reshape(tokens, HEADS, EXPERTS, HEAD_DIM)
-        value_rows = jnp.sum(gates[:, 0, :, :, None] * projected, axis=2).astype(jnp.bfloat16)
-        heads_in = to_heads(
-            jnp.concatenate(
-                [rotated, value_rows.reshape(seq_count, sub_rows, 1, HEADS, HEAD_DIM)], axis=2
-            ),
-            3,
-        )
-        memory = passed_along(heads_in[1:], "seq", 1)
-        query_heads = heads_in[0]
-        keys = jnp.concatenate([memory[0], heads_in[1]], axis=1)
-        values = jnp.concatenate([memory[1], heads_in[2]], axis=1)
-        attended, tops, totals = attend_forward(
-            query_heads, keys, values, seq_start, lengths, segment
-        )
-        attended_rows = to_tokens(attended.astype(jnp.bfloat16)[None], sub_rows).reshape(
-            tokens, HEADS, HEAD_DIM
-        )
-        mixed = padded(
-            [
-                (gates[:, 1, :, :, None] * attended_rows[:, :, None, :].astype(jnp.float32))
-                .astype(jnp.bfloat16)
-                .reshape(tokens, group * HEAD_DIM)
-            ],
-            out_width,
-        )
-        residual = hidden + contract_last(mixed, out_w)
+        residual = hidden + contract_last(mixed[:, :out_width], out_w)
         normed_two, inverse_two = layer_stats(residual)
         second_in = (normed_two * gains[:, 2] + gains[:, 3]).astype(jnp.bfloat16)
         up = jnp.dot(second_in, ffn_w[:, :FF], preferred_element_type=jnp.float32)
@@ -635,17 +929,11 @@
                 normed_one,
                 inverse_one,
                 first_in,
-                gate_prob,
+                entered,
                 chosen_here,
-                gates,
-                projected,
-                query_heads,
-                keys,
-                values,
-                tops,
-                totals,
-                attended_rows,
                 mixed,
+                attended,
+                saved,
                 normed_two,
                 inverse_two,
                 second_in,
@@ -661,17 +949,11 @@
             normed_one,
             inverse_one,
             first_in,
-            gate_prob,
+            entered,
             chosen_here,
-            gates,
-            projected,
-            query_heads,
-            keys,
-            values,
-            tops,
-            totals,
-            attended_rows,
             mixed,
+            attended,
+            saved,
             normed_two,
             inverse_two,
             second_in,
@@ -689,44 +971,19 @@
         bias_two_grad = jnp.sum(grad_second, axis=0)
         grad_residual = grad_hidden + norm_back(grad_second, normed_two, inverse_two, gains[:, 2])
         residual_low = grad_residual.astype(jnp.bfloat16)
-        grad_mixed = lax.optimization_barrier(
-            jnp.dot(residual_low, out_w, preferred_element_type=jnp.float32)
-        )[:, : group * HEAD_DIM].reshape(tokens, HEADS, EXPERTS, HEAD_DIM)
-        grad_gate_out = jnp.sum(
-            grad_mixed * attended_rows[:, :, None, :].astype(jnp.float32), axis=-1
+        grad_in = attention_backward(
+            jnp.dot(residual_low, out_w, preferred_element_type=jnp.float32),
+            attended,
+            entered,
+            chosen_here,
+            turn_cos,
+            turn_sin,
+            lengths,
+            saved,
+            chunk_whole(in_width),
+            3 + LAYERS + layer,
         )
-        grad_att_rows = jnp.sum(grad_mixed * gates[:, 1, :, :, None], axis=2).astype(jnp.bfloat16)
-        grad_heads_in = to_heads(
-            grad_att_rows.reshape(seq_count, sub_rows, 1, HEADS, HEAD_DIM), 1
-        )[0]
-        grad_query, grad_keys, grad_values = attend_backward(
-            query_heads, keys, values, grad_heads_in, tops, totals, seq_start, lengths, segment
-        )
-        grad_kv = jnp.stack([grad_keys, grad_values], axis=0)
-        kv_back = passed_along(grad_kv[:, :, :segment].astype(jnp.bfloat16), "seq", -1)
-        grad_kv_own = (grad_kv[:, :, segment:] + kv_back.astype(jnp.float32)).astype(jnp.bfloat16)
-        grads_tok = to_tokens(
-            jnp.concatenate([grad_query.astype(jnp.bfloat16)[None], grad_kv_own], axis=0), sub_rows
-        )
-        grads_tok = grads_tok.astype(jnp.float32)
-        grad_qk = (
-            rotate_back(grads_tok[:, :, :2], cosines, sines)
-            .astype(jnp.bfloat16)
-            .reshape(tokens, query_end)
-        )
-        grad_value_rows = grads_tok[:, :, 2].reshape(tokens, HEADS, HEAD_DIM)
-        grad_proj = (
-            (gates[:, 0, :, :, None] * grad_value_rows[:, :, None, :])
-            .astype(jnp.bfloat16)
-            .reshape(tokens, group * HEAD_DIM)
-        )
-        grad_gate_value = jnp.sum(projected * grad_value_rows[:, :, None, :], axis=-1)
-        grad_gates = jnp.stack([grad_gate_value, grad_gate_out], axis=1) * chosen_here
-        grad_logit = (
-            (grad_gates * gate_prob * (1.0 - gate_prob)).astype(jnp.bfloat16).reshape(tokens, -1)
-        )
-        grad_in = padded([grad_qk, grad_proj, grad_logit], in_width)
-        grad_first = contract_last(grad_in, in_w)
+        grad_first = contract_last(grad_in[:, :in_width], in_w)
         gain_one_grad = jnp.sum(grad_first * normed_one, axis=0)
         bias_one_grad = jnp.sum(grad_first, axis=0)
         grad_hidden = grad_residual + norm_back(grad_first, normed_one, inverse_one, gains[:, 0])
@@ -737,8 +994,8 @@
         near = at // 128 * 128
         norm_grads = jnp.pad(norm_grads, ((0, 0), (at - near, 128 - 4 - (at - near))))
         pairs += [
-            (first_in, padded([grad_in], chunk_whole(in_width))),
-            (residual_low, padded([mixed], chunk_whole(out_width))),
+            (first_in, grad_in),
+            (residual_low, mixed),
             (second_in, grad_up),
             (grad_low, act),
         ]

time: 967 us -> 884 us (0.914)
  Pallas kernels: 340 us -> 513 us
  local copies, waits for them, and re-layouts: 142 us -> 31.5 us
  matrix products: 170 us -> 78.9 us
  waiting for transfers between devices: 135 us -> 209 us
  blocking collectives: 59.8 us -> 0 us
  other arithmetic: 67 us -> 25.5 us
  starting transfers between devices: 27 us -> 0.12 us
    pallas_call x0 -> x4, Pallas kernels: none -> 176 us  [the longest x2 90.1 us: attention_backward(): pl.pallas_call(kernel, in_specs=[pl.BlockSpec(memory_space=pltpu.SMEM)] +...]
    all_gather x2, waiting for transfers between devices: 13 us -> 91.7 us  [the longest x1 91.6 us: local(): both = lax.all_gather(attn_low, everyone, axis=0, tiled=True)]
    dot_general x12 -> x2, matrix products: 77.5 us -> 6.89 us  [local(): entered = jnp.dot(first_in, in_w, preferred_element_type=jnp.float32)]
    all_to_all x5 -> x0, waiting for transfers between devices: 67.6 us -> none  [the longest x4 41.8 us: to_tokens(): got = lax.all_to_all(sent, 'head', split_axis=0, concat_axis=0, tiled=True)]
    all_gather x1, waiting for transfers between devices: 53.3 us -> 118 us  [local(): lax.all_gather(matrix_low[0, :, output_end:], everyone, axis=0, tiled=True)]
    all_to_all x3 -> x0, blocking collectives: 59.8 us -> none  [to_heads(): got = lax.all_to_all(sent, 'head', split_axis=0, concat_axis=0, tiled=True)]
    slice x30 -> x3, local copies, waits for them, and re-layouts: 30.7 us -> 0.05 us  [local(): chosen_here = chosen[layer].reshape(tokens, router_cols)]
    all_to_all x5 -> x0, starting transfers between devices: 19.4 us -> none  [the longest x4 15.9 us: to_tokens(): got = lax.all_to_all(sent, 'head', split_axis=0, concat_axis=0, tiled=True)]
  transfers between devices with their start and end apart: 12 -> 3, of which waited for: 6 -> 2; matrix products, arithmetic and copies ran while one was open for 18% -> 4% of each run, Pallas kernels for 11% -> 21%
where the time goes in v4:
time: 884 us; the launch traced here: 874 us
  Pallas kernels  513 us (58%)
  waiting for transfers between devices  209 us (24%)
  matrix products  78.9 us (9%)
  local copies, waits for them, and re-layouts  31.5 us (4%)
  other arithmetic  25.5 us (3%)
  between operations  15.5 us (2%)
    pallas_call x1, Pallas kernels, reduce_weight_grads(): pl.pallas_call(kernel, grid=(chunks + starts[depth],), in_specs=[in_place...  237 us
    all_gather x1, waiting for transfers between devices, local(): lax.all_gather(matrix_low[0, :, output_end:], everyone, axis=0, tiled=True)  118 us
    pallas_call x1, Pallas kernels, gather_rows(): pl.pallas_call(kernel, in_specs=[in_place] * total, out_specs=[in_place]...  99.8 us
    all_gather x1, waiting for transfers between devices, local(): both = lax.all_gather(attn_low, everyone, axis=0, tiled=True)  91.6 us
    pallas_call x2, Pallas kernels, attention_backward(): pl.pallas_call(kernel, in_specs=[pl.BlockSpec(memory_space=pltpu.SMEM)] +...  90.1 us
    pallas_call x2, Pallas kernels, attention_forward(): pl.pallas_call(kernel, in_specs=[pl.BlockSpec(memory_space=pltpu.SMEM)] +...  86.3 us
    dot_general x8, matrix products, contract_last(): lax.dot_general(left, right, (((1,), (1,)), ((), ())), preferred_element_...  37.8 us
  transfers between devices with their start and end apart: 3, of which 2 were waited for; matrix products, arithmetic and copies ran while one was open for 4% of the time, Pallas kernels for 21%

profile of v4, /device:TPU:0, one launch (start us, length us, event | category | flops | bytes accessed | tf_op | source)
XLA Modules:
  0.0 873.6 jit_solution(8827464831488722447)
XLA Ops:
  7.2 2.2 convert_element_type.107
  9.4 1.0 slice_bitcast_fusion
  10.8 0.8 concatenate.27
  11.6 117.6 %all-gather.9.cloned.1.call-done = bf16[1,1024,8192]{2,1,0:T(8,128)(2,1)} async-done(((bf16[1,32,8192]{2,1,0:T(8,128)(2,1)}), bf16[1,1024,8192]{2,1,0:T(8,128)(2,1)}) %all-gather.9.cloned.1.call-update) | async-done | bytes 16777232 | tf_op jit(solution)/shard_map/all_gather | solution.py:894
  129.3 91.6 %all-gather.5.cloned.1.call-done = bf16[1024,5504]{1,0:T(8,128)(2,1)} async-done(((bf16[32,5504]{1,0:T(8,128)(2,1)}), bf16[1024,5504]{1,0:T(8,128)(2,1)}) %all-gather.5.cloned.1.call-update) | async-done | bytes 11272208 | tf_op jit(solution)/shard_map/all_gather | solution.py:898
  221.7 0.8 copy.48.refs_2_.refs_4_
  222.4 0.7 concatenate.24.refs_1_
  223.1 0.8 concatenate.23.refs_0_
  223.9 0.6 pad_bitcast_fusion.refs_2_
  224.5 99.8 %shard_map.201 = (bf16[2,2,2,2,2,32,3200]{6,5,4,3,2,1,0:T(8,128)(2,1)}, bf16[2,2,2,2,2,32,2304]{6,5,4,3,2,1,0:T(8,128)(2,1)}, f32[2,2,2,2,2,8,128]{6,5,4,3,2,1,0:T(8,128)}) custom-call(bf16[32,3200]{1,0:T(8,128)(2,1)} %concatenate.23.refs_0_, bf16[32,2304]{1,0:T(8,128)(2,1)} %concatenate.24.refs_1_, f32[8,128]{1,0:T(8,128)} %pad_bitcast_fusion.refs_2_), custom_call_target="tpu_custom_call" | custom-call | tf_op jit(solution)/shard_map/pallas_call | solution.py:191
  324.3 0.9 reduce_sum.271
  325.2 0.7 reshape.284
  325.9 1.1 slice.174
  327.1 0.3 fusion.62
  327.8 0.3 multiply_reduce_fusion.11
  328.2 0.3 add_convert_fusion.5
  328.5 5.0 fusion.81.refs_1_.refs_3_
  333.5 52.9 %shard_map.202 = (bf16[256,2560]{1,0:T(8,128)(2,1)S(1)}, bf16[256,512]{1,0:T(8,128)(2,1)S(1)}, bf16[2,4,128,128]{3,2,1,0:T(8,128)(2,1)S(1)}, bf16[2,2,4,128,128]...) custom-call(s32[2]{0:T(128)S(1)} %copy-done.36, f32[256,3200]{1,0:T(8,128)S(1)} %fusion.81.refs_1_.refs_3_, ...), custom_call_target="tpu_custom_call" | custom-call | tf_op jit(solution)/shard_map/pallas_call | solution.py:622
  386.5 0.6 compare_select_fusion
  387.0 1.8 fusion.78
  389.4 0.9 bitcast_convert_fusion.refs_3_
  390.6 8.8 %multiply_convert_fusion.1 = (bf16[256,4096]{1,0:T(8,128)(2,1)S(1)}, f32[256,4096]{1,0:T(8,128)}) fusion(bf16[256,1024]{1,0:T(8,128)(2,1)S(1)} %add_convert_fusion.4.refs_6_, bf16[1024,8192]{1,0:T(8,128)(2,1)} %bitcast.114), kind=kOutput, calls=%fused_computation.40 | convolution fusion | flops 2156920832 | bytes 15204352 | tf_op jit(solution)/shard_map/dot_general | solution.py:924
  399.4 6.6 fusion.79
  406.5 1.0 slice_reduce_fusion.1
  407.8 1.9 fusion.18.refs_1_.refs_3_
  409.8 0.8 copy-done.9
  410.6 33.4 %shard_map.203 = (bf16[256,2560]{1,0:T(8,128)(2,1)S(1)}, bf16[256,512]{1,0:T(8,128)(2,1)S(1)}, bf16[2,4,128,128]{3,2,1,0:T(8,128)(2,1)S(1)}, bf16[2,2,4,128,128]...) custom-call(s32[2]{0:T(128)S(1)} %copy-done.36, f32[256,3200]{1,0:T(8,128)S(1)} %fusion.18.refs_1_.refs_3_, ...), custom_call_target="tpu_custom_call" | custom-call | tf_op jit(solution)/shard_map/pallas_call | solution.py:622
  444.0 1.5 fusion.80
  445.8 0.3 add_convert_fusion.2.refs_2_
  446.1 8.2 multiply_convert_fusion
  454.3 1.0 copy-done.57
  455.3 5.0 fusion.33.refs_10_
  460.3 6.2 multiply_reduce_fusion.2
  466.6 0.4 fusion.72
  467.0 3.8 fusion.34.refs_1_
  470.9 43.6 %shard_map.204.refs_8_ = bf16[256,3584]{1,0:T(8,128)(2,1)S(1)} custom-call(s32[2]{0:T(128)S(1)} %copy-done.36, f32[256,2304]{1,0:T(8,128)S(1)} %fusion.34.refs_1_, bf16[256,512]{1,0:T(8,128)(2,1)S(1)} %copy-done.33, f32[256,3200]{1,0:T(8,128)} %copy-done.1, f32[256,40]{1,0:T(8,128)S(1)} %copy-done.18, f32[128,112]{1,0:T(8,128)S(1)} %pad_maximum_fusion.1.refs_3_.refs_5_, ...), custom_call_target="tpu_custom_call" | custom-call | tf_op jit(solution)/shard_map/pallas_call | solution.py:809
  514.5 5.7 multiply_reduce_fusion.3
  520.3 0.4 fusion.71
  520.7 1.8 copy-done.58
  522.5 7.1 fusion.26.refs_14_
  529.6 6.1 multiply_reduce_fusion
  535.8 1.4 fusion.70
  537.2 1.4 fusion.82.refs_1_
  539.0 46.5 %shard_map.205.refs_12_ = bf16[256,3584]{1,0:T(8,128)(2,1)S(1)} custom-call(s32[2]{0:T(128)S(1)} %copy-done.36, f32[256,2304]{1,0:T(8,128)S(1)} %fusion.82.refs_1_, bf16[256,512]{1,0:T(8,128)(2,1)S(1)} %copy-done.29, f32[256,3200]{1,0:T(8,128)} %copy-done, f32[256,40]{1,0:T(8,128)S(1)} %copy-done.17, f32[128,112]{1,0:T(8,128)S(1)} %pad_maximum_fusion.1.refs_3_.refs_5_, ...), custom_call_target="tpu_custom_call" | custom-call | tf_op jit(solution)/shard_map/pallas_call | solution.py:809
  585.6 3.3 multiply_reduce_fusion.1
  589.7 1.0 copy-done.6
  590.7 1.0 copy-done.8
  591.8 1.0 copy-done.10
  592.8 1.0 copy-done.12
  593.9 1.3 copy-done.15
  595.2 1.0 copy-done.27
  596.2 236.5 %shard_map.206 = f32[32,28672]{1,0:T(8,128)} custom-call(bf16[256,1024]{1,0:T(8,128)(2,1)S(1)} %copy-done.10, bf16[256,1024]{1,0:T(8,128)(2,1)S(1)} %get-tuple-element.81.refs_1_, bf16[256,1024]{1,0:T(8,128)(2,1)S(1)} %copy-done.12, bf16[256,1024]{1,0:T(8,128)(2,1)S(1)} %copy-done.4, bf16[256,1024]{1,0:T(8,128)(2,1)S(1)} %copy-done.27, ...), custom_call_target="tpu_custom_call" | custom-call | tf_op jit(solution)/shard_map/pallas_call | solution.py:373
  832.7 1.4 slice_bitcast_fusion.6
  834.2 1.8 fusion.74
  836.0 1.9 fusion.75
  837.9 2.7 fusion.73
  840.6 0.6 broadcast_multiply_fusion
  841.1 0.6 broadcast_multiply_fusion.1
  841.7 1.4 concatenate.28
  843.1 2.7 concatenate.29
  845.8 3.0 add_convert_fusion.1
  848.9 1.5 fusion.66
  850.3 9.8 %fusion.68 = (bf16[2,32,13568]{2,1,0:T(8,128)(2,1)}, f32[2,32,13568]{2,1,0:T(8,128)}, f32[2,32,13568]{2,1,0:T(8,128)}, f32[2,32,13568]{2,1,0:T(8,128)}, f32[2,32,13568]{2,1,0:T(8,128)}) fusion(f32[2,32,13568]{2,1,0:T(8,128)S(1)} %copy-done.37, f32[13568]{0:T(1024)S(1)} %select_select_fusion, f32[2,32,13568]{2,1,0:T(8,128)} %param.15, ...), kind=kLoop, calls=%fused_computation.152 | loop fusion | flops 14761984 | bytes 29578240 | tf_op jit(solution)/shard_map/convert_element_type | solution.py:1035
  860.1 6.6 fusion.55
  (200 shorter events, 4.4 us)
Async XLA Ops:
  7.2 3.4 copy-start.52
  7.2 213.8 %copy-start.53 = (s32[2,2,128,2,4,2]{2,5,4,3,1,0:T(2,128)S(1)}, s32[2,2,128,2,4,2]{2,5,4,3,1,0:T(2,128)}, u32[]{:S(2)}) copy-start(s32[2,2,128,2,4,2]{2,5,4,3,1,0:T(2,128)} %param.12) | copy-start | bytes 98308
  7.2 122.0 %all-gather.9.cloned.1.call-start = ((), (), s32[]{:S(2)}) async-start(), calls=%async_computation.2 | async-start | bytes 17301504 | tf_op jit(solution)/shard_map/all_gather | solution.py:894
  9.4 211.6 %copy-start.36 = (s32[2]{0:T(128)S(1)}, s32[2]{0:T(128)}, u32[]{:S(2)}) copy-start(s32[2]{0:T(128)} %refs_0_.7) | copy-start | bytes 28
  10.5 317.2 %copy-start.44 = (bf16[2,128,1024]{2,1,0:T(8,128)(2,1)S(1)}, bf16[2,128,1024]{2,1,0:T(8,128)(2,1)}, u32[]{:S(2)}) copy-start(bf16[2,128,1024]{2,1,0:T(8,128)(2,1)} %param.10) | copy-start | bytes 1572868
  10.5 210.4 %all-gather.5.cloned.1.call-start = ((), (), s32[]{:S(2)}) async-start(), calls=%async_computation | async-start | bytes 11624448 | tf_op jit(solution)/shard_map/all_gather | solution.py:898
  129.2 316.9 %all-gather.7.cloned.1.call-start = ((), (), s32[]{:S(2)}) async-start(), calls=%async_computation.1 | async-start | bytes 17301504 | tf_op jit(solution)/shard_map/all_gather | solution.py:902
  221.7 111.8 %copy-start.16 = (f32[256,40]{1,0:T(8,128)}, f32[256,40]{1,0:T(8,128)S(1)}, u32[]{:S(2)}) copy-start(f32[256,40]{1,0:T(8,128)S(1)} %copy.46.refs_2_.refs_4_) | copy-start | bytes 122884
  327.8 257.7 %copy-start.54 = (f32[256]{0:T(256)}, f32[256]{0:T(256)S(1)}, u32[]{:S(2)}) copy-start(f32[256]{0:T(256)S(1)} %get-tuple-element.108) | copy-start | bytes 3076
  328.1 257.4 %copy-start.56 = (f32[256]{0:T(256)}, f32[256]{0:T(256)S(1)}, u32[]{:S(2)}) copy-start(f32[256]{0:T(256)S(1)} %get-tuple-element.106) | copy-start | bytes 3076
  328.2 58.9 %slice-start.5 = ((s8[4718592]{0:T(1024)(128)(4,1)}), s8[4194304]{0:T(1024)(128)(4,1)S(1)}, s32[]{:S(2)}) async-start(s8[4718592]{0:T(1024)(128)(4,1)} %bitcast.118), calls=%async_computation.8 | async-start | bytes 8388608
  328.5 58.6 %slice-start.6 = ((s8[4718592]{0:T(1024)(128)(4,1)}), s8[524288]{0:T(1024)(128)(4,1)S(1)}, s32[]{:S(2)}) async-start(s8[4718592]{0:T(1024)(128)(4,1)} %bitcast.118), calls=%async_computation.9 | async-start | bytes 1048576
  333.4 55.4 %copy-start = (f32[256,3200]{1,0:T(8,128)}, f32[256,3200]{1,0:T(8,128)S(1)}, u32[]{:S(2)}) copy-start(f32[256,3200]{1,0:T(8,128)S(1)} %fusion.81.refs_1_.refs_3_) | copy-start | bytes 9830404
  386.4 2.5 copy-start.13
  386.4 2.5 copy-start.19
  386.4 2.5 copy-start.21
  386.4 2.5 copy-start.28
  386.4 2.5 copy-start.30
  387.0 2.2 copy-start.51
  389.4 10.1 %copy-start.42 = (f32[2,128,1024]{2,1,0:T(8,128)}, f32[2,128,1024]{2,1,0:T(8,128)S(1)}, u32[]{:S(2)}) copy-start(f32[2,128,1024]{2,1,0:T(8,128)S(1)} %convert_multiply_fusion) | copy-start | bytes 3145732
  390.3 16.0 %slice-start.2 = ((s8[11272192]{0:T(1024)(128)(4,1)}), s8[4194304]{0:T(1024)(128)(4,1)S(1)}, s32[]{:S(2)}) async-start(s8[11272192]{0:T(1024)(128)(4,1)} %bitcast.111), calls=%async_computation.5 | async-start | bytes 8388608
  390.6 8.9 %copy-start.7 = (bf16[256,1024]{1,0:T(8,128)(2,1)}, bf16[256,1024]{1,0:T(8,128)(2,1)S(1)}, u32[]{:S(2)}) copy-start(bf16[256,1024]{1,0:T(8,128)(2,1)S(1)} %add_convert_fusion.4.refs_6_) | copy-start | bytes 1572868
  390.6 15.7 %slice-start.3 = ((s8[11272192]{0:T(1024)(128)(4,1)}), s8[4194304]{0:T(1024)(128)(4,1)S(1)}, s32[]{:S(2)}) async-start(s8[11272192]{0:T(1024)(128)(4,1)} %bitcast.111), calls=%async_computation.6 | async-start | bytes 8388608
  390.6 15.7 %slice-start.4 = ((s8[11272192]{0:T(1024)(128)(4,1)}), s8[2883584]{0:T(1024)(128)(4,1)S(1)}, s32[]{:S(2)}) async-start(s8[11272192]{0:T(1024)(128)(4,1)} %bitcast.111), calls=%async_computation.7 | async-start | bytes 5767168
  399.4 6.6 copy-start.48
  406.0 37.9 %copy-start.40 = (f32[256,1024]{1,0:T(8,128)}, f32[256,1024]{1,0:T(8,128)S(1)}, u32[]{:S(2)}) copy-start(f32[256,1024]{1,0:T(8,128)S(1)} %get-tuple-element.118) | copy-start | bytes 3145732
  407.8 2.8 copy-start.18
  410.5 34.9 %copy-start.1 = (f32[256,3200]{1,0:T(8,128)}, f32[256,3200]{1,0:T(8,128)S(1)}, u32[]{:S(2)}) copy-start(f32[256,3200]{1,0:T(8,128)S(1)} %fusion.18.refs_1_.refs_3_) | copy-start | bytes 9830404
  443.9 1.6 copy-start.14
  443.9 1.6 copy-start.23
  443.9 1.6 copy-start.25
  443.9 1.6 copy-start.32
  444.0 1.6 copy-start.34
  445.5 21.1 %copy-start.38 = (f32[256,1024]{1,0:T(8,128)}, f32[256,1024]{1,0:T(8,128)S(1)}, u32[]{:S(2)}) copy-start(f32[256,1024]{1,0:T(8,128)S(1)} %get-tuple-element.120) | copy-start | bytes 3145732
  446.1 8.2 copy-start.11
  446.1 8.2 copy-start.4
  446.1 9.2 %copy-start.57 = (bf16[1024,8192]{1,0:T(8,128)(2,1)S(1)}, bf16[1024,8192]{1,0:T(8,128)(2,1)}, u32[]{:S(2)}) copy-start(bf16[1024,8192]{1,0:T(8,128)(2,1)} %all-gather.7.cloned.1.call-done) | copy-start | bytes 50331652
  460.3 6.2 copy-start.49
  460.3 6.3 copy-start.43
  467.0 3.9 copy-start.24
  467.0 3.9 copy-start.26
  467.0 3.9 copy-start.33
  467.0 3.9 copy-start.35
  470.9 43.6 %copy-start.41 = (f32[256,1024]{1,0:T(8,128)S(1)}, f32[256,1024]{1,0:T(8,128)}, u32[]{:S(2)}) copy-start(f32[256,1024]{1,0:T(8,128)} %copy-done.40) | copy-start | bytes 3145732
  514.5 5.8 copy-start.2
  520.3 2.2 copy-start.58
  520.7 16.5 %slice-start.7 = ((s8[4718592]{0:T(1024)(128)(4,1)}), s8[4194304]{0:T(1024)(128)(4,1)S(1)}, s32[]{:S(2)}) async-start(s8[4718592]{0:T(1024)(128)(4,1)} %bitcast.121), calls=%async_computation.10 | async-start | bytes 8388608
  522.5 14.7 %slice-start.8 = ((s8[4718592]{0:T(1024)(128)(4,1)}), s8[524288]{0:T(1024)(128)(4,1)S(1)}, s32[]{:S(2)}) async-start(s8[4718592]{0:T(1024)(128)(4,1)} %bitcast.121), calls=%async_computation.11 | async-start | bytes 1048576
  529.6 6.1 copy-start.50
  535.7 49.8 %slice-start = ((s8[6553600]{0:T(1024)(128)(4,1)}), s8[4194304]{0:T(1024)(128)(4,1)S(1)}, s32[]{:S(2)}) async-start(s8[6553600]{0:T(1024)(128)(4,1)} %bitcast.108), calls=%async_computation.3 | async-start | bytes 8388608
  537.2 1.5 copy-start.5
  537.2 1.5 copy-start.17
  537.2 1.5 copy-start.20
  537.2 1.6 copy-start.22
  537.2 1.7 copy-start.29
  537.2 1.8 copy-start.31
  537.2 48.3 %slice-start.1 = ((s8[6553600]{0:T(1024)(128)(4,1)}), s8[2359296]{0:T(1024)(128)(4,1)S(1)}, s32[]{:S(2)}) async-start(s8[6553600]{0:T(1024)(128)(4,1)} %bitcast.108), calls=%async_computation.4 | async-start | bytes 4718592
  539.0 46.6 %copy-start.45 = (bf16[2,128,1024]{2,1,0:T(8,128)(2,1)S(1)}, bf16[2,128,1024]{2,1,0:T(8,128)(2,1)}, u32[]{:S(2)}) copy-start(bf16[2,128,1024]{2,1,0:T(8,128)(2,1)} %param.10) | copy-start | bytes 1572868
  585.5 3.3 copy-start.3
  840.6 5.3 copy-start.55
  843.1 7.2 copy-start.37
  845.8 4.5 copy-start.46
  850.3 9.8 %copy-start.39 = (f32[256,1024]{1,0:T(8,128)S(1)}, f32[256,1024]{1,0:T(8,128)}, u32[]{:S(2)}) copy-start(f32[256,1024]{1,0:T(8,128)} %copy-done.38) | copy-start | bytes 3145732
  850.3 9.8 %copy-start.47 = (bf16[256,4096]{1,0:T(8,128)(2,1)S(1)}, bf16[256,4096]{1,0:T(8,128)(2,1)}, u32[]{:S(2)}) copy-start(bf16[256,4096]{1,0:T(8,128)(2,1)} %get-tuple-element.121.refs_11_) | copy-start | bytes 6291460
  (7 other events, 7.3 us)
Sparse Core Ops, SparseCore 0:
  11.6 117.5 all-gather.8
  132.6 88.2 all-gather.4
  224.5 158.2 all-gather.6

commit v5 on v4

--- a/solution.py
+++ b/solution.py
@@ -128,7 +128,7 @@
     pl.semaphore_wait(barrier, len(partners))
 
 
-def gather_rows(shares, pieces, name):
+def gather_rows(share, counts, unit, name):
     dims, dp_dims, seq_dims, head_dims = mesh_bits()
     orders = (
         head_dims + dp_dims[::-1] + seq_dims,
@@ -136,69 +136,136 @@
         dp_dims + head_dims + seq_dims,
     )
     depth = len(dims)
-    total = len(shares)
+    rows, width = share.shape
+    units = width // unit
+    near = (3 * units + 4) // 8
+    pieces, start = ([], 0)
+    for which, count in ((0, near), (1, near), (2, units - 2 * near)):
+        pieces.append((start, count, which))
+        start += count * unit
     lag, slots = (2, 4)
-    steps = max(piece[3] for piece in pieces) + lag * depth
+    ring = (depth + 1) * lag + 6
+    steps = max(count for _, count, _ in pieces) + lag * depth
 
     def kernel(*refs):
-        ins, outs = (refs[:total], refs[total : 2 * total])
-        send_sem, recv_sem, local_sem = refs[2 * total :]
+        share_ref, counts_ref, out_ref, counts_out = refs[:4]
+        send_sem, recv_sem, load_sem, store_sem, small_send, small_recv, small_load = refs[4:11]
+        buffers = refs[11:]
         bits, partners = my_bits(dims)
-        own = [
-            pltpu.make_async_copy(ins[index], outs[index].at[tuple(bits)], local_sem.at[index])
-            for index in range(total)
-        ]
-        for copy in own:
-            copy.start()
+
+        def at_stage(which, stage):
+            done = orders[which][:stage]
+            return tuple(slice(None) if dim in done else bits[dim] for dim in range(depth))
+
+        def columns(number, chunk):
+            return pl.ds(pl.multiple_of(pieces[number][0] + chunk * unit, 128), unit)
+
+        def exchange(number, stage, chunk):
+            which = pieces[number][2]
+            view = buffers[number].at[(lax.rem(chunk, ring),) + at_stage(which, stage)]
+            slot = lax.rem(chunk, slots)
+            return sent_to(
+                view,
+                view,
+                send_sem.at[number, stage, slot],
+                recv_sem.at[number, stage, slot],
+                partners[orders[which][stage]],
+            )
+
+        def load(number, chunk):
+            return pltpu.make_async_copy(
+                share_ref.at[:, columns(number, chunk)],
+                buffers[number].at[(lax.rem(chunk, ring),) + tuple(bits)],
+                load_sem.at[number, lax.rem(chunk, slots)],
+            )
+
+        def store(number, chunk):
+            return pltpu.make_async_copy(
+                buffers[number].at[lax.rem(chunk, ring)],
+                out_ref.at[(slice(None),) * (depth + 1) + (columns(number, chunk),)],
+                store_sem.at[number, lax.rem(chunk, slots)],
+            )
+
+        def small(stage):
+            view = counts_out.at[at_stage(0, stage)]
+            return sent_to(
+                view, view, small_send.at[stage], small_recv.at[stage], partners[orders[0][stage]]
+            )
+
+        own_counts = pltpu.make_async_copy(counts_ref, counts_out.at[tuple(bits)], small_load)
+        own_counts.start()
+        for number in range(len(pieces)):
+            for chunk in range(2):
+                load(number, jnp.int32(chunk)).start()
         greet(partners)
-        for copy in own:
-            copy.wait()
-
-        def exchange(number, stage, chunk):
-            array, start, width, _, which = pieces[number]
-            done = orders[which][:stage]
-            at = tuple(slice(None) if dim in done else bits[dim] for dim in range(depth))
-            columns = pl.ds(pl.multiple_of(start + chunk * width, 128), width)
-            view = outs[array].at[at + (slice(None), columns)]
-            slot = lax.rem(chunk, slots)
-            return pltpu.make_async_remote_copy(
-                src_ref=view,
-                dst_ref=view,
-                send_sem=send_sem.at[number, stage, slot],
-                recv_sem=recv_sem.at[number, stage, slot],
-                device_id=partners[orders[which][stage]],
-                device_id_type=pl.DeviceIdType.MESH,
-            )
+        own_counts.wait()
 
         def body(step, carry):
             for stage in range(depth, -1, -1):
                 chunk = step - lag * stage
                 for number, piece in enumerate(pieces):
 
-                    @pl.when((chunk >= 0) & (chunk < piece[3]))
-                    def _(stage=stage, chunk=chunk, number=number):
+                    @pl.when((chunk >= 0) & (chunk < piece[1]))
+                    def _(stage=stage, chunk=chunk, number=number, piece=piece):
                         if stage > 0:
                             exchange(number, stage - 1, chunk).wait()
+                        else:
+                            load(number, chunk).wait()
+
+                            @pl.when(chunk + 2 < piece[1])
+                            def _():
+                                load(number, chunk + 2).start()
+
                         if stage < depth:
                             exchange(number, stage, chunk).start()
+                        else:
+
+                            @pl.when(chunk >= slots)
+                            def _():
+                                store(number, chunk - slots).wait()
+
+                            store(number, chunk).start()
+
+                @pl.when(chunk == 0)
+                def _(stage=stage):
+                    if stage > 0:
+                        small(stage - 1).wait()
+                    if stage < depth:
+                        small(stage).start()
 
             return carry
 
         lax.fori_loop(0, steps, body, 0)
+        for number, piece in enumerate(pieces):
+            for back in range(min(slots, piece[1])):
+                store(number, jnp.int32(piece[1] - 1 - back)).wait()
 
     in_place = pl.BlockSpec(memory_space=pl.ANY)
     semaphores = pltpu.SemaphoreType.DMA((len(pieces), depth, slots))
-    gathered = pl.pallas_call(
+    local = pltpu.SemaphoreType.DMA((len(pieces), slots))
+    gathered, all_counts = pl.pallas_call(
         kernel,
-        in_specs=[in_place] * total,
-        out_specs=[in_place] * total,
+        in_specs=[in_place] * 2,
+        out_specs=[in_place] * 2,
         out_shape=[
-            jax.ShapeDtypeStruct((2,) * depth + share.shape, share.dtype) for share in shares
+            jax.ShapeDtypeStruct((2,) * depth + value.shape, value.dtype)
+            for value in (share, counts)
         ],
-        scratch_shapes=[semaphores, semaphores, pltpu.SemaphoreType.DMA((total,))],
-        compiler_params=pltpu.CompilerParams(collective_id=name, has_side_effects=True),
-    )(*shares)
-    return [value.reshape(-1, value.shape[-1]) for value in gathered]
+        scratch_shapes=[
+            semaphores,
+            semaphores,
+            local,
+            local,
+            pltpu.SemaphoreType.DMA((depth,)),
+            pltpu.SemaphoreType.DMA((depth,)),
+            pltpu.SemaphoreType.DMA,
+        ]
+        + [pltpu.VMEM((ring,) + (2,) * depth + (rows, unit), share.dtype) for _ in pieces],
+        compiler_params=pltpu.CompilerParams(
+            collective_id=name, has_side_effects=True, vmem_limit_bytes=48 << 20
+        ),
+    )(share, counts)
+    return (gathered.reshape(-1, width), all_counts.reshape(-1, counts.shape[1]))
 
 
 def halving_plan(width):
@@ -401,17 +468,6 @@
     have = sum(piece.shape[1] for piece in pieces)
     fill = jnp.zeros((pieces[0].shape[0], width - have), pieces[0].dtype)
     return jnp.concatenate(list(pieces) + [fill], axis=1)
-
-
-def columns_plan(array, width):
-    unit = 256 if width % 256 == 0 else 128
-    units = width // unit
-    near = (3 * units + 4) // 8
-    plan, start = ([], 0)
-    for which, count in ((0, near), (1, near), (2, units - 2 * near)):
-        plan.append((array, start, unit, count, which))
-        start += count * unit
-    return plan
 
 
 LANES = 128
@@ -877,29 +933,24 @@
     out_low = [
         padded([matrix_low[layer, :, value_end:output_end]], out_width) for layer in range(LAYERS)
     ]
-    counts = jnp.pad(load_part.reshape(-1), (0, (-load_part.size) % 1024)).reshape(8, -1)
-    in_first, out_first, counts = gather_rows(
-        [in_low[0], out_low[0], counts],
-        columns_plan(0, in_width) + columns_plan(1, out_width) + [(2, 0, counts.shape[1], 1, 0)],
-        2,
-    )
-    loads = (
-        jnp.sum(counts.reshape(-1, load_part.size + (-load_part.size) % 1024), axis=0)[
-            : load_part.size
-        ]
-        .reshape(load_part.shape)
-    )
-    everyone = ("dp", "seq", "head")
-    in_ws, out_ws = ([in_first], [out_first])
-    ffn_ws = [lax.all_gather(matrix_low[0, :, output_end:], everyone, axis=0, tiled=True)]
-    for layer in range(1, LAYERS):
-        attn_low = jnp.concatenate([in_low[layer], out_low[layer]], axis=1)
-        ffn_ws[-1], attn_low = lax.optimization_barrier((ffn_ws[-1], attn_low))
-        both = lax.all_gather(attn_low, everyone, axis=0, tiled=True)
-        both, ffn_low = lax.optimization_barrier((both, matrix_low[layer, :, output_end:]))
-        in_ws.append(both[:, :in_width])
-        out_ws.append(both[:, in_width:])
-        ffn_ws.append(lax.all_gather(ffn_low, everyone, axis=0, tiled=True))
+    ffn_low = [matrix_low[layer, :, output_end:] for layer in range(LAYERS)]
+    size = load_part.size
+    counts = jnp.pad(load_part.reshape(-1), (0, (-size) % 1024)).reshape(8, -1)
+    early = []
+    for layer in range(LAYERS):
+        early += [in_low[layer], out_low[layer]] + ([ffn_low[layer]] if layer + 1 < LAYERS else [])
+    gathered, counts = gather_rows(jnp.concatenate(early, axis=1), counts, 128, 2)
+    counts, late = lax.optimization_barrier((counts, ffn_low[-1]))
+    loads = jnp.sum(counts.reshape(-1, size + (-size) % 1024), axis=0)[:size].reshape(
+        load_part.shape
+    )
+    late = lax.all_gather(late, ("dp", "seq", "head"), axis=0, tiled=True)
+    pieces, start = ([], 0)
+    for value in early:
+        pieces.append(gathered[:, start : start + value.shape[1]])
+        start += value.shape[1]
+    pieces.append(late)
+    in_ws, out_ws, ffn_ws = (pieces[0::3], pieces[1::3], pieces[2::3])
     hidden = inputs.astype(jnp.float32).reshape(tokens, width)
     kept = []
     for layer in range(LAYERS):

time: 884 us -> 785 us (0.89)
  waiting for transfers between devices: 209 us -> 0.04 us
  Pallas kernels: 513 us -> 610 us
  matrix products: 78.9 us -> 93.3 us
    all_gather x3 -> x1, waiting for transfers between devices: 209 us -> 0.02 us  [local(): late = lax.all_gather(late, ('dp', 'seq', 'head'), axis=0, tiled=True)]
    pallas_call x1, Pallas kernels: 99.8 us -> 178 us  [gather_rows(): pl.pallas_call(kernel, in_specs=[in_place] * 2, out_specs=[in_place] * 2,...]
    pallas_call x2, Pallas kernels: 86.3 us -> 103 us  [attention_forward(): pl.pallas_call(kernel, in_specs=[pl.BlockSpec(memory_space=pltpu.SMEM)] +...]
  transfers between devices with their start and end apart: 3 -> 1, of which waited for: 2 -> 0; matrix products, arithmetic and copies ran while one was open for 4% -> 6% of each run, Pallas kernels for 21% -> 13%
where the time goes in v5:
time: 785 us; the launch traced here: 775 us
  Pallas kernels  610 us (78%)
  matrix products  93.3 us (12%)
  local copies, waits for them, and re-layouts  30.2 us (4%)
  other arithmetic  25.8 us (3%)
  between operations  15.6 us (2%)
    pallas_call x1, Pallas kernels, reduce_weight_grads(): pl.pallas_call(kernel, grid=(chunks + starts[depth],), in_specs=[in_place...  238 us
    pallas_call x1, Pallas kernels, gather_rows(): pl.pallas_call(kernel, in_specs=[in_place] * 2, out_specs=[in_place] * 2,...  178 us
    pallas_call x2, Pallas kernels, attention_forward(): pl.pallas_call(kernel, in_specs=[pl.BlockSpec(memory_space=pltpu.SMEM)] +...  103 us
    pallas_call x2, Pallas kernels, attention_backward(): pl.pallas_call(kernel, in_specs=[pl.BlockSpec(memory_space=pltpu.SMEM)] +...  91.2 us
    dot_general x8, matrix products, contract_last(): lax.dot_general(left, right, (((1,), (1,)), ((), ())), preferred_element_...  44.8 us
    dot_general x2, matrix products, local(): up = jnp.dot(second_in, ffn_w[:, :FF], preferred_element_type=jnp.float32)  16.9 us
  transfers between devices with their start and end apart: 1, of which 0 were waited for; matrix products, arithmetic and copies ran while one was open for 6% of the time, Pallas kernels for 13%

profile of v5, /device:TPU:0, one launch (start us, length us, event | category | flops | bytes accessed | tf_op | source)
XLA Modules:
  0.0 774.9 jit_solution(11556040151691283743)
XLA Ops:
  7.3 2.2 convert_element_type.103
  9.6 0.9 slice_bitcast_fusion
  11.1 0.4 concatenate.17.refs_0_
  11.5 178.2 %shard_map.201 = (bf16[2,2,2,2,2,32,19200]{6,5,4,3,2,1,0:T(8,128)(2,1)}, f32[2,2,2,2,2,8,128]{6,5,4,3,2,1,0:T(8,128)S(1)}) custom-call(bf16[32,19200]{1,0:T(8,128)(2,1)S(1)} %concatenate.17.refs_0_, f32[8,128]{1,0:T(8,128)S(1)} %pad_bitcast_fusion.refs_1_), custom_call_target="tpu_custom_call" | custom-call | tf_op jit(solution)/shard_map/pallas_call | solution.py:246
  189.9 0.8 copy.51.refs_2_.refs_4_
  190.7 0.7 reshape.266
  191.4 1.2 fusion.82
  193.0 0.3 fusion.72
  193.7 0.3 multiply_reduce_fusion.11
  194.0 0.3 add_convert_fusion.4.refs_4_
  194.3 5.1 fusion.22.refs_1_.refs_3_
  199.4 0.8 copy-done.6
  200.2 42.4 %shard_map.202 = (bf16[256,2560]{1,0:T(8,128)(2,1)S(1)}, bf16[256,512]{1,0:T(8,128)(2,1)S(1)}, bf16[2,4,128,128]{3,2,1,0:T(8,128)(2,1)S(1)}, bf16[2,2,4,128,128]...) custom-call(s32[2]{0:T(128)S(1)} %copy-done.37, f32[256,3200]{1,0:T(8,128)S(1)} %fusion.22.refs_1_.refs_3_, ...), custom_call_target="tpu_custom_call" | custom-call | tf_op jit(solution)/shard_map/pallas_call | solution.py:678
  242.6 5.1 fusion.89
  247.7 0.2 multiply_reduce_fusion.10
  248.0 0.3 add_convert_fusion.3.refs_6_
  248.3 8.8 %multiply_convert_fusion.1 = (bf16[256,4096]{1,0:T(8,128)(2,1)S(1)}, f32[256,4096]{1,0:T(8,128)}) fusion(bf16[256,1024]{1,0:T(8,128)(2,1)S(1)} %add_convert_fusion.3.refs_6_, bf16[1024,19200]{1,0:T(8,128)(2,1)} %bitcast.115), kind=kOutput, calls=%fused_computation.44 | convolution fusion | flops 2156920832 | bytes 15204352 | tf_op jit(solution)/shard_map/dot_general | solution.py:975
  257.0 6.6 fusion.90
  263.7 0.2 multiply_reduce_fusion.9
  264.0 0.3 add_convert_fusion.2.refs_0_
  264.2 6.7 fusion.18.refs_1_.refs_3_
  270.9 0.8 copy-done.10
  271.7 60.5 %shard_map.203 = (bf16[256,2560]{1,0:T(8,128)(2,1)S(1)}, bf16[256,512]{1,0:T(8,128)(2,1)S(1)}, bf16[2,4,128,128]{3,2,1,0:T(8,128)(2,1)S(1)}, bf16[2,2,4,128,128]...) custom-call(s32[2]{0:T(128)S(1)} %copy-done.37, f32[256,3200]{1,0:T(8,128)S(1)} %fusion.18.refs_1_.refs_3_, ...), custom_call_target="tpu_custom_call" | custom-call | tf_op jit(solution)/shard_map/pallas_call | solution.py:678
  332.3 0.6 compare_select_fusion
  332.9 4.5 fusion.91
  337.5 0.2 multiply_reduce_fusion.8
  337.7 0.6 select_select_fusion
  338.6 0.9 copy-done.41
  339.5 0.2 add_convert_fusion.1.refs_2_
  339.8 8.2 %multiply_convert_fusion = (bf16[256,4096]{1,0:T(8,128)(2,1)}, f32[256,4096]{1,0:T(8,128)S(1)}) fusion(bf16[256,1024]{1,0:T(8,128)(2,1)S(1)} %add_convert_fusion.1.refs_2_, bf16[1024,8192]{1,0:T(8,128)(2,1)} %all-gather.2.cloned.1.call-done), kind=kOutput, calls=%fused_computation.43 | convolution fusion | flops 2156920832 | bytes 15204352 | tf_op jit(solution)/shard_map/dot_general | solution.py:975
  348.0 0.9 copy-done.59
  348.9 5.1 fusion.37.refs_10_
  354.1 2.8 multiply_reduce_fusion.2
  356.9 1.4 fusion.81
  358.3 3.8 fusion.38.refs_1_
  362.2 44.9 %shard_map.204.refs_8_ = bf16[256,3584]{1,0:T(8,128)(2,1)S(1)} custom-call(s32[2]{0:T(128)S(1)} %copy-done.37, f32[256,2304]{1,0:T(8,128)S(1)} %fusion.38.refs_1_, bf16[256,512]{1,0:T(8,128)(2,1)S(1)} %copy-done.34, f32[256,3200]{1,0:T(8,128)} %copy-done.1, f32[256,40]{1,0:T(8,128)S(1)} %copy-done.19, f32[128,112]{1,0:T(8,128)S(1)} %pad_maximum_fusion.1.refs_3_.refs_5_, ...), custom_call_target="tpu_custom_call" | custom-call | tf_op jit(solution)/shard_map/pallas_call | solution.py:865
  407.2 6.6 multiply_reduce_fusion.3
  413.8 0.2 copy.58
  414.1 0.8 pad.12.clone
  414.9 2.7 fusion.80
  417.7 6.8 fusion.30.refs_14_
  424.5 6.1 multiply_reduce_fusion
  430.7 1.4 fusion.79
  432.2 4.0 fusion.42.refs_1_
  436.2 46.2 %shard_map.205.refs_12_ = bf16[256,3584]{1,0:T(8,128)(2,1)S(1)} custom-call(s32[2]{0:T(128)S(1)} %copy-done.37, f32[256,2304]{1,0:T(8,128)S(1)} %fusion.42.refs_1_, bf16[256,512]{1,0:T(8,128)(2,1)S(1)} %copy-done.30, f32[256,3200]{1,0:T(8,128)} %copy-done, f32[256,40]{1,0:T(8,128)S(1)} %copy-done.18, f32[128,112]{1,0:T(8,128)S(1)} %pad_maximum_fusion.1.refs_3_.refs_5_, ...), custom_call_target="tpu_custom_call" | custom-call | tf_op jit(solution)/shard_map/pallas_call | solution.py:865
  482.5 6.6 multiply_reduce_fusion.1
  489.5 1.0 copy-done.5
  490.5 1.0 copy-done.7
  491.6 1.0 copy-done.9
  492.6 1.0 copy-done.11
  493.7 1.0 copy-done.13
  494.7 1.3 copy-done.16
  496.0 0.9 copy-done.20
  497.0 237.7 %shard_map.206 = f32[32,28672]{1,0:T(8,128)} custom-call(bf16[256,1024]{1,0:T(8,128)(2,1)S(1)} %copy-done.11, bf16[256,1024]{1,0:T(8,128)(2,1)S(1)} %get-tuple-element.71.refs_1_, bf16[256,1024]{1,0:T(8,128)(2,1)S(1)} %copy-done.13, bf16[256,1024]{1,0:T(8,128)(2,1)S(1)} %bitcast_convert_fusion.refs_3_, bf16[256,1024]{1,0:T(8,128)(2,1)S(1)} %copy-done.7, ...), custom_call_target="tpu_custom_call" | custom-call | tf_op jit(solution)/shard_map/pallas_call | solution.py:440
  734.7 0.8 slice_bitcast_fusion.7
  735.5 1.9 fusion.84
  737.4 1.9 fusion.85
  739.4 3.0 fusion.83
  742.4 2.6 concatenate.20
  745.0 2.5 concatenate.21
  747.5 2.6 add_convert_fusion
  750.1 0.7 fusion.75
  750.8 10.3 %fusion.77 = (bf16[2,32,13568]{2,1,0:T(8,128)(2,1)}, f32[2,32,13568]{2,1,0:T(8,128)}, f32[2,32,13568]{2,1,0:T(8,128)}, f32[2,32,13568]{2,1,0:T(8,128)}, f32[2,32,13568]{2,1,0:T(8,128)}) fusion(f32[2,32,13568]{2,1,0:T(8,128)} %param.14, f32[13568]{0:T(1024)S(1)} %copy-done.52, f32[2,32,13568]{2,1,0:T(8,128)} %param.15, f32[2,32,13568]{2,1,0:T(8,128)} %param.16, ...), kind=kLoop, calls=%fused_computation.153 | loop fusion | flops 14761984 | bytes 29578240 | tf_op jit(solution)/shard_map/convert_element_type | solution.py:1086
  761.0 6.6 fusion.65
  (175 shorter events, 2.5 us)
Async XLA Ops:
  7.2 332.6 %all-gather.2.cloned.1.call-start = ((), (), s32[]{:S(2)}) async-start(), calls=%async_computation | async-start | bytes 17301504 | tf_op jit(solution)/shard_map/all_gather | solution.py:947
  7.2 3.3 copy-start.53
  7.2 3.3 copy-start.57
  7.2 3.4 copy-start.37
  10.5 183.0 %copy-start.43 = (bf16[2,128,1024]{2,1,0:T(8,128)(2,1)S(1)}, bf16[2,128,1024]{2,1,0:T(8,128)(2,1)}, u32[]{:S(2)}) copy-start(bf16[2,128,1024]{2,1,0:T(8,128)(2,1)} %param.10) | copy-start | bytes 1572868
  189.9 9.5 %copy-start.17 = (f32[256,40]{1,0:T(8,128)}, f32[256,40]{1,0:T(8,128)S(1)}, u32[]{:S(2)}) copy-start(f32[256,40]{1,0:T(8,128)S(1)} %copy.48.refs_2_.refs_4_) | copy-start | bytes 122884
  199.4 0.8 copy-start.6
  200.1 47.5 %copy-start = (f32[256,3200]{1,0:T(8,128)}, f32[256,3200]{1,0:T(8,128)S(1)}, u32[]{:S(2)}) copy-start(f32[256,3200]{1,0:T(8,128)S(1)} %fusion.22.refs_1_.refs_3_) | copy-start | bytes 9830404
  242.5 5.1 copy-start.14
  242.6 5.1 copy-start.21
  242.6 5.1 copy-start.23
  242.6 5.1 copy-start.29
  242.6 5.1 copy-start.31
  247.7 9.3 %copy-start.38 = (f32[256,1024]{1,0:T(8,128)}, f32[256,1024]{1,0:T(8,128)S(1)}, u32[]{:S(2)}) copy-start(f32[256,1024]{1,0:T(8,128)S(1)} %get-tuple-element.107) | copy-start | bytes 3145732
  248.3 8.8 %copy-start.8 = (bf16[256,1024]{1,0:T(8,128)(2,1)}, bf16[256,1024]{1,0:T(8,128)(2,1)S(1)}, u32[]{:S(2)}) copy-start(bf16[256,1024]{1,0:T(8,128)(2,1)S(1)} %add_convert_fusion.3.refs_6_) | copy-start | bytes 1572868
  257.0 6.6 copy-start.48
  263.6 143.5 %copy-start.40 = (f32[256,1024]{1,0:T(8,128)}, f32[256,1024]{1,0:T(8,128)S(1)}, u32[]{:S(2)}) copy-start(f32[256,1024]{1,0:T(8,128)S(1)} %get-tuple-element.111) | copy-start | bytes 3145732
  264.2 7.5 copy-start.19
  270.9 0.8 copy-start.10
  271.7 65.7 %copy-start.1 = (f32[256,3200]{1,0:T(8,128)}, f32[256,3200]{1,0:T(8,128)S(1)}, u32[]{:S(2)}) copy-start(f32[256,3200]{1,0:T(8,128)S(1)} %fusion.18.refs_1_.refs_3_) | copy-start | bytes 9830404
  332.3 5.2 copy-start.15
  332.3 5.2 copy-start.25
  332.3 5.2 copy-start.27
  332.3 5.2 copy-start.33
  332.3 5.2 copy-start.35
  332.9 5.5 copy-start.51
  338.5 1.0 copy-start.41
  339.8 8.2 %copy-start.12 = (bf16[256,1024]{1,0:T(8,128)(2,1)}, bf16[256,1024]{1,0:T(8,128)(2,1)S(1)}, u32[]{:S(2)}) copy-start(bf16[256,1024]{1,0:T(8,128)(2,1)S(1)} %add_convert_fusion.1.refs_2_) | copy-start | bytes 1572868
  339.8 9.1 %copy-start.59 = (bf16[1024,8192]{1,0:T(8,128)(2,1)S(1)}, bf16[1024,8192]{1,0:T(8,128)(2,1)}, u32[]{:S(2)}) copy-start(bf16[1024,8192]{1,0:T(8,128)(2,1)} %all-gather.2.cloned.1.call-done) | copy-start | bytes 50331652
  354.1 2.8 copy-start.49
  354.1 2.8 copy-start.42
  358.3 3.9 copy-start.26
  358.3 3.9 copy-start.28
  358.3 3.9 copy-start.34
  358.3 3.9 copy-start.36
  407.2 6.6 copy-start.2
  414.0 3.6 copy-start.60
  417.7 6.9 copy-start.39
  424.5 6.1 copy-start.50
  432.1 4.0 copy-start.4
  432.1 4.0 copy-start.18
  432.1 4.0 copy-start.22
  432.1 4.0 copy-start.24
  432.2 4.0 copy-start.30
  432.2 4.0 copy-start.32
  436.2 46.3 %copy-start.44 = (bf16[2,128,1024]{2,1,0:T(8,128)(2,1)S(1)}, bf16[2,128,1024]{2,1,0:T(8,128)(2,1)}, u32[]{:S(2)}) copy-start(bf16[2,128,1024]{2,1,0:T(8,128)(2,1)} %param.10) | copy-start | bytes 1572868
  482.5 6.6 copy-start.3
  489.5 1.0 copy-start.5
  490.5 1.0 copy-start.7
  491.6 1.0 copy-start.9
  492.6 1.0 copy-start.11
  493.7 1.0 copy-start.13
  494.7 1.3 copy-start.16
  496.0 0.9 copy-start.20
  742.4 5.2 copy-start.46
  745.0 5.1 copy-start.54
  745.0 5.1 copy-start.55
  745.0 5.1 copy-start.56
  745.0 5.1 copy-start.58
  745.0 5.8 copy-start.52
  747.5 3.3 copy-start.45
  750.8 10.3 %copy-start.47 = (bf16[256,4096]{1,0:T(8,128)(2,1)S(1)}, bf16[256,4096]{1,0:T(8,128)(2,1)}, u32[]{:S(2)}) copy-start(bf16[256,4096]{1,0:T(8,128)(2,1)} %get-tuple-element.114.refs_11_) | copy-start | bytes 6291460
Sparse Core Ops, SparseCore 0:
  189.8 147.7 all-gather.1

commit v6 on v5

--- a/solution.py
+++ b/solution.py
@@ -24,6 +24,7 @@
 NORM_RATE = 0.5
 MASKED = -1e30
 CHUNK = 512
+NATIVE = ((LAYERS - 1, "up"), (LAYERS - 1, "down"))
 
 
 def column_bounds():
@@ -299,11 +300,7 @@
     for left, right in pairs:
         firsts.append(firsts[-1] + right.shape[1] // width)
     chunks = firsts[-1]
-    per_layer = len(pairs) // len(extras)
-    spots = [
-        (firsts[per_layer * index] + near // width, near % width)
-        for index, (_, near) in enumerate(extras)
-    ]
+    spots = [(firsts[pair] + near // width, near % width) for _, pair, near in extras]
     starts = [sum(lags[:stage]) for stage in range(depth + 1)]
     count_pairs, count_extras = (len(pairs), len(extras))
 
@@ -436,7 +433,7 @@
                 pltpu.SemaphoreType.DMA((slots,)),
             ]
     in_place = pl.BlockSpec(memory_space=pl.ANY)
-    whole = [value.reshape((2,) * depth + (rows, 128)) for value, _ in extras]
+    whole = [value.reshape((2,) * depth + (rows, 128)) for value, _, _ in extras]
     return pl.pallas_call(
         kernel,
         grid=(chunks + starts[depth],),
@@ -454,6 +451,20 @@
             dimension_semantics=("arbitrary",),
         ),
     )(*[left for left, _ in pairs], *[right for _, right in pairs], *whole)
+
+
+def reduction_order(tensor):
+    dp, seq = (lax.axis_size("dp"), lax.axis_size("seq"))
+    count, width = tensor.shape
+    split = tensor.reshape(count, dp, seq, width // (dp * seq))
+    return split.transpose(0, 2, 1, 3).reshape(count, width)
+
+
+def reduced_natively(left, right):
+    share = contract_first(reduction_order(left), right).astype(jnp.bfloat16)
+    for axis in ("seq", "dp"):
+        share = lax.psum_scatter(share, axis, scatter_dimension=0, tiled=True)
+    return share
 
 
 def lane_whole(count):
@@ -721,7 +732,7 @@
         length_ref, grad_ref, attended_ref, entered_ref, chosen_ref, cos_ref, sin_ref = refs[:7]
         query_ref, key_ref, value_ref, result_ref = refs[7:11]
         out_buf, heads_buf, mem_out, mem_in, own_buf, done_buf, back_buf = refs[11:18]
-        out_sem, in_sem, mem_sem, done_sem, back_sem = refs[18:]
+        out_sem, in_sem, mem_sem, query_sem, done_sem, back_sem = refs[18:]
         me = lax.axis_index("head")
         start = lax.axis_index("seq") * segment
         turn, wind = (cos_ref[...], sin_ref[...])
@@ -741,15 +752,34 @@
                 mem_out.at[b], mem_in.at[b], mem_sem.at[0, b], mem_sem.at[1, b], across("seq", -1)
             )
 
+        def queries_home(b, side):
+            there = across("head", side)
+            return sent_to(
+                done_buf.at[b, there["head"], 0],
+                back_buf.at[b, me, 0],
+                query_sem.at[0, b, side - 1],
+                query_sem.at[1, b, side - 1],
+                there,
+            )
+
         def homeward(b, side):
             there = across("head", side)
             return sent_to(
-                done_buf.at[b, there["head"]],
-                back_buf.at[b, me],
+                done_buf.at[b, there["head"], 1:3],
+                back_buf.at[b, me, 1:3],
                 done_sem.at[b, side - 1],
                 back_sem.at[b, side - 1],
                 there,
             )
+
+        def join_memory(b):
+            onward(b).wait_recv()
+            for kind in range(2):
+                total = own_buf[b, kind] + mem_in[b, kind].astype(jnp.float32)
+                done_buf[b, :, kind + 1] = total.astype(jnp.bfloat16).reshape(heads, sub, LANES)
+            for side in sides:
+                homeward(b, side).start()
+            back_buf[b, me] = done_buf[b, me]
 
         meet(-1)
         lane = lax.broadcasted_iota(jnp.int32, (sub, router_cols), 1)
@@ -809,23 +839,21 @@
                 grad_keys += jnp.dot(grad_raw, here, preferred_element_type=jnp.float32)
                 grad_query = contract_rows(keys_all, grad_raw).T.astype(jnp.bfloat16)
                 done_buf[b, tile, 0] = grad_query.reshape(QUERY_TILE // sub, sub, LANES)
+                if b > 0 and first == 0:
+                    join_memory(b - 1)
             for kind, grads in enumerate((grad_keys, grad_values)):
                 mem_out[b, kind] = grads[:segment].astype(jnp.bfloat16)
                 own_buf[b, kind] = grads[segment:]
             onward(b).start()
-        for b in range(seq_count):
-            onward(b).wait_recv()
-            for kind in range(2):
-                total = own_buf[b, kind] + mem_in[b, kind].astype(jnp.float32)
-                done_buf[b, :, kind + 1] = total.astype(jnp.bfloat16).reshape(heads, sub, LANES)
             for side in sides:
-                homeward(b, side).start()
-            back_buf[b, me] = done_buf[b, me]
+                queries_home(b, side).start()
+        join_memory(seq_count - 1)
         used = value_end + router_cols
         result_ref[:, used:] = jnp.zeros((tokens, grad_width - used), jnp.bfloat16)
         for b in range(seq_count):
             rows = slice(b * sub, (b + 1) * sub)
             for side in sides:
+                queries_home(b, side).wait_recv()
                 homeward(b, side).wait_recv()
             gate_grad = gate_grads[b]
             for head in range(HEADS):
@@ -858,6 +886,7 @@
             onward(b).wait_send()
             for side in sides:
                 outward(b, side).wait_send()
+                queries_home(b, side).wait_send()
                 homeward(b, side).wait_send()
 
     vmem = pl.BlockSpec(memory_space=pltpu.VMEM)
@@ -878,6 +907,7 @@
             paired,
             paired,
             pltpu.SemaphoreType.DMA((2, seq_count)),
+            pltpu.SemaphoreType.DMA((2, seq_count, heads - 1)),
             paired,
             paired,
         ],
@@ -994,7 +1024,7 @@
         )
     output = hidden.reshape(seq_count, sub_rows, width).astype(jnp.bfloat16)
     grad_hidden = (cotangent.astype(jnp.float32) * valid[:, :, None]).reshape(tokens, width)
-    pairs, extras = ([], [])
+    pairs, extras, native = ([], [], {})
     for layer in reversed(range(LAYERS)):
         (
             normed_one,
@@ -1044,31 +1074,35 @@
         at = value_end + router_cols
         near = at // 128 * 128
         norm_grads = jnp.pad(norm_grads, ((0, 0), (at - near, 128 - 4 - (at - near))))
-        pairs += [
-            (first_in, grad_in),
-            (residual_low, mixed),
-            (second_in, grad_up),
-            (grad_low, act),
-        ]
-        extras.append((norm_grads, near))
+        extras.append((norm_grads, len(pairs), near))
+        pairs += [(first_in, grad_in), (residual_low, mixed)]
+        for kind, pair in (("up", (second_in, grad_up)), ("down", (grad_low, act))):
+            if (layer, kind) in NATIVE:
+                native[layer, kind] = reduced_natively(*pair)
+            else:
+                pairs.append(pair)
+    names = list(native)
+    halves, begun = lax.optimization_barrier(([native[name] for name in names], pairs[0][1]))
+    pairs[0] = (pairs[0][0], begun)
+    for name, half in zip(names, halves):
+        native[name] = lax.psum_scatter(half, "head", scatter_dimension=0, tiled=True).astype(
+            jnp.float32
+        )
     reduced = reduce_weight_grads(pairs, extras, CHUNK)
     matrix_rows = [None] * LAYERS
     small_rows = [None] * LAYERS
     start = 0
-    for slot, layer in enumerate(reversed(range(LAYERS))):
-        widths = [right.shape[1] for _, right in pairs[4 * slot : 4 * slot + 4]]
-        begins = [start + sum(widths[:group_index]) for group_index in range(4)]
-        start += sum(widths)
-        shares = [
-            reduced[:, begin : begin + used]
-            for begin, used in zip(
-                begins, (value_end, output_end - value_end, FF, FF)
-            )
-        ]
-        matrix_rows[layer] = jnp.concatenate(shares, axis=1)
-        small_rows[layer] = reduced[
-            :, begins[0] + value_end : begins[0] + value_end + router_cols + 4
-        ]
+    for layer in reversed(range(LAYERS)):
+        shares = {}
+        for kind, used in (("in", in_width), ("out", output_end - value_end), ("up", FF), ("down", FF)):
+            if (layer, kind) in NATIVE:
+                shares[kind] = native[layer, kind]
+            else:
+                shares[kind] = reduced[:, start : start + used]
+                start += chunk_whole(used)
+        small_rows[layer] = shares["in"][:, value_end : value_end + router_cols + 4]
+        shares["in"] = shares["in"][:, :value_end]
+        matrix_rows[layer] = jnp.concatenate(list(shares.values()), axis=1)
     input_grad = grad_hidden.reshape(seq_count, sub_rows, width).astype(jnp.bfloat16)
     matrix_grad = jnp.stack(matrix_rows, axis=0)
     small_grad = jnp.stack(small_rows, axis=0)

time: 785 us -> 756 us (0.963)
  Pallas kernels: 610 us -> 552 us
  waiting for transfers between devices: 0.04 us -> 20.2 us
  matrix products: 93.3 us -> 109 us
    pallas_call x1, Pallas kernels: 238 us -> 185 us  [reduce_weight_grads(): pl.pallas_call(kernel, grid=(chunks + starts[depth],), in_specs=[in_place...]
    reduce_scatter x0 -> x6, waiting for transfers between devices: none -> 19.6 us  [the longest x4 19.6 us: reduced_natively(): share = lax.psum_scatter(share, axis, scatter_dimension=0, tiled=True)]
    dot_general x0 -> x2, matrix products: none -> 10.8 us  [contract_first(): lax.dot_general(left, right, (((0,), (0,)), ((), ())), preferred_element_...]
  transfers between devices with their start and end apart: 1 -> 7, of which waited for: 0 -> 1; matrix products, arithmetic and copies ran while one was open for 6% -> 17% of each run, Pallas kernels for 13% -> 50%
where the time goes in v6:
time: 756 us; the launch traced here: 752 us
  Pallas kernels  552 us (73%)
  matrix products  109 us (14%)
  local copies, waits for them, and re-layouts  32.1 us (4%)
  other arithmetic  23.3 us (3%)
  waiting for transfers between devices  20.2 us (3%)
  between operations  15.6 us (2%)
    pallas_call x1, Pallas kernels, reduce_weight_grads(): pl.pallas_call(kernel, grid=(chunks + starts[depth],), in_specs=[in_place...  185 us
    pallas_call x1, Pallas kernels, gather_rows(): pl.pallas_call(kernel, in_specs=[in_place] * 2, out_specs=[in_place] * 2,...  178 us
    pallas_call x2, Pallas kernels, attention_forward(): pl.pallas_call(kernel, in_specs=[pl.BlockSpec(memory_space=pltpu.SMEM)] +...  105 us
    pallas_call x2, Pallas kernels, attention_backward(): pl.pallas_call(kernel, in_specs=[pl.BlockSpec(memory_space=pltpu.SMEM)] +...  84.4 us
    dot_general x8, matrix products, contract_last(): lax.dot_general(left, right, (((1,), (1,)), ((), ())), preferred_element_...  49.9 us
    reduce_scatter x4, waiting for transfers between devices, reduced_natively(): share = lax.psum_scatter(share, axis, scatter_dimension=0, tiled=True)  19.6 us
  transfers between devices with their start and end apart: 7, of which 1 were waited for; matrix products, arithmetic and copies ran while one was open for 17% of the time, Pallas kernels for 50%

profile of v6, /device:TPU:0, one launch (start us, length us, event | category | flops | bytes accessed | tf_op | source)
XLA Modules:
  0.0 752.5 jit_solution(15965263424121381765)
XLA Ops:
  7.3 2.2 convert_element_type.121
  9.6 0.9 slice_bitcast_fusion
  11.1 0.4 concatenate.16.refs_0_
  11.5 178.2 %shard_map.201 = (bf16[2,2,2,2,2,32,19200]{6,5,4,3,2,1,0:T(8,128)(2,1)}, f32[2,2,2,2,2,8,128]{6,5,4,3,2,1,0:T(8,128)S(1)}) custom-call(bf16[32,19200]{1,0:T(8,128)(2,1)S(1)} %concatenate.16.refs_0_, f32[8,128]{1,0:T(8,128)S(1)} %pad_bitcast_fusion.refs_1_), custom_call_target="tpu_custom_call" | custom-call | tf_op jit(solution)/shard_map/pallas_call | solution.py:247
  189.7 0.6 copy-done.32
  190.6 0.8 copy.65.refs_2_.refs_4_
  191.4 1.2 fusion.71
  192.6 0.4 convert_element_type.147
  193.0 0.8 copy.69
  193.8 1.2 fusion.83
  195.4 0.3 fusion.73
  196.7 5.2 fusion.22.refs_1_.refs_3_
  201.8 0.8 copy-done.4
  202.6 50.5 %shard_map.202 = (bf16[256,2560]{1,0:T(8,128)(2,1)S(1)}, bf16[256,512]{1,0:T(8,128)(2,1)S(1)}, bf16[2,4,128,128]{3,2,1,0:T(8,128)(2,1)S(1)}, bf16[2,2,4,128,128]...) custom-call(s32[2]{0:T(128)S(1)} %copy-done.34, f32[256,3200]{1,0:T(8,128)S(1)} %fusion.22.refs_1_.refs_3_, ...), custom_call_target="tpu_custom_call" | custom-call | tf_op jit(solution)/shard_map/pallas_call | solution.py:689
  253.2 5.4 fusion.89
  259.2 8.8 %multiply_convert_fusion.1 = (bf16[256,4096]{1,0:T(8,128)(2,1)S(1)}, f32[256,4096]{1,0:T(8,128)}) fusion(bf16[256,1024]{1,0:T(8,128)(2,1)S(1)} %add_convert_fusion.3.refs_4_, bf16[1024,19200]{1,0:T(8,128)(2,1)} %bitcast.125), kind=kOutput, calls=%fused_computation.46 | convolution fusion | flops 2156920832 | bytes 15204352 | tf_op jit(solution)/shard_map/dot_general | solution.py:1005
  268.1 6.7 fusion.90
  275.3 4.8 fusion.18.refs_1_.refs_3_
  280.2 0.8 copy-done.8
  281.0 54.5 %shard_map.203 = (bf16[256,2560]{1,0:T(8,128)(2,1)S(1)}, bf16[256,512]{1,0:T(8,128)(2,1)S(1)}, bf16[2,4,128,128]{3,2,1,0:T(8,128)(2,1)S(1)}, bf16[2,2,4,128,128]...) custom-call(s32[2]{0:T(128)S(1)} %copy-done.34, f32[256,3200]{1,0:T(8,128)S(1)} %fusion.18.refs_1_.refs_3_, ...), custom_call_target="tpu_custom_call" | custom-call | tf_op jit(solution)/shard_map/pallas_call | solution.py:689
  335.5 4.8 fusion.91
  341.0 5.7 fusion.6
  346.7 2.0 copy-done.58
  348.7 4.9 convolution_convert_fusion
  353.7 0.4 reshape.275
  354.1 0.5 copy.68
  354.6 1.3 bitcast_convert_fusion
  355.9 7.6 %fusion.37 = bf16[256,4096]{1,0:T(8,128)(2,1)S(1)} fusion(f32[256,4096]{1,0:T(8,128)} %copy-done.58, bf16[256,1024]{1,0:T(8,128)(2,1)S(1)} %bitcast_convert_fusion, bf16[1024,8192]{1,0:T(8,128)(2,1)} %all-gather.2.cloned.1.call-done), kind=kOutput, calls=%fused_computation.44 | convolution fusion | flops 2168455168 | bytes 15204352 | tf_op jit(solution)/shard_map/dot_general | solution.py:1047
  363.6 1.3 copy-done.44
  364.9 5.9 convolution_convert_fusion.1
  370.9 0.5 reduce-scatter.13.cloned.1.call-update
  371.4 19.5 %reduce-scatter.7.cloned.1.call-done = bf16[512,4096]{1,0:T(8,128)(2,1)} async-done(((bf16[1024,4096]{1,0:T(8,128)(2,1)}), bf16[512,4096]{1,0:T(8,128)(2,1)}) %reduce-scatter.7.cloned.1.call-update) | async-done | bytes 4194320 | tf_op jit(solution)/shard_map/reduce_scatter | solution.py:466
  391.1 0.7 reshape.281
  391.8 0.5 compare_select_fusion
  392.3 0.6 select_select_fusion
  393.0 6.9 multiply_reduce_fusion.2
  399.9 0.4 fusion.82
  400.3 4.5 fusion.38.refs_1_
  404.9 42.2 %shard_map.204.refs_6_ = bf16[256,3584]{1,0:T(8,128)(2,1)S(1)} custom-call(s32[2]{0:T(128)S(1)} %copy-done.34, f32[256,2304]{1,0:T(8,128)S(1)} %fusion.38.refs_1_, bf16[256,512]{1,0:T(8,128)(2,1)S(1)} %copy-done.29, f32[256,3200]{1,0:T(8,128)} %copy-done.1, f32[256,40]{1,0:T(8,128)S(1)} %copy-done.15, f32[128,112]{1,0:T(8,128)S(1)} %pad_maximum_fusion.1.refs_3_.refs_5_, ...), custom_call_target="tpu_custom_call" | custom-call | tf_op jit(solution)/shard_map/pallas_call | solution.py:894
  447.1 6.3 multiply_reduce_fusion.3
  453.5 0.4 fusion.81
  453.9 1.8 copy-done.60
  455.6 7.2 fusion.30.refs_10_
  462.9 6.8 multiply_reduce_fusion
  469.7 1.4 fusion.80
  471.1 4.1 fusion.42.refs_1_
  475.3 42.2 %shard_map.205.refs_8_ = bf16[256,3584]{1,0:T(8,128)(2,1)S(1)} custom-call(s32[2]{0:T(128)S(1)} %copy-done.34, f32[256,2304]{1,0:T(8,128)S(1)} %fusion.42.refs_1_, bf16[256,512]{1,0:T(8,128)(2,1)S(1)} %copy-done.25, f32[256,3200]{1,0:T(8,128)} %copy-done, f32[256,40]{1,0:T(8,128)S(1)} %copy-done.14, f32[128,112]{1,0:T(8,128)S(1)} %pad_maximum_fusion.1.refs_3_.refs_5_, ...), custom_call_target="tpu_custom_call" | custom-call | tf_op jit(solution)/shard_map/pallas_call | solution.py:894
  517.7 5.7 multiply_reduce_fusion.1
  523.7 1.2 add_convert_fusion
  524.9 7.2 fusion.65
  532.2 0.9 copy.74
  533.1 1.1 pad.12.clone
  534.2 0.9 copy.75
  535.1 1.1 pad.13.clone
  536.2 1.3 copy-done.12
  537.5 184.7 %shard_map.206 = f32[32,20480]{1,0:T(8,128)} custom-call(bf16[256,1024]{1,0:T(8,128)(2,1)S(1)} %copy-done.9, bf16[256,1024]{1,0:T(8,128)(2,1)S(1)} %get-tuple-element.77.refs_1_, bf16[256,1024]{1,0:T(8,128)(2,1)S(1)} %copy-done.5, bf16[256,1024]{1,0:T(8,128)(2,1)S(1)} %get-tuple-element.73.refs_3_, bf16[256,1024]{1,0:T(8,128)(2,1)S(1)} %copy-done.7, ...), custom_call_target="tpu_custom_call" | custom-call | tf_op jit(solution)/shard_map/pallas_call | solution.py:437
  722.2 2.3 slice.177
  724.5 1.9 fusion.84
  726.4 2.2 fusion.85
  728.6 2.5 concatenate.19
  731.1 0.8 slice_bitcast_fusion.7
  731.9 1.5 fusion.76
  733.4 2.5 concatenate.20
  735.9 9.6 %fusion.78 = (bf16[2,32,13568]{2,1,0:T(8,128)(2,1)}, f32[2,32,13568]{2,1,0:T(8,128)}, f32[2,32,13568]{2,1,0:T(8,128)}, f32[2,32,13568]{2,1,0:T(8,128)}, f32[2,32,13568]{2,1,0:T(8,128)}) fusion(f32[2,32,13568]{2,1,0:T(8,128)S(1)} %copy-done.35, f32[13568]{0:T(1024)S(1)} %copy-done.48, f32[2,32,13568]{2,1,0:T(8,128)} %param.15, f32[2,32,13568]{2,1,0:T(8,128)} %param.16, ...), kind=kLoop, calls=%fused_computation.156 | loop fusion | flops 14761984 | bytes 29578240 | tf_op jit(solution)/shard_map/convert_element_type | solution.py:1120
  (199 shorter events, 4.5 us)
Async XLA Ops:
  7.2 333.8 %all-gather.2.cloned.1.call-start = ((), (), s32[]{:S(2)}) async-start(), calls=%async_computation.6 | async-start | bytes 17301504 | tf_op jit(solution)/shard_map/all_gather | solution.py:977
  7.2 3.3 copy-start.49
  7.2 3.3 copy-start.50
  7.2 3.4 copy-start.34
  9.6 181.8 %copy-start.47 = (bf16[2,128,1024]{2,1,0:T(8,128)(2,1)S(1)}, bf16[2,128,1024]{2,1,0:T(8,128)(2,1)}, u32[]{:S(2)}) copy-start(bf16[2,128,1024]{2,1,0:T(8,128)(2,1)} %param.11) | copy-start | bytes 1572868
  11.5 184.4 %copy-start.41 = (bf16[2,128,1024]{2,1,0:T(8,128)(2,1)S(1)}, bf16[2,128,1024]{2,1,0:T(8,128)(2,1)}, u32[]{:S(2)}) copy-start(bf16[2,128,1024]{2,1,0:T(8,128)(2,1)} %param.10) | copy-start | bytes 1572868
  190.4 180.5 %reduce-scatter.11.cloned.1.call-start = ((), (), s32[]{:S(2)}) async-start(), calls=%async_computation.9 | async-start | bytes 12582912 | tf_op jit(solution)/shard_map/reduce_scatter | solution.py:466
  190.6 11.2 %copy-start.13 = (f32[256,40]{1,0:T(8,128)}, f32[256,40]{1,0:T(8,128)S(1)}, u32[]{:S(2)}) copy-start(f32[256,40]{1,0:T(8,128)S(1)} %copy.62.refs_2_.refs_4_) | copy-start | bytes 122884
  202.6 56.0 %copy-start = (f32[256,3200]{1,0:T(8,128)}, f32[256,3200]{1,0:T(8,128)S(1)}, u32[]{:S(2)}) copy-start(f32[256,3200]{1,0:T(8,128)S(1)} %fusion.22.refs_1_.refs_3_) | copy-start | bytes 9830404
  253.1 5.5 copy-start.10
  253.1 5.5 copy-start.16
  253.2 5.5 copy-start.18
  253.2 5.5 copy-start.24
  253.2 5.5 copy-start.26
  259.2 8.9 %copy-start.6 = (bf16[256,1024]{1,0:T(8,128)(2,1)}, bf16[256,1024]{1,0:T(8,128)(2,1)S(1)}, u32[]{:S(2)}) copy-start(bf16[256,1024]{1,0:T(8,128)(2,1)S(1)} %add_convert_fusion.3.refs_4_) | copy-start | bytes 1572868
  268.1 6.7 copy-start.45
  274.7 60.8 %copy-start.39 = (f32[256,1024]{1,0:T(8,128)}, f32[256,1024]{1,0:T(8,128)S(1)}, u32[]{:S(2)}) copy-start(f32[256,1024]{1,0:T(8,128)S(1)} %get-tuple-element.117) | copy-start | bytes 3145732
  275.3 5.7 copy-start.15
  281.0 59.4 %copy-start.1 = (f32[256,3200]{1,0:T(8,128)}, f32[256,3200]{1,0:T(8,128)S(1)}, u32[]{:S(2)}) copy-start(f32[256,3200]{1,0:T(8,128)S(1)} %fusion.18.refs_1_.refs_3_) | copy-start | bytes 9830404
  335.4 4.9 copy-start.11
  335.5 4.9 copy-start.20
  335.5 4.9 copy-start.22
  335.5 4.9 copy-start.28
  335.5 4.9 copy-start.30
  340.4 59.5 %copy-start.36 = (f32[256,1024]{1,0:T(8,128)}, f32[256,1024]{1,0:T(8,128)S(1)}, u32[]{:S(2)}) copy-start(f32[256,1024]{1,0:T(8,128)S(1)} %get-tuple-element.119) | copy-start | bytes 3145732
  346.7 2.0 copy-start.58
  353.7 37.3 %reduce-scatter.7.cloned.1.call-start = ((), (), s32[]{:S(2)}) async-start(), calls=%async_computation.7 | async-start | bytes 12582912 | tf_op jit(solution)/shard_map/reduce_scatter | solution.py:466
  370.8 146.7 %reduce-scatter.13.cloned.1.call-start = ((), (), s32[]{:S(2)}) async-start(), calls=%async_computation.10 | async-start | bytes 5242880 | tf_op jit(solution)/shard_map/reduce_scatter | solution.py:466
  370.9 20.2 %copy-start.33 = (f32[2,2,2,2,2,8,128]{6,5,4,3,2,1,0:T(8,128)S(1)}, f32[2,2,2,2,2,8,128]{6,5,4,3,2,1,0:T(8,128)}, u32[]{:S(2)}) copy-start(f32[2,2,2,2,2,8,128]{6,5,4,3,2,1,0:T(8,128)} %copy-done.32) | copy-start | bytes 393220
  371.4 146.1 %reduce-scatter.9.cloned.1.call-start = ((), (), s32[]{:S(2)}) async-start(), calls=%async_computation.8 | async-start | bytes 5242880 | tf_op jit(solution)/shard_map/reduce_scatter | solution.py:466
  391.0 342.4 %reduce-scatter.15.cloned.1.call-start = ((), (), s32[]{:S(2)}) async-start(), calls=%async_computation.11 | async-start | bytes 1310720 | tf_op jit(solution)/shard_map/reduce_scatter | solution.py:1088
  393.0 6.9 copy-start.38
  400.3 4.6 copy-start.21
  400.3 4.6 copy-start.23
  400.3 4.6 copy-start.29
  400.3 4.6 copy-start.31
  404.9 42.2 %copy-start.40 = (f32[256,1024]{1,0:T(8,128)S(1)}, f32[256,1024]{1,0:T(8,128)}, u32[]{:S(2)}) copy-start(f32[256,1024]{1,0:T(8,128)} %copy-done.39) | copy-start | bytes 3145732
  447.1 6.3 copy-start.2
  453.5 2.2 copy-start.60
  462.9 6.8 copy-start.46
  471.1 4.1 copy-start.14
  471.1 4.2 copy-start.17
  471.1 4.2 copy-start.19
  471.1 4.2 copy-start.25
  471.1 4.2 copy-start.27
  517.5 6.0 copy-start.3
  517.6 5.9 copy-start.52
  517.6 5.9 copy-start.51
  517.6 5.9 copy-start.54
  517.6 5.9 copy-start.53
  517.6 5.9 copy-start.56
  517.6 6.0 copy-start.55
  517.6 215.8 %reduce-scatter.17.cloned.1.call-start = ((), (), s32[]{:S(2)}) async-start(), calls=%async_computation.12 | async-start | bytes 1310720 | tf_op jit(solution)/shard_map/reduce_scatter | solution.py:1088
  517.7 6.0 copy-start.42
  517.7 6.0 copy-start.43
  517.7 7.2 copy-start.37
  517.7 7.2 copy-start.59
  524.9 11.3 %copy-start.5 = (bf16[256,1024]{1,0:T(8,128)(2,1)S(1)}, bf16[256,1024]{1,0:T(8,128)(2,1)}, u32[]{:S(2)}) copy-start(bf16[256,1024]{1,0:T(8,128)(2,1)} %copy-done.4) | copy-start | bytes 1572868
  524.9 11.3 %copy-start.7 = (bf16[256,1024]{1,0:T(8,128)(2,1)S(1)}, bf16[256,1024]{1,0:T(8,128)(2,1)}, u32[]{:S(2)}) copy-start(bf16[256,1024]{1,0:T(8,128)(2,1)} %copy-done.6) | copy-start | bytes 1572868
  524.9 11.3 %copy-start.9 = (bf16[256,1024]{1,0:T(8,128)(2,1)S(1)}, bf16[256,1024]{1,0:T(8,128)(2,1)}, u32[]{:S(2)}) copy-start(bf16[256,1024]{1,0:T(8,128)(2,1)} %copy-done.8) | copy-start | bytes 1572868
  536.2 1.3 copy-start.12
  722.2 9.7 %copy-start.57 = (f32[44]{0:T(128)S(1)}, f32[44]{0:T(128)}, u32[]{:S(2)}) copy-start(f32[44]{0:T(128)} %compare_select_fusion) | copy-start | bytes 532
  726.4 9.5 %copy-start.35 = (f32[2,32,13568]{2,1,0:T(8,128)S(1)}, f32[2,32,13568]{2,1,0:T(8,128)}, u32[]{:S(2)}) copy-start(f32[2,32,13568]{2,1,0:T(8,128)} %param.14) | copy-start | bytes 10420228
  726.4 9.5 %copy-start.48 = (f32[13568]{0:T(1024)S(1)}, f32[13568]{0:T(1024)}, u32[]{:S(2)}) copy-start(f32[13568]{0:T(1024)} %select_select_fusion) | copy-start | bytes 162820
  (4 other events, 3.6 us)
Sparse Core Ops, SparseCore 0:
  190.5 144.4 all-gather.1
  353.8 16.6 reduce-scatter.10
  372.9 18.0 reduce-scatter.6
  393.8 53.9 reduce-scatter.12
  450.9 52.6 reduce-scatter.8
  517.7 30.2 reduce-scatter.14
  550.4 41.6 reduce-scatter.16

commit v7 on v6

--- a/solution.py
+++ b/solution.py
@@ -24,7 +24,7 @@
 NORM_RATE = 0.5
 MASKED = -1e30
 CHUNK = 512
-NATIVE = ((LAYERS - 1, "up"), (LAYERS - 1, "down"))
+NATIVE = ((LAYERS - 1, "down"),)
 
 
 def column_bounds():
@@ -139,13 +139,14 @@
     depth = len(dims)
     rows, width = share.shape
     units = width // unit
-    near = (3 * units + 4) // 8
+    near = (11 * units + 16) // 32
     pieces, start = ([], 0)
     for which, count in ((0, near), (1, near), (2, units - 2 * near)):
         pieces.append((start, count, which))
         start += count * unit
-    lag, slots = (2, 4)
-    ring = (depth + 1) * lag + 6
+    lag, slots = (3, 6)
+    local_slots = 2
+    ring = (depth + 1) * lag + local_slots + 2
     steps = max(count for _, count, _ in pieces) + lag * depth
 
     def kernel(*refs):
@@ -177,14 +178,14 @@
             return pltpu.make_async_copy(
                 share_ref.at[:, columns(number, chunk)],
                 buffers[number].at[(lax.rem(chunk, ring),) + tuple(bits)],
-                load_sem.at[number, lax.rem(chunk, slots)],
+                load_sem.at[number, lax.rem(chunk, local_slots)],
             )
 
         def store(number, chunk):
             return pltpu.make_async_copy(
                 buffers[number].at[lax.rem(chunk, ring)],
                 out_ref.at[(slice(None),) * (depth + 1) + (columns(number, chunk),)],
-                store_sem.at[number, lax.rem(chunk, slots)],
+                store_sem.at[number, lax.rem(chunk, local_slots)],
             )
 
         def small(stage):
@@ -196,7 +197,7 @@
         own_counts = pltpu.make_async_copy(counts_ref, counts_out.at[tuple(bits)], small_load)
         own_counts.start()
         for number in range(len(pieces)):
-            for chunk in range(2):
+            for chunk in range(local_slots):
                 load(number, jnp.int32(chunk)).start()
         greet(partners)
         own_counts.wait()
@@ -213,17 +214,17 @@
                         else:
                             load(number, chunk).wait()
 
-                            @pl.when(chunk + 2 < piece[1])
+                            @pl.when(chunk + local_slots < piece[1])
                             def _():
-                                load(number, chunk + 2).start()
+                                load(number, chunk + local_slots).start()
 
                         if stage < depth:
                             exchange(number, stage, chunk).start()
                         else:
 
-                            @pl.when(chunk >= slots)
+                            @pl.when(chunk >= local_slots)
                             def _():
-                                store(number, chunk - slots).wait()
+                                store(number, chunk - local_slots).wait()
 
                             store(number, chunk).start()
 
@@ -238,12 +239,12 @@
 
         lax.fori_loop(0, steps, body, 0)
         for number, piece in enumerate(pieces):
-            for back in range(min(slots, piece[1])):
+            for back in range(min(local_slots, piece[1])):
                 store(number, jnp.int32(piece[1] - 1 - back)).wait()
 
     in_place = pl.BlockSpec(memory_space=pl.ANY)
     semaphores = pltpu.SemaphoreType.DMA((len(pieces), depth, slots))
-    local = pltpu.SemaphoreType.DMA((len(pieces), slots))
+    local = pltpu.SemaphoreType.DMA((len(pieces), local_slots))
     gathered, all_counts = pl.pallas_call(
         kernel,
         in_specs=[in_place] * 2,
@@ -291,26 +292,34 @@
     return dims, stages, lags
 
 
-def reduce_weight_grads(pairs, extras, width):
+def reduce_weight_grads(lefts, segments, doubles, extras, width):
     dims, stages, lags = halving_plan(width)
     depth = len(dims)
-    tokens, model = pairs[0][0].shape
+    half = width // 2
+    tokens, model = lefts[0].shape
     rows = model >> depth
     firsts = [0]
-    for left, right in pairs:
-        firsts.append(firsts[-1] + right.shape[1] // width)
-    chunks = firsts[-1]
-    spots = [(firsts[pair] + near // width, near % width) for _, pair, near in extras]
+    for _, _, _, count in segments:
+        firsts.append(firsts[-1] + count)
+    chunks = firsts[-1] // 2
+    spots = [(where // 2, where % 2 * half) for _, where in extras]
     starts = [sum(lags[:stage]) for stage in range(depth + 1)]
-    count_pairs, count_extras = (len(pairs), len(extras))
+    rights = [right for _, right, _, _ in segments] + [right for _, _, _, right in doubles]
+    count_lefts, count_rights, count_extras = (len(lefts), len(rights), len(extras))
+    first_use = [
+        min(firsts[index] // 2 for index, segment in enumerate(segments) if segment[0] == left)
+        for left in range(count_lefts)
+    ]
+    for where, _, left, _ in doubles:
+        first_use[left] = min(first_use[left], where // 2)
 
     def kernel(*refs):
-        lefts = refs[:count_pairs]
-        rights = refs[count_pairs : 2 * count_pairs]
-        added = refs[2 * count_pairs : 2 * count_pairs + count_extras]
-        rest = refs[2 * count_pairs + count_extras :]
-        out_ref, left_buf, turned, right_buf, load_sem = rest[:5]
-        pool = iter(rest[5:])
+        left_refs = refs[:count_lefts]
+        right_refs = refs[count_lefts : count_lefts + count_rights]
+        rest = refs[count_lefts + count_rights :]
+        added, rest = (rest[:count_extras], rest[count_extras:])
+        out_ref, left_buf, turned, right_buf, double_buf, left_sem, right_sem, double_sem = rest[:8]
+        pool = iter(rest[8:])
         buffers = [[tuple(next(pool) for _ in range(4)) for _ in parts] for parts in stages]
         step = pl.program_id(0)
         bits, partners = my_bits(dims)
@@ -329,28 +338,41 @@
             )
 
         def load_left(index):
-            return pltpu.make_async_copy(lefts[index], left_buf, load_sem.at[2])
-
-        def load_right(index, chunk):
+            return pltpu.make_async_copy(left_refs[index], left_buf.at[index], left_sem.at[index])
+
+        def load_right(index, at, chunk, side):
+            columns = pl.ds(pl.multiple_of(at * half, half), half)
             slot = lax.rem(chunk, 2)
-            columns = pl.ds(pl.multiple_of((chunk - firsts[index]) * width, width), width)
             return pltpu.make_async_copy(
-                rights[index].at[:, columns], right_buf.at[slot], load_sem.at[slot]
+                right_refs[index].at[:, columns],
+                right_buf.at[slot, side],
+                right_sem.at[slot, side],
+            )
+
+        def load_double(index):
+            return pltpu.make_async_copy(
+                right_refs[len(segments) + index].at[:, 0:half], double_buf, double_sem
             )
 
         def prefetch(chunk):
-            for index in range(count_pairs):
-
-                @pl.when((chunk >= firsts[index]) & (chunk < firsts[index + 1]))
+            for side in range(2):
+                place = 2 * chunk + side
+                for index, (_, _, begin, _) in enumerate(segments):
+
+                    @pl.when((place >= firsts[index]) & (place < firsts[index + 1]))
+                    def _(index=index, begin=begin, place=place, side=side):
+                        load_right(index, place - firsts[index] + begin, chunk, side).start()
+
+            for index, (where, _, _, _) in enumerate(doubles):
+
+                @pl.when(chunk == where // 2)
                 def _(index=index):
-                    load_right(index, chunk).start()
-
-                @pl.when(chunk == firsts[index])
-                def _(index=index):
-                    load_left(index).start()
+                    load_double(index).start()
 
         @pl.when(step == 0)
         def _():
+            for index in range(count_lefts):
+                load_left(index).start()
             prefetch(step)
             greet(partners)
 
@@ -364,29 +386,56 @@
             @pl.when((chunk >= 0) & (chunk < chunks))
             def _(stage=stage, chunk=chunk):
                 if stage == 0:
-                    for first in firsts[:-1]:
-
-                        @pl.when(chunk == first)
-                        def _():
-                            load_left(0).wait()
-                            turned[...] = left_buf[...].T
-
-                    load_right(0, lax.rem(chunk, 2)).wait()
-                    product = jnp.dot(
-                        turned[...],
-                        right_buf[lax.rem(chunk, 2)],
-                        preferred_element_type=jnp.float32,
-                    )
                     slot = lax.rem(chunk, 2 * lags[0])
-                    for part, (start, count, dim, left) in enumerate(stages[0]):
-                        piece = product[:, start : start + count].astype(jnp.bfloat16)
-                        buffers[0][part][0][slot] = piece.reshape((2,) * depth + (rows, count))
+                    near = lax.rem(chunk, 2)
+                    own = buffers[0][0][0]
+                    for index in range(count_lefts):
+
+                        @pl.when(chunk == first_use[index])
+                        def _(index=index):
+                            load_left(index).wait()
+                            turned[index] = left_buf[index].T
+
+                    for side in range(2):
+                        place = 2 * chunk + side
+                        which = jnp.int32(segments[0][0])
+                        for index, segment in enumerate(segments):
+                            which = jnp.where(place >= firsts[index], segment[0], which)
+                        load_right(0, 0, chunk, side).wait()
+                        for where, kept, _, _ in doubles:
+                            if where % 2 == side:
+
+                                @pl.when(chunk == where // 2)
+                                def _(kept=kept, side=side):
+                                    right_buf[near, side, :, kept:] = jnp.zeros(
+                                        (tokens, half - kept), jnp.bfloat16
+                                    )
+
+                        product = jnp.dot(
+                            turned[which],
+                            right_buf[near, side],
+                            preferred_element_type=jnp.float32,
+                        )
+                        own[(slot, Ellipsis, slice(side * half, side * half + half))] = (
+                            product.astype(jnp.bfloat16).reshape((2,) * depth + (rows, half))
+                        )
+                    for index, (where, _, left, _) in enumerate(doubles):
+
+                        @pl.when(chunk == where // 2)
+                        def _(index=index, where=where, left=left):
+                            load_double(index).wait()
+                            product = jnp.dot(
+                                turned[left], double_buf[...], preferred_element_type=jnp.float32
+                            ).reshape((2,) * depth + (rows, half))
+                            begin = where % 2 * half
+                            at = (slot, Ellipsis, slice(begin, begin + half))
+                            own[at] = (own[at].astype(jnp.float32) + product).astype(jnp.bfloat16)
+
                     for index in range(count_extras):
 
                         @pl.when(chunk == spots[index][0])
                         def _(index=index):
                             at = (slot, Ellipsis, slice(spots[index][1], spots[index][1] + 128))
-                            own = buffers[0][0][0]
                             total = own[at].astype(jnp.float32) + added[index][...].astype(
                                 jnp.float32
                             )
@@ -418,10 +467,13 @@
                         exchange(stage, part, lax.rem(chunk, 2 * lags[stage])).start()
 
     scratch = [
-        pltpu.VMEM((tokens, model), jnp.bfloat16),
-        pltpu.VMEM((model, tokens), jnp.bfloat16),
-        pltpu.VMEM((2, tokens, width), jnp.bfloat16),
-        pltpu.SemaphoreType.DMA((3,)),
+        pltpu.VMEM((count_lefts, tokens, model), jnp.bfloat16),
+        pltpu.VMEM((count_lefts, model, tokens), jnp.bfloat16),
+        pltpu.VMEM((2, 2, tokens, half), jnp.bfloat16),
+        pltpu.VMEM((tokens, half), jnp.bfloat16),
+        pltpu.SemaphoreType.DMA((count_lefts,)),
+        pltpu.SemaphoreType.DMA((2, 2)),
+        pltpu.SemaphoreType.DMA,
     ]
     for stage, parts in enumerate(stages):
         slots = 2 * lags[stage]
@@ -433,11 +485,11 @@
                 pltpu.SemaphoreType.DMA((slots,)),
             ]
     in_place = pl.BlockSpec(memory_space=pl.ANY)
-    whole = [value.reshape((2,) * depth + (rows, 128)) for value, _, _ in extras]
+    whole = [value.reshape((2,) * depth + (rows, 128)) for value, _ in extras]
     return pl.pallas_call(
         kernel,
         grid=(chunks + starts[depth],),
-        in_specs=[in_place] * (2 * count_pairs)
+        in_specs=[in_place] * (count_lefts + count_rights)
         + [pl.BlockSpec(value.shape, lambda step: (0,) * (depth + 2)) for value in whole],
         out_specs=pl.BlockSpec(
             (rows, width), lambda step: (0, jnp.clip(step - starts[depth], 0, chunks - 1))
@@ -450,7 +502,7 @@
             vmem_limit_bytes=48 << 20,
             dimension_semantics=("arbitrary",),
         ),
-    )(*[left for left, _ in pairs], *[right for _, right in pairs], *whole)
+    )(*lefts, *rights, *whole)
 
 
 def reduction_order(tensor):
@@ -462,17 +514,13 @@
 
 def reduced_natively(left, right):
     share = contract_first(reduction_order(left), right).astype(jnp.bfloat16)
-    for axis in ("seq", "dp"):
+    for axis in ("seq", "dp", "head"):
         share = lax.psum_scatter(share, axis, scatter_dimension=0, tiled=True)
     return share
 
 
 def lane_whole(count):
     return count + (-count) % 128
-
-
-def chunk_whole(count):
-    return count + (-count) % CHUNK
 
 
 def padded(pieces, width):
@@ -556,7 +604,7 @@
     return tensor[:, index : index + 1]
 
 
-def attention_forward(entered, chosen, turn_cos, turn_sin, lengths, mixed_width, name):
+def attention_forward(entered, chosen, turn_cos, turn_sin, lengths, shift, name):
     seq_count = lengths.shape[0]
     tokens = entered.shape[0]
     sub = tokens // seq_count
@@ -659,8 +707,7 @@
             key_ref[b, 1] = heads_buf[b, 1]
             value_ref[b, 0] = mem_buf[b, 1]
             value_ref[b, 1] = heads_buf[b, 2]
-        used = HEADS * EXPERTS * HEAD_DIM
-        mixed_ref[:, used:] = jnp.zeros((tokens, mixed_width - used), jnp.bfloat16)
+        mixed_ref[:, :shift] = jnp.zeros((tokens, shift), jnp.bfloat16)
         for b in range(seq_count):
             rows = slice(b * sub, (b + 1) * sub)
             for side in sides:
@@ -672,7 +719,8 @@
                 for expert in range(EXPERTS):
                     index = head * EXPERTS + expert
                     gate = column(gates_of[b], HEADS * EXPERTS + index)
-                    mixed_ref[rows, index * HEAD_DIM : (index + 1) * HEAD_DIM] = (
+                    at = shift + index * HEAD_DIM
+                    mixed_ref[rows, at : at + HEAD_DIM] = (
                         gate * wide
                     ).astype(jnp.bfloat16)
         for b in range(seq_count):
@@ -691,7 +739,7 @@
         in_specs=[pl.BlockSpec(memory_space=pltpu.SMEM)] + [vmem] * 4,
         out_specs=[vmem] * 5,
         out_shape=[
-            shape(tokens, mixed_width),
+            shape(tokens, shift + HEADS * EXPERTS * HEAD_DIM),
             shape(tokens, HEADS * LANES),
             shape(seq_count, heads, sub, LANES),
             shape(seq_count, 2, heads, sub, LANES),
@@ -716,7 +764,7 @@
 
 
 def attention_backward(
-    grad_mixed, attended, entered, chosen, turn_cos, turn_sin, lengths, saved, grad_width, name
+    grad_mixed, attended, entered, chosen, turn_cos, turn_sin, lengths, saved, shift, grad_width, name
 ):
     query, keys, values = saved
     seq_count = lengths.shape[0]
@@ -730,9 +778,9 @@
 
     def kernel(*refs):
         length_ref, grad_ref, attended_ref, entered_ref, chosen_ref, cos_ref, sin_ref = refs[:7]
-        query_ref, key_ref, value_ref, result_ref = refs[7:11]
-        out_buf, heads_buf, mem_out, mem_in, own_buf, done_buf, back_buf = refs[11:18]
-        out_sem, in_sem, mem_sem, query_sem, done_sem, back_sem = refs[18:]
+        query_ref, key_ref, value_ref, result_ref, logit_ref = refs[7:12]
+        out_buf, heads_buf, mem_out, mem_in, own_buf, done_buf, back_buf = refs[12:19]
+        out_sem, in_sem, mem_sem, query_sem, done_sem, back_sem = refs[19:]
         me = lax.axis_index("head")
         start = lax.axis_index("seq") * segment
         turn, wind = (cos_ref[...], sin_ref[...])
@@ -797,7 +845,8 @@
                 total = jnp.zeros((sub, HEAD_DIM), jnp.float32)
                 for expert in range(EXPERTS):
                     index = head * EXPERTS + expert
-                    part = grad_ref[rows, index * HEAD_DIM : (index + 1) * HEAD_DIM]
+                    at = shift + index * HEAD_DIM
+                    part = grad_ref[rows, at : at + HEAD_DIM]
                     total += column(gates, HEADS * EXPERTS + index) * part
                     gate_grad = jnp.where(
                         lane == HEADS * EXPERTS + index,
@@ -850,6 +899,7 @@
         join_memory(seq_count - 1)
         used = value_end + router_cols
         result_ref[:, used:] = jnp.zeros((tokens, grad_width - used), jnp.bfloat16)
+        logit_ref[:, router_cols:] = jnp.zeros((tokens, CHUNK // 2 - router_cols), jnp.bfloat16)
         for b in range(seq_count):
             rows = slice(b * sub, (b + 1) * sub)
             for side in sides:
@@ -879,9 +929,11 @@
                         column(gates_of[b], index) * grad_value
                     ).astype(jnp.bfloat16)
             prob = probs_of[b]
-            result_ref[rows, value_end:used] = (
-                gate_grad * chosen_ref[rows, :] * prob * (1.0 - prob)
-            ).astype(jnp.bfloat16)
+            grad_logit = (gate_grad * chosen_ref[rows, :] * prob * (1.0 - prob)).astype(
+                jnp.bfloat16
+            )
+            result_ref[rows, value_end:used] = grad_logit
+            logit_ref[rows, :router_cols] = grad_logit
         for b in range(seq_count):
             onward(b).wait_send()
             for side in sides:
@@ -894,8 +946,11 @@
     return pl.pallas_call(
         kernel,
         in_specs=[pl.BlockSpec(memory_space=pltpu.SMEM)] + [vmem] * 9,
-        out_specs=vmem,
-        out_shape=jax.ShapeDtypeStruct((tokens, grad_width), jnp.bfloat16),
+        out_specs=[vmem] * 2,
+        out_shape=[
+            jax.ShapeDtypeStruct((tokens, count), jnp.bfloat16)
+            for count in (grad_width, CHUNK // 2)
+        ],
         scratch_shapes=[
             pltpu.VMEM((seq_count, heads, sub, LANES), jnp.bfloat16),
             pltpu.VMEM((seq_count, heads, sub, LANES), jnp.bfloat16),
@@ -953,7 +1008,10 @@
     )
     load_part = jnp.sum(chosen * valid[None, :, :, None, None, None], axis=(1, 2))
     in_width = lane_whole(value_end + router_cols + 4)
-    out_width = lane_whole(output_end - value_end)
+    half = CHUNK // 2
+    shift = value_end % half
+    in_grad_width = value_end + (-value_end) % half
+    out_width = shift + output_end - value_end
     matrix_low = matrix.astype(jnp.bfloat16)
     small_low = small.astype(jnp.bfloat16)
     in_low = [
@@ -961,7 +1019,8 @@
         for layer in range(LAYERS)
     ]
     out_low = [
-        padded([matrix_low[layer, :, value_end:output_end]], out_width) for layer in range(LAYERS)
+        jnp.pad(matrix_low[layer, :, value_end:output_end], ((0, 0), (shift, 0)))
+        for layer in range(LAYERS)
     ]
     ffn_low = [matrix_low[layer, :, output_end:] for layer in range(LAYERS)]
     size = load_part.size
@@ -996,10 +1055,10 @@
             turn_cos,
             turn_sin,
             lengths,
-            chunk_whole(out_width),
+            shift,
             3 + layer,
         )
-        residual = hidden + contract_last(mixed[:, :out_width], out_w)
+        residual = hidden + contract_last(mixed, out_w)
         normed_two, inverse_two = layer_stats(residual)
         second_in = (normed_two * gains[:, 2] + gains[:, 3]).astype(jnp.bfloat16)
         up = jnp.dot(second_in, ffn_w[:, :FF], preferred_element_type=jnp.float32)
@@ -1024,7 +1083,7 @@
         )
     output = hidden.reshape(seq_count, sub_rows, width).astype(jnp.bfloat16)
     grad_hidden = (cotangent.astype(jnp.float32) * valid[:, :, None]).reshape(tokens, width)
-    pairs, extras, native = ([], [], {})
+    lefts, segments, doubles, extras, native, bases = ([], [], [], [], {}, {})
     for layer in reversed(range(LAYERS)):
         (
             normed_one,
@@ -1052,7 +1111,7 @@
         bias_two_grad = jnp.sum(grad_second, axis=0)
         grad_residual = grad_hidden + norm_back(grad_second, normed_two, inverse_two, gains[:, 2])
         residual_low = grad_residual.astype(jnp.bfloat16)
-        grad_in = attention_backward(
+        grad_in, grad_logit = attention_backward(
             jnp.dot(residual_low, out_w, preferred_element_type=jnp.float32),
             attended,
             entered,
@@ -1061,7 +1120,8 @@
             turn_sin,
             lengths,
             saved,
-            chunk_whole(in_width),
+            shift,
+            in_grad_width,
             3 + LAYERS + layer,
         )
         grad_first = contract_last(grad_in[:, :in_width], in_w)
@@ -1071,38 +1131,40 @@
         norm_grads = jnp.stack(
             [gain_one_grad, bias_one_grad, gain_two_grad, bias_two_grad], axis=1
         ).astype(jnp.bfloat16)
-        at = value_end + router_cols
-        near = at // 128 * 128
-        norm_grads = jnp.pad(norm_grads, ((0, 0), (at - near, 128 - 4 - (at - near))))
-        extras.append((norm_grads, len(pairs), near))
-        pairs += [(first_in, grad_in), (residual_low, mixed)]
+        norm_grads = jnp.pad(norm_grads, ((0, 0), (router_cols, 128 - 4 - router_cols)))
+        base = sum(segment[3] for segment in segments)
+        bases[layer] = base * half
+        one = len(lefts)
+        lefts += [first_in, residual_low]
+        in_halves = grad_in.shape[1] // half
+        segments += [
+            (one, grad_in, 0, in_halves),
+            (one + 1, mixed, 1, mixed.shape[1] // half - 1),
+        ]
+        doubles.append((base + in_halves - 1, shift, one + 1, mixed))
         for kind, pair in (("up", (second_in, grad_up)), ("down", (grad_low, act))):
             if (layer, kind) in NATIVE:
                 native[layer, kind] = reduced_natively(*pair)
             else:
-                pairs.append(pair)
+                segments.append((len(lefts), pair[1], 0, FF // half))
+                lefts.append(pair[0])
+        extras.append((norm_grads, sum(segment[3] for segment in segments)))
+        segments.append((one, grad_logit, 0, 1))
     names = list(native)
-    halves, begun = lax.optimization_barrier(([native[name] for name in names], pairs[0][1]))
-    pairs[0] = (pairs[0][0], begun)
-    for name, half in zip(names, halves):
-        native[name] = lax.psum_scatter(half, "head", scatter_dimension=0, tiled=True).astype(
-            jnp.float32
-        )
-    reduced = reduce_weight_grads(pairs, extras, CHUNK)
+    begun = segments[-1][1]
+    partial, begun = lax.optimization_barrier(([native[name] for name in names], begun))
+    segments[-1] = (segments[-1][0], begun) + segments[-1][2:]
+    for name, value in zip(names, partial):
+        native[name] = value.astype(jnp.float32)
+    reduced = reduce_weight_grads(lefts, segments, doubles, extras, CHUNK)
     matrix_rows = [None] * LAYERS
     small_rows = [None] * LAYERS
-    start = 0
-    for layer in reversed(range(LAYERS)):
-        shares = {}
-        for kind, used in (("in", in_width), ("out", output_end - value_end), ("up", FF), ("down", FF)):
-            if (layer, kind) in NATIVE:
-                shares[kind] = native[layer, kind]
-            else:
-                shares[kind] = reduced[:, start : start + used]
-                start += chunk_whole(used)
-        small_rows[layer] = shares["in"][:, value_end : value_end + router_cols + 4]
-        shares["in"] = shares["in"][:, :value_end]
-        matrix_rows[layer] = jnp.concatenate(list(shares.values()), axis=1)
+    for layer in range(LAYERS):
+        base = bases[layer]
+        rest = [native[layer, kind] for kind in ("up", "down") if (layer, kind) in NATIVE]
+        used = output_end + FF * (2 - len(rest))
+        matrix_rows[layer] = jnp.concatenate([reduced[:, base : base + used]] + rest, axis=1)
+        small_rows[layer] = reduced[:, base + used : base + used + router_cols + 4]
     input_grad = grad_hidden.reshape(seq_count, sub_rows, width).astype(jnp.bfloat16)
     matrix_grad = jnp.stack(matrix_rows, axis=0)
     small_grad = jnp.stack(small_rows, axis=0)

time: 756 us -> 748 us (0.989)
    pallas_call x1, Pallas kernels: 185 us -> 194 us  [reduce_weight_grads(): pl.pallas_call(kernel, grid=(chunks + starts[depth],), in_specs=[in_place...]
    reduce_scatter x4 -> x3, waiting for transfers between devices: 19.6 us -> 18 us  [reduced_natively(): share = lax.psum_scatter(share, axis, scatter_dimension=0, tiled=True)]
  transfers between devices with their start and end apart: 7 -> 4, of which waited for: 1 -> 2; matrix products, arithmetic and copies ran while one was open for 17% -> 15% of each run, Pallas kernels for 50% -> 26%
where the time goes in v7:
time: 748 us; the launch traced here: 745 us
  Pallas kernels  557 us (74%)
  matrix products  105 us (14%)
  local copies, waits for them, and re-layouts  26.3 us (4%)
  other arithmetic  23.1 us (3%)
  waiting for transfers between devices  18.1 us (2%)
  between operations  15.4 us (2%)
    pallas_call x1, Pallas kernels, reduce_weight_grads(): pl.pallas_call(kernel, grid=(chunks + starts[depth],), in_specs=[in_place...  194 us
    pallas_call x1, Pallas kernels, gather_rows(): pl.pallas_call(kernel, in_specs=[in_place] * 2, out_specs=[in_place] * 2,...  172 us
    pallas_call x2, Pallas kernels, attention_forward(): pl.pallas_call(kernel, in_specs=[pl.BlockSpec(memory_space=pltpu.SMEM)] +...  105 us
    pallas_call x2, Pallas kernels, attention_backward(): pl.pallas_call(kernel, in_specs=[pl.BlockSpec(memory_space=pltpu.SMEM)] +...  85.3 us
    dot_general x8, matrix products, contract_last(): lax.dot_general(left, right, (((1,), (1,)), ((), ())), preferred_element_...  51.9 us
    reduce_scatter x3, waiting for transfers between devices, reduced_natively(): share = lax.psum_scatter(share, axis, scatter_dimension=0, tiled=True)  18 us
  transfers between devices with their start and end apart: 4, of which 2 were waited for; matrix products, arithmetic and copies ran while one was open for 15% of the time, Pallas kernels for 26%

profile of v7, /device:TPU:0, one launch (start us, length us, event | category | flops | bytes accessed | tf_op | source)
XLA Modules:
  0.0 744.7 jit_solution(3690281012850381247)
XLA Ops:
  7.3 2.2 convert_element_type.118
  9.6 0.9 slice_bitcast_fusion.1
  11.3 0.4 concatenate.12.refs_0_
  11.7 172.1 %shard_map.201 = (bf16[2,2,2,2,2,32,19200]{6,5,4,3,2,1,0:T(8,128)(2,1)}, f32[2,2,2,2,2,8,128]{6,5,4,3,2,1,0:T(8,128)S(1)}) custom-call(bf16[32,19200]{1,0:T(8,128)(2,1)S(1)} %concatenate.12.refs_0_, f32[8,128]{1,0:T(8,128)S(1)} %pad_bitcast_fusion.refs_1_), custom_call_target="tpu_custom_call" | custom-call | tf_op jit(solution)/shard_map/pallas_call | solution.py:248
  184.2 1.1 fusion.69
  185.4 0.4 convert_element_type.143
  185.8 0.7 copy.65
  186.5 1.2 fusion.81
  189.3 5.1 fusion.22.refs_1_.refs_3_
  194.5 0.8 copy-done.5
  195.3 42.1 %shard_map.202 = (bf16[256,2304]{1,0:T(8,128)(2,1)S(1)}, bf16[256,512]{1,0:T(8,128)(2,1)S(1)}, bf16[2,4,128,128]{3,2,1,0:T(8,128)(2,1)S(1)}, bf16[2,2,4,128,128]...) custom-call(s32[2]{0:T(128)S(1)} %copy-done.28, f32[256,3200]{1,0:T(8,128)S(1)} %fusion.22.refs_1_.refs_3_, ...), custom_call_target="tpu_custom_call" | custom-call | tf_op jit(solution)/shard_map/pallas_call | solution.py:737
  237.4 5.2 fusion.85
  243.2 8.7 %multiply_convert_fusion.1 = (bf16[256,4096]{1,0:T(8,128)(2,1)S(1)}, f32[256,4096]{1,0:T(8,128)}) fusion(bf16[256,1024]{1,0:T(8,128)(2,1)S(1)} %add_convert_fusion.3.refs_5_, bf16[1024,19200]{1,0:T(8,128)(2,1)} %bitcast.121), kind=kOutput, calls=%fused_computation.45 | convolution fusion | flops 2156920832 | bytes 15204352 | tf_op jit(solution)/shard_map/dot_general | solution.py:1064
  252.0 6.6 fusion.86
  259.2 6.2 fusion.18.refs_1_.refs_3_
  265.4 0.8 copy-done.9
  266.2 63.4 %shard_map.203 = (bf16[256,2304]{1,0:T(8,128)(2,1)S(1)}, bf16[256,512]{1,0:T(8,128)(2,1)S(1)}, bf16[2,4,128,128]{3,2,1,0:T(8,128)(2,1)S(1)}, bf16[2,2,4,128,128]...) custom-call(s32[2]{0:T(128)S(1)} %copy-done.28, f32[256,3200]{1,0:T(8,128)S(1)} %fusion.18.refs_1_.refs_3_, ...), custom_call_target="tpu_custom_call" | custom-call | tf_op jit(solution)/shard_map/pallas_call | solution.py:737
  329.7 4.3 fusion.87
  334.3 0.7 copy-done.30
  335.4 5.9 fusion.6
  341.3 2.0 copy-done.74
  343.3 4.8 convolution_convert_fusion
  348.3 0.7 reshape.273
  349.0 0.5 compare_select_fusion
  349.5 0.6 select_select_fusion
  350.1 1.3 bitcast_convert_fusion
  351.4 12.7 %reduce-scatter.4.cloned.1.call-done = bf16[512,4096]{1,0:T(8,128)(2,1)} async-done(((bf16[1024,4096]{1,0:T(8,128)(2,1)}), bf16[512,4096]{1,0:T(8,128)(2,1)}) %reduce-scatter.4.cloned.1.call-update) | async-done | bytes 4194320 | tf_op jit(solution)/shard_map/reduce_scatter | solution.py:518
  364.3 7.5 %fusion.37.refs_9_ = bf16[256,4096]{1,0:T(8,128)(2,1)S(1)} fusion(f32[256,4096]{1,0:T(8,128)} %copy-done.74, bf16[256,1024]{1,0:T(8,128)(2,1)S(1)} %bitcast_convert_fusion, bf16[1024,8192]{1,0:T(8,128)(2,1)} %all-gather.2.cloned.1.call-done), kind=kOutput, calls=%fused_computation.43 | convolution fusion | flops 2168455168 | bytes 15204352 | tf_op jit(solution)/shard_map/dot_general | solution.py:1106
  371.8 7.2 multiply_reduce_fusion.2
  379.0 0.4 fusion.80
  379.4 3.7 fusion.38.refs_1_
  383.2 42.7 %shard_map.204 = (bf16[256,3328]{1,0:T(8,128)(2,1)S(1)}, bf16[256,256]{1,0:T(8,128)(2,1)S(1)}) custom-call(s32[2]{0:T(128)S(1)} %copy-done.28, f32[256,2304]{1,0:T(8,128)S(1)} %fusion.38.refs_1_, bf16[256,512]{1,0:T(8,128)(2,1)S(1)} %get-tuple-element.38.refs_2_, f32[256,3200]{1,0:T(8,128)} %copy-done.1, f32[256,40]{1,0:T(8,128)S(1)} %copy.62.refs_2_.refs_4_, ...), custom_call_target="tpu_custom_call" | custom-call | tf_op jit(solution)/shard_map/pallas_call | solution.py:946
  425.9 6.2 multiply_reduce_fusion.3
  432.2 0.4 fusion.79
  432.6 1.8 copy-done.75
  434.3 6.9 fusion.30.refs_13_
  441.3 6.7 multiply_reduce_fusion
  448.0 1.4 fusion.78
  449.3 3.8 fusion.42.refs_1_
  453.3 42.6 %shard_map.205 = (bf16[256,3328]{1,0:T(8,128)(2,1)S(1)}, bf16[256,256]{1,0:T(8,128)(2,1)S(1)}) custom-call(s32[2]{0:T(128)S(1)} %copy-done.28, f32[256,2304]{1,0:T(8,128)S(1)} %fusion.42.refs_1_, bf16[256,512]{1,0:T(8,128)(2,1)S(1)} %copy-done.21, f32[256,3200]{1,0:T(8,128)} %copy-done, f32[256,40]{1,0:T(8,128)S(1)} %copy.59.refs_2_.refs_4_, ...), custom_call_target="tpu_custom_call" | custom-call | tf_op jit(solution)/shard_map/pallas_call | solution.py:946
  495.9 0.6 copy-done.26
  496.6 7.1 multiply_reduce_fusion.1
  504.2 0.7 stack.65
  504.9 0.7 stack.66
  505.6 0.7 stack.63
  506.3 0.7 stack.64
  507.2 0.9 pad.22.clone
  508.0 0.7 broadcast_multiply_fusion
  508.7 0.7 broadcast_multiply_fusion.1
  509.4 2.9 add_convert_fusion
  512.3 8.6 %fusion.65 = bf16[256,1024]{1,0:T(8,128)(2,1)} fusion(f32[256,1024]{1,0:T(8,128)} %copy-done.30, bf16[1024,8192]{1,0:T(8,128)(2,1)} %all-gather.2.cloned.1.call-done, f32[256,4096]{1,0:T(8,128)} %copy-done.74), kind=kOutput, calls=%fused_computation.66 | convolution fusion | flops 2157445120 | bytes 14155776 | tf_op jit(solution)/shard_map/dot_general | solution.py:89
  520.8 5.3 reduce-scatter.8.cloned.1.call-done
  526.2 1.0 copy-done.8
  527.2 1.0 copy-done.10
  528.2 1.0 copy-done.12
  529.3 0.9 copy-done.15
  530.2 0.9 copy-done.25
  531.1 0.9 copy-done.27
  532.0 194.2 %shard_map.206 = f32[32,23552]{1,0:T(8,128)} custom-call(bf16[256,1024]{1,0:T(8,128)(2,1)S(1)} %copy-done.10, bf16[256,1024]{1,0:T(8,128)(2,1)S(1)} %get-tuple-element.83.refs_1_, bf16[256,1024]{1,0:T(8,128)(2,1)S(1)} %copy-done.12, bf16[256,1024]{1,0:T(8,128)(2,1)S(1)} %copy-done.6, bf16[256,1024]{1,0:T(8,128)(2,1)S(1)} %get-tuple-element.79.refs_4_, ...), custom_call_target="tpu_custom_call" | custom-call | tf_op jit(solution)/shard_map/pallas_call | solution.py:489
  726.3 0.8 slice_bitcast_fusion.8
  727.2 1.7 slice_bitcast_fusion
  729.1 0.7 fusion.74
  729.8 1.1 copy-done.38
  730.9 7.1 fusion.76
  (218 shorter events, 5.6 us)
Async XLA Ops:
  7.2 328.2 %all-gather.2.cloned.1.call-start = ((), (), s32[]{:S(2)}) async-start(), calls=%async_computation.3 | async-start | bytes 17301504 | tf_op jit(solution)/shard_map/all_gather | solution.py:1036
  7.2 3.3 copy-start.46
  7.2 3.3 copy-start.52
  7.2 3.4 copy-start.28
  9.6 174.6 %copy-start.43 = (bf16[2,128,1024]{2,1,0:T(8,128)(2,1)S(1)}, bf16[2,128,1024]{2,1,0:T(8,128)(2,1)}, u32[]{:S(2)}) copy-start(bf16[2,128,1024]{2,1,0:T(8,128)(2,1)} %param.11) | copy-start | bytes 1572868
  11.7 176.8 %copy-start.37 = (bf16[2,128,1024]{2,1,0:T(8,128)(2,1)S(1)}, bf16[2,128,1024]{2,1,0:T(8,128)(2,1)}, u32[]{:S(2)}) copy-start(bf16[2,128,1024]{2,1,0:T(8,128)(2,1)} %param.10) | copy-start | bytes 1572868
  183.9 180.3 %reduce-scatter.4.cloned.1.call-start = ((), (), s32[]{:S(2)}) async-start(), calls=%async_computation.4 | async-start | bytes 12582912 | tf_op jit(solution)/shard_map/reduce_scatter | solution.py:518
  188.7 5.8 copy-start.65
  189.0 5.5 copy-start.67
  195.3 47.3 %copy-start = (f32[256,3200]{1,0:T(8,128)}, f32[256,3200]{1,0:T(8,128)S(1)}, u32[]{:S(2)}) copy-start(f32[256,3200]{1,0:T(8,128)S(1)} %fusion.22.refs_1_.refs_3_) | copy-start | bytes 9830404
  237.3 5.3 copy-start.2
  237.3 5.3 copy-start.16
  237.4 5.3 copy-start.18
  237.4 5.3 copy-start.20
  237.4 5.3 copy-start.22
  242.7 9.3 %copy-start.32 = (f32[256,1024]{1,0:T(8,128)}, f32[256,1024]{1,0:T(8,128)S(1)}, u32[]{:S(2)}) copy-start(f32[256,1024]{1,0:T(8,128)S(1)} %get-tuple-element.115) | copy-start | bytes 3145732
  242.7 9.3 %copy-start.53 = (f32[256]{0:T(256)}, f32[256]{0:T(256)S(1)}, u32[]{:S(2)}) copy-start(f32[256]{0:T(256)S(1)} %broadcast_multiply_fusion.10) | copy-start | bytes 3076
  243.0 9.0 %copy-start.59 = (f32[256]{0:T(256)}, f32[256]{0:T(256)S(1)}, u32[]{:S(2)}) copy-start(f32[256]{0:T(256)S(1)} %add_rsqrt_fusion.2) | copy-start | bytes 3076
  243.2 8.8 %copy-start.7 = (bf16[256,1024]{1,0:T(8,128)(2,1)}, bf16[256,1024]{1,0:T(8,128)(2,1)S(1)}, u32[]{:S(2)}) copy-start(bf16[256,1024]{1,0:T(8,128)(2,1)S(1)} %add_convert_fusion.3.refs_5_) | copy-start | bytes 1572868
  252.0 6.6 copy-start.40
  258.6 71.1 %copy-start.35 = (f32[256,1024]{1,0:T(8,128)}, f32[256,1024]{1,0:T(8,128)S(1)}, u32[]{:S(2)}) copy-start(f32[256,1024]{1,0:T(8,128)S(1)} %get-tuple-element.119) | copy-start | bytes 3145732
  258.6 6.8 copy-start.55
  258.9 6.5 copy-start.61
  258.9 75.4 %copy-start.48 = (f32[1024,1]{0,1:T(1,128)}, f32[1024,1]{0,1:T(1,128)S(1)}, u32[]{:S(2)}) copy-start(f32[1024,1]{0,1:T(1,128)S(1)} %get-tuple-element.101) | copy-start | bytes 12292
  266.2 67.8 %copy-start.1 = (f32[256,3200]{1,0:T(8,128)}, f32[256,3200]{1,0:T(8,128)S(1)}, u32[]{:S(2)}) copy-start(f32[256,3200]{1,0:T(8,128)S(1)} %fusion.18.refs_1_.refs_3_) | copy-start | bytes 9830404
  329.7 4.4 copy-start.3
  334.1 7.2 copy-start.57
  334.3 7.0 copy-start.63
  335.3 6.0 copy-start.11
  348.2 148.4 %reduce-scatter.6.cloned.1.call-start = ((), (), s32[]{:S(2)}) async-start(), calls=%async_computation.5 | async-start | bytes 5242880 | tf_op jit(solution)/shard_map/reduce_scatter | solution.py:518
  364.2 7.6 %copy-start.31 = (f32[256,1024]{1,0:T(8,128)S(1)}, f32[256,1024]{1,0:T(8,128)}, u32[]{:S(2)}) copy-start(f32[256,1024]{1,0:T(8,128)} %copy-done.30) | copy-start | bytes 3145732
  364.2 162.0 %reduce-scatter.8.cloned.1.call-start = ((), (), s32[]{:S(2)}) async-start(), calls=%async_computation.6 | async-start | bytes 1310720 | tf_op jit(solution)/shard_map/reduce_scatter | solution.py:518
  364.2 7.5 %copy-start.49 = (f32[1024,1]{0,1:T(1,128)S(1)}, f32[1024,1]{0,1:T(1,128)}, u32[]{:S(2)}) copy-start(f32[1024,1]{0,1:T(1,128)} %copy-done.48) | copy-start | bytes 12292
  364.2 7.5 %copy-start.58 = (f32[256]{0:T(256)S(1)}, f32[256]{0:T(256)}, u32[]{:S(2)}) copy-start(f32[256]{0:T(256)} %copy-done.57) | copy-start | bytes 3076
  364.3 7.5 %copy-start.64 = (f32[256]{0:T(256)S(1)}, f32[256]{0:T(256)}, u32[]{:S(2)}) copy-start(f32[256]{0:T(256)} %copy-done.63) | copy-start | bytes 3076
  371.8 7.2 copy-start.41
  371.8 7.2 copy-start.34
  383.2 42.7 %copy-start.36 = (f32[256,1024]{1,0:T(8,128)S(1)}, f32[256,1024]{1,0:T(8,128)}, u32[]{:S(2)}) copy-start(f32[256,1024]{1,0:T(8,128)} %copy-done.35) | copy-start | bytes 3145732
  383.2 42.7 %copy-start.56 = (f32[256]{0:T(256)S(1)}, f32[256]{0:T(256)}, u32[]{:S(2)}) copy-start(f32[256]{0:T(256)} %copy-done.55) | copy-start | bytes 3076
  383.2 42.7 %copy-start.62 = (f32[256]{0:T(256)S(1)}, f32[256]{0:T(256)}, u32[]{:S(2)}) copy-start(f32[256]{0:T(256)} %copy-done.61) | copy-start | bytes 3076
  425.9 6.3 copy-start.13
  425.9 6.3 copy-start.24
  434.3 6.9 copy-start.33
  434.3 6.9 copy-start.54
  434.3 6.9 copy-start.60
  441.3 6.7 copy-start.42
  449.3 3.9 copy-start.17
  449.3 3.9 copy-start.19
  449.3 3.9 copy-start.21
  449.3 3.9 copy-start.23
  453.2 43.3 %copy-start.66 = (f32[256]{0:T(256)S(1)}, f32[256]{0:T(256)}, u32[]{:S(2)}) copy-start(f32[256]{0:T(256)} %copy-done.65) | copy-start | bytes 3076
  453.2 43.3 %copy-start.68 = (f32[256]{0:T(256)S(1)}, f32[256]{0:T(256)}, u32[]{:S(2)}) copy-start(f32[256]{0:T(256)} %copy-done.67) | copy-start | bytes 3076
  496.5 7.2 copy-start.14
  496.6 7.2 copy-start.70
  496.6 7.2 copy-start.69
  496.6 7.2 copy-start.72
  496.6 7.2 copy-start.71
  512.3 13.9 %copy-start.4 = (bf16[256,2304]{1,0:T(8,128)(2,1)S(1)}, bf16[256,2304]{1,0:T(8,128)(2,1)}, u32[]{:S(2)}) copy-start(bf16[256,2304]{1,0:T(8,128)(2,1)} %copy-done.3) | copy-start | bytes 3538948
  512.3 13.9 %copy-start.6 = (bf16[256,1024]{1,0:T(8,128)(2,1)S(1)}, bf16[256,1024]{1,0:T(8,128)(2,1)}, u32[]{:S(2)}) copy-start(bf16[256,1024]{1,0:T(8,128)(2,1)} %copy-done.5) | copy-start | bytes 1572868
  532.0 197.8 %copy-start.39 = (f32[2,32,13568]{2,1,0:T(8,128)S(1)}, f32[2,32,13568]{2,1,0:T(8,128)}, u32[]{:S(2)}) copy-start(f32[2,32,13568]{2,1,0:T(8,128)} %param.16) | copy-start | bytes 10420228
  726.3 2.7 slice-start
  727.2 2.7 copy-start.29
  727.2 3.7 copy-start.38
  727.2 3.7 copy-start.45
  (17 other events, 24.0 us)
Sparse Core Ops, SparseCore 0:
  184.0 148.0 all-gather.1
  348.3 15.8 reduce-scatter.3
  367.4 53.9 reduce-scatter.5
  496.7 29.4 reduce-scatter.7

commit v8 on v7

--- a/solution.py
+++ b/solution.py
@@ -276,7 +276,7 @@
     orders = (
         (0, width // 2, first + dp_dims[::-1] + head_dims[::-1]),
         (width // 2, width // 4, first + dp_dims + head_dims[::-1]),
-        (3 * width // 4, width // 4, first + head_dims[::-1] + dp_dims[::-1]),
+        (3 * width // 4, width // 4, first + head_dims[::-1] + dp_dims),
     )
     stages = []
     for stage in range(len(dims)):

time: 748 us -> 741 us (level)
  Pallas kernels: 557 us -> 549 us
    pallas_call x1, Pallas kernels: 194 us -> 187 us  [reduce_weight_grads(): pl.pallas_call(kernel, grid=(chunks + starts[depth],), in_specs=[in_place...]
  transfers between devices with their start and end apart: 4 -> 4, of which waited for: 2 -> 2; matrix products, arithmetic and copies ran while one was open for 15% -> 16% of each run, Pallas kernels for 26% -> 26%
where the time goes in v8:
time: 741 us; the launch traced here: 737 us
  Pallas kernels  549 us (74%)
  matrix products  105 us (14%)
  local copies, waits for them, and re-layouts  26.3 us (4%)
  other arithmetic  23.1 us (3%)
  waiting for transfers between devices  18.1 us (2%)
  between operations  15.4 us (2%)
    pallas_call x1, Pallas kernels, reduce_weight_grads(): pl.pallas_call(kernel, grid=(chunks + starts[depth],), in_specs=[in_place...  187 us
    pallas_call x1, Pallas kernels, gather_rows(): pl.pallas_call(kernel, in_specs=[in_place] * 2, out_specs=[in_place] * 2,...  172 us
    pallas_call x2, Pallas kernels, attention_forward(): pl.pallas_call(kernel, in_specs=[pl.BlockSpec(memory_space=pltpu.SMEM)] +...  105 us
    pallas_call x2, Pallas kernels, attention_backward(): pl.pallas_call(kernel, in_specs=[pl.BlockSpec(memory_space=pltpu.SMEM)] +...  85.3 us
    dot_general x8, matrix products, contract_last(): lax.dot_general(left, right, (((1,), (1,)), ((), ())), preferred_element_...  51.9 us
    reduce_scatter x3, waiting for transfers between devices, reduced_natively(): share = lax.psum_scatter(share, axis, scatter_dimension=0, tiled=True)  18 us
  transfers between devices with their start and end apart: 4, of which 2 were waited for; matrix products, arithmetic and copies ran while one was open for 16% of the time, Pallas kernels for 26%

profile of v8, /device:TPU:0, one launch (start us, length us, event | category | flops | bytes accessed | tf_op | source)
XLA Modules:
  0.0 737.0 jit_solution(1620210396551873294)
XLA Ops:
  7.3 2.2 convert_element_type.118
  9.6 0.9 slice_bitcast_fusion.1
  11.3 0.4 concatenate.12.refs_0_
  11.7 172.1 %shard_map.201 = (bf16[2,2,2,2,2,32,19200]{6,5,4,3,2,1,0:T(8,128)(2,1)}, f32[2,2,2,2,2,8,128]{6,5,4,3,2,1,0:T(8,128)S(1)}) custom-call(bf16[32,19200]{1,0:T(8,128)(2,1)S(1)} %concatenate.12.refs_0_, f32[8,128]{1,0:T(8,128)S(1)} %pad_bitcast_fusion.refs_1_), custom_call_target="tpu_custom_call" | custom-call | tf_op jit(solution)/shard_map/pallas_call | solution.py:248
  184.2 1.1 fusion.69
  185.4 0.4 convert_element_type.143
  185.8 0.7 copy.65
  186.5 1.2 fusion.81
  189.3 5.1 fusion.22.refs_1_.refs_3_
  194.5 0.8 copy-done.5
  195.3 42.1 %shard_map.202 = (bf16[256,2304]{1,0:T(8,128)(2,1)S(1)}, bf16[256,512]{1,0:T(8,128)(2,1)S(1)}, bf16[2,4,128,128]{3,2,1,0:T(8,128)(2,1)S(1)}, bf16[2,2,4,128,128]...) custom-call(s32[2]{0:T(128)S(1)} %copy-done.28, f32[256,3200]{1,0:T(8,128)S(1)} %fusion.22.refs_1_.refs_3_, ...), custom_call_target="tpu_custom_call" | custom-call | tf_op jit(solution)/shard_map/pallas_call | solution.py:737
  237.4 5.2 fusion.85
  243.2 8.7 %multiply_convert_fusion.1 = (bf16[256,4096]{1,0:T(8,128)(2,1)S(1)}, f32[256,4096]{1,0:T(8,128)}) fusion(bf16[256,1024]{1,0:T(8,128)(2,1)S(1)} %add_convert_fusion.3.refs_5_, bf16[1024,19200]{1,0:T(8,128)(2,1)} %bitcast.121), kind=kOutput, calls=%fused_computation.45 | convolution fusion | flops 2156920832 | bytes 15204352 | tf_op jit(solution)/shard_map/dot_general | solution.py:1064
  252.0 6.6 fusion.86
  259.2 6.2 fusion.18.refs_1_.refs_3_
  265.4 0.8 copy-done.9
  266.2 63.4 %shard_map.203 = (bf16[256,2304]{1,0:T(8,128)(2,1)S(1)}, bf16[256,512]{1,0:T(8,128)(2,1)S(1)}, bf16[2,4,128,128]{3,2,1,0:T(8,128)(2,1)S(1)}, bf16[2,2,4,128,128]...) custom-call(s32[2]{0:T(128)S(1)} %copy-done.28, f32[256,3200]{1,0:T(8,128)S(1)} %fusion.18.refs_1_.refs_3_, ...), custom_call_target="tpu_custom_call" | custom-call | tf_op jit(solution)/shard_map/pallas_call | solution.py:737
  329.7 4.3 fusion.87
  334.3 0.7 copy-done.30
  335.4 5.9 fusion.6
  341.3 2.0 copy-done.74
  343.3 4.8 convolution_convert_fusion
  348.3 0.7 reshape.273
  349.0 0.5 compare_select_fusion
  349.5 0.6 select_select_fusion
  350.1 1.3 bitcast_convert_fusion
  351.4 12.7 %reduce-scatter.4.cloned.1.call-done = bf16[512,4096]{1,0:T(8,128)(2,1)} async-done(((bf16[1024,4096]{1,0:T(8,128)(2,1)}), bf16[512,4096]{1,0:T(8,128)(2,1)}) %reduce-scatter.4.cloned.1.call-update) | async-done | bytes 4194320 | tf_op jit(solution)/shard_map/reduce_scatter | solution.py:518
  364.3 7.5 %fusion.37.refs_9_ = bf16[256,4096]{1,0:T(8,128)(2,1)S(1)} fusion(f32[256,4096]{1,0:T(8,128)} %copy-done.74, bf16[256,1024]{1,0:T(8,128)(2,1)S(1)} %bitcast_convert_fusion, bf16[1024,8192]{1,0:T(8,128)(2,1)} %all-gather.2.cloned.1.call-done), kind=kOutput, calls=%fused_computation.43 | convolution fusion | flops 2168455168 | bytes 15204352 | tf_op jit(solution)/shard_map/dot_general | solution.py:1106
  371.8 7.2 multiply_reduce_fusion.2
  379.0 0.4 fusion.80
  379.4 3.7 fusion.38.refs_1_
  383.2 42.7 %shard_map.204 = (bf16[256,3328]{1,0:T(8,128)(2,1)S(1)}, bf16[256,256]{1,0:T(8,128)(2,1)S(1)}) custom-call(s32[2]{0:T(128)S(1)} %copy-done.28, f32[256,2304]{1,0:T(8,128)S(1)} %fusion.38.refs_1_, bf16[256,512]{1,0:T(8,128)(2,1)S(1)} %get-tuple-element.38.refs_2_, f32[256,3200]{1,0:T(8,128)} %copy-done.1, f32[256,40]{1,0:T(8,128)S(1)} %copy.62.refs_2_.refs_4_, ...), custom_call_target="tpu_custom_call" | custom-call | tf_op jit(solution)/shard_map/pallas_call | solution.py:946
  425.9 6.2 multiply_reduce_fusion.3
  432.2 0.4 fusion.79
  432.6 1.8 copy-done.75
  434.3 6.9 fusion.30.refs_13_
  441.3 6.7 multiply_reduce_fusion
  448.0 1.4 fusion.78
  449.3 3.8 fusion.42.refs_1_
  453.3 42.6 %shard_map.205 = (bf16[256,3328]{1,0:T(8,128)(2,1)S(1)}, bf16[256,256]{1,0:T(8,128)(2,1)S(1)}) custom-call(s32[2]{0:T(128)S(1)} %copy-done.28, f32[256,2304]{1,0:T(8,128)S(1)} %fusion.42.refs_1_, bf16[256,512]{1,0:T(8,128)(2,1)S(1)} %copy-done.21, f32[256,3200]{1,0:T(8,128)} %copy-done, f32[256,40]{1,0:T(8,128)S(1)} %copy.59.refs_2_.refs_4_, ...), custom_call_target="tpu_custom_call" | custom-call | tf_op jit(solution)/shard_map/pallas_call | solution.py:946
  495.9 0.6 copy-done.26
  496.6 7.1 multiply_reduce_fusion.1
  504.2 0.7 stack.65
  504.9 0.7 stack.66
  505.6 0.7 stack.63
  506.3 0.7 stack.64
  507.2 0.9 pad.22.clone
  508.0 0.7 broadcast_multiply_fusion
  508.7 0.7 broadcast_multiply_fusion.1
  509.4 2.9 add_convert_fusion
  512.3 8.6 %fusion.65 = bf16[256,1024]{1,0:T(8,128)(2,1)} fusion(f32[256,1024]{1,0:T(8,128)} %copy-done.30, bf16[1024,8192]{1,0:T(8,128)(2,1)} %all-gather.2.cloned.1.call-done, f32[256,4096]{1,0:T(8,128)} %copy-done.74), kind=kOutput, calls=%fused_computation.66 | convolution fusion | flops 2157445120 | bytes 14155776 | tf_op jit(solution)/shard_map/dot_general | solution.py:89
  520.8 5.3 reduce-scatter.8.cloned.1.call-done
  526.2 1.0 copy-done.8
  527.2 1.0 copy-done.10
  528.2 1.0 copy-done.12
  529.3 0.9 copy-done.15
  530.2 0.9 copy-done.25
  531.1 0.9 copy-done.27
  532.0 186.5 %shard_map.206 = f32[32,23552]{1,0:T(8,128)} custom-call(bf16[256,1024]{1,0:T(8,128)(2,1)S(1)} %copy-done.10, bf16[256,1024]{1,0:T(8,128)(2,1)S(1)} %get-tuple-element.83.refs_1_, bf16[256,1024]{1,0:T(8,128)(2,1)S(1)} %copy-done.12, bf16[256,1024]{1,0:T(8,128)(2,1)S(1)} %copy-done.6, bf16[256,1024]{1,0:T(8,128)(2,1)S(1)} %get-tuple-element.79.refs_4_, ...), custom_call_target="tpu_custom_call" | custom-call | tf_op jit(solution)/shard_map/pallas_call | solution.py:489
  718.6 0.8 slice_bitcast_fusion.8
  719.5 1.7 slice_bitcast_fusion
  721.4 0.7 fusion.74
  722.1 1.1 copy-done.38
  723.2 7.1 fusion.76
  (218 shorter events, 5.6 us)
Async XLA Ops:
  7.2 328.2 %all-gather.2.cloned.1.call-start = ((), (), s32[]{:S(2)}) async-start(), calls=%async_computation.3 | async-start | bytes 17301504 | tf_op jit(solution)/shard_map/all_gather | solution.py:1036
  7.2 3.3 copy-start.46
  7.2 3.3 copy-start.52
  7.2 3.4 copy-start.28
  9.6 174.6 %copy-start.43 = (bf16[2,128,1024]{2,1,0:T(8,128)(2,1)S(1)}, bf16[2,128,1024]{2,1,0:T(8,128)(2,1)}, u32[]{:S(2)}) copy-start(bf16[2,128,1024]{2,1,0:T(8,128)(2,1)} %param.11) | copy-start | bytes 1572868
  11.7 176.8 %copy-start.37 = (bf16[2,128,1024]{2,1,0:T(8,128)(2,1)S(1)}, bf16[2,128,1024]{2,1,0:T(8,128)(2,1)}, u32[]{:S(2)}) copy-start(bf16[2,128,1024]{2,1,0:T(8,128)(2,1)} %param.10) | copy-start | bytes 1572868
  183.9 180.3 %reduce-scatter.4.cloned.1.call-start = ((), (), s32[]{:S(2)}) async-start(), calls=%async_computation.4 | async-start | bytes 12582912 | tf_op jit(solution)/shard_map/reduce_scatter | solution.py:518
  188.7 5.8 copy-start.65
  189.0 5.5 copy-start.67
  195.3 47.3 %copy-start = (f32[256,3200]{1,0:T(8,128)}, f32[256,3200]{1,0:T(8,128)S(1)}, u32[]{:S(2)}) copy-start(f32[256,3200]{1,0:T(8,128)S(1)} %fusion.22.refs_1_.refs_3_) | copy-start | bytes 9830404
  237.3 5.3 copy-start.2
  237.3 5.3 copy-start.16
  237.4 5.3 copy-start.18
  237.4 5.3 copy-start.20
  237.4 5.3 copy-start.22
  242.7 9.3 %copy-start.32 = (f32[256,1024]{1,0:T(8,128)}, f32[256,1024]{1,0:T(8,128)S(1)}, u32[]{:S(2)}) copy-start(f32[256,1024]{1,0:T(8,128)S(1)} %get-tuple-element.115) | copy-start | bytes 3145732
  242.7 9.3 %copy-start.53 = (f32[256]{0:T(256)}, f32[256]{0:T(256)S(1)}, u32[]{:S(2)}) copy-start(f32[256]{0:T(256)S(1)} %broadcast_multiply_fusion.10) | copy-start | bytes 3076
  243.0 9.0 %copy-start.59 = (f32[256]{0:T(256)}, f32[256]{0:T(256)S(1)}, u32[]{:S(2)}) copy-start(f32[256]{0:T(256)S(1)} %add_rsqrt_fusion.2) | copy-start | bytes 3076
  243.2 8.8 %copy-start.7 = (bf16[256,1024]{1,0:T(8,128)(2,1)}, bf16[256,1024]{1,0:T(8,128)(2,1)S(1)}, u32[]{:S(2)}) copy-start(bf16[256,1024]{1,0:T(8,128)(2,1)S(1)} %add_convert_fusion.3.refs_5_) | copy-start | bytes 1572868
  252.0 6.6 copy-start.40
  258.6 71.1 %copy-start.35 = (f32[256,1024]{1,0:T(8,128)}, f32[256,1024]{1,0:T(8,128)S(1)}, u32[]{:S(2)}) copy-start(f32[256,1024]{1,0:T(8,128)S(1)} %get-tuple-element.119) | copy-start | bytes 3145732
  258.6 6.8 copy-start.55
  258.9 6.5 copy-start.61
  258.9 75.4 %copy-start.48 = (f32[1024,1]{0,1:T(1,128)}, f32[1024,1]{0,1:T(1,128)S(1)}, u32[]{:S(2)}) copy-start(f32[1024,1]{0,1:T(1,128)S(1)} %get-tuple-element.101) | copy-start | bytes 12292
  266.2 67.8 %copy-start.1 = (f32[256,3200]{1,0:T(8,128)}, f32[256,3200]{1,0:T(8,128)S(1)}, u32[]{:S(2)}) copy-start(f32[256,3200]{1,0:T(8,128)S(1)} %fusion.18.refs_1_.refs_3_) | copy-start | bytes 9830404
  329.7 4.4 copy-start.3
  334.1 7.2 copy-start.57
  334.3 7.0 copy-start.63
  335.3 6.0 copy-start.11
  348.2 148.4 %reduce-scatter.6.cloned.1.call-start = ((), (), s32[]{:S(2)}) async-start(), calls=%async_computation.5 | async-start | bytes 5242880 | tf_op jit(solution)/shard_map/reduce_scatter | solution.py:518
  364.2 7.6 %copy-start.31 = (f32[256,1024]{1,0:T(8,128)S(1)}, f32[256,1024]{1,0:T(8,128)}, u32[]{:S(2)}) copy-start(f32[256,1024]{1,0:T(8,128)} %copy-done.30) | copy-start | bytes 3145732
  364.2 162.0 %reduce-scatter.8.cloned.1.call-start = ((), (), s32[]{:S(2)}) async-start(), calls=%async_computation.6 | async-start | bytes 1310720 | tf_op jit(solution)/shard_map/reduce_scatter | solution.py:518
  364.2 7.5 %copy-start.49 = (f32[1024,1]{0,1:T(1,128)S(1)}, f32[1024,1]{0,1:T(1,128)}, u32[]{:S(2)}) copy-start(f32[1024,1]{0,1:T(1,128)} %copy-done.48) | copy-start | bytes 12292
  364.2 7.5 %copy-start.58 = (f32[256]{0:T(256)S(1)}, f32[256]{0:T(256)}, u32[]{:S(2)}) copy-start(f32[256]{0:T(256)} %copy-done.57) | copy-start | bytes 3076
  364.3 7.5 %copy-start.64 = (f32[256]{0:T(256)S(1)}, f32[256]{0:T(256)}, u32[]{:S(2)}) copy-start(f32[256]{0:T(256)} %copy-done.63) | copy-start | bytes 3076
  371.8 7.2 copy-start.41
  371.8 7.2 copy-start.34
  383.2 42.7 %copy-start.36 = (f32[256,1024]{1,0:T(8,128)S(1)}, f32[256,1024]{1,0:T(8,128)}, u32[]{:S(2)}) copy-start(f32[256,1024]{1,0:T(8,128)} %copy-done.35) | copy-start | bytes 3145732
  383.2 42.7 %copy-start.56 = (f32[256]{0:T(256)S(1)}, f32[256]{0:T(256)}, u32[]{:S(2)}) copy-start(f32[256]{0:T(256)} %copy-done.55) | copy-start | bytes 3076
  383.2 42.7 %copy-start.62 = (f32[256]{0:T(256)S(1)}, f32[256]{0:T(256)}, u32[]{:S(2)}) copy-start(f32[256]{0:T(256)} %copy-done.61) | copy-start | bytes 3076
  425.9 6.3 copy-start.13
  425.9 6.3 copy-start.24
  434.3 6.9 copy-start.33
  434.3 6.9 copy-start.54
  434.3 6.9 copy-start.60
  441.3 6.7 copy-start.42
  449.3 3.9 copy-start.17
  449.3 3.9 copy-start.19
  449.3 3.9 copy-start.21
  449.3 3.9 copy-start.23
  453.2 43.3 %copy-start.66 = (f32[256]{0:T(256)S(1)}, f32[256]{0:T(256)}, u32[]{:S(2)}) copy-start(f32[256]{0:T(256)} %copy-done.65) | copy-start | bytes 3076
  453.2 43.3 %copy-start.68 = (f32[256]{0:T(256)S(1)}, f32[256]{0:T(256)}, u32[]{:S(2)}) copy-start(f32[256]{0:T(256)} %copy-done.67) | copy-start | bytes 3076
  496.5 7.2 copy-start.14
  496.6 7.2 copy-start.70
  496.6 7.2 copy-start.69
  496.6 7.2 copy-start.72
  496.6 7.2 copy-start.71
  512.3 13.9 %copy-start.4 = (bf16[256,2304]{1,0:T(8,128)(2,1)S(1)}, bf16[256,2304]{1,0:T(8,128)(2,1)}, u32[]{:S(2)}) copy-start(bf16[256,2304]{1,0:T(8,128)(2,1)} %copy-done.3) | copy-start | bytes 3538948
  512.3 13.9 %copy-start.6 = (bf16[256,1024]{1,0:T(8,128)(2,1)S(1)}, bf16[256,1024]{1,0:T(8,128)(2,1)}, u32[]{:S(2)}) copy-start(bf16[256,1024]{1,0:T(8,128)(2,1)} %copy-done.5) | copy-start | bytes 1572868
  532.0 190.1 %copy-start.39 = (f32[2,32,13568]{2,1,0:T(8,128)S(1)}, f32[2,32,13568]{2,1,0:T(8,128)}, u32[]{:S(2)}) copy-start(f32[2,32,13568]{2,1,0:T(8,128)} %param.16) | copy-start | bytes 10420228
  718.6 2.7 slice-start
  719.4 2.7 copy-start.29
  719.5 3.7 copy-start.38
  719.5 3.7 copy-start.45
  (17 other events, 24.0 us)
Sparse Core Ops, SparseCore 0:
  184.0 148.0 all-gather.1
  348.3 15.8 reduce-scatter.3
  367.4 53.9 reduce-scatter.5
  496.7 29.4 reduce-scatter.7

commit v9 on v8

--- a/solution.py
+++ b/solution.py
@@ -1028,7 +1028,7 @@
     early = []
     for layer in range(LAYERS):
         early += [in_low[layer], out_low[layer]] + ([ffn_low[layer]] if layer + 1 < LAYERS else [])
-    gathered, counts = gather_rows(jnp.concatenate(early, axis=1), counts, 128, 2)
+    gathered, counts = gather_rows(jnp.concatenate(early, axis=1), counts, 256, 2)
     counts, late = lax.optimization_barrier((counts, ffn_low[-1]))
     loads = jnp.sum(counts.reshape(-1, size + (-size) % 1024), axis=0)[:size].reshape(
         load_part.shape

time: 741 us -> 738 us (level)
  no operation moved by 1% of the time
where the time goes in v9:
time: 738 us; the launch traced here: 734 us
  Pallas kernels  545 us (74%)
  matrix products  105 us (14%)
  local copies, waits for them, and re-layouts  26.3 us (4%)
  other arithmetic  23.1 us (3%)
  waiting for transfers between devices  19.3 us (3%)
  between operations  15.4 us (2%)
    pallas_call x1, Pallas kernels, reduce_weight_grads(): pl.pallas_call(kernel, grid=(chunks + starts[depth],), in_specs=[in_place...  187 us
    pallas_call x1, Pallas kernels, gather_rows(): pl.pallas_call(kernel, in_specs=[in_place] * 2, out_specs=[in_place] * 2,...  169 us
    pallas_call x2, Pallas kernels, attention_forward(): pl.pallas_call(kernel, in_specs=[pl.BlockSpec(memory_space=pltpu.SMEM)] +...  104 us
    pallas_call x2, Pallas kernels, attention_backward(): pl.pallas_call(kernel, in_specs=[pl.BlockSpec(memory_space=pltpu.SMEM)] +...  85.2 us
    dot_general x8, matrix products, contract_last(): lax.dot_general(left, right, (((1,), (1,)), ((), ())), preferred_element_...  52.1 us
    reduce_scatter x3, waiting for transfers between devices, reduced_natively(): share = lax.psum_scatter(share, axis, scatter_dimension=0, tiled=True)  19.2 us
  transfers between devices with their start and end apart: 4, of which 2 were waited for; matrix products, arithmetic and copies ran while one was open for 16% of the time, Pallas kernels for 26%

profile of v9, /device:TPU:0, one launch (start us, length us, event | category | flops | bytes accessed | tf_op | source)
XLA Modules:
  0.0 734.3 jit_solution(2908691078486766086)
XLA Ops:
  7.3 2.2 convert_element_type.118
  9.6 0.9 slice_bitcast_fusion.1
  11.3 0.4 concatenate.12.refs_0_
  11.7 169.0 %shard_map.201 = (bf16[2,2,2,2,2,32,19200]{6,5,4,3,2,1,0:T(8,128)(2,1)}, f32[2,2,2,2,2,8,128]{6,5,4,3,2,1,0:T(8,128)S(1)}) custom-call(bf16[32,19200]{1,0:T(8,128)(2,1)S(1)} %concatenate.12.refs_0_, f32[8,128]{1,0:T(8,128)S(1)} %pad_bitcast_fusion.refs_1_), custom_call_target="tpu_custom_call" | custom-call | tf_op jit(solution)/shard_map/pallas_call | solution.py:248
  181.1 1.1 fusion.69
  182.3 0.4 convert_element_type.143
  182.6 0.7 copy.65
  183.4 1.2 fusion.81
  186.2 5.1 fusion.22.refs_1_.refs_3_
  191.3 0.8 copy-done.5
  192.1 42.1 %shard_map.202 = (bf16[256,2304]{1,0:T(8,128)(2,1)S(1)}, bf16[256,512]{1,0:T(8,128)(2,1)S(1)}, bf16[2,4,128,128]{3,2,1,0:T(8,128)(2,1)S(1)}, bf16[2,2,4,128,128]...) custom-call(s32[2]{0:T(128)S(1)} %copy-done.28, f32[256,3200]{1,0:T(8,128)S(1)} %fusion.22.refs_1_.refs_3_, ...), custom_call_target="tpu_custom_call" | custom-call | tf_op jit(solution)/shard_map/pallas_call | solution.py:737
  234.3 5.2 fusion.85
  240.1 8.7 %multiply_convert_fusion.1 = (bf16[256,4096]{1,0:T(8,128)(2,1)S(1)}, f32[256,4096]{1,0:T(8,128)}) fusion(bf16[256,1024]{1,0:T(8,128)(2,1)S(1)} %add_convert_fusion.3.refs_5_, bf16[1024,19200]{1,0:T(8,128)(2,1)} %bitcast.121), kind=kOutput, calls=%fused_computation.45 | convolution fusion | flops 2156920832 | bytes 15204352 | tf_op jit(solution)/shard_map/dot_general | solution.py:1064
  248.9 6.6 fusion.86
  256.1 6.7 fusion.18.refs_1_.refs_3_
  262.8 0.8 copy-done.9
  263.6 62.1 %shard_map.203 = (bf16[256,2304]{1,0:T(8,128)(2,1)S(1)}, bf16[256,512]{1,0:T(8,128)(2,1)S(1)}, bf16[2,4,128,128]{3,2,1,0:T(8,128)(2,1)S(1)}, bf16[2,2,4,128,128]...) custom-call(s32[2]{0:T(128)S(1)} %copy-done.28, f32[256,3200]{1,0:T(8,128)S(1)} %fusion.18.refs_1_.refs_3_, ...), custom_call_target="tpu_custom_call" | custom-call | tf_op jit(solution)/shard_map/pallas_call | solution.py:737
  325.7 4.5 fusion.87
  330.6 0.7 copy-done.30
  331.6 5.9 fusion.6
  337.6 2.0 copy-done.74
  339.5 4.8 convolution_convert_fusion
  344.5 0.7 reshape.273
  345.2 0.5 compare_select_fusion
  345.8 0.6 select_select_fusion
  346.4 1.3 bitcast_convert_fusion
  347.7 13.8 %reduce-scatter.4.cloned.1.call-done = bf16[512,4096]{1,0:T(8,128)(2,1)} async-done(((bf16[1024,4096]{1,0:T(8,128)(2,1)}), bf16[512,4096]{1,0:T(8,128)(2,1)}) %reduce-scatter.4.cloned.1.call-update) | async-done | bytes 4194320 | tf_op jit(solution)/shard_map/reduce_scatter | solution.py:518
  361.6 7.4 %fusion.37.refs_9_ = bf16[256,4096]{1,0:T(8,128)(2,1)S(1)} fusion(f32[256,4096]{1,0:T(8,128)} %copy-done.74, bf16[256,1024]{1,0:T(8,128)(2,1)S(1)} %bitcast_convert_fusion, bf16[1024,8192]{1,0:T(8,128)(2,1)} %all-gather.2.cloned.1.call-done), kind=kOutput, calls=%fused_computation.43 | convolution fusion | flops 2168455168 | bytes 15204352 | tf_op jit(solution)/shard_map/dot_general | solution.py:1106
  369.1 7.2 multiply_reduce_fusion.2
  376.3 0.4 fusion.80
  376.7 3.7 fusion.38.refs_1_
  380.5 42.7 %shard_map.204 = (bf16[256,3328]{1,0:T(8,128)(2,1)S(1)}, bf16[256,256]{1,0:T(8,128)(2,1)S(1)}) custom-call(s32[2]{0:T(128)S(1)} %copy-done.28, f32[256,2304]{1,0:T(8,128)S(1)} %fusion.38.refs_1_, bf16[256,512]{1,0:T(8,128)(2,1)S(1)} %get-tuple-element.38.refs_2_, f32[256,3200]{1,0:T(8,128)} %copy-done.1, f32[256,40]{1,0:T(8,128)S(1)} %copy.62.refs_2_.refs_4_, ...), custom_call_target="tpu_custom_call" | custom-call | tf_op jit(solution)/shard_map/pallas_call | solution.py:946
  423.2 6.2 multiply_reduce_fusion.3
  429.5 0.4 fusion.79
  429.9 1.8 copy-done.75
  431.7 6.9 fusion.30.refs_13_
  438.6 6.7 multiply_reduce_fusion
  445.3 1.4 fusion.78
  446.7 3.8 fusion.42.refs_1_
  450.6 42.5 %shard_map.205 = (bf16[256,3328]{1,0:T(8,128)(2,1)S(1)}, bf16[256,256]{1,0:T(8,128)(2,1)S(1)}) custom-call(s32[2]{0:T(128)S(1)} %copy-done.28, f32[256,2304]{1,0:T(8,128)S(1)} %fusion.42.refs_1_, bf16[256,512]{1,0:T(8,128)(2,1)S(1)} %copy-done.21, f32[256,3200]{1,0:T(8,128)} %copy-done, f32[256,40]{1,0:T(8,128)S(1)} %copy.59.refs_2_.refs_4_, ...), custom_call_target="tpu_custom_call" | custom-call | tf_op jit(solution)/shard_map/pallas_call | solution.py:946
  493.1 0.6 copy-done.26
  493.9 7.1 multiply_reduce_fusion.1
  501.5 0.7 stack.65
  502.2 0.7 stack.66
  502.8 0.7 stack.63
  503.5 0.7 stack.64
  504.4 0.9 pad.22.clone
  505.3 0.7 broadcast_multiply_fusion
  506.0 0.7 broadcast_multiply_fusion.1
  506.6 2.9 add_convert_fusion
  509.5 8.5 %fusion.65 = bf16[256,1024]{1,0:T(8,128)(2,1)} fusion(f32[256,1024]{1,0:T(8,128)} %copy-done.30, bf16[1024,8192]{1,0:T(8,128)(2,1)} %all-gather.2.cloned.1.call-done, f32[256,4096]{1,0:T(8,128)} %copy-done.74), kind=kOutput, calls=%fused_computation.66 | convolution fusion | flops 2157445120 | bytes 14155776 | tf_op jit(solution)/shard_map/dot_general | solution.py:89
  518.1 5.4 reduce-scatter.8.cloned.1.call-done
  523.5 1.0 copy-done.8
  524.5 1.0 copy-done.10
  525.6 1.0 copy-done.12
  526.6 0.9 copy-done.15
  527.5 0.9 copy-done.25
  528.5 0.9 copy-done.27
  529.4 186.5 %shard_map.206 = f32[32,23552]{1,0:T(8,128)} custom-call(bf16[256,1024]{1,0:T(8,128)(2,1)S(1)} %copy-done.10, bf16[256,1024]{1,0:T(8,128)(2,1)S(1)} %get-tuple-element.83.refs_1_, bf16[256,1024]{1,0:T(8,128)(2,1)S(1)} %copy-done.12, bf16[256,1024]{1,0:T(8,128)(2,1)S(1)} %copy-done.6, bf16[256,1024]{1,0:T(8,128)(2,1)S(1)} %get-tuple-element.79.refs_4_, ...), custom_call_target="tpu_custom_call" | custom-call | tf_op jit(solution)/shard_map/pallas_call | solution.py:489
  715.9 0.8 slice_bitcast_fusion.8
  716.8 1.7 slice_bitcast_fusion
  718.7 0.7 fusion.74
  719.4 1.1 copy-done.38
  720.5 7.1 fusion.76
  (218 shorter events, 5.6 us)
Async XLA Ops:
  7.2 324.4 %all-gather.2.cloned.1.call-start = ((), (), s32[]{:S(2)}) async-start(), calls=%async_computation.3 | async-start | bytes 17301504 | tf_op jit(solution)/shard_map/all_gather | solution.py:1036
  7.2 3.3 copy-start.46
  7.2 3.3 copy-start.52
  7.2 3.4 copy-start.28
  9.6 171.5 %copy-start.43 = (bf16[2,128,1024]{2,1,0:T(8,128)(2,1)S(1)}, bf16[2,128,1024]{2,1,0:T(8,128)(2,1)}, u32[]{:S(2)}) copy-start(bf16[2,128,1024]{2,1,0:T(8,128)(2,1)} %param.11) | copy-start | bytes 1572868
  11.7 173.7 %copy-start.37 = (bf16[2,128,1024]{2,1,0:T(8,128)(2,1)S(1)}, bf16[2,128,1024]{2,1,0:T(8,128)(2,1)}, u32[]{:S(2)}) copy-start(bf16[2,128,1024]{2,1,0:T(8,128)(2,1)} %param.10) | copy-start | bytes 1572868
  180.8 180.7 %reduce-scatter.4.cloned.1.call-start = ((), (), s32[]{:S(2)}) async-start(), calls=%async_computation.4 | async-start | bytes 12582912 | tf_op jit(solution)/shard_map/reduce_scatter | solution.py:518
  185.6 5.7 copy-start.65
  185.9 5.4 copy-start.67
  192.1 47.4 %copy-start = (f32[256,3200]{1,0:T(8,128)}, f32[256,3200]{1,0:T(8,128)S(1)}, u32[]{:S(2)}) copy-start(f32[256,3200]{1,0:T(8,128)S(1)} %fusion.22.refs_1_.refs_3_) | copy-start | bytes 9830404
  234.3 5.3 copy-start.2
  234.3 5.3 copy-start.16
  234.3 5.3 copy-start.18
  234.3 5.3 copy-start.20
  234.3 5.3 copy-start.22
  239.6 9.3 %copy-start.32 = (f32[256,1024]{1,0:T(8,128)}, f32[256,1024]{1,0:T(8,128)S(1)}, u32[]{:S(2)}) copy-start(f32[256,1024]{1,0:T(8,128)S(1)} %get-tuple-element.115) | copy-start | bytes 3145732
  239.6 9.3 %copy-start.53 = (f32[256]{0:T(256)}, f32[256]{0:T(256)S(1)}, u32[]{:S(2)}) copy-start(f32[256]{0:T(256)S(1)} %broadcast_multiply_fusion.10) | copy-start | bytes 3076
  239.9 9.0 %copy-start.59 = (f32[256]{0:T(256)}, f32[256]{0:T(256)S(1)}, u32[]{:S(2)}) copy-start(f32[256]{0:T(256)S(1)} %add_rsqrt_fusion.2) | copy-start | bytes 3076
  240.1 8.8 %copy-start.7 = (bf16[256,1024]{1,0:T(8,128)(2,1)}, bf16[256,1024]{1,0:T(8,128)(2,1)S(1)}, u32[]{:S(2)}) copy-start(bf16[256,1024]{1,0:T(8,128)(2,1)S(1)} %add_convert_fusion.3.refs_5_) | copy-start | bytes 1572868
  248.9 6.6 copy-start.40
  255.5 70.2 %copy-start.35 = (f32[256,1024]{1,0:T(8,128)}, f32[256,1024]{1,0:T(8,128)S(1)}, u32[]{:S(2)}) copy-start(f32[256,1024]{1,0:T(8,128)S(1)} %get-tuple-element.119) | copy-start | bytes 3145732
  255.5 7.3 copy-start.55
  255.8 7.0 copy-start.61
  255.8 74.8 %copy-start.48 = (f32[1024,1]{0,1:T(1,128)}, f32[1024,1]{0,1:T(1,128)S(1)}, u32[]{:S(2)}) copy-start(f32[1024,1]{0,1:T(1,128)S(1)} %get-tuple-element.101) | copy-start | bytes 12292
  263.6 66.7 %copy-start.1 = (f32[256,3200]{1,0:T(8,128)}, f32[256,3200]{1,0:T(8,128)S(1)}, u32[]{:S(2)}) copy-start(f32[256,3200]{1,0:T(8,128)S(1)} %fusion.18.refs_1_.refs_3_) | copy-start | bytes 9830404
  325.7 4.6 copy-start.3
  330.3 7.2 copy-start.57
  330.6 7.0 copy-start.63
  331.6 6.0 copy-start.11
  344.4 149.4 %reduce-scatter.6.cloned.1.call-start = ((), (), s32[]{:S(2)}) async-start(), calls=%async_computation.5 | async-start | bytes 5242880 | tf_op jit(solution)/shard_map/reduce_scatter | solution.py:518
  361.5 7.5 %copy-start.31 = (f32[256,1024]{1,0:T(8,128)S(1)}, f32[256,1024]{1,0:T(8,128)}, u32[]{:S(2)}) copy-start(f32[256,1024]{1,0:T(8,128)} %copy-done.30) | copy-start | bytes 3145732
  361.5 161.9 %reduce-scatter.8.cloned.1.call-start = ((), (), s32[]{:S(2)}) async-start(), calls=%async_computation.6 | async-start | bytes 1310720 | tf_op jit(solution)/shard_map/reduce_scatter | solution.py:518
  361.6 7.5 %copy-start.49 = (f32[1024,1]{0,1:T(1,128)S(1)}, f32[1024,1]{0,1:T(1,128)}, u32[]{:S(2)}) copy-start(f32[1024,1]{0,1:T(1,128)} %copy-done.48) | copy-start | bytes 12292
  361.6 7.5 %copy-start.58 = (f32[256]{0:T(256)S(1)}, f32[256]{0:T(256)}, u32[]{:S(2)}) copy-start(f32[256]{0:T(256)} %copy-done.57) | copy-start | bytes 3076
  361.6 7.5 %copy-start.64 = (f32[256]{0:T(256)S(1)}, f32[256]{0:T(256)}, u32[]{:S(2)}) copy-start(f32[256]{0:T(256)} %copy-done.63) | copy-start | bytes 3076
  369.1 7.2 copy-start.41
  369.1 7.2 copy-start.34
  380.5 42.7 %copy-start.36 = (f32[256,1024]{1,0:T(8,128)S(1)}, f32[256,1024]{1,0:T(8,128)}, u32[]{:S(2)}) copy-start(f32[256,1024]{1,0:T(8,128)} %copy-done.35) | copy-start | bytes 3145732
  380.5 42.7 %copy-start.56 = (f32[256]{0:T(256)S(1)}, f32[256]{0:T(256)}, u32[]{:S(2)}) copy-start(f32[256]{0:T(256)} %copy-done.55) | copy-start | bytes 3076
  380.5 42.7 %copy-start.62 = (f32[256]{0:T(256)S(1)}, f32[256]{0:T(256)}, u32[]{:S(2)}) copy-start(f32[256]{0:T(256)} %copy-done.61) | copy-start | bytes 3076
  423.2 6.3 copy-start.13
  423.2 6.3 copy-start.24
  431.7 6.9 copy-start.33
  431.7 6.9 copy-start.54
  431.7 6.9 copy-start.60
  438.6 6.7 copy-start.42
  446.7 3.9 copy-start.17
  446.7 3.9 copy-start.19
  446.7 3.9 copy-start.21
  446.7 3.9 copy-start.23
  450.6 43.2 %copy-start.66 = (f32[256]{0:T(256)S(1)}, f32[256]{0:T(256)}, u32[]{:S(2)}) copy-start(f32[256]{0:T(256)} %copy-done.65) | copy-start | bytes 3076
  450.6 43.2 %copy-start.68 = (f32[256]{0:T(256)S(1)}, f32[256]{0:T(256)}, u32[]{:S(2)}) copy-start(f32[256]{0:T(256)} %copy-done.67) | copy-start | bytes 3076
  493.8 7.2 copy-start.14
  493.8 7.2 copy-start.70
  493.8 7.2 copy-start.69
  493.9 7.2 copy-start.72
  493.9 7.2 copy-start.71
  509.5 14.0 %copy-start.4 = (bf16[256,2304]{1,0:T(8,128)(2,1)S(1)}, bf16[256,2304]{1,0:T(8,128)(2,1)}, u32[]{:S(2)}) copy-start(bf16[256,2304]{1,0:T(8,128)(2,1)} %copy-done.3) | copy-start | bytes 3538948
  509.5 14.0 %copy-start.6 = (bf16[256,1024]{1,0:T(8,128)(2,1)S(1)}, bf16[256,1024]{1,0:T(8,128)(2,1)}, u32[]{:S(2)}) copy-start(bf16[256,1024]{1,0:T(8,128)(2,1)} %copy-done.5) | copy-start | bytes 1572868
  529.4 190.1 %copy-start.39 = (f32[2,32,13568]{2,1,0:T(8,128)S(1)}, f32[2,32,13568]{2,1,0:T(8,128)}, u32[]{:S(2)}) copy-start(f32[2,32,13568]{2,1,0:T(8,128)} %param.16) | copy-start | bytes 10420228
  715.9 2.7 slice-start
  716.8 2.7 copy-start.29
  716.8 3.7 copy-start.38
  716.8 3.7 copy-start.45
  (17 other events, 24.0 us)
Sparse Core Ops, SparseCore 0:
  180.9 148.5 all-gather.1
  344.5 16.9 reduce-scatter.3
  364.7 53.9 reduce-scatter.5
  493.9 29.4 reduce-scatter.7

commit v10 on v9

--- a/solution.py
+++ b/solution.py
@@ -147,7 +147,7 @@
     lag, slots = (3, 6)
     local_slots = 2
     ring = (depth + 1) * lag + local_slots + 2
-    steps = max(count for _, count, _ in pieces) + lag * depth
+    steps = max(count for _, count, _ in pieces) + lag * depth - 1
 
     def kernel(*refs):
         share_ref, counts_ref, out_ref, counts_out = refs[:4]
@@ -204,7 +204,7 @@
 
         def body(step, carry):
             for stage in range(depth, -1, -1):
-                chunk = step - lag * stage
+                chunk = step - lag * stage + (1 if stage == depth else 0)
                 for number, piece in enumerate(pieces):
 
                     @pl.when((chunk >= 0) & (chunk < piece[1]))

time: 738 us -> 738 us (level)
  no operation moved by 1% of the time
where the time goes in v10:
time: 738 us; the launch traced here: 734 us
  Pallas kernels  545 us (74%)
  matrix products  105 us (14%)
  local copies, waits for them, and re-layouts  26.3 us (4%)
  other arithmetic  23.1 us (3%)
  waiting for transfers between devices  19.3 us (3%)
  between operations  15.4 us (2%)
    pallas_call x1, Pallas kernels, reduce_weight_grads(): pl.pallas_call(kernel, grid=(chunks + starts[depth],), in_specs=[in_place...  187 us
    pallas_call x1, Pallas kernels, gather_rows(): pl.pallas_call(kernel, in_specs=[in_place] * 2, out_specs=[in_place] * 2,...  169 us
    pallas_call x2, Pallas kernels, attention_forward(): pl.pallas_call(kernel, in_specs=[pl.BlockSpec(memory_space=pltpu.SMEM)] +...  104 us
    pallas_call x2, Pallas kernels, attention_backward(): pl.pallas_call(kernel, in_specs=[pl.BlockSpec(memory_space=pltpu.SMEM)] +...  85.2 us
    dot_general x8, matrix products, contract_last(): lax.dot_general(left, right, (((1,), (1,)), ((), ())), preferred_element_...  52.1 us
    reduce_scatter x3, waiting for transfers between devices, reduced_natively(): share = lax.psum_scatter(share, axis, scatter_dimension=0, tiled=True)  19.2 us
  transfers between devices with their start and end apart: 4, of which 2 were waited for; matrix products, arithmetic and copies ran while one was open for 16% of the time, Pallas kernels for 26%

profile of v10, /device:TPU:0, one launch (start us, length us, event | category | flops | bytes accessed | tf_op | source)
XLA Modules:
  0.0 734.3 jit_solution(3581528719252868487)
XLA Ops:
  7.3 2.2 convert_element_type.118
  9.6 0.9 slice_bitcast_fusion.1
  11.3 0.4 concatenate.12.refs_0_
  11.7 169.0 %shard_map.201 = (bf16[2,2,2,2,2,32,19200]{6,5,4,3,2,1,0:T(8,128)(2,1)}, f32[2,2,2,2,2,8,128]{6,5,4,3,2,1,0:T(8,128)S(1)}) custom-call(bf16[32,19200]{1,0:T(8,128)(2,1)S(1)} %concatenate.12.refs_0_, f32[8,128]{1,0:T(8,128)S(1)} %pad_bitcast_fusion.refs_1_), custom_call_target="tpu_custom_call" | custom-call | tf_op jit(solution)/shard_map/pallas_call | solution.py:248
  181.1 1.1 fusion.69
  182.3 0.4 convert_element_type.143
  182.6 0.7 copy.65
  183.4 1.2 fusion.81
  186.2 5.1 fusion.22.refs_1_.refs_3_
  191.3 0.8 copy-done.5
  192.1 42.1 %shard_map.202 = (bf16[256,2304]{1,0:T(8,128)(2,1)S(1)}, bf16[256,512]{1,0:T(8,128)(2,1)S(1)}, bf16[2,4,128,128]{3,2,1,0:T(8,128)(2,1)S(1)}, bf16[2,2,4,128,128]...) custom-call(s32[2]{0:T(128)S(1)} %copy-done.28, f32[256,3200]{1,0:T(8,128)S(1)} %fusion.22.refs_1_.refs_3_, ...), custom_call_target="tpu_custom_call" | custom-call | tf_op jit(solution)/shard_map/pallas_call | solution.py:737
  234.3 5.2 fusion.85
  240.1 8.7 %multiply_convert_fusion.1 = (bf16[256,4096]{1,0:T(8,128)(2,1)S(1)}, f32[256,4096]{1,0:T(8,128)}) fusion(bf16[256,1024]{1,0:T(8,128)(2,1)S(1)} %add_convert_fusion.3.refs_5_, bf16[1024,19200]{1,0:T(8,128)(2,1)} %bitcast.121), kind=kOutput, calls=%fused_computation.45 | convolution fusion | flops 2156920832 | bytes 15204352 | tf_op jit(solution)/shard_map/dot_general | solution.py:1064
  248.9 6.6 fusion.86
  256.1 6.7 fusion.18.refs_1_.refs_3_
  262.8 0.8 copy-done.9
  263.6 62.1 %shard_map.203 = (bf16[256,2304]{1,0:T(8,128)(2,1)S(1)}, bf16[256,512]{1,0:T(8,128)(2,1)S(1)}, bf16[2,4,128,128]{3,2,1,0:T(8,128)(2,1)S(1)}, bf16[2,2,4,128,128]...) custom-call(s32[2]{0:T(128)S(1)} %copy-done.28, f32[256,3200]{1,0:T(8,128)S(1)} %fusion.18.refs_1_.refs_3_, ...), custom_call_target="tpu_custom_call" | custom-call | tf_op jit(solution)/shard_map/pallas_call | solution.py:737
  325.7 4.5 fusion.87
  330.6 0.7 copy-done.30
  331.6 5.9 fusion.6
  337.6 2.0 copy-done.74
  339.5 4.8 convolution_convert_fusion
  344.5 0.7 reshape.273
  345.2 0.5 compare_select_fusion
  345.8 0.6 select_select_fusion
  346.4 1.3 bitcast_convert_fusion
  347.7 13.8 %reduce-scatter.4.cloned.1.call-done = bf16[512,4096]{1,0:T(8,128)(2,1)} async-done(((bf16[1024,4096]{1,0:T(8,128)(2,1)}), bf16[512,4096]{1,0:T(8,128)(2,1)}) %reduce-scatter.4.cloned.1.call-update) | async-done | bytes 4194320 | tf_op jit(solution)/shard_map/reduce_scatter | solution.py:518
  361.6 7.4 %fusion.37.refs_9_ = bf16[256,4096]{1,0:T(8,128)(2,1)S(1)} fusion(f32[256,4096]{1,0:T(8,128)} %copy-done.74, bf16[256,1024]{1,0:T(8,128)(2,1)S(1)} %bitcast_convert_fusion, bf16[1024,8192]{1,0:T(8,128)(2,1)} %all-gather.2.cloned.1.call-done), kind=kOutput, calls=%fused_computation.43 | convolution fusion | flops 2168455168 | bytes 15204352 | tf_op jit(solution)/shard_map/dot_general | solution.py:1106
  369.1 7.2 multiply_reduce_fusion.2
  376.3 0.4 fusion.80
  376.7 3.7 fusion.38.refs_1_
  380.5 42.7 %shard_map.204 = (bf16[256,3328]{1,0:T(8,128)(2,1)S(1)}, bf16[256,256]{1,0:T(8,128)(2,1)S(1)}) custom-call(s32[2]{0:T(128)S(1)} %copy-done.28, f32[256,2304]{1,0:T(8,128)S(1)} %fusion.38.refs_1_, bf16[256,512]{1,0:T(8,128)(2,1)S(1)} %get-tuple-element.38.refs_2_, f32[256,3200]{1,0:T(8,128)} %copy-done.1, f32[256,40]{1,0:T(8,128)S(1)} %copy.62.refs_2_.refs_4_, ...), custom_call_target="tpu_custom_call" | custom-call | tf_op jit(solution)/shard_map/pallas_call | solution.py:946
  423.2 6.2 multiply_reduce_fusion.3
  429.5 0.4 fusion.79
  429.9 1.8 copy-done.75
  431.7 6.9 fusion.30.refs_13_
  438.6 6.7 multiply_reduce_fusion
  445.3 1.4 fusion.78
  446.7 3.8 fusion.42.refs_1_
  450.6 42.5 %shard_map.205 = (bf16[256,3328]{1,0:T(8,128)(2,1)S(1)}, bf16[256,256]{1,0:T(8,128)(2,1)S(1)}) custom-call(s32[2]{0:T(128)S(1)} %copy-done.28, f32[256,2304]{1,0:T(8,128)S(1)} %fusion.42.refs_1_, bf16[256,512]{1,0:T(8,128)(2,1)S(1)} %copy-done.21, f32[256,3200]{1,0:T(8,128)} %copy-done, f32[256,40]{1,0:T(8,128)S(1)} %copy.59.refs_2_.refs_4_, ...), custom_call_target="tpu_custom_call" | custom-call | tf_op jit(solution)/shard_map/pallas_call | solution.py:946
  493.1 0.6 copy-done.26
  493.9 7.1 multiply_reduce_fusion.1
  501.5 0.7 stack.65
  502.2 0.7 stack.66
  502.8 0.7 stack.63
  503.5 0.7 stack.64
  504.4 0.9 pad.22.clone
  505.3 0.7 broadcast_multiply_fusion
  506.0 0.7 broadcast_multiply_fusion.1
  506.6 2.9 add_convert_fusion
  509.5 8.5 %fusion.65 = bf16[256,1024]{1,0:T(8,128)(2,1)} fusion(f32[256,1024]{1,0:T(8,128)} %copy-done.30, bf16[1024,8192]{1,0:T(8,128)(2,1)} %all-gather.2.cloned.1.call-done, f32[256,4096]{1,0:T(8,128)} %copy-done.74), kind=kOutput, calls=%fused_computation.66 | convolution fusion | flops 2157445120 | bytes 14155776 | tf_op jit(solution)/shard_map/dot_general | solution.py:89
  518.1 5.4 reduce-scatter.8.cloned.1.call-done
  523.5 1.0 copy-done.8
  524.5 1.0 copy-done.10
  525.6 1.0 copy-done.12
  526.6 0.9 copy-done.15
  527.5 0.9 copy-done.25
  528.5 0.9 copy-done.27
  529.4 186.5 %shard_map.206 = f32[32,23552]{1,0:T(8,128)} custom-call(bf16[256,1024]{1,0:T(8,128)(2,1)S(1)} %copy-done.10, bf16[256,1024]{1,0:T(8,128)(2,1)S(1)} %get-tuple-element.83.refs_1_, bf16[256,1024]{1,0:T(8,128)(2,1)S(1)} %copy-done.12, bf16[256,1024]{1,0:T(8,128)(2,1)S(1)} %copy-done.6, bf16[256,1024]{1,0:T(8,128)(2,1)S(1)} %get-tuple-element.79.refs_4_, ...), custom_call_target="tpu_custom_call" | custom-call | tf_op jit(solution)/shard_map/pallas_call | solution.py:489
  715.9 0.8 slice_bitcast_fusion.8
  716.8 1.7 slice_bitcast_fusion
  718.7 0.7 fusion.74
  719.4 1.1 copy-done.38
  720.5 7.1 fusion.76
  (218 shorter events, 5.6 us)
Async XLA Ops:
  7.2 324.4 %all-gather.2.cloned.1.call-start = ((), (), s32[]{:S(2)}) async-start(), calls=%async_computation.3 | async-start | bytes 17301504 | tf_op jit(solution)/shard_map/all_gather | solution.py:1036
  7.2 3.3 copy-start.46
  7.2 3.3 copy-start.52
  7.2 3.4 copy-start.28
  9.6 171.5 %copy-start.43 = (bf16[2,128,1024]{2,1,0:T(8,128)(2,1)S(1)}, bf16[2,128,1024]{2,1,0:T(8,128)(2,1)}, u32[]{:S(2)}) copy-start(bf16[2,128,1024]{2,1,0:T(8,128)(2,1)} %param.11) | copy-start | bytes 1572868
  11.7 173.7 %copy-start.37 = (bf16[2,128,1024]{2,1,0:T(8,128)(2,1)S(1)}, bf16[2,128,1024]{2,1,0:T(8,128)(2,1)}, u32[]{:S(2)}) copy-start(bf16[2,128,1024]{2,1,0:T(8,128)(2,1)} %param.10) | copy-start | bytes 1572868
  180.8 180.7 %reduce-scatter.4.cloned.1.call-start = ((), (), s32[]{:S(2)}) async-start(), calls=%async_computation.4 | async-start | bytes 12582912 | tf_op jit(solution)/shard_map/reduce_scatter | solution.py:518
  185.6 5.7 copy-start.65
  185.9 5.4 copy-start.67
  192.1 47.4 %copy-start = (f32[256,3200]{1,0:T(8,128)}, f32[256,3200]{1,0:T(8,128)S(1)}, u32[]{:S(2)}) copy-start(f32[256,3200]{1,0:T(8,128)S(1)} %fusion.22.refs_1_.refs_3_) | copy-start | bytes 9830404
  234.3 5.3 copy-start.2
  234.3 5.3 copy-start.16
  234.3 5.3 copy-start.18
  234.3 5.3 copy-start.20
  234.3 5.3 copy-start.22
  239.6 9.3 %copy-start.32 = (f32[256,1024]{1,0:T(8,128)}, f32[256,1024]{1,0:T(8,128)S(1)}, u32[]{:S(2)}) copy-start(f32[256,1024]{1,0:T(8,128)S(1)} %get-tuple-element.115) | copy-start | bytes 3145732
  239.6 9.3 %copy-start.53 = (f32[256]{0:T(256)}, f32[256]{0:T(256)S(1)}, u32[]{:S(2)}) copy-start(f32[256]{0:T(256)S(1)} %broadcast_multiply_fusion.10) | copy-start | bytes 3076
  239.9 9.0 %copy-start.59 = (f32[256]{0:T(256)}, f32[256]{0:T(256)S(1)}, u32[]{:S(2)}) copy-start(f32[256]{0:T(256)S(1)} %add_rsqrt_fusion.2) | copy-start | bytes 3076
  240.1 8.8 %copy-start.7 = (bf16[256,1024]{1,0:T(8,128)(2,1)}, bf16[256,1024]{1,0:T(8,128)(2,1)S(1)}, u32[]{:S(2)}) copy-start(bf16[256,1024]{1,0:T(8,128)(2,1)S(1)} %add_convert_fusion.3.refs_5_) | copy-start | bytes 1572868
  248.9 6.6 copy-start.40
  255.5 70.2 %copy-start.35 = (f32[256,1024]{1,0:T(8,128)}, f32[256,1024]{1,0:T(8,128)S(1)}, u32[]{:S(2)}) copy-start(f32[256,1024]{1,0:T(8,128)S(1)} %get-tuple-element.119) | copy-start | bytes 3145732
  255.5 7.3 copy-start.55
  255.8 7.0 copy-start.61
  255.8 74.8 %copy-start.48 = (f32[1024,1]{0,1:T(1,128)}, f32[1024,1]{0,1:T(1,128)S(1)}, u32[]{:S(2)}) copy-start(f32[1024,1]{0,1:T(1,128)S(1)} %get-tuple-element.101) | copy-start | bytes 12292
  263.6 66.7 %copy-start.1 = (f32[256,3200]{1,0:T(8,128)}, f32[256,3200]{1,0:T(8,128)S(1)}, u32[]{:S(2)}) copy-start(f32[256,3200]{1,0:T(8,128)S(1)} %fusion.18.refs_1_.refs_3_) | copy-start | bytes 9830404
  325.7 4.6 copy-start.3
  330.3 7.2 copy-start.57
  330.6 7.0 copy-start.63
  331.6 6.0 copy-start.11
  344.4 149.4 %reduce-scatter.6.cloned.1.call-start = ((), (), s32[]{:S(2)}) async-start(), calls=%async_computation.5 | async-start | bytes 5242880 | tf_op jit(solution)/shard_map/reduce_scatter | solution.py:518
  361.5 7.5 %copy-start.31 = (f32[256,1024]{1,0:T(8,128)S(1)}, f32[256,1024]{1,0:T(8,128)}, u32[]{:S(2)}) copy-start(f32[256,1024]{1,0:T(8,128)} %copy-done.30) | copy-start | bytes 3145732
  361.5 161.9 %reduce-scatter.8.cloned.1.call-start = ((), (), s32[]{:S(2)}) async-start(), calls=%async_computation.6 | async-start | bytes 1310720 | tf_op jit(solution)/shard_map/reduce_scatter | solution.py:518
  361.6 7.5 %copy-start.49 = (f32[1024,1]{0,1:T(1,128)S(1)}, f32[1024,1]{0,1:T(1,128)}, u32[]{:S(2)}) copy-start(f32[1024,1]{0,1:T(1,128)} %copy-done.48) | copy-start | bytes 12292
  361.6 7.5 %copy-start.58 = (f32[256]{0:T(256)S(1)}, f32[256]{0:T(256)}, u32[]{:S(2)}) copy-start(f32[256]{0:T(256)} %copy-done.57) | copy-start | bytes 3076
  361.6 7.5 %copy-start.64 = (f32[256]{0:T(256)S(1)}, f32[256]{0:T(256)}, u32[]{:S(2)}) copy-start(f32[256]{0:T(256)} %copy-done.63) | copy-start | bytes 3076
  369.1 7.2 copy-start.41
  369.1 7.2 copy-start.34
  380.5 42.7 %copy-start.36 = (f32[256,1024]{1,0:T(8,128)S(1)}, f32[256,1024]{1,0:T(8,128)}, u32[]{:S(2)}) copy-start(f32[256,1024]{1,0:T(8,128)} %copy-done.35) | copy-start | bytes 3145732
  380.5 42.7 %copy-start.56 = (f32[256]{0:T(256)S(1)}, f32[256]{0:T(256)}, u32[]{:S(2)}) copy-start(f32[256]{0:T(256)} %copy-done.55) | copy-start | bytes 3076
  380.5 42.7 %copy-start.62 = (f32[256]{0:T(256)S(1)}, f32[256]{0:T(256)}, u32[]{:S(2)}) copy-start(f32[256]{0:T(256)} %copy-done.61) | copy-start | bytes 3076
  423.2 6.3 copy-start.13
  423.2 6.3 copy-start.24
  431.7 6.9 copy-start.33
  431.7 6.9 copy-start.54
  431.7 6.9 copy-start.60
  438.6 6.7 copy-start.42
  446.7 3.9 copy-start.17
  446.7 3.9 copy-start.19
  446.7 3.9 copy-start.21
  446.7 3.9 copy-start.23
  450.6 43.2 %copy-start.66 = (f32[256]{0:T(256)S(1)}, f32[256]{0:T(256)}, u32[]{:S(2)}) copy-start(f32[256]{0:T(256)} %copy-done.65) | copy-start | bytes 3076
  450.6 43.2 %copy-start.68 = (f32[256]{0:T(256)S(1)}, f32[256]{0:T(256)}, u32[]{:S(2)}) copy-start(f32[256]{0:T(256)} %copy-done.67) | copy-start | bytes 3076
  493.8 7.2 copy-start.14
  493.8 7.2 copy-start.70
  493.8 7.2 copy-start.69
  493.9 7.2 copy-start.72
  493.9 7.2 copy-start.71
  509.5 14.0 %copy-start.4 = (bf16[256,2304]{1,0:T(8,128)(2,1)S(1)}, bf16[256,2304]{1,0:T(8,128)(2,1)}, u32[]{:S(2)}) copy-start(bf16[256,2304]{1,0:T(8,128)(2,1)} %copy-done.3) | copy-start | bytes 3538948
  509.5 14.0 %copy-start.6 = (bf16[256,1024]{1,0:T(8,128)(2,1)S(1)}, bf16[256,1024]{1,0:T(8,128)(2,1)}, u32[]{:S(2)}) copy-start(bf16[256,1024]{1,0:T(8,128)(2,1)} %copy-done.5) | copy-start | bytes 1572868
  529.4 190.1 %copy-start.39 = (f32[2,32,13568]{2,1,0:T(8,128)S(1)}, f32[2,32,13568]{2,1,0:T(8,128)}, u32[]{:S(2)}) copy-start(f32[2,32,13568]{2,1,0:T(8,128)} %param.16) | copy-start | bytes 10420228
  715.9 2.7 slice-start
  716.8 2.7 copy-start.29
  716.8 3.7 copy-start.38
  716.8 3.7 copy-start.45
  (17 other events, 24.0 us)
Sparse Core Ops, SparseCore 0:
  180.9 148.5 all-gather.1
  344.5 16.9 reduce-scatter.3
  364.7 53.9 reduce-scatter.5
  493.9 29.4 reduce-scatter.7
